TPU v7x, 32 devices: a whole 2x2x4 slice. The times are simulated.
32 devices in a mesh: band: 4 (over y, x), patch: 8 (over z, core).
Axes of the slice: x: 2, y: 2, z: 4, core: 2. Of those that a mesh axis runs over, the one named last changes fastest.
Arguments:
- emissivity: float32 [32, 65536], P('band', 'patch'), may hold values from 0.1 to 0.9
- blackbody: float32 [32, 65536], P('band', 'patch'), may hold values from 0.2 to 2
- loss_weights: float32 [32, 65536], P('band', 'patch'), may hold values from 0.5 to 1.5
- view_blocks: bfloat16 [8, 4, 8, 16, 256, 256], P('patch', 'band'), may hold values from 0 to 0.012207031
- column_blocks: int32 [8, 4, 8, 16], P('patch', 'band'), may hold values from 0 to 255, as said below
- patch_owner: int32 [8, 4, 2048, 1], P('patch', 'band'), may hold values from 0 to 31; in each aligned block of 2048 rows (0 to 2047, 2048 to 4095, ..., all dimensions but the last counted through in order) at most 192 rows name the same one
- patch_surface: int32 [8, 4, 2048], P('patch', 'band'), may hold values from 0 to 1023
Outputs:
- radiosity: float32 [32, 8, 4, 2048], P(None, 'patch', 'band')
- surface_grad: float32 [32, 32768], P(None, ('band', 'patch'))
Inputs may be any that keep to these rules, and one draw needn't show every extreme that they name: column_blocks[g, s, r] lists 16 different row-block indices, all among the 96 row blocks of patch groups g - 1, g and g + 1, wrapping around the 8 groups. `patch_owner`: among the 2048 patches of one row-block range no owner is named more than 192 times.
All inputs are finite; a program needn't handle non-finite values.
Results may differ from a plain program's by a relative error of at most 0.0005.
Values may be sent and summed in bfloat16 or wider, within the bound.
No kernel may reach another device: no remote copies, remote signals or barrier semaphores. Data moves between devices by JAX's collectives and lax.ppermute only.
A program may use at most 128 MiB of HBM per device.

v0:
```python
import jax
import jax.numpy as jnp
from jax import lax
from jax.sharding import PartitionSpec as P


def passed_along(block, axis, distance):
    devices = range(lax.axis_size(axis))
    route = [((i - distance) % len(devices), i) for i in devices]
    return lax.ppermute(block, axis, route)


def body(
    emissivity, blackbody, loss_weights, view_blocks, column_blocks, patch_owner, patch_surface
):
    emissive, planck, weighting = (
        lax.all_to_all(emissivity, "band", split_axis=1, concat_axis=0, tiled=True),
        lax.all_to_all(blackbody, "band", split_axis=1, concat_axis=0, tiled=True),
        lax.all_to_all(loss_weights, "band", split_axis=1, concat_axis=0, tiled=True),
    )
    band_count = emissive.shape[0]
    patch_rows = emissive.shape[1]
    rb_count = view_blocks.shape[2]
    depth = view_blocks.shape[3]
    width = view_blocks.shape[4]
    split_count = lax.axis_size("band")
    group_count = lax.axis_size("patch")
    per_group = split_count * rb_count
    block_total = group_count * per_group
    window_start = (lax.axis_index("patch") - 1) * per_group
    offsets = jnp.mod(column_blocks.reshape(rb_count, depth) - window_start, block_total)
    flat_offsets = offsets.reshape(rb_count * depth)
    matrix = view_blocks.reshape(rb_count, depth, width, width)
    emission = emissive * planck
    reflect = 1.0 - emissive

    def window(vector):
        gathered = lax.all_gather(vector, "band", axis=1, tiled=True)
        lower_rows = passed_along(gathered, "patch", 1)
        upper_rows = passed_along(gathered, "patch", -1)
        joined = jnp.concatenate([lower_rows, gathered, upper_rows], axis=1)
        return joined.reshape(band_count, 3 * per_group, width)

    def forward(vector):
        blocks = window(vector)
        picked = blocks[:, offsets]
        result = jnp.einsum("rkij,brkj->bri", matrix, picked, preferred_element_type=jnp.float32)
        return result.reshape(band_count, patch_rows)

    def adjoint(vector):
        partial_terms = jnp.einsum(
            "rkij,bri->brkj",
            matrix,
            vector.reshape(band_count, rb_count, width),
            preferred_element_type=jnp.float32,
        )
        empty = jnp.zeros((band_count, 3 * per_group, width), jnp.float32)
        totals = empty.at[:, flat_offsets].add(
            partial_terms.reshape(band_count, rb_count * depth, width)
        )
        totals = totals.reshape(band_count, 3, split_count, patch_rows)
        from_upper = passed_along(totals[:, 0].astype(jnp.bfloat16), "patch", -1).astype(
            jnp.float32
        )
        from_lower = passed_along(totals[:, 2], "patch", 1)
        combined = totals[:, 1] + from_upper + from_lower
        return lax.psum_scatter(combined, "band", scatter_dimension=1, tiled=True).reshape(
            band_count, patch_rows
        )

    incident_zero = forward(emission.astype(jnp.bfloat16))
    rad_one = emission + reflect * incident_zero
    incident_one = forward(rad_one.astype(jnp.bfloat16))
    radiosity = emission + reflect * incident_one
    adjoint_one = adjoint((reflect * weighting).astype(jnp.bfloat16))
    adjoint_zero = adjoint((reflect * adjoint_one).astype(jnp.bfloat16))
    gradient = (weighting + adjoint_one + adjoint_zero) * planck - (
        weighting * incident_one + adjoint_one * incident_zero
    )
    device_count = split_count * group_count
    capacity = max(2, 3 * patch_rows // device_count)
    surface_count = patch_rows // 2
    owners = patch_owner.reshape(patch_rows)
    locals_index = patch_surface.reshape(patch_rows)
    owner_hits = (owners[:, None] == jnp.arange(device_count, dtype=jnp.int32)[None, :]).astype(
        jnp.int32
    )
    running = jnp.cumsum(owner_hits, axis=0)
    slot_index = jnp.sum(running * owner_hits, axis=1) - 1
    send_values = (
        jnp.zeros((band_count, device_count, capacity), jnp.float32)
        .at[:, owners, slot_index]
        .set(gradient)
    )
    send_labels = (
        jnp.full((1, device_count, capacity), surface_count, jnp.int32)
        .at[0, owners, slot_index]
        .set(locals_index)
    )
    got_values, got_labels = (
        lax.all_to_all(send_values, ("band", "patch"), split_axis=1, concat_axis=1, tiled=True),
        lax.all_to_all(send_labels, ("band", "patch"), split_axis=1, concat_axis=1, tiled=True),
    )
    flat_values = got_values.reshape(band_count, device_count * capacity)
    flat_labels = got_labels.reshape(device_count * capacity)
    surface_sums = jax.ops.segment_sum(flat_values.T, flat_labels, surface_count + 1)[
        :surface_count
    ].T
    surface_counts = jax.ops.segment_sum(
        jnp.ones((device_count * capacity,), jnp.float32), flat_labels, surface_count + 1
    )[:surface_count]
    surface_grad = surface_sums / jnp.maximum(surface_counts, 1.0)[None, :]
    return (radiosity.reshape(band_count, 1, 1, patch_rows), surface_grad)


def solution(mesh):
    in_specs = (
        P("band", "patch"),
        P("band", "patch"),
        P("band", "patch"),
        P("patch", "band", None, None, None, None),
        P("patch", "band", None, None),
        P("patch", "band", None, None),
        P("patch", "band", None),
    )
    out_specs = (P(None, "patch", "band", None), P(None, ("band", "patch")))
    return jax.shard_map(body, mesh=mesh, in_specs=in_specs, out_specs=out_specs, check_vma=False)
```

profile of v0, /device:TPU:0, one launch (start us, length us, event | category | flops | bytes accessed | tf_op | source)
XLA Modules:
  0.0 335.8 jit_solution(3225798159353689433)
XLA Ops:
  7.2 5.2 %all-to-all-start = ((f32[8,4,2048]{2,0,1:T(8,128)}), f32[8,4,2048]{2,0,1:T(8,128)S(1)}, u32[]{:S(2)}, u32[]{:S(2)}) async-start(f32[8,4,2048]{2,0,1:T(8,128)} %bitcast.215), calls=%async_computation | async-start | bytes 524288 | tf_op jit(solution)/shard_map/all_to_all | solution.py:17
  14.0 9.1 %reduce-window.6 = s32[32,16,128]{2,1,0:T(8,128)S(1)} reduce-window(s32[32,16,128]{2,1,0:T(8,128)S(1)} %fusion.35, s32[]{:T(128)} %constant.21.clone.1), window={size=1x1x128 pad=0_0x0_0x127_0}, to_apply=%region_0.1 | reduce-window | flops 8323072 | bytes 524292 | tf_op jit(solution)/shard_map/reduce-window
  27.0 8.2 %scatter_custom_fusion.4 = s32[6144]{0:T(1024)S(1)} fusion(s32[2048]{0:T(1024)S(1)} %broadcast_select_fusion.1, s32[2048]{0:T(1024)} %bitcast.222, s32[]{:T(128)} %constant.29.clone.1), kind=kCustom, calls=%fused_computation.78 | custom fusion | bytes 25088
  36.0 4.2 %all-to-all-start.3 = ((f32[8,4,2048]{2,0,1:T(8,128)}), f32[8,4,2048]{2,0,1:T(8,128)S(1)}, u32[]{:S(2)}, u32[]{:S(2)}) async-start(f32[8,4,2048]{2,0,1:T(8,128)} %bitcast.30), calls=%async_computation.3 | async-start | bytes 524288 | tf_op jit(solution)/shard_map/all_to_all | solution.py:19
  40.4 5.2 %all-to-all-done.3 = f32[8,4,2048]{2,0,1:T(8,128)S(1)} async-done(((f32[8,4,2048]{2,0,1:T(8,128)}), f32[8,4,2048]{2,0,1:T(8,128)S(1)}, u32[]{:S(2)}, u32[]{:S(2)}) %all-to-all-start.3) | async-done | bytes 262176 | tf_op jit(solution)/shard_map/all_to_all | solution.py:19
  45.6 4.1 %all-to-all-start.1 = ((f32[8,4,2048]{2,0,1:T(8,128)}), f32[8,4,2048]{2,0,1:T(8,128)}, u32[]{:S(2)}, u32[]{:S(2)}) async-start(f32[8,4,2048]{2,0,1:T(8,128)} %bitcast.2), calls=%async_computation.1 | async-start | bytes 524288 | tf_op jit(solution)/shard_map/all_to_all | solution.py:18
  49.8 10.6 %fusion.2 = f32[8,32,16,256]{3,1,2,0:T(8,128)} fusion(bf16[1,1,8,16,256,256]{5,4,3,2,1,0:T(8,128)(2,1)} %param.10, bf16[32,8,256,1]{2,1,0,3:T(8,128)(2,1)S(1)} %bitcast.214), kind=kOutput, calls=%fused_computation.10 | convolution fusion | flops 536870912 | bytes 21102592 | tf_op jit(solution)/shard_map/rkij,bri->brkj/dot_general | solution.py:51
  60.8 13.5 %scatter_fusion = f32[32,96,256]{2,0,1:T(8,128)S(1)} fusion(f32[32,96,256]{2,0,1:T(8,128)S(1)} %broadcast.223.clone, s32[128]{0:T(128)S(1)} %fusion.45, f32[128,32,256]{2,1,0:T(8,128)} %bitcast.195), kind=kCustom, calls=%fused_computation.2 | custom fusion | flops 1048576 | bytes 12583424 | tf_op jit(solution)/shard_map/scatter-add | solution.py:58
  74.3 3.5 %copy.102 = f32[32,96,256]{2,1,0:T(8,128)} copy(f32[32,96,256]{2,0,1:T(8,128)S(1)} %scatter_fusion) | data formatting | bytes 6291456 | tf_op jit(solution)/shard_map/scatter-add | solution.py:58
  77.8 3.4 %reshape.298 = f32[32,3,4,2048]{3,2,1,0:T(4,128)S(1)} reshape(f32[32,96,256]{2,1,0:T(8,128)} %copy.102) | data formatting | bytes 6291456 | tf_op jit(solution)/shard_map/reshape | solution.py:61
  81.2 1.5 fusion.47
  83.7 3.5 %collective-permute-start.4 = (bf16[32,4,2048]{2,1,0:T(4,128)(2,1)}, bf16[32,4,2048]{2,1,0:T(4,128)(2,1)S(1)}, u32[]{:S(2)}, u32[]{:S(2)}) collective-permute-start(bf16[32,4,2048]{2,1,0:T(4,128)(2,1)} %fusion.17), channel_id=1, source_target_pairs={{1,0},{2,1},{3,2},{4,3},{5,4},{6,5},{7,6},{0,7},{9,8},{10,9},{11,1... | collective-permute-start | bytes 1572872 | tf_op jit(solution)/shard_map/ppermute | solution.py:10
  87.2 4.5 %all-to-all-start.2 = ((s32[1,32,192]{2,0,1:T(1,128)}), s32[1,32,192]{2,0,1:T(1,128)S(1)}, u32[]{:S(2)}, u32[]{:S(2)}) async-start(s32[1,32,192]{2,0,1:T(1,128)} %reshape.309), calls=%async_computation.2 | async-start | bytes 65536 | tf_op jit(solution)/shard_map/all_to_all | solution.py:102
  92.7 10.4 %all_gather.6 = bf16[32,8192]{1,0:T(8,128)(2,1)S(1)} all-gather(bf16[32,2048]{1,0:T(8,128)(2,1)S(1)} %fusion.38), channel_id=1, replica_groups=mesh['band'=4,'patch'=8] {'band'}, dimensions={1}, use_global_device_ids=true | all-gather | bytes 655360 | tf_op jit(solution)/shard_map/all_gather | solution.py:38
  103.2 3.5 %collective-permute-start.1 = (bf16[32,8192]{1,0:T(8,128)(2,1)S(1)}, bf16[32,8192]{1,0:T(8,128)(2,1)S(1)}, u32[]{:S(2)}, u32[]{:S(2)}) collective-permute-start(bf16[32,8192]{1,0:T(8,128)(2,1)S(1)} %all_gather.6), channel_id=1, source_target_pairs={{1,0},{2,1},{3,2},{4,3},{5,4},{6,5},{7,6},{0,7},{9,8},{10,9},{11,1... | collective-permute-start | bytes 1572872 | tf_op jit(solution)/shard_map/ppermute | solution.py:10
  106.7 2.0 fusion.16
  108.7 1.6 copy.105
  110.5 6.7 %collective-permute-done = bf16[32,8192]{1,0:T(8,128)(2,1)S(1)} collective-permute-done((bf16[32,8192]{1,0:T(8,128)(2,1)S(1)}, bf16[32,8192]{1,0:T(8,128)(2,1)S(1)}, u32[]{:S(2)}, u32[]{:S(2)}) %collective-permute-start) | collective-permute-done | bytes 524320 | tf_op jit(solution)/shard_map/ppermute | solution.py:10
  117.4 1.4 copy.163
  118.7 2.1 gather_fusion
  120.9 10.9 %fusion.10 = f32[8,4,8,256]{3,2,1,0:T(8,128)S(1)} fusion(bf16[32,8,16,256]{3,0,2,1:T(8,128)(2,1)S(1)} %bitcast.198, bf16[1,1,8,16,256,256]{5,4,3,2,1,0:T(8,128)(2,1)} %param.10), kind=kOutput, calls=%fused_computation.22 | convolution fusion | flops 536870912 | bytes 19136512 | tf_op jit(solution)/shard_map/rkij,brkj->bri/dot_general | solution.py:47
  132.5 4.0 %reduce-scatter.7.cloned.1.call-done = f32[32,1,2048]{2,0,1:T(8,128)} async-done(((f32[32,4,2048]{2,0,1:T(8,128)}), f32[32,1,2048]{2,0,1:T(8,128)}) %reduce-scatter.7.cloned.1.call-update) | async-done | bytes 262160
  136.5 1.0 copy.137
  137.6 10.6 %fusion = f32[8,32,16,256]{3,1,2,0:T(8,128)} fusion(bf16[1,1,8,16,256,256]{5,4,3,2,1,0:T(8,128)(2,1)} %param.10, bf16[32,8,256,1]{2,1,0,3:T(8,128)(2,1)S(1)} %bitcast.213), kind=kOutput, calls=%fused_computation.8 | convolution fusion | flops 536870912 | bytes 21102592 | tf_op jit(solution)/shard_map/rkij,bri->brkj/dot_general | solution.py:51
  148.6 13.5 %scatter_fusion.1 = f32[32,96,256]{2,0,1:T(8,128)S(1)} fusion(f32[32,96,256]{2,0,1:T(8,128)S(1)} %broadcast.223, s32[128]{0:T(128)S(1)} %fusion.45, f32[128,32,256]{2,1,0:T(8,128)} %bitcast.194), kind=kCustom, calls=%fused_computation.3 | custom fusion | flops 1048576 | bytes 12583424 | tf_op jit(solution)/shard_map/scatter-add | solution.py:58
  162.0 3.5 %copy.107 = f32[32,96,256]{2,1,0:T(8,128)} copy(f32[32,96,256]{2,0,1:T(8,128)S(1)} %scatter_fusion.1) | data formatting | bytes 6291456 | tf_op jit(solution)/shard_map/scatter-add | solution.py:58
  165.5 3.4 %reshape.302 = f32[32,3,4,2048]{3,2,1,0:T(4,128)S(1)} reshape(f32[32,96,256]{2,1,0:T(8,128)} %copy.107) | data formatting | bytes 6291456 | tf_op jit(solution)/shard_map/reshape | solution.py:61
  169.4 3.6 %collective-permute-start.6 = (bf16[32,4,2048]{2,1,0:T(4,128)(2,1)S(1)}, bf16[32,4,2048]{2,1,0:T(4,128)(2,1)S(1)}, u32[]{:S(2)}, u32[]{:S(2)}) collective-permute-start(bf16[32,4,2048]{2,1,0:T(4,128)(2,1)S(1)} %fusion.18), channel_id=1, source_target_pairs={{1,0},{2,1},{3,2},{4,3},{5,4},{6,5},{7,6},{0,7},{9,8},{10,9},{11,1... | collective-permute-start | bytes 1572872 | tf_op jit(solution)/shard_map/ppermute | solution.py:10
  174.0 10.6 %all_gather.7 = bf16[32,8192]{1,0:T(8,128)(2,1)S(1)} all-gather(bf16[32,2048]{1,0:T(8,128)(2,1)S(1)} %fusion.33), channel_id=1, replica_groups=mesh['band'=4,'patch'=8] {'band'}, dimensions={1}, use_global_device_ids=true | all-gather | bytes 655360 | tf_op jit(solution)/shard_map/all_gather | solution.py:38
  184.6 3.5 %collective-permute-start.3 = (bf16[32,8192]{1,0:T(8,128)(2,1)S(1)}, bf16[32,8192]{1,0:T(8,128)(2,1)S(1)}, u32[]{:S(2)}, u32[]{:S(2)}) collective-permute-start(bf16[32,8192]{1,0:T(8,128)(2,1)S(1)} %all_gather.7), channel_id=1, source_target_pairs={{1,0},{2,1},{3,2},{4,3},{5,4},{6,5},{7,6},{0,7},{9,8},{10,9},{11,1... | collective-permute-start | bytes 1572872 | tf_op jit(solution)/shard_map/ppermute | solution.py:10
  188.2 4.1 %collective-permute-done.7 = f32[32,4,2048]{2,1,0:T(4,128)S(1)} collective-permute-done((f32[32,4,2048]{2,1,0:T(4,128)S(1)}, f32[32,4,2048]{2,1,0:T(4,128)S(1)}, u32[]{:S(2)}, u32[]{:S(2)}) %collective-permute-start.7) | collective-permute-done | bytes 1048608 | tf_op jit(solution)/shard_map/ppermute | solution.py:10
  192.7 1.6 copy.110
  194.3 7.7 %collective-permute-done.2 = bf16[32,8192]{1,0:T(8,128)(2,1)S(1)} collective-permute-done((bf16[32,8192]{1,0:T(8,128)(2,1)S(1)}, bf16[32,8192]{1,0:T(8,128)(2,1)S(1)}, u32[]{:S(2)}, u32[]{:S(2)}) %collective-permute-start.2) | collective-permute-done | bytes 524320 | tf_op jit(solution)/shard_map/ppermute | solution.py:10
  202.1 1.4 copy.162
  203.5 2.2 gather_fusion.1
  205.7 10.9 %fusion.4 = f32[8,32,256,1]{2,1,3,0:T(8,128)S(1)} fusion(bf16[32,8,16,256]{3,0,2,1:T(8,128)(2,1)S(1)} %bitcast.197, bf16[1,1,8,16,256,256]{5,4,3,2,1,0:T(8,128)(2,1)} %param.10), kind=kOutput, calls=%fused_computation.12 | convolution fusion | flops 536870912 | bytes 19136512 | tf_op jit(solution)/shard_map/rkij,brkj->bri/dot_general | solution.py:47
  216.6 4.1 %reduce-scatter.9.cloned.1.call-done = f32[32,1,2048]{2,0,1:T(8,128)} async-done(((f32[32,4,2048]{2,0,1:T(8,128)}), f32[32,1,2048]{2,0,1:T(8,128)}) %reduce-scatter.9.cloned.1.call-update) | async-done | bytes 262160
  220.8 1.2 fusion.29
  222.0 1.3 copy.112
  223.3 6.7 %scatter_custom_fusion.5 = f32[32,6144]{0,1:T(8,128)S(1)} fusion(s32[2048]{0:T(1024)S(1)} %broadcast_select_fusion, f32[2048,32]{1,0:T(8,128)} %copy.112, f32[]{:T(128)} %constant.25.clone.1), kind=kCustom, calls=%fused_computation.20 | custom fusion | bytes 786944
  230.0 2.2 copy.113
  232.2 4.6 %all-to-all-start.4 = ((f32[32,32,192]{2,0,1:T(8,128)}), f32[32,32,192]{2,0,1:T(8,128)S(1)}, u32[]{:S(2)}, u32[]{:S(2)}) async-start(f32[32,32,192]{2,0,1:T(8,128)} %copy.113), calls=%async_computation.4 | async-start | bytes 2097152 | tf_op jit(solution)/shard_map/all_to_all | solution.py:101
  237.1 42.7 %scatter_custom_fusion.3 = f32[1025]{0:T(1024)S(1)} fusion(s32[6144]{0:T(1024)S(1)} %reshape.348, f32[6144]{0:T(1024)S(1)} %broadcast.242, f32[]{:T(128)} %constant.25.clone.1), kind=kCustom, calls=%fused_computation.87 | custom fusion | flops 6144 | bytes 4104 | tf_op jit(solution)/shard_map/scatter-add | solution.py:109
  279.7 1.1 copy.98
  283.5 1.3 reshape.305
  284.7 2.0 copy.115
  286.7 40.1 %scatter_custom_fusion.2 = f32[1025,32]{1,0:T(8,128)} fusion(s32[6144]{0:T(1024)S(1)} %reshape.348, f32[6144,32]{1,0:T(8,128)S(1)} %copy.115, f32[]{:T(128)} %constant.25.clone.1), kind=kCustom, calls=%fused_computation.37 | custom fusion | flops 196608 | bytes 131204 | tf_op jit(solution)/shard_map/scatter-add | solution.py:106
  326.9 1.2 fusion.19
  (82 shorter events, 16.1 us)
Async XLA Ops:
  7.2 19.7 %copy-start.7 = (s32[3]{0:T(128)S(1)}, s32[3]{0:T(128)}, u32[]{:S(2)}) copy-start(s32[3]{0:T(128)} %constant.59) | copy-start | bytes 40
  7.2 19.7 %copy-start.8 = (s32[3]{0:T(128)S(1)}, s32[3]{0:T(128)}, u32[]{:S(2)}) copy-start(s32[3]{0:T(128)} %constant.62) | copy-start | bytes 40
  7.2 28.8 %all-to-all-start = ((f32[8,4,2048]{2,0,1:T(8,128)}), f32[8,4,2048]{2,0,1:T(8,128)S(1)}, u32[]{:S(2)}, u32[]{:S(2)}) async-start(f32[8,4,2048]{2,0,1:T(8,128)} %bitcast.215), calls=%async_computation | async-start | bytes 524288 | tf_op jit(solution)/shard_map/all_to_all | solution.py:17
  36.0 9.6 %all-to-all-start.3 = ((f32[8,4,2048]{2,0,1:T(8,128)}), f32[8,4,2048]{2,0,1:T(8,128)S(1)}, u32[]{:S(2)}, u32[]{:S(2)}) async-start(f32[8,4,2048]{2,0,1:T(8,128)} %bitcast.30), calls=%async_computation.3 | async-start | bytes 524288 | tf_op jit(solution)/shard_map/all_to_all | solution.py:19
  40.3 20.1 %copy-start.5 = (f32[4,8,8,256]{3,2,1,0:T(8,128)}, f32[4,8,8,256]{3,2,1,0:T(8,128)S(1)}, u32[]{:S(2)}) copy-start(f32[4,8,8,256]{3,2,1,0:T(8,128)S(1)} %copy.135) | copy-start | bytes 786436
  45.6 14.8 %copy-start.3 = (f32[8,4,2048]{2,0,1:T(8,128)}, f32[8,4,2048]{2,0,1:T(8,128)S(1)}, u32[]{:S(2)}) copy-start(f32[8,4,2048]{2,0,1:T(8,128)S(1)} %all-to-all-done.3) | copy-start | bytes 786436
  45.6 41.6 %all-to-all-start.1 = ((f32[8,4,2048]{2,0,1:T(8,128)}), f32[8,4,2048]{2,0,1:T(8,128)}, u32[]{:S(2)}, u32[]{:S(2)}) async-start(f32[8,4,2048]{2,0,1:T(8,128)} %bitcast.2), calls=%async_computation.1 | async-start | bytes 524288 | tf_op jit(solution)/shard_map/all_to_all | solution.py:18
  82.7 24.1 %collective-permute-start.5 = (f32[32,4,2048]{2,1,0:T(4,128)}, f32[32,4,2048]{2,1,0:T(4,128)}, u32[]{:S(2)}, u32[]{:S(2)}) collective-permute-start(f32[32,4,2048]{2,1,0:T(4,128)} %get-tuple-element.19), channel_id=1, source_target_pairs={{7,0},{0,1},{1,2},{2,3},{3,4},{4,5},{5,6},{6,7},{15,8},{8,9},{9,10... | collective-permute-start | bytes 3145736 | tf_op jit(solution)/shard_map/ppermute | solution.py:10
  83.7 23.0 %collective-permute-start.4 = (bf16[32,4,2048]{2,1,0:T(4,128)(2,1)}, bf16[32,4,2048]{2,1,0:T(4,128)(2,1)S(1)}, u32[]{:S(2)}, u32[]{:S(2)}) collective-permute-start(bf16[32,4,2048]{2,1,0:T(4,128)(2,1)} %fusion.17), channel_id=1, source_target_pairs={{1,0},{2,1},{3,2},{4,3},{5,4},{6,5},{7,6},{0,7},{9,8},{10,9},{11,1... | collective-permute-start | bytes 1572872 | tf_op jit(solution)/shard_map/ppermute | solution.py:10
  87.2 145.0 %all-to-all-start.2 = ((s32[1,32,192]{2,0,1:T(1,128)}), s32[1,32,192]{2,0,1:T(1,128)S(1)}, u32[]{:S(2)}, u32[]{:S(2)}) async-start(s32[1,32,192]{2,0,1:T(1,128)} %reshape.309), calls=%async_computation.2 | async-start | bytes 65536 | tf_op jit(solution)/shard_map/all_to_all | solution.py:102
  91.7 44.8 %reduce-scatter.7.cloned.1.call-start = ((), (), s32[]{:S(2)}) async-start(), calls=%async_computation.7 | async-start | bytes 1310720
  103.2 14.1 %collective-permute-start = (bf16[32,8192]{1,0:T(8,128)(2,1)S(1)}, bf16[32,8192]{1,0:T(8,128)(2,1)S(1)}, u32[]{:S(2)}, u32[]{:S(2)}) collective-permute-start(bf16[32,8192]{1,0:T(8,128)(2,1)S(1)} %all_gather.6), channel_id=1, source_target_pairs={{7,0},{0,1},{1,2},{2,3},{3,4},{4,5},{5,6},{6,7},{15,8},{8,9},{9,10... | collective-permute-start | bytes 1572872 | tf_op jit(solution)/shard_map/ppermute | solution.py:10
  103.2 14.1 %collective-permute-start.1 = (bf16[32,8192]{1,0:T(8,128)(2,1)S(1)}, bf16[32,8192]{1,0:T(8,128)(2,1)S(1)}, u32[]{:S(2)}, u32[]{:S(2)}) collective-permute-start(bf16[32,8192]{1,0:T(8,128)(2,1)S(1)} %all_gather.6), channel_id=1, source_target_pairs={{1,0},{2,1},{3,2},{4,3},{5,4},{6,5},{7,6},{0,7},{9,8},{10,9},{11,1... | collective-permute-start | bytes 1572872 | tf_op jit(solution)/shard_map/ppermute | solution.py:10
  110.3 110.5 %reduce-scatter.9.cloned.1.call-start = ((), (), s32[]{:S(2)}) async-start(), calls=%async_computation.8 | async-start | bytes 1310720
  120.9 16.7 %copy-start.6 = (f32[4,8,8,256]{3,2,1,0:T(8,128)S(1)}, f32[4,8,8,256]{3,2,1,0:T(8,128)}, u32[]{:S(2)}) copy-start(f32[4,8,8,256]{3,2,1,0:T(8,128)} %copy-done.5) | copy-start | bytes 786436
  169.0 4.0 %copy-start.1 = (f32[8,4,8,256]{3,2,0,1:T(8,128)S(1)}, f32[8,4,8,256]{3,2,0,1:T(8,128)}, u32[]{:S(2)}) copy-start(f32[8,4,8,256]{3,2,0,1:T(8,128)} %copy.133) | copy-start | bytes 786436
  169.1 23.1 %collective-permute-start.7 = (f32[32,4,2048]{2,1,0:T(4,128)S(1)}, f32[32,4,2048]{2,1,0:T(4,128)S(1)}, u32[]{:S(2)}, u32[]{:S(2)}) collective-permute-start(f32[32,4,2048]{2,1,0:T(4,128)S(1)} %get-tuple-element.17), channel_id=1, source_target_pairs={{7,0},{0,1},{1,2},{2,3},{3,4},{4,5},{5,6},{6,7},{15,8},{8,9},{9,10... | collective-permute-start | bytes 3145736 | tf_op jit(solution)/shard_map/ppermute | solution.py:10
  169.4 18.8 %collective-permute-start.6 = (bf16[32,4,2048]{2,1,0:T(4,128)(2,1)S(1)}, bf16[32,4,2048]{2,1,0:T(4,128)(2,1)S(1)}, u32[]{:S(2)}, u32[]{:S(2)}) collective-permute-start(bf16[32,4,2048]{2,1,0:T(4,128)(2,1)S(1)} %fusion.18), channel_id=1, source_target_pairs={{1,0},{2,1},{3,2},{4,3},{5,4},{6,5},{7,6},{0,7},{9,8},{10,9},{11,1... | collective-permute-start | bytes 1572872 | tf_op jit(solution)/shard_map/ppermute | solution.py:10
  184.6 17.4 %collective-permute-start.2 = (bf16[32,8192]{1,0:T(8,128)(2,1)S(1)}, bf16[32,8192]{1,0:T(8,128)(2,1)S(1)}, u32[]{:S(2)}, u32[]{:S(2)}) collective-permute-start(bf16[32,8192]{1,0:T(8,128)(2,1)S(1)} %all_gather.7), channel_id=1, source_target_pairs={{7,0},{0,1},{1,2},{2,3},{3,4},{4,5},{5,6},{6,7},{15,8},{8,9},{9,10... | collective-permute-start | bytes 1572872 | tf_op jit(solution)/shard_map/ppermute | solution.py:10
  184.6 17.4 %collective-permute-start.3 = (bf16[32,8192]{1,0:T(8,128)(2,1)S(1)}, bf16[32,8192]{1,0:T(8,128)(2,1)S(1)}, u32[]{:S(2)}, u32[]{:S(2)}) collective-permute-start(bf16[32,8192]{1,0:T(8,128)(2,1)S(1)} %all_gather.7), channel_id=1, source_target_pairs={{1,0},{2,1},{3,2},{4,3},{5,4},{6,5},{7,6},{0,7},{9,8},{10,9},{11,1... | collective-permute-start | bytes 1572872 | tf_op jit(solution)/shard_map/ppermute | solution.py:10
  205.7 15.1 %copy-start.2 = (f32[8,4,8,256]{3,2,0,1:T(8,128)S(1)}, f32[8,4,8,256]{3,2,0,1:T(8,128)}, u32[]{:S(2)}) copy-start(f32[8,4,8,256]{3,2,0,1:T(8,128)} %copy.133) | copy-start | bytes 786436
  205.7 15.1 %copy-start.4 = (f32[8,4,2048]{2,0,1:T(8,128)S(1)}, f32[8,4,2048]{2,0,1:T(8,128)}, u32[]{:S(2)}) copy-start(f32[8,4,2048]{2,0,1:T(8,128)} %copy-done.3) | copy-start | bytes 786436
  216.6 5.4 %copy-start = (f32[8,32,256,1]{2,1,3,0:T(8,128)}, f32[8,32,256,1]{2,1,3,0:T(8,128)S(1)}, u32[]{:S(2)}) copy-start(f32[8,32,256,1]{2,1,3,0:T(8,128)S(1)} %fusion.4) | copy-start | bytes 786436
  232.2 50.6 %all-to-all-start.4 = ((f32[32,32,192]{2,0,1:T(8,128)}), f32[32,32,192]{2,0,1:T(8,128)S(1)}, u32[]{:S(2)}, u32[]{:S(2)}) async-start(f32[32,32,192]{2,0,1:T(8,128)} %copy.113), calls=%async_computation.4 | async-start | bytes 2097152 | tf_op jit(solution)/shard_map/all_to_all | solution.py:101
Sparse Core Ops, SparseCore 0:
  110.4 26.0 reduce-scatter.6
  194.4 26.2 reduce-scatter.8
where the time goes:
time: 339 us; the launch traced here: 336 us
  other arithmetic  132 us (39%)
  local copies, waits for them, and re-layouts  56.3 us (17%)
  matrix products  43 us (13%)
  starting transfers between devices  37.1 us (11%)
  waiting for transfers between devices  31.9 us (9%)
  blocking collectives  21 us (6%)
  between operations  14.5 us (4%)
    scatter-add x1, other arithmetic, body(): jax.ops.segment_sum(jnp.ones((device_count * capacity,), jnp.float32), fl...  42.7 us
    scatter-add x1, other arithmetic, body(): jax.ops.segment_sum(flat_values.T, flat_labels, surface_count + 1)  40.1 us
    scatter-add x2, other arithmetic, adjoint(): empty.at[:, flat_offsets]  26.9 us
    dot_general x2, matrix products, forward(): jnp.einsum('rkij,brkj->bri', matrix, picked, preferred_element_type=jnp.f...  21.8 us
    dot_general x2, matrix products, adjoint(): jnp.einsum('rkij,bri->brkj', matrix, vector.reshape(band_count, rb_count,...  21.2 us
    all_gather x2, blocking collectives, window(): gathered = lax.all_gather(vector, 'band', axis=1, tiled=True)  21 us
    ppermute x8, waiting for transfers between devices, passed_along(): return lax.ppermute(block, axis, route)  18.5 us
    unnamed x25, local copies, waits for them, and re-layouts  18 us
  transfers between devices with their start and end apart: 15, of which 6 were waited for; matrix products, arithmetic and copies ran while one was open for 55% of the time, Pallas kernels for 0%

commit v1 on v0

v1 whole, which is shorter than its diff:
```python
import jax
import jax.numpy as jnp
from jax import lax
from jax.experimental import pallas as pl
from jax.experimental.pallas import tpu as pltpu
from jax.sharding import PartitionSpec as P

F32 = jnp.float32
BF16 = jnp.bfloat16
LANES = 128
MIB = 1 << 20
VMEM = pl.BlockSpec(memory_space=pltpu.VMEM)
SMEM = pl.BlockSpec(memory_space=pltpu.SMEM)


def local_kernel(kernel, outs, ins, scratch=(), limit=24 * MIB, flops=0, touched=0):
    return pl.pallas_call(
        kernel,
        out_shape=outs,
        in_specs=ins,
        out_specs=jax.tree.map(lambda _: VMEM, outs),
        scratch_shapes=scratch,
        compiler_params=pltpu.CompilerParams(vmem_limit_bytes=limit),
        cost_estimate=pl.CostEstimate(flops=flops, bytes_accessed=touched, transcendentals=0),
    )


def shape(dims, dtype):
    return jax.ShapeDtypeStruct(dims, dtype)


def nt(a, b):
    return lax.dot_general(a, b, (((1,), (1,)), ((), ())), preferred_element_type=F32)


def nn(a, b):
    return lax.dot_general(a, b, (((1,), (0,)), ((), ())), preferred_element_type=F32)


def body(
    emissivity, blackbody, loss_weights, view_blocks, column_blocks, patch_owner, patch_surface
):
    split = lax.axis_size("band")
    groups = lax.axis_size("patch")
    devices = split * groups
    part_bands = emissivity.shape[0]
    bands = part_bands * split
    rb_count, depth, width = view_blocks.shape[2:5]
    rows = rb_count * width
    per_group = split * rb_count
    capacity = max(2, 3 * rows // devices)
    surfaces = rows // 2
    pack = LANES // bands
    share = capacity // pack
    me = lax.axis_index("patch")

    def inner(block):
        return lax.ppermute(block, "patch", [(i, i ^ 1) for i in range(groups)])

    def outer(block):
        return lax.ppermute(
            block, "patch", [(i, (i + (1 if i % 2 else -1)) % groups) for i in range(groups)]
        )

    def exchange(block):
        return lax.all_to_all(block, "band", 0, 0)

    columns = column_blocks.reshape(rb_count * depth)
    column_group = columns // per_group
    third = jnp.where(column_group == me, 0, jnp.where(column_group == (me ^ 1), 1, 2))
    slots = third * per_group + columns % per_group
    matrix = view_blocks.reshape(rb_count, depth, width, width)
    block_shape = (rb_count, bands, width)
    gathered_shape = (split, rb_count, bands, width)
    pass_flops = 2 * bands * rb_count * depth * width * width

    def prepare(e_ref, b_ref, w_ref, small_ref, full_ref):
        for c in range(per_group):
            cut = slice(c * width, (c + 1) * width)
            owner, r = c // rb_count, c % rb_count
            e, b, w = e_ref[:, cut], b_ref[:, cut], w_ref[:, cut]
            start = (e * b).astype(BF16)
            for d in range(split):
                small_ref[d, c] = start
            small_ref[owner, per_group + r] = ((1.0 - e) * w).astype(BF16)
            full_ref[owner, 0, r] = e
            full_ref[owner, 1, r] = b
            full_ref[owner, 2, r] = w

    small, full = local_kernel(
        prepare,
        (
            shape((split, per_group + rb_count, part_bands, width), BF16),
            shape((split, 3, rb_count, part_bands, width), F32),
        ),
        [VMEM] * 3,
    )(emissivity, blackbody, loss_weights)
    small = exchange(small)
    full = exchange(full)

    def of(ref, which, r):
        return jnp.concatenate([ref[s, which, r] for s in range(split)], axis=0)

    def scatter_products(slots_ref, m_ref, own_ref, in_ref, out_ref, held, total):
        total[...] = jnp.zeros_like(total)

        def step(i, carry):
            for q in range(2):
                r = i * 2 + q
                u = held[r]
                for k in range(depth):
                    s = slots_ref[r * depth + k]
                    total[s] += nn(u, m_ref[r, k])
            return carry

        lax.fori_loop(0, rb_count // 2, step, 0)
        for s in range(split):
            at = s * rb_count
            own_ref[s] = total[at : at + rb_count]
            in_ref[s] = total[per_group + at : per_group + at + rb_count].astype(BF16)
            out_ref[s] = total[2 * per_group + at : 2 * per_group + at + rb_count].astype(BF16)

    part_outs = (shape(gathered_shape, F32), shape(gathered_shape, BF16), shape(gathered_shape, BF16))
    part_scratch = [pltpu.VMEM(block_shape, BF16), pltpu.VMEM((3 * per_group, bands, width), F32)]

    def adjoint_first(slots_ref, m_ref, small_ref, own_ref, in_ref, out_ref, held, total):
        for r in range(rb_count):
            u = [small_ref[s, per_group + r].astype(F32) for s in range(split)]
            held[r] = jnp.concatenate(u, axis=0).astype(BF16)
        scatter_products(slots_ref, m_ref, own_ref, in_ref, out_ref, held, total)

    def arrived(got_ref, far_ref, r):
        value = far_ref[r]
        for s in range(split):
            value = value + got_ref[s, r].astype(F32)
        return value

    def adjoint_second(
        slots_ref, m_ref, got_ref, far_ref, full_ref, one_ref, own_ref, in_ref, out_ref, held, total
    ):
        for r in range(rb_count):
            value = arrived(got_ref, far_ref, r)
            one_ref[r] = value
            held[r] = ((1.0 - of(full_ref, 0, r)) * value).astype(BF16)
        scatter_products(slots_ref, m_ref, own_ref, in_ref, out_ref, held, total)

    def collect(own, near, far):
        far = exchange(far)
        near = inner(near)
        far = outer(jnp.sum(far.astype(F32), axis=0))
        return exchange((own + near.astype(F32)).astype(BF16)), far

    def products(slots_ref, m_ref, held, finish):
        def step(i, carry):
            for q in range(2):
                r = i * 2 + q
                value = jnp.zeros((bands, width), F32)
                for k in range(depth):
                    value = value + nt(held[slots_ref[r * depth + k]], m_ref[r, k])
                finish(r, value)
            return carry

        lax.fori_loop(0, rb_count // 2, step, 0)

    def forward_first(slots_ref, m_ref, own_ref, in_ref, out_ref, full_ref, zero_ref, rad_ref, held):
        for third_index, ref in enumerate((own_ref, in_ref, out_ref)):

            def fill(c, carry, third_index=third_index, ref=ref):
                pieces = [ref[s, c].astype(F32) for s in range(split)]
                held[third_index * per_group + c] = jnp.concatenate(pieces, axis=0).astype(BF16)
                return carry

            lax.fori_loop(0, per_group, fill, 0)

        def finish(r, value):
            e, b = of(full_ref, 0, r), of(full_ref, 1, r)
            zero_ref[r] = value
            rad = (e * b + (1.0 - e) * value).astype(BF16)
            for d in range(split):
                rad_ref[d, r] = rad

        products(slots_ref, m_ref, held, finish)

    def forward_second(slots_ref, m_ref, own_ref, in_ref, out_ref, full_ref, one_ref, rad_ref, held):
        for third_index, ref in enumerate((own_ref, in_ref, out_ref)):
            for s in range(split):
                at = third_index * per_group + s * rb_count
                held[at : at + rb_count] = ref[s]

        def finish(r, value):
            e, b = of(full_ref, 0, r), of(full_ref, 1, r)
            one_ref[r] = value
            cut = pl.ds(pl.multiple_of(r * width, width), width)
            rad_ref[:, cut] = e * b + (1.0 - e) * value

        products(slots_ref, m_ref, held, finish)

    window_scratch = [pltpu.VMEM((3 * per_group, bands, width), BF16)]

    def route(owner_ref, surface_ref, place_ref, first_ref, label_ref):
        names = lax.broadcasted_iota(jnp.int32, (devices, width), 0)
        upper = (
            lax.broadcasted_iota(jnp.int32, (width, width), 0)
            <= lax.broadcasted_iota(jnp.int32, (width, width), 1)
        ).astype(BF16)
        hits, ranks = [], []
        count = jnp.zeros((devices, 1), F32)
        for c in range(rb_count):
            hit = (owner_ref[:, c * width : (c + 1) * width] == names).astype(F32)
            rank = nn(hit.astype(BF16), upper) + count
            count = rank[:, width - 1 : width]
            hits.append(hit)
            ranks.append(rank)
        below = (
            lax.broadcasted_iota(jnp.int32, (devices, devices), 1)
            < lax.broadcasted_iota(jnp.int32, (devices, devices), 0)
        ).astype(BF16)
        first = nn(below, jnp.broadcast_to(count, (devices, LANES)).astype(BF16))
        first_ref[...] = first.astype(jnp.int32)
        fixed = names.astype(F32) * capacity
        padded = []
        for c in range(rb_count):
            cut = slice(c * width, (c + 1) * width)
            rank = ranks[c] - 1.0
            place = jnp.sum(hits[c] * (rank + first[:, :1]), axis=0, keepdims=True)
            place_ref[:, cut] = place.astype(jnp.int32)
            slot = jnp.sum(hits[c] * (rank + fixed), axis=0, keepdims=True)
            padded.append(slot.astype(jnp.int32))
        padded = jnp.concatenate(padded, axis=1)
        surface = surface_ref[...]
        digit = lax.broadcasted_iota(jnp.int32, (8, rows), 0)
        digits = jnp.where(
            digit == 0, surface >> 8, jnp.where(digit == 1, surface & 255, 1)
        ).astype(F32).astype(BF16)

        def step(i, carry):
            wanted = lax.broadcasted_iota(jnp.int32, (width, rows), 0) + i * width
            chosen = jnp.where(padded == wanted, 1.0, 0.0).astype(BF16)
            found = nt(digits, chosen)
            label = jnp.where(found[2:3] > 0.5, found[0:1] * 256.0 + found[1:2], float(surfaces))
            cut = pl.ds(pl.multiple_of(i * width, width), width)
            label_ref[:, cut] = label.astype(jnp.int32)
            return carry

        lax.fori_loop(0, devices * capacity // width, step, 0)

    place, first, labels = local_kernel(
        route,
        (
            shape((1, rows), jnp.int32),
            shape((devices, LANES), jnp.int32),
            shape((1, devices * capacity), jnp.int32),
        ),
        [VMEM] * 2,
        flops=rows * devices * capacity * 4,
    )(patch_owner.reshape(1, rows), patch_surface.reshape(1, rows))
    first = first[:, 0]

    def pack_rows(
        first_ref,
        place_ref,
        got_ref,
        far_ref,
        adj_ref,
        zero_ref,
        one_ref,
        full_ref,
        send_ref,
        grad,
        ordered,
    ):
        for r in range(rb_count):
            b, w = of(full_ref, 1, r), of(full_ref, 2, r)
            a = adj_ref[r]
            value = (w + a + arrived(got_ref, far_ref, r)) * b - (w * one_ref[r] + a * zero_ref[r])
            high = value.astype(BF16).astype(F32)
            low = value - high
            both = jnp.concatenate([high] * pack + [low] * pack, axis=0)
            grad[:, r * width : (r + 1) * width] = both.astype(BF16)
        ordered[rows:] = jnp.zeros((capacity, LANES), F32)
        place_row = place_ref[...]

        def order(i, carry):
            wanted = lax.broadcasted_iota(jnp.int32, (width, rows), 0) + i * width
            chosen = jnp.where(place_row == wanted, 1.0, 0.0).astype(BF16)
            moved = nt(chosen, grad[...])
            cut = pl.ds(pl.multiple_of(i * width, width), width)
            ordered[cut] = moved[:, :LANES] + moved[:, LANES:]
            return carry

        lax.fori_loop(0, rb_count, order, 0)
        lane = lax.broadcasted_iota(jnp.int32, (share, LANES), 1) // bands

        def fill(o, carry):
            at = first_ref[o]
            value = ordered[pl.ds(at, share)]
            for q in range(1, pack):
                value = jnp.where(lane == q, ordered[pl.ds(at + q * share, share)], value)
            send_ref[o] = value
            return carry

        lax.fori_loop(0, devices, fill, 0)

    received = devices * share

    def choose(label_ref, chosen_ref, count_ref):
        ones = jnp.ones((8, received), BF16)

        def step(i, carry):
            wanted = lax.broadcasted_iota(jnp.int32, (LANES, received), 0) + i * LANES
            cut = pl.ds(pl.multiple_of(i * LANES, LANES), LANES)
            count = jnp.zeros((8, LANES), F32)
            for q in range(pack):
                chosen = jnp.where(label_ref[q : q + 1] == wanted, 1.0, 0.0).astype(BF16)
                chosen_ref[q, cut] = chosen
                count = count + nt(ones, chosen)
            count_ref[:, cut] = jnp.maximum(count, 1.0)
            return carry

        lax.fori_loop(0, surfaces // LANES, step, 0)

    def reduce_rows(chosen_ref, count_ref, got_ref, out_ref, parts):
        lane = lax.broadcasted_iota(jnp.int32, (received, LANES), 1) // bands
        value = got_ref[...]
        high = value.astype(BF16).astype(F32)
        low = value - high
        for q in range(pack):
            parts[q, :, :LANES] = jnp.where(lane == q, high, 0.0).astype(BF16)
            parts[q, :, LANES:] = jnp.where(lane == q, low, 0.0).astype(BF16)

        def step(i, carry):
            cut = pl.ds(pl.multiple_of(i * LANES, LANES), LANES)
            total = jnp.zeros((LANES, 2 * LANES), F32)
            for q in range(pack):
                total = total + nn(chosen_ref[q, cut], parts[q])
            turned = (total[:, :LANES] + total[:, LANES:]).T
            sums = turned[:bands]
            for q in range(1, pack):
                sums = sums + turned[q * bands : (q + 1) * bands]
            out_ref[:, cut] = sums / count_ref[:1, cut]
            return carry

        lax.fori_loop(0, surfaces // LANES, step, 0)

    own, near, far = local_kernel(
        adjoint_first, part_outs, [SMEM, VMEM, VMEM], part_scratch, flops=pass_flops
    )(slots, matrix, small)
    start = small[:, :per_group]
    start_in, start_out = inner(start), outer(start)
    got_one, far_one = collect(own, near, far)

    zero, rad = local_kernel(
        forward_first,
        (shape(block_shape, F32), shape(gathered_shape, BF16)),
        [SMEM] + [VMEM] * 5,
        window_scratch,
        flops=pass_flops,
    )(slots, matrix, start, start_in, start_out, full)
    rad = exchange(rad)
    rad_in, rad_out = inner(rad), outer(rad)

    adjoint_one, own, near, far = local_kernel(
        adjoint_second,
        (shape(block_shape, F32),) + part_outs,
        [SMEM] + [VMEM] * 4,
        part_scratch,
        flops=pass_flops,
    )(slots, matrix, got_one, far_one, full)
    got_zero, far_zero = collect(own, near, far)

    one, radiosity = local_kernel(
        forward_second,
        (shape(block_shape, F32), shape((bands, rows), F32)),
        [SMEM] + [VMEM] * 5,
        window_scratch,
        flops=pass_flops,
    )(slots, matrix, rad, rad_in, rad_out, full)

    labels = lax.all_to_all(labels.reshape(devices, capacity), ("band", "patch"), 0, 0, tiled=True)
    labels = jnp.swapaxes(labels.reshape(devices, pack, share), 0, 1).reshape(pack, received)
    chosen, counts = local_kernel(
        choose,
        (shape((pack, surfaces, received), BF16), shape((8, surfaces), F32)),
        [VMEM],
    )(labels)

    send = local_kernel(
        pack_rows,
        shape((devices, share, LANES), F32),
        [SMEM] + [VMEM] * 7,
        [pltpu.VMEM((2 * LANES, rows), BF16), pltpu.VMEM((rows + capacity, LANES), F32)],
    )(first, place, got_zero, far_zero, adjoint_one, zero, one, full)
    send = lax.all_to_all(send, ("band", "patch"), 0, 0, tiled=True)
    surface_grad = local_kernel(
        reduce_rows,
        shape((bands, surfaces), F32),
        [VMEM] * 3,
        [pltpu.VMEM((pack, received, 2 * LANES), BF16)],
    )(chosen, counts, send.reshape(received, LANES))
    return (radiosity.reshape(bands, 1, 1, rows), surface_grad)


def solution(mesh):
    in_specs = (
        P("band", "patch"),
        P("band", "patch"),
        P("band", "patch"),
        P("patch", "band", None, None, None, None),
        P("patch", "band", None, None),
        P("patch", "band", None, None),
        P("patch", "band", None),
    )
    out_specs = (P(None, "patch", "band", None), P(None, ("band", "patch")))
    return jax.shard_map(body, mesh=mesh, in_specs=in_specs, out_specs=out_specs, check_vma=False)
```

time: 339 us -> 189 us (0.56)
  other arithmetic: 132 us -> 7.85 us
  Pallas kernels: 0 us -> 52.3 us
  matrix products: 43 us -> 0 us
  local copies, waits for them, and re-layouts: 56.3 us -> 34.9 us
  between operations: 14.5 us -> 0.85 us
  blocking collectives: 21 us -> 13.1 us
  starting transfers between devices: 37.1 us -> 43.8 us
  waiting for transfers between devices: 31.9 us -> 35.4 us
    scatter-add x4 -> x0, other arithmetic: 110 us -> none  [the longest x1 42.7 us: body(): jax.ops.segment_sum(jnp.ones((device_count * capacity,), jnp.float32), fl...]
    pallas_call x0 -> x9, Pallas kernels: none -> 52.3 us  [the longest x1 10.5 us: body(): local_kernel(route, (shape((1, rows), jnp.int32), shape((devices, LANES),...]
    dot_general x4 -> x0, matrix products: 43 us -> none  [the longest x2 21.8 us: forward(): jnp.einsum('rkij,brkj->bri', matrix, picked, preferred_element_type=jnp.f...]
    all_to_all x5 -> x8, waiting for transfers between devices: 5.26 us -> 28.4 us  [the longest x6 16.8 us: exchange(): return lax.all_to_all(block, 'band', 0, 0)]
    all_gather x2 -> x0, blocking collectives: 21 us -> none  [window(): gathered = lax.all_gather(vector, 'band', axis=1, tiled=True)]
    unnamed x25 -> x29, local copies, waits for them, and re-layouts: 18 us -> 32.6 us
    all_to_all x5 -> x8, starting transfers between devices: 22.6 us -> 36.1 us  [the longest x6 24 us: exchange(): return lax.all_to_all(block, 'band', 0, 0)]
    all_to_all x0 -> x1, blocking collectives: none -> 13.1 us  [exchange(): return lax.all_to_all(block, 'band', 0, 0)]
  transfers between devices with their start and end apart: 15 -> 16, of which waited for: 6 -> 5; matrix products, arithmetic and copies ran while one was open for 55% -> 6% of each run, Pallas kernels for 0% -> 24%
where the time goes in v1:
time: 189 us; the launch traced here: 188 us
  Pallas kernels  52.3 us (28%)
  starting transfers between devices  43.8 us (23%)
  waiting for transfers between devices  35.4 us (19%)
  local copies, waits for them, and re-layouts  34.9 us (18%)
  blocking collectives  13.1 us (7%)
  other arithmetic  7.85 us (4%)
    unnamed x29, local copies, waits for them, and re-layouts  32.6 us
    all_to_all x6, starting transfers between devices, exchange(): return lax.all_to_all(block, 'band', 0, 0)  24 us
    all_to_all x6, waiting for transfers between devices, exchange(): return lax.all_to_all(block, 'band', 0, 0)  16.8 us
    all_to_all x1, blocking collectives, exchange(): return lax.all_to_all(block, 'band', 0, 0)  13.1 us
    all_to_all x1, waiting for transfers between devices, body(): send = lax.all_to_all(send, ('band', 'patch'), 0, 0, tiled=True)  11.6 us
    pallas_call x1, Pallas kernels, body(): local_kernel(route, (shape((1, rows), jnp.int32), shape((devices, LANES),...  10.5 us
    ppermute x4, starting transfers between devices, outer(): lax.ppermute(block, 'patch', [(i, (i + (1 if i % 2 else -1)) % groups) fo...  7.7 us
    pallas_call x1, Pallas kernels, body(): local_kernel(forward_first, (shape(block_shape, F32), shape(gathered_shap...  7.1 us
  transfers between devices with their start and end apart: 16, of which 5 were waited for; matrix products, arithmetic and copies ran while one was open for 6% of the time, Pallas kernels for 24%

profile of v1, /device:TPU:0, one launch (start us, length us, event | category | flops | bytes accessed | tf_op | source)
XLA Modules:
  0.0 188.2 jit_solution(14765452404905906034)
XLA Ops:
  0.6 0.9 copy-done.7
  1.6 0.9 copy-done.8
  2.5 0.9 copy-done.9
  3.5 1.2 shard_map.86
  4.7 5.2 %all-to-all-start = ((bf16[4,40,8,256]{3,2,1,0:T(8,128)(2,1)}), bf16[4,40,8,256]{3,2,1,0:T(8,128)(2,1)S(1)}, u32[]{:S(2)}, u32[]{:S(2)}) async-start(bf16[4,40,8,256]{3,2,1,0:T(8,128)(2,1)} %get-tuple-element.20), calls=%async_computation | async-start | bytes 1310720 | tf_op jit(solution)/shard_map/all_to_all | solution.py:66
  9.9 0.8 reshape.33
  10.6 8.7 %all-to-all-done.small_ref = bf16[4,40,8,256]{3,2,1,0:T(8,128)(2,1)S(1)} async-done(((bf16[4,40,8,256]{3,2,1,0:T(8,128)(2,1)}), bf16[4,40,8,256]{3,2,1,0:T(8,128)(2,1)S(1)}, u32[]{:S(2)}, u32[]{:S(2)}) %all-to-all-start) | async-done | bytes 655392 | tf_op jit(solution)/shard_map/all_to_all | solution.py:66
  19.3 3.5 %all-to-all-start.1 = ((f32[4,3,8,8,256]{4,3,2,1,0:T(8,128)}), f32[4,3,8,8,256]{4,3,2,1,0:T(8,128)S(1)}, u32[]{:S(2)}, u32[]{:S(2)}) async-start(f32[4,3,8,8,256]{4,3,2,1,0:T(8,128)} %get-tuple-element.21), calls=%async_computation.1 | async-start | bytes 1572864 | tf_op jit(solution)/shard_map/all_to_all | solution.py:66
  22.8 5.8 %copy-done = bf16[1,1,8,16,256,256]{5,4,3,2,1,0:T(8,128)(2,1)S(1)} copy-done((bf16[1,1,8,16,256,256]{5,4,3,2,1,0:T(8,128)(2,1)S(1)}, bf16[1,1,8,16,256,256]{5,4,3,2,1,0:T(8,128)(2,1)}, u32[]{:S(2)}) %copy-start) | copy-done | bytes 16777240
  28.6 5.0 %shard_map.91 = (f32[4,8,32,256]{3,2,1,0:T(8,128)S(1)}, bf16[4,8,32,256]{3,2,1,0:T(8,128)(2,1)S(1)}, bf16[4,8,32,256]{3,2,1,0:T(8,128)(2,1)}) custom-call(s32[128]{0:T(128)S(1)} %fusion.slots_ref, bf16[8,16,256,256]{3,2,1,0:T(8,128)(2,1)S(1)} %bitcast.8, bf16[4,40,8,256]{3,2,1,0:T(8,128)(2,1)S(1)} %all-to-all-done.small_ref), custom_call_target="tpu_custom_call" | custom-call | flops 536870912 | tf_op jit(solution)/shard_map/pallas_call | solution.py:345
  33.5 4.2 %all-to-all-start.5 = ((bf16[4,8,32,256]{3,2,1,0:T(8,128)(2,1)}), bf16[4,8,32,256]{3,2,1,0:T(8,128)(2,1)}, u32[]{:S(2)}, u32[]{:S(2)}) async-start(bf16[4,8,32,256]{3,2,1,0:T(8,128)(2,1)} %get-tuple-element.31), calls=%async_computation.5 | async-start | bytes 1048576 | tf_op jit(solution)/shard_map/all_to_all | solution.py:66
  37.7 3.8 %collective-permute-start.1 = (bf16[4,32,8,256]{3,2,1,0:T(8,128)(2,1)S(1)}, bf16[4,32,8,256]{3,2,1,0:T(8,128)(2,1)S(1)}, u32[]{:S(2)}, u32[]{:S(2)}) collective-permute-start(bf16[4,32,8,256]{3,2,1,0:T(8,128)(2,1)S(1)} %slice.8.own_ref), channel_id=1, source_target_pairs={{0,7},{1,2},{2,1},{3,4},{4,3},{5,6},{6,5},{7,0},{8,15},{9,10},{10,... | collective-permute-start | bytes 1572872 | tf_op jit(solution)/shard_map/ppermute | solution.py:61
  41.5 2.0 %add_convert_fusion.1 = bf16[4,8,32,256]{3,2,1,0:T(8,128)(2,1)} fusion(f32[4,8,32,256]{3,2,1,0:T(8,128)S(1)} %get-tuple-element.29, bf16[4,8,32,256]{3,2,1,0:T(8,128)(2,1)} %collective-permute-done.4), kind=kLoop, calls=%fused_computation.3 | loop fusion | flops 786432 | bytes 2097152 | tf_op jit(solution)/shard_map/convert_element_type | solution.py:151
  43.5 3.4 %all-to-all-done.5 = bf16[4,8,32,256]{3,2,1,0:T(8,128)(2,1)} async-done(((bf16[4,8,32,256]{3,2,1,0:T(8,128)(2,1)}), bf16[4,8,32,256]{3,2,1,0:T(8,128)(2,1)}, u32[]{:S(2)}, u32[]{:S(2)}) %all-to-all-start.5) | async-done | bytes 524320 | tf_op jit(solution)/shard_map/all_to_all | solution.py:66
  47.0 3.5 %all-to-all-start.4 = ((bf16[4,8,32,256]{3,2,1,0:T(8,128)(2,1)}), bf16[4,8,32,256]{3,2,1,0:T(8,128)(2,1)S(1)}, u32[]{:S(2)}, u32[]{:S(2)}) async-start(bf16[4,8,32,256]{3,2,1,0:T(8,128)(2,1)} %add_convert_fusion.1), calls=%async_computation.4 | async-start | bytes 1048576 | tf_op jit(solution)/shard_map/all_to_all | solution.py:66
  50.4 1.1 convert_reduce_fusion.1
  51.6 3.2 %collective-permute-start.5 = (f32[8,32,256]{2,1,0:T(8,128)S(1)}, f32[8,32,256]{2,1,0:T(8,128)S(1)}, u32[]{:S(2)}, u32[]{:S(2)}) collective-permute-start(f32[8,32,256]{2,1,0:T(8,128)S(1)} %convert_reduce_fusion.1), channel_id=1, source_target_pairs={{0,7},{1,2},{2,1},{3,4},{4,3},{5,6},{6,5},{7,0},{8,15},{9,10},{10,... | collective-permute-start | bytes 786440 | tf_op jit(solution)/shard_map/ppermute | solution.py:61
  54.7 7.0 %collective-permute-done.5.far_ref = f32[8,32,256]{2,1,0:T(8,128)S(1)} collective-permute-done((f32[8,32,256]{2,1,0:T(8,128)S(1)}, f32[8,32,256]{2,1,0:T(8,128)S(1)}, u32[]{:S(2)}, u32[]{:S(2)}) %collective-permute-start.5) | collective-permute-done | bytes 262176 | tf_op jit(solution)/shard_map/ppermute | solution.py:61
  61.8 0.7 copy-done.5
  62.5 5.8 %copy-done.1 = bf16[1,1,8,16,256,256]{5,4,3,2,1,0:T(8,128)(2,1)S(1)} copy-done((bf16[1,1,8,16,256,256]{5,4,3,2,1,0:T(8,128)(2,1)S(1)}, bf16[1,1,8,16,256,256]{5,4,3,2,1,0:T(8,128)(2,1)}, u32[]{:S(2)}) %copy-start.1) | copy-done | bytes 16777240
  68.3 0.9 copy-done.6
  69.2 5.2 %shard_map.92 = (f32[8,32,256]{2,1,0:T(8,128)S(1)}, f32[4,8,32,256]{3,2,1,0:T(8,128)S(1)}, bf16[4,8,32,256]{3,2,1,0:T(8,128)(2,1)}, bf16[4,8,32,256]{3,2,1,0:T(8,128)(2,1)}) custom-call(s32[128]{0:T(128)S(1)} %fusion.slots_ref, bf16[8,16,256,256]{3,2,1,0:T(8,128)(2,1)S(1)} %bitcast.9, bf16[4,8,32,256]{3,2,1,0:T(8,128)(2,1)S(1)} %all-to-all-done.4.got_ref, ...), custom_call_target="tpu_custom_call" | custom-call | flops 536870912 | tf_op jit(solution)/shard_map/pallas_call | solution.py:362
  74.5 7.1 %shard_map.87 = (f32[8,32,256]{2,1,0:T(8,128)S(1)}, bf16[4,8,32,256]{3,2,1,0:T(8,128)(2,1)S(1)}) custom-call(s32[128]{0:T(128)S(1)} %fusion.slots_ref, bf16[8,16,256,256]{3,2,1,0:T(8,128)(2,1)S(1)} %bitcast.10, bf16[4,32,8,256]{3,2,1,0:T(8,128)(2,1)S(1)} %slice.8.own_ref, bf16[4,32,8,256]{3,2,1,0:T(8,128)(2,1)} %collective-permute-done.in_ref, ...), custom_call_target="tpu_custom_call" | custom-call | flops 536870912 | tf_op jit(solution)/shard_map/pallas_call | solution.py:352
  81.6 13.1 %all_to_all.50.own_ref = bf16[4,8,32,256]{3,2,1,0:T(8,128)(2,1)S(1)} all-to-all(bf16[4,8,32,256]{3,2,1,0:T(8,128)(2,1)S(1)} %get-tuple-element.22), channel_id=1, replica_groups=mesh['band'=4,'patch'=8] {'band'}, dimensions={0} | all-to-all | bytes 1048576 | tf_op jit(solution)/shard_map/all_to_all | solution.py:66
  94.7 4.3 %all-to-all-start.7 = ((bf16[4,8,32,256]{3,2,1,0:T(8,128)(2,1)}), bf16[4,8,32,256]{3,2,1,0:T(8,128)(2,1)}, u32[]{:S(2)}, u32[]{:S(2)}) async-start(bf16[4,8,32,256]{3,2,1,0:T(8,128)(2,1)} %get-tuple-element.34), calls=%async_computation.7 | async-start | bytes 1048576 | tf_op jit(solution)/shard_map/all_to_all | solution.py:66
  98.9 0.8 collective-permute-start.3
  99.7 2.0 %add_convert_fusion = bf16[4,8,32,256]{3,2,1,0:T(8,128)(2,1)} fusion(f32[4,8,32,256]{3,2,1,0:T(8,128)S(1)} %get-tuple-element.32, bf16[4,8,32,256]{3,2,1,0:T(8,128)(2,1)} %collective-permute-done.6), kind=kLoop, calls=%fused_computation.1 | loop fusion | flops 786432 | bytes 2097152 | tf_op jit(solution)/shard_map/convert_element_type | solution.py:151
  101.8 4.7 %all-to-all-done.7 = bf16[4,8,32,256]{3,2,1,0:T(8,128)(2,1)} async-done(((bf16[4,8,32,256]{3,2,1,0:T(8,128)(2,1)}), bf16[4,8,32,256]{3,2,1,0:T(8,128)(2,1)}, u32[]{:S(2)}, u32[]{:S(2)}) %all-to-all-start.7) | async-done | bytes 524320 | tf_op jit(solution)/shard_map/all_to_all | solution.py:66
  106.4 3.5 %all-to-all-start.6 = ((bf16[4,8,32,256]{3,2,1,0:T(8,128)(2,1)}), bf16[4,8,32,256]{3,2,1,0:T(8,128)(2,1)S(1)}, u32[]{:S(2)}, u32[]{:S(2)}) async-start(bf16[4,8,32,256]{3,2,1,0:T(8,128)(2,1)} %add_convert_fusion), calls=%async_computation.6 | async-start | bytes 1048576 | tf_op jit(solution)/shard_map/all_to_all | solution.py:66
  109.9 1.8 convert_reduce_fusion
  111.8 0.7 copy-done.13
  112.5 10.5 %shard_map.89 = (s32[1,2048]{1,0:T(1,128)S(1)}, s32[32,128]{1,0:T(8,128)S(1)}, s32[1,6144]{1,0:T(1,128)S(1)}) custom-call(s32[1,2048]{1,0:T(1,128)S(1)} %bitcast.14, s32[1,2048]{1,0:T(1,128)S(1)} %bitcast.15), custom_call_target="tpu_custom_call" | custom-call | flops 50331648 | tf_op jit(solution)/shard_map/pallas_call | solution.py:247
  123.0 0.5 broadcast.22
  123.5 0.7 reduce.6
  124.2 0.7 all_to_all.40
  124.9 0.1 slice_reduce_fusion.first_ref
  125.1 6.2 %all-to-all-start.3 = ((s32[32,1,192]{2,1,0:T(1,128)}), s32[32,1,192]{2,1,0:T(1,128)S(1)}, u32[]{:S(2)}, u32[]{:S(2)}) async-start(s32[32,1,192]{2,1,0:T(1,128)} %all_to_all.40), calls=%async_computation.3 | async-start | bytes 65536 | tf_op jit(solution)/shard_map/all_to_all | solution.py:379
  131.3 5.8 %copy-done.2 = bf16[1,1,8,16,256,256]{5,4,3,2,1,0:T(8,128)(2,1)S(1)} copy-done((bf16[1,1,8,16,256,256]{5,4,3,2,1,0:T(8,128)(2,1)S(1)}, bf16[1,1,8,16,256,256]{5,4,3,2,1,0:T(8,128)(2,1)}, u32[]{:S(2)}) %copy-start.2) | copy-done | bytes 16777240
  137.1 6.4 %shard_map.88 = (f32[8,32,256]{2,1,0:T(8,128)S(1)}, f32[32,2048]{1,0:T(8,128)S(1)}) custom-call(s32[128]{0:T(128)S(1)} %fusion.slots_ref, bf16[8,16,256,256]{3,2,1,0:T(8,128)(2,1)S(1)} %bitcast.11, bf16[4,8,32,256]{3,2,1,0:T(8,128)(2,1)S(1)} %all_to_all.50.own_ref, bf16[4,8,32,256]{3,2,1,0:T(8,128)(2,1)} %collective-permute-done.2.in_ref, ...), custom_call_target="tpu_custom_call" | custom-call | flops 536870912 | tf_op jit(solution)/shard_map/pallas_call | solution.py:371
  143.6 5.8 %shard_map.93 = f32[32,48,128]{2,1,0:T(8,128)} custom-call(s32[32]{0:T(128)S(1)} %slice_reduce_fusion.first_ref, s32[1,2048]{1,0:T(1,128)S(1)} %get-tuple-element.28.place_ref, bf16[4,8,32,256]{3,2,1,0:T(8,128)(2,1)S(1)} %all-to-all-done.6.got_ref, f32[8,32,256]{2,1,0:T(8,128)S(1)} %collective-permute-done.7.far_ref, f32[8,32,256]{2,1,0:T(8,128)S(1)} %copy-done.11, ...), custom_call_target="tpu_custom_call" | custom-call | tf_op jit(solution)/shard_map/pallas_call | solution.py:387
  149.4 5.8 %all-to-all-start.8 = ((f32[32,48,128]{2,1,0:T(8,128)}), f32[32,48,128]{2,1,0:T(8,128)S(1)}, u32[]{:S(2)}, u32[]{:S(2)}) async-start(f32[32,48,128]{2,1,0:T(8,128)} %shard_map.93), calls=%async_computation.8 | async-start | bytes 1572864 | tf_op jit(solution)/shard_map/all_to_all | solution.py:393
  155.4 0.1 reshape.39.label_ref
  155.5 4.5 %shard_map.90 = (bf16[4,1024,1536]{2,1,0:T(8,128)(2,1)S(1)}, f32[8,1024]{1,0:T(8,128)S(1)}) custom-call(s32[4,1536]{1,0:T(4,128)S(1)} %reshape.39.label_ref), custom_call_target="tpu_custom_call" | custom-call | tf_op jit(solution)/shard_map/pallas_call | solution.py:381
  160.1 4.5 %copy-done.3 = bf16[4,1024,1536]{2,1,0:T(8,128)(2,1)} copy-done((bf16[4,1024,1536]{2,1,0:T(8,128)(2,1)}, bf16[4,1024,1536]{2,1,0:T(8,128)(2,1)S(1)}, u32[]{:S(2)}) %copy-start.3) | copy-done | bytes 12582936
  164.6 1.0 copy.14
  165.6 11.6 %all-to-all-done.8 = f32[32,48,128]{2,1,0:T(8,128)S(1)} async-done(((f32[32,48,128]{2,1,0:T(8,128)}), f32[32,48,128]{2,1,0:T(8,128)S(1)}, u32[]{:S(2)}, u32[]{:S(2)}) %all-to-all-start.8) | async-done | bytes 786464 | tf_op jit(solution)/shard_map/all_to_all | solution.py:393
  177.2 4.6 %copy-done.4 = bf16[4,1024,1536]{2,1,0:T(8,128)(2,1)S(1)} copy-done((bf16[4,1024,1536]{2,1,0:T(8,128)(2,1)S(1)}, bf16[4,1024,1536]{2,1,0:T(8,128)(2,1)}, u32[]{:S(2)}) %copy-start.4) | copy-done | bytes 12582936
  181.8 6.5 %shard_map.94 = f32[32,1024]{1,0:T(8,128)} custom-call(bf16[4,1024,1536]{2,1,0:T(8,128)(2,1)S(1)} %copy-done.4, f32[8,1024]{1,0:T(8,128)S(1)} %get-tuple-element.26.count_ref, f32[1536,128]{1,0:T(8,128)S(1)} %bitcast.12), custom_call_target="tpu_custom_call" | custom-call | tf_op jit(solution)/shard_map/pallas_call | solution.py:394
  (38 shorter events, 0.3 us)
Async XLA Ops:
  0.6 1.0 copy-start.7
  1.6 0.9 copy-start.8
  2.5 0.9 copy-start.9
  4.7 14.6 %all-to-all-start = ((bf16[4,40,8,256]{3,2,1,0:T(8,128)(2,1)}), bf16[4,40,8,256]{3,2,1,0:T(8,128)(2,1)S(1)}, u32[]{:S(2)}, u32[]{:S(2)}) async-start(bf16[4,40,8,256]{3,2,1,0:T(8,128)(2,1)} %get-tuple-element.20), calls=%async_computation | async-start | bytes 1310720 | tf_op jit(solution)/shard_map/all_to_all | solution.py:66
  19.3 14.3 %all-to-all-start.1 = ((f32[4,3,8,8,256]{4,3,2,1,0:T(8,128)}), f32[4,3,8,8,256]{4,3,2,1,0:T(8,128)S(1)}, u32[]{:S(2)}, u32[]{:S(2)}) async-start(f32[4,3,8,8,256]{4,3,2,1,0:T(8,128)} %get-tuple-element.21), calls=%async_computation.1 | async-start | bytes 1572864 | tf_op jit(solution)/shard_map/all_to_all | solution.py:66
  22.8 5.8 %copy-start = (bf16[1,1,8,16,256,256]{5,4,3,2,1,0:T(8,128)(2,1)S(1)}, bf16[1,1,8,16,256,256]{5,4,3,2,1,0:T(8,128)(2,1)}, u32[]{:S(2)}) copy-start(bf16[1,1,8,16,256,256]{5,4,3,2,1,0:T(8,128)(2,1)} %param.10) | copy-start | bytes 50331652
  33.5 8.0 %collective-permute-start.4 = (bf16[4,8,32,256]{3,2,1,0:T(8,128)(2,1)S(1)}, bf16[4,8,32,256]{3,2,1,0:T(8,128)(2,1)}, u32[]{:S(2)}, u32[]{:S(2)}) collective-permute-start(bf16[4,8,32,256]{3,2,1,0:T(8,128)(2,1)S(1)} %get-tuple-element.30), channel_id=1, source_target_pairs={{0,1},{1,0},{2,3},{3,2},{4,5},{5,4},{6,7},{7,6},{8,9},{9,8},{10,11... | collective-permute-start | bytes 1572872 | tf_op jit(solution)/shard_map/ppermute | solution.py:58
  33.5 13.4 %all-to-all-start.5 = ((bf16[4,8,32,256]{3,2,1,0:T(8,128)(2,1)}), bf16[4,8,32,256]{3,2,1,0:T(8,128)(2,1)}, u32[]{:S(2)}, u32[]{:S(2)}) async-start(bf16[4,8,32,256]{3,2,1,0:T(8,128)(2,1)} %get-tuple-element.31), calls=%async_computation.5 | async-start | bytes 1048576 | tf_op jit(solution)/shard_map/all_to_all | solution.py:66
  37.7 36.7 %collective-permute-start.1 = (bf16[4,32,8,256]{3,2,1,0:T(8,128)(2,1)S(1)}, bf16[4,32,8,256]{3,2,1,0:T(8,128)(2,1)S(1)}, u32[]{:S(2)}, u32[]{:S(2)}) collective-permute-start(bf16[4,32,8,256]{3,2,1,0:T(8,128)(2,1)S(1)} %slice.8.own_ref), channel_id=1, source_target_pairs={{0,7},{1,2},{2,1},{3,4},{4,3},{5,6},{6,5},{7,0},{8,15},{9,10},{10,... | collective-permute-start | bytes 1572872 | tf_op jit(solution)/shard_map/ppermute | solution.py:61
  41.5 32.9 %collective-permute-start = (bf16[4,32,8,256]{3,2,1,0:T(8,128)(2,1)S(1)}, bf16[4,32,8,256]{3,2,1,0:T(8,128)(2,1)}, u32[]{:S(2)}, u32[]{:S(2)}) collective-permute-start(bf16[4,32,8,256]{3,2,1,0:T(8,128)(2,1)S(1)} %slice.8.own_ref), channel_id=1, source_target_pairs={{0,1},{1,0},{2,3},{3,2},{4,5},{5,4},{6,7},{7,6},{8,9},{9,8},{10,11... | collective-permute-start | bytes 1572872 | tf_op jit(solution)/shard_map/ppermute | solution.py:58
  47.0 15.5 %all-to-all-start.4 = ((bf16[4,8,32,256]{3,2,1,0:T(8,128)(2,1)}), bf16[4,8,32,256]{3,2,1,0:T(8,128)(2,1)S(1)}, u32[]{:S(2)}, u32[]{:S(2)}) async-start(bf16[4,8,32,256]{3,2,1,0:T(8,128)(2,1)} %add_convert_fusion.1), calls=%async_computation.4 | async-start | bytes 1048576 | tf_op jit(solution)/shard_map/all_to_all | solution.py:66
  51.6 10.2 %collective-permute-start.5 = (f32[8,32,256]{2,1,0:T(8,128)S(1)}, f32[8,32,256]{2,1,0:T(8,128)S(1)}, u32[]{:S(2)}, u32[]{:S(2)}) collective-permute-start(f32[8,32,256]{2,1,0:T(8,128)S(1)} %convert_reduce_fusion.1), channel_id=1, source_target_pairs={{0,7},{1,2},{2,1},{3,4},{4,3},{5,6},{6,5},{7,0},{8,15},{9,10},{10,... | collective-permute-start | bytes 786440 | tf_op jit(solution)/shard_map/ppermute | solution.py:61
  61.8 0.7 copy-start.5
  62.5 5.8 %copy-start.1 = (bf16[1,1,8,16,256,256]{5,4,3,2,1,0:T(8,128)(2,1)S(1)}, bf16[1,1,8,16,256,256]{5,4,3,2,1,0:T(8,128)(2,1)}, u32[]{:S(2)}) copy-start(bf16[1,1,8,16,256,256]{5,4,3,2,1,0:T(8,128)(2,1)} %param.10) | copy-start | bytes 50331652
  68.3 0.9 copy-start.6
  74.4 20.2 %copy-start.10 = (f32[8,32,256]{2,1,0:T(8,128)}, f32[8,32,256]{2,1,0:T(8,128)S(1)}, u32[]{:S(2)}) copy-start(f32[8,32,256]{2,1,0:T(8,128)S(1)} %get-tuple-element.35.adj_ref) | copy-start | bytes 786436
  74.4 37.3 %copy-start.12 = (s32[1,1,2048,1]{2,3,1,0:T(1,128)S(1)}, s32[1,1,2048,1]{2,3,1,0:T(1,128)}, u32[]{:S(2)}) copy-start(s32[1,1,2048,1]{2,3,1,0:T(1,128)} %param.12) | copy-start | bytes 24580
  74.4 25.3 %collective-permute-start.6 = (bf16[4,8,32,256]{3,2,1,0:T(8,128)(2,1)}, bf16[4,8,32,256]{3,2,1,0:T(8,128)(2,1)}, u32[]{:S(2)}, u32[]{:S(2)}) collective-permute-start(bf16[4,8,32,256]{3,2,1,0:T(8,128)(2,1)} %get-tuple-element.33), channel_id=1, source_target_pairs={{0,1},{1,0},{2,3},{3,2},{4,5},{5,4},{6,7},{7,6},{8,9},{9,8},{10,11... | collective-permute-start | bytes 1572872 | tf_op jit(solution)/shard_map/ppermute | solution.py:58
  94.6 48.9 %copy-start.11 = (f32[8,32,256]{2,1,0:T(8,128)S(1)}, f32[8,32,256]{2,1,0:T(8,128)}, u32[]{:S(2)}) copy-start(f32[8,32,256]{2,1,0:T(8,128)} %copy-done.10) | copy-start | bytes 786436
  94.7 11.8 %all-to-all-start.7 = ((bf16[4,8,32,256]{3,2,1,0:T(8,128)(2,1)}), bf16[4,8,32,256]{3,2,1,0:T(8,128)(2,1)}, u32[]{:S(2)}, u32[]{:S(2)}) async-start(bf16[4,8,32,256]{3,2,1,0:T(8,128)(2,1)} %get-tuple-element.34), calls=%async_computation.7 | async-start | bytes 1048576 | tf_op jit(solution)/shard_map/all_to_all | solution.py:66
  98.9 32.4 %collective-permute-start.3 = (bf16[4,8,32,256]{3,2,1,0:T(8,128)(2,1)S(1)}, bf16[4,8,32,256]{3,2,1,0:T(8,128)(2,1)S(1)}, u32[]{:S(2)}, u32[]{:S(2)}) collective-permute-start(bf16[4,8,32,256]{3,2,1,0:T(8,128)(2,1)S(1)} %all_to_all.50.own_ref), channel_id=1, source_target_pairs={{0,7},{1,2},{2,1},{3,4},{4,3},{5,6},{6,5},{7,0},{8,15},{9,10},{10,... | collective-permute-start | bytes 1572872 | tf_op jit(solution)/shard_map/ppermute | solution.py:61
  99.7 31.6 %collective-permute-start.2 = (bf16[4,8,32,256]{3,2,1,0:T(8,128)(2,1)S(1)}, bf16[4,8,32,256]{3,2,1,0:T(8,128)(2,1)}, u32[]{:S(2)}, u32[]{:S(2)}) collective-permute-start(bf16[4,8,32,256]{3,2,1,0:T(8,128)(2,1)S(1)} %all_to_all.50.own_ref), channel_id=1, source_target_pairs={{0,1},{1,0},{2,3},{3,2},{4,5},{5,4},{6,7},{7,6},{8,9},{9,8},{10,11... | collective-permute-start | bytes 1572872 | tf_op jit(solution)/shard_map/ppermute | solution.py:58
  106.4 18.6 %all-to-all-start.6 = ((bf16[4,8,32,256]{3,2,1,0:T(8,128)(2,1)}), bf16[4,8,32,256]{3,2,1,0:T(8,128)(2,1)S(1)}, u32[]{:S(2)}, u32[]{:S(2)}) async-start(bf16[4,8,32,256]{3,2,1,0:T(8,128)(2,1)} %add_convert_fusion), calls=%async_computation.6 | async-start | bytes 1048576 | tf_op jit(solution)/shard_map/all_to_all | solution.py:66
  111.8 31.8 %collective-permute-start.7 = (f32[8,32,256]{2,1,0:T(8,128)}, f32[8,32,256]{2,1,0:T(8,128)S(1)}, u32[]{:S(2)}, u32[]{:S(2)}) collective-permute-start(f32[8,32,256]{2,1,0:T(8,128)} %convert_reduce_fusion), channel_id=1, source_target_pairs={{0,7},{1,2},{2,1},{3,4},{4,3},{5,6},{6,5},{7,0},{8,15},{9,10},{10,... | collective-permute-start | bytes 786440 | tf_op jit(solution)/shard_map/ppermute | solution.py:61
  111.8 0.7 copy-start.13
  125.1 24.3 %all-to-all-start.3 = ((s32[32,1,192]{2,1,0:T(1,128)}), s32[32,1,192]{2,1,0:T(1,128)S(1)}, u32[]{:S(2)}, u32[]{:S(2)}) async-start(s32[32,1,192]{2,1,0:T(1,128)} %all_to_all.40), calls=%async_computation.3 | async-start | bytes 65536 | tf_op jit(solution)/shard_map/all_to_all | solution.py:379
  131.3 5.8 %copy-start.2 = (bf16[1,1,8,16,256,256]{5,4,3,2,1,0:T(8,128)(2,1)S(1)}, bf16[1,1,8,16,256,256]{5,4,3,2,1,0:T(8,128)(2,1)}, u32[]{:S(2)}) copy-start(bf16[1,1,8,16,256,256]{5,4,3,2,1,0:T(8,128)(2,1)} %param.10) | copy-start | bytes 50331652
  149.4 27.8 %all-to-all-start.8 = ((f32[32,48,128]{2,1,0:T(8,128)}), f32[32,48,128]{2,1,0:T(8,128)S(1)}, u32[]{:S(2)}, u32[]{:S(2)}) async-start(f32[32,48,128]{2,1,0:T(8,128)} %shard_map.93), calls=%async_computation.8 | async-start | bytes 1572864 | tf_op jit(solution)/shard_map/all_to_all | solution.py:393
  160.1 4.5 %copy-start.3 = (bf16[4,1024,1536]{2,1,0:T(8,128)(2,1)}, bf16[4,1024,1536]{2,1,0:T(8,128)(2,1)S(1)}, u32[]{:S(2)}) copy-start(bf16[4,1024,1536]{2,1,0:T(8,128)(2,1)S(1)} %get-tuple-element.25.chosen_ref) | copy-start | bytes 37748740
  177.2 4.6 %copy-start.4 = (bf16[4,1024,1536]{2,1,0:T(8,128)(2,1)S(1)}, bf16[4,1024,1536]{2,1,0:T(8,128)(2,1)}, u32[]{:S(2)}) copy-start(bf16[4,1024,1536]{2,1,0:T(8,128)(2,1)} %copy-done.3) | copy-start | bytes 37748740

commit v2 on v0

v2 whole, which is shorter than its diff:
```python
import jax
import jax.numpy as jnp
from jax import lax
from jax.experimental import pallas as pl
from jax.experimental.pallas import tpu as pltpu
from jax.sharding import PartitionSpec as P

F32 = jnp.float32
BF16 = jnp.bfloat16
I32 = jnp.int32
LANES = 128
MIB = 1 << 20
VMEM = pl.BlockSpec(memory_space=pltpu.VMEM)
TOP = 32767.0


def shape(dims, dtype):
    return jax.ShapeDtypeStruct(dims, dtype)


def whole(dims):
    return pl.BlockSpec(dims, lambda i, *_: (0,) * len(dims))


def along(dims, axis):
    return pl.BlockSpec(dims, lambda i, *_: tuple(i if d == axis else 0 for d in range(len(dims))))


def nt(a, b):
    return lax.dot_general(a, b, (((1,), (1,)), ((), ())), preferred_element_type=F32)


def nn(a, b):
    return lax.dot_general(a, b, (((1,), (0,)), ((), ())), preferred_element_type=F32)


def iota(dims, axis):
    return lax.broadcasted_iota(I32, dims, axis)


def kernel_call(kernel, steps, scalars, ins, outs, args, scratch=(), limit=24 * MIB, flops=0):
    return pl.pallas_call(
        kernel,
        out_shape=[o for _, o in outs],
        grid_spec=pltpu.PrefetchScalarGridSpec(
            num_scalar_prefetch=scalars,
            grid=(steps,),
            in_specs=ins,
            out_specs=[s for s, _ in outs],
            scratch_shapes=scratch,
        ),
        compiler_params=pltpu.CompilerParams(vmem_limit_bytes=limit),
        cost_estimate=pl.CostEstimate(flops=flops, bytes_accessed=flops // 32, transcendentals=0),
    )(*args)


def body(
    emissivity, blackbody, loss_weights, view_blocks, column_blocks, patch_owner, patch_surface
):
    split = lax.axis_size("band")
    groups = lax.axis_size("patch")
    devices = split * groups
    part_bands = emissivity.shape[0]
    bands = part_bands * split
    rb_count, depth, width = view_blocks.shape[2:5]
    rows = rb_count * width
    per_group = split * rb_count
    capacity = max(2, 3 * rows // devices)
    surfaces = rows // 2
    me = lax.axis_index("patch")

    team_of = [(g, (g + 1) % groups) for g in range(1, groups, 2)]
    teams = [[b * groups + g for g in pair for b in range(split)] for pair in team_of]

    def place_in_team():
        return 1 - lax.axis_index("patch") % 2

    def inner(block):
        return lax.ppermute(block, "patch", [(i, i ^ 1) for i in range(groups)])

    def outer(block):
        return lax.ppermute(
            block, "patch", [(i, (i + (1 if i % 2 else -1)) % groups) for i in range(groups)]
        )

    def across(block, d):
        return lax.ppermute(block, "band", [(i, i ^ d) for i in range(split)])

    def team_exchange(block):
        return lax.all_to_all(
            block, ("band", "patch"), 0, 0, axis_index_groups=teams, tiled=True
        )

    columns = column_blocks.reshape(rb_count * depth)
    column_group = columns // per_group
    third = jnp.where(column_group == me, 0, jnp.where(column_group == (me ^ 1), 1, 2))
    slots = third * per_group + columns % per_group
    matrix = view_blocks.reshape(rb_count, depth, width, width)
    block_shape = (rb_count, bands, width)
    team_shape = (2 * split,) + block_shape
    part_shape = (split,) + block_shape
    pass_flops = 2 * bands * rb_count * depth * width * width
    once = rb_count // 4
    half = depth // 2

    def prepare(e_ref, b_ref, w_ref, start_ref, full_ref):
        for r in range(rb_count):
            cut = slice(r * width, (r + 1) * width)
            e, b, w = e_ref[:, cut], b_ref[:, cut], w_ref[:, cut]
            start = (e * b).astype(BF16)
            for d in range(2 * split):
                start_ref[d, r] = start
            full_ref[0, 0, r] = e
            full_ref[0, 1, r] = b
            full_ref[0, 2, r] = w

    piece = (3, rb_count, part_bands, width)
    start, full = kernel_call(
        prepare,
        split,
        0,
        [along((part_bands, rows), 1)] * 3,
        [
            (
                along((2 * split, rb_count, part_bands, width), 1),
                shape((2 * split, per_group, part_bands, width), BF16),
            ),
            (along((1,) + piece, 0), shape((split,) + piece, F32)),
        ],
        (emissivity, blackbody, loss_weights),
    )

    band = lax.axis_index("band")
    pieces = [
        across(lax.dynamic_index_in_dim(full, band ^ d, keepdims=False), d) if d else
        lax.dynamic_index_in_dim(full, band, keepdims=False)
        for d in range(split)
    ]
    start = team_exchange(start)

    def scatter_products(slots_ref, m_refs, value_of, outs, total):
        i = pl.program_id(0)

        @pl.when(i == 0)
        def _():
            total[...] = jnp.zeros_like(total)

        for q in range(once):
            u = value_of(q)
            for k in range(depth):
                s = slots_ref[(i * once + q) * depth + k]
                total[s] += nn(u, m_refs[k // half][q, k % half])

        @pl.when(i == pl.num_programs(0) - 1)
        def _():
            for third_index, out_ref in enumerate(outs):
                for s in range(split):
                    at = third_index * per_group + s * rb_count
                    out_ref[s] = total[at : at + rb_count].astype(out_ref.dtype)

    matrix_specs = [
        pl.BlockSpec((once, half, width, width), lambda i, *_, h=h: (i, h, 0, 0)) for h in (0, 1)
    ]
    part_outs = [(whole(part_shape), shape(part_shape, t)) for t in (F32, BF16, BF16)]
    total_scratch = [pltpu.VMEM((3 * per_group, bands, width), F32)]
    step_rows = along((once, bands, width), 0)
    full_rows = along((3, once, bands, width), 1)

    def adjoint_first(slots_ref, m0, m1, *refs):
        piece_refs, (full_ref, own_ref, near_ref, far_ref, total) = refs[:split], refs[split:]
        b = lax.axis_index("band")
        for d in range(split):
            at = pl.ds(pl.multiple_of((b ^ d) * part_bands, part_bands), part_bands)
            for a in range(3):
                for q in range(once):
                    full_ref[a, q, at, :] = piece_refs[d][a, q]

        def value_of(q):
            return ((1.0 - full_ref[0, q]) * full_ref[2, q]).astype(BF16)

        scatter_products(slots_ref, (m0, m1), value_of, (own_ref, near_ref, far_ref), total)

    def adjoint_second(slots_ref, m0, m1, got_ref, full_ref, one_ref, own_ref, near_ref, far_ref, total):
        def value_of(q):
            value = got_ref[0, q].astype(F32)
            for s in range(1, 2 * split):
                value = value + got_ref[s, q].astype(F32)
            one_ref[q] = value
            return ((1.0 - full_ref[0, q]) * value).astype(BF16)

        scatter_products(slots_ref, (m0, m1), value_of, (own_ref, near_ref, far_ref), total)

    def merge(own_ref, near_ref, far_ref, pay_ref):
        mine = place_in_team() * split
        for s in range(split):
            pay_ref[mine + s] = (own_ref[s] + near_ref[s].astype(F32)).astype(BF16)
            pay_ref[split - mine + s] = far_ref[s]

    def collect(own, near, far):
        (pay,) = kernel_call(
            merge,
            1,
            0,
            [whole(part_shape)] * 3,
            [(whole(team_shape), shape(team_shape, BF16))],
            (own, inner(near), far),
        )
        return team_exchange(pay)

    def products(slots_ref, m_refs, held, finish):
        i = pl.program_id(0)
        for q in range(once):
            value = jnp.zeros((bands, width), F32)
            for k in range(depth):
                s = slots_ref[(i * once + q) * depth + k]
                value = value + nt(held[s], m_refs[k // half][q, k % half])
            finish(q, value)

    def forward_first(slots_ref, m0, m1, team_ref, near_ref, full_ref, zero_ref, rad_ref, held):
        @pl.when(pl.program_id(0) == 0)
        def _():
            mine = place_in_team() * split

            def fill(c, carry):
                for third_index, (ref, first) in enumerate(
                    ((team_ref, mine), (near_ref, 0), (team_ref, split - mine))
                ):
                    parts = [ref[first + s, c].astype(F32) for s in range(split)]
                    held[third_index * per_group + c] = jnp.concatenate(parts, axis=0).astype(BF16)
                return carry

            lax.fori_loop(0, per_group, fill, 0)

        def finish(q, value):
            zero_ref[q] = value
            e, b = full_ref[0, q], full_ref[1, q]
            rad_ref[q] = (e * b + (1.0 - e) * value).astype(BF16)

        products(slots_ref, (m0, m1), held, finish)

    def forward_second(slots_ref, m0, m1, *refs):
        piece_refs, (full_ref, one_ref, rad_ref, held) = refs[:split], refs[split:]

        @pl.when(pl.program_id(0) == 0)
        def _():
            b = lax.axis_index("band")
            for d in range(split):
                for third_index in range(3):
                    at = third_index * per_group + (b ^ d) * rb_count
                    held[pl.ds(at, rb_count)] = piece_refs[d][third_index]

        def finish(q, value):
            one_ref[q] = value
            e, b = full_ref[0, q], full_ref[1, q]
            rad_ref[:, q * width : (q + 1) * width] = e * b + (1.0 - e) * value

        products(slots_ref, (m0, m1), held, finish)

    window_scratch = [pltpu.VMEM((3 * per_group, bands, width), BF16)]

    tail = max(0, capacity - LANES)
    seats = LANES + (LANES // 2 if tail else 0)
    value_rows = bands + (bands // 2 if tail else 0)
    send_rows = value_rows + 8

    def route(owner_ref, surface_ref, rank_ref, label_ref):
        names = iota((devices, width), 0)
        upper = (iota((width, width), 0) <= iota((width, width), 1)).astype(BF16)
        seat = iota((seats, width), 0)
        count = jnp.zeros((devices, 1), F32)
        found = jnp.zeros((3 * devices, seats), F32)
        for c in range(rb_count):
            cut = slice(c * width, (c + 1) * width)
            hit = (owner_ref[:, cut] == names).astype(F32)
            rank = nn(hit.astype(BF16), upper) + count
            count = rank[:, width - 1 : width]
            place = jnp.sum(hit * rank, axis=0, keepdims=True).astype(I32) - 1
            rank_ref[:, cut] = place
            seated = (seat == place).astype(F32).astype(BF16)
            surface = surface_ref[:, cut]
            high = (surface >> 7).astype(F32)
            low = (surface & 127).astype(F32)
            marks = jnp.concatenate([hit, hit * high, hit * low], axis=0).astype(BF16)
            found = found + nt(marks, seated)
        taken, high, low = (found[a * devices : (a + 1) * devices] for a in range(3))
        label_ref[...] = jnp.where(taken > 0.5, high * 128.0 + low, float(surfaces))

    rank, labels = kernel_call(
        route,
        1,
        0,
        [whole((1, rows))] * 2,
        [
            (whole((1, rows)), shape((1, rows), I32)),
            (whole((devices, seats)), shape((devices, seats), F32)),
        ],
        (patch_owner.reshape(1, rows), patch_surface.reshape(1, rows)),
    )

    owners_once = 4

    def pack_rows(
        got_ref, adj_ref, zero_ref, one_ref, full_ref, owner_ref, rank_ref, label_ref,
        send_ref, grad, digits, seated, most,
    ):
        i = pl.program_id(0)

        @pl.when(i == 0)
        def _():
            most[...] = jnp.full_like(most, 1e-30)

        for q in range(once):
            b, w = full_ref[1, q], full_ref[2, q]
            a = adj_ref[q]
            last = got_ref[0, q].astype(F32)
            for s in range(1, 2 * split):
                last = last + got_ref[s, q].astype(F32)
            value = (w + a + last) * b - (w * one_ref[q] + a * zero_ref[q])
            cut = pl.ds(pl.multiple_of((i * once + q) * width, width), width)
            grad[:, cut] = value
            most[...] = jnp.maximum(most[...], jnp.max(jnp.abs(value), axis=1, keepdims=True))

        @pl.when(i == pl.num_programs(0) - 1)
        def _():
            power = jnp.floor(jnp.log2(most[...])) - 14.0
            power = jnp.where(most[...] * jnp.exp2(-power) > TOP, power + 1.0, power)
            scale = jnp.exp2(-power)[:, :1]
            ordinal = jnp.round(jnp.clip(grad[...] * scale, -TOP, TOP))
            high = ordinal.astype(BF16)
            digits[:bands] = high
            digits[bands:] = (ordinal - high.astype(F32)).astype(BF16)
            seated[...] = (iota((seats, rows), 0) == rank_ref[...]).astype(F32).astype(BF16)
            powers = power.T[:1]
            powers = jnp.concatenate([powers, jnp.zeros((1, LANES - bands), F32)], axis=1)

            def step(c, carry):
                hits = []
                for j in range(owners_once):
                    hit = (owner_ref[...] == c * owners_once + j).astype(F32).astype(BF16)
                    hits.append(digits[...] * hit)
                moved = nt(jnp.concatenate(hits, axis=0), seated[...])
                for j in range(owners_once):
                    at = 2 * bands * j
                    block = moved[at : at + bands] + moved[at + bands : at + 2 * bands]
                    label = label_ref[pl.ds(c * owners_once + j, 1)]
                    parts = [block[:, :LANES]]
                    extra = [label[:, :LANES]]
                    if tail:
                        over = block[:, LANES:]
                        parts.append(
                            jnp.concatenate([over[: bands // 2], over[bands // 2 :]], axis=1)
                        )
                        over = label[:, LANES:]
                        extra.append(jnp.concatenate([over, over], axis=1))
                    else:
                        extra.append(jnp.zeros((1, LANES), F32))
                    extra.append(powers)
                    extra.append(jnp.zeros((5, LANES), F32))
                    out = jnp.concatenate(parts + [jnp.concatenate(extra, axis=0)], axis=0)
                    send_ref[c * owners_once + j] = out.astype(I32).astype(jnp.int16)
                return carry

            lax.fori_loop(0, devices // owners_once, step, 0)

    sources_once = 4
    tops = surfaces // LANES
    lot = sources_once * LANES * (2 if tail else 1)
    top_rows = 2 * bands + 16

    def reduce_rows(got_ref, out_ref, scales, total):
        power = got_ref[:, value_rows + 2].astype(F32)
        scale = jnp.exp2(power).T[:bands]
        for s in range(devices):
            scales[s] = jnp.broadcast_to(scale[:, s : s + 1], (bands, LANES))
        total[...] = jnp.zeros_like(total)
        left = iota((bands // 2, LANES), 1) < LANES // 2
        first_half = iota((1, LANES), 1) < LANES // 2

        def step(c, carry):
            values, labels, once_each = [], [], []
            for j in range(sources_once):
                source = c * sources_once + j
                got = got_ref[source].astype(F32)
                grown = scales[source]
                values.append(got[:bands] * grown)
                labels.append(got[value_rows : value_rows + 1])
                once_each.append(jnp.ones((1, LANES), F32))
                if tail:
                    over = got[bands:value_rows]
                    low = jnp.where(left, over * grown[: bands // 2], 0.0)
                    high = jnp.where(left, 0.0, over * grown[bands // 2 :])
                    values.append(jnp.concatenate([low, high], axis=0))
                    labels.append(got[value_rows + 1 : value_rows + 2])
                    once_each.append(jnp.where(first_half, 1.0, 0.0))
            value = jnp.concatenate(values, axis=1)
            label = jnp.concatenate(labels, axis=1).astype(I32)
            counted = jnp.concatenate(once_each, axis=1)
            high = value.astype(BF16)
            low = (value - high.astype(F32)).astype(BF16)
            counted = jnp.broadcast_to(counted, (16, lot)).astype(BF16)
            both = jnp.concatenate([high, low, counted], axis=0)
            seated = (iota((LANES, lot), 0) == (label & 127)).astype(F32).astype(BF16)
            chosen = [both * (label >> 7 == t).astype(F32).astype(BF16) for t in range(tops)]
            total[...] += nt(jnp.concatenate(chosen, axis=0), seated)
            return carry

        lax.fori_loop(0, devices // sources_once, step, 0)
        for t in range(tops):
            at = t * top_rows
            sums = total[at : at + bands] + total[at + bands : at + 2 * bands]
            count = jnp.maximum(total[at + 2 * bands : at + 2 * bands + 1], 1.0)
            out_ref[:, t * LANES : (t + 1) * LANES] = sums / count

    full, own, near, far = kernel_call(
        adjoint_first,
        4,
        1,
        matrix_specs + [along((3, once, part_bands, width), 1)] * split,
        [(full_rows, shape((3,) + block_shape, F32))] + part_outs,
        (slots, matrix, matrix) + tuple(pieces),
        total_scratch,
        flops=pass_flops,
    )
    got_one = collect(own, near, far)

    mine = (1 - me % 2) * split
    start_near = inner(lax.dynamic_slice_in_dim(start, mine, split, axis=0))
    zero, rad = kernel_call(
        forward_first,
        4,
        1,
        matrix_specs + [whole(start.shape), whole(start_near.shape), full_rows],
        [(step_rows, shape(block_shape, F32)), (step_rows, shape(block_shape, BF16))],
        (slots, matrix, matrix, start, start_near, full),
        window_scratch,
        flops=pass_flops,
    )
    rad = jnp.stack([rad, inner(rad), outer(rad)])
    rads = [rad] + [across(rad, d) for d in range(1, split)]

    adjoint_one, own, near, far = kernel_call(
        adjoint_second,
        4,
        1,
        matrix_specs + [along((2 * split, once, bands, width), 1), full_rows],
        [(step_rows, shape(block_shape, F32))] + part_outs,
        (slots, matrix, matrix, got_one, full),
        total_scratch,
        flops=pass_flops,
    )
    got_zero = collect(own, near, far)

    one, radiosity = kernel_call(
        forward_second,
        4,
        1,
        matrix_specs + [whole((3,) + block_shape)] * split + [full_rows],
        [
            (step_rows, shape(block_shape, F32)),
            (along((bands, once * width), 1), shape((bands, rows), F32)),
        ],
        (slots, matrix, matrix) + tuple(rads) + (full,),
        window_scratch,
        flops=pass_flops,
    )

    (send,) = kernel_call(
        pack_rows,
        4,
        0,
        [along((2 * split, once, bands, width), 1)]
        + [step_rows] * 3
        + [full_rows, whole((1, rows)), whole((1, rows)), whole((devices, seats))],
        [
            (
                whole((devices, send_rows, LANES)),
                shape((devices, send_rows, LANES), jnp.int16),
            )
        ],
        (
            got_zero,
            adjoint_one,
            zero,
            one,
            full,
            patch_owner.reshape(1, rows),
            rank,
            labels,
        ),
        [
            pltpu.VMEM((bands, rows), F32),
            pltpu.VMEM((2 * bands, rows), BF16),
            pltpu.VMEM((seats, rows), BF16),
            pltpu.VMEM((bands, LANES), F32),
        ],
    )
    send = lax.all_to_all(send, ("band", "patch"), 0, 0, tiled=True)
    (surface_grad,) = kernel_call(
        reduce_rows,
        1,
        0,
        [whole((devices, send_rows, LANES))],
        [(whole((bands, surfaces)), shape((bands, surfaces), F32))],
        (send,),
        [
            pltpu.VMEM((devices, bands, LANES), F32),
            pltpu.VMEM((tops * top_rows, LANES), F32),
        ],
    )
    return (radiosity.reshape(bands, 1, 1, rows), surface_grad)


def solution(mesh):
    in_specs = (
        P("band", "patch"),
        P("band", "patch"),
        P("band", "patch"),
        P("patch", "band", None, None, None, None),
        P("patch", "band", None, None),
        P("patch", "band", None, None),
        P("patch", "band", None),
    )
    out_specs = (P(None, "patch", "band", None), P(None, ("band", "patch")))
    return jax.shard_map(body, mesh=mesh, in_specs=in_specs, out_specs=out_specs, check_vma=False)
```

time: 339 us -> 155 us (0.46)
  other arithmetic: 132 us -> 0.06 us
  matrix products: 43 us -> 0 us
  Pallas kernels: 0 us -> 38.9 us
  local copies, waits for them, and re-layouts: 56.3 us -> 23.9 us
  waiting for transfers between devices: 31.9 us -> 48.3 us
  between operations: 14.5 us -> 0.81 us
  starting transfers between devices: 37.1 us -> 24.3 us
    scatter-add x4 -> x0, other arithmetic: 110 us -> none  [the longest x1 42.7 us: body(): jax.ops.segment_sum(jnp.ones((device_count * capacity,), jnp.float32), fl...]
    dot_general x4 -> x0, matrix products: 43 us -> none  [the longest x2 21.8 us: forward(): jnp.einsum('rkij,brkj->bri', matrix, picked, preferred_element_type=jnp.f...]
    pallas_call x0 -> x10, Pallas kernels: none -> 38.9 us  [kernel_call(): pl.pallas_call(kernel, out_shape=[o for _, o in outs], grid_spec=pltpu.Pr...]
    all_gather x2 -> x0, blocking collectives: 21 us -> none  [window(): gathered = lax.all_gather(vector, 'band', axis=1, tiled=True)]
    all_to_all x0 -> x1, blocking collectives: none -> 18.1 us  [team_exchange(): lax.all_to_all(block, ('band', 'patch'), 0, 0, axis_index_groups=teams, t...]
    ppermute x8 -> x11, waiting for transfers between devices: 18.5 us -> 34.3 us  [the longest x6 22.7 us: across(): return lax.ppermute(block, 'band', [(i, i ^ d) for i in range(split)])]
    reshape x8 -> x1, local copies, waits for them, and re-layouts: 11.7 us -> 0.76 us  [body(): columns = column_blocks.reshape(rb_count * depth)]
    another operation x3 -> x1, other arithmetic: 9.41 us -> 0.05 us  [body(): rad = jnp.stack([rad, inner(rad), outer(rad)])]
  transfers between devices with their start and end apart: 15 -> 14, of which waited for: 6 -> 9; matrix products, arithmetic and copies ran while one was open for 55% -> 1% of each run, Pallas kernels for 0% -> 14%
where the time goes in v2:
time: 155 us; the launch traced here: 154 us
  waiting for transfers between devices  48.3 us (31%)
  Pallas kernels  38.9 us (25%)
  starting transfers between devices  24.3 us (16%)
  local copies, waits for them, and re-layouts  23.9 us (15%)
  blocking collectives  18.1 us (12%)
    pallas_call x10, Pallas kernels, kernel_call(): pl.pallas_call(kernel, out_shape=[o for _, o in outs], grid_spec=pltpu.Pr...  38.9 us
    unnamed x23, local copies, waits for them, and re-layouts  23.1 us
    ppermute x6, waiting for transfers between devices, across(): return lax.ppermute(block, 'band', [(i, i ^ d) for i in range(split)])  22.7 us
    all_to_all x1, blocking collectives, team_exchange(): lax.all_to_all(block, ('band', 'patch'), 0, 0, axis_index_groups=teams, t...  18.1 us
    all_to_all x1, waiting for transfers between devices, body(): send = lax.all_to_all(send, ('band', 'patch'), 0, 0, tiled=True)  14 us
    all_to_all x2, starting transfers between devices, team_exchange(): lax.all_to_all(block, ('band', 'patch'), 0, 0, axis_index_groups=teams, t...  13.1 us
    ppermute x6, starting transfers between devices, across(): return lax.ppermute(block, 'band', [(i, i ^ d) for i in range(split)])  8.1 us
    ppermute x1, waiting for transfers between devices, outer(): lax.ppermute(block, 'patch', [(i, (i + (1 if i % 2 else -1)) % groups) fo...  5.97 us
  transfers between devices with their start and end apart: 14, of which 9 were waited for; matrix products, arithmetic and copies ran while one was open for 1% of the time, Pallas kernels for 14%

profile of v2, /device:TPU:0, one launch (start us, length us, event | category | flops | bytes accessed | tf_op | source)
XLA Modules:
  0.0 154.5 jit_solution(3530524768966205949)
XLA Ops:
  0.7 0.9 copy-done.6
  1.6 0.9 copy-done.7
  2.6 0.9 copy-done.8
  3.5 0.3 shard_map.86
  3.8 1.0 copy-done.5
  4.8 0.1 dynamic-slice_bitcast_fusion
  4.9 3.0 %collective-permute-start.1 = (f32[3,8,8,256]{3,2,1,0:T(8,128)S(1)}, f32[3,8,8,256]{3,2,1,0:T(8,128)S(1)}, u32[]{:S(2)}, u32[]{:S(2)}) collective-permute-start(f32[3,8,8,256]{3,2,1,0:T(8,128)S(1)} %get-tuple-element.38), channel_id=1, source_target_pairs={{0,8},{8,0},{16,24},{24,16},{1,9},{9,1},{17,25},{25,17},{2,10},{10... | collective-permute-start | bytes 589832 | tf_op jit(solution)/shard_map/ppermute | solution.py:87
  7.9 1.5 collective-permute-start.2
  9.4 0.0 collective-permute-start.3
  9.4 0.8 reshape.20
  10.2 3.4 %collective-permute-done.1.refs_1_ = f32[3,8,8,256]{3,2,1,0:T(8,128)S(1)} collective-permute-done((f32[3,8,8,256]{3,2,1,0:T(8,128)S(1)}, f32[3,8,8,256]{3,2,1,0:T(8,128)S(1)}, u32[]{:S(2)}, u32[]{:S(2)}) %collective-permute-start.1) | collective-permute-done | bytes 196640 | tf_op jit(solution)/shard_map/ppermute | solution.py:87
  13.6 4.8 %collective-permute-done.2.refs_2_ = f32[3,8,8,256]{3,2,1,0:T(8,128)S(1)} collective-permute-done((f32[3,8,8,256]{3,2,1,0:T(8,128)S(1)}, f32[3,8,8,256]{3,2,1,0:T(8,128)S(1)}, u32[]{:S(2)}, u32[]{:S(2)}) %collective-permute-start.2) | collective-permute-done | bytes 196640 | tf_op jit(solution)/shard_map/ppermute | solution.py:87
  18.5 0.0 collective-permute-done.3.refs_3_
  18.5 5.8 %copy-done = bf16[1,1,8,16,256,256]{5,4,3,2,1,0:T(8,128)(2,1)S(1)} copy-done((bf16[1,1,8,16,256,256]{5,4,3,2,1,0:T(8,128)(2,1)S(1)}, bf16[1,1,8,16,256,256]{5,4,3,2,1,0:T(8,128)(2,1)}, u32[]{:S(2)}) %copy-start) | copy-done | bytes 16777240
  24.2 5.6 %shard_map.87 = (f32[3,8,32,256]{3,2,1,0:T(8,128)S(1)}, f32[4,8,32,256]{3,2,1,0:T(8,128)S(1)}, bf16[4,8,32,256]{3,2,1,0:T(8,128)(2,1)S(1)}, bf16[4,8,32,256]{3,2,1,0:T(8,128)(2,1)S(1)}) custom-call(s32[128]{0:T(128)S(1)} %fusion.slots_ref, bf16[8,16,256,256]{3,2,1,0:T(8,128)(2,1)S(1)} %bitcast.17, bf16[8,16,256,256]{3,2,1,0:T(8,128)(2,1)S(1)} %bitcast.18, ...), custom_call_target="tpu_custom_call" | custom-call | flops 536870912 | bytes 16777216 | tf_op jit(solution)/shard_map/pallas_call | solution.py:42
  29.9 0.1 collective-permute-start.9
  30.0 1.9 %collective-permute-done.9.near_ref = bf16[4,8,32,256]{3,2,1,0:T(8,128)(2,1)S(1)} collective-permute-done((bf16[4,8,32,256]{3,2,1,0:T(8,128)(2,1)S(1)}, bf16[4,8,32,256]{3,2,1,0:T(8,128)(2,1)S(1)}, u32[]{:S(2)}, u32[]{:S(2)}) %collective-permute-start.9) | collective-permute-done | bytes 524320 | tf_op jit(solution)/shard_map/ppermute | solution.py:79
  31.9 0.1 shard_map.90
  32.0 18.1 %all_to_all.20.got_ref = bf16[8,8,32,256]{3,2,1,0:T(8,128)(2,1)S(1)} all-to-all(bf16[8,8,32,256]{3,2,1,0:T(8,128)(2,1)S(1)} %shard_map.90), channel_id=1, replica_groups={{1,9,17,25,2,10,18,26},{3,11,19,27,4,12,20,28},{5,13,21,29,6,14,22,30},..., dimensions={0} | all-to-all | bytes 2097152 | tf_op jit(solution)/shard_map/all_to_all | solution.py:90
  50.1 6.5 %all-to-all-start = ((bf16[8,32,8,256]{3,2,1,0:T(8,128)(2,1)}), bf16[8,32,8,256]{3,2,1,0:T(8,128)(2,1)S(1)}, u32[]{:S(2)}, u32[]{:S(2)}) async-start(bf16[8,32,8,256]{3,2,1,0:T(8,128)(2,1)} %copy-done.5), calls=%async_computation | async-start | bytes 2097152 | tf_op jit(solution)/shard_map/all_to_all | solution.py:90
  56.6 5.8 %copy-done.1 = bf16[1,1,8,16,256,256]{5,4,3,2,1,0:T(8,128)(2,1)S(1)} copy-done((bf16[1,1,8,16,256,256]{5,4,3,2,1,0:T(8,128)(2,1)S(1)}, bf16[1,1,8,16,256,256]{5,4,3,2,1,0:T(8,128)(2,1)}, u32[]{:S(2)}) %copy-start.1) | copy-done | bytes 16777240
  62.4 5.5 %shard_map.91 = (f32[8,32,256]{2,1,0:T(8,128)S(1)}, f32[4,8,32,256]{3,2,1,0:T(8,128)S(1)}, bf16[4,8,32,256]{3,2,1,0:T(8,128)(2,1)S(1)}, bf16[4,8,32,256]{3,2,1,0:T(8,128)(2,1)S(1)}) custom-call(s32[128]{0:T(128)S(1)} %fusion.slots_ref, bf16[8,16,256,256]{3,2,1,0:T(8,128)(2,1)S(1)} %bitcast.19, bf16[8,16,256,256]{3,2,1,0:T(8,128)(2,1)S(1)} %bitcast.20, ...), custom_call_target="tpu_custom_call" | custom-call | flops 536870912 | bytes 16777216 | tf_op jit(solution)/shard_map/pallas_call | solution.py:42
  67.9 0.1 collective-permute-start.10
  68.0 1.9 %collective-permute-done.10.near_ref = bf16[4,8,32,256]{3,2,1,0:T(8,128)(2,1)S(1)} collective-permute-done((bf16[4,8,32,256]{3,2,1,0:T(8,128)(2,1)S(1)}, bf16[4,8,32,256]{3,2,1,0:T(8,128)(2,1)S(1)}, u32[]{:S(2)}, u32[]{:S(2)}) %collective-permute-start.10) | collective-permute-done | bytes 524320 | tf_op jit(solution)/shard_map/ppermute | solution.py:79
  69.9 0.1 shard_map.92
  70.0 1.0 copy-done.4
  71.0 0.0 all-to-all-done.team_ref
  71.0 6.6 %all-to-all-start.2 = ((bf16[8,8,32,256]{3,2,1,0:T(8,128)(2,1)}), bf16[8,8,32,256]{3,2,1,0:T(8,128)(2,1)S(1)}, u32[]{:S(2)}, u32[]{:S(2)}) async-start(bf16[8,8,32,256]{3,2,1,0:T(8,128)(2,1)} %copy-done.4), calls=%async_computation.2 | async-start | bytes 2097152 | tf_op jit(solution)/shard_map/all_to_all | solution.py:90
  77.7 0.1 collective-permute-start
  77.7 1.9 %collective-permute-done.near_ref = bf16[4,32,8,256]{3,2,1,0:T(8,128)(2,1)S(1)} collective-permute-done((bf16[4,32,8,256]{3,2,1,0:T(8,128)(2,1)S(1)}, bf16[4,32,8,256]{3,2,1,0:T(8,128)(2,1)S(1)}, u32[]{:S(2)}, u32[]{:S(2)}) %collective-permute-start) | collective-permute-done | bytes 524320 | tf_op jit(solution)/shard_map/ppermute | solution.py:79
  79.6 5.8 %copy-done.2 = bf16[1,1,8,16,256,256]{5,4,3,2,1,0:T(8,128)(2,1)S(1)} copy-done((bf16[1,1,8,16,256,256]{5,4,3,2,1,0:T(8,128)(2,1)S(1)}, bf16[1,1,8,16,256,256]{5,4,3,2,1,0:T(8,128)(2,1)}, u32[]{:S(2)}) %copy-start.2) | copy-done | bytes 16777240
  85.4 7.4 %shard_map.88 = (f32[8,32,256]{2,1,0:T(8,128)S(1)}, bf16[8,32,256]{2,1,0:T(8,128)(2,1)S(1)}) custom-call(s32[128]{0:T(128)S(1)} %fusion.slots_ref, bf16[8,16,256,256]{3,2,1,0:T(8,128)(2,1)S(1)} %bitcast.21, bf16[8,16,256,256]{3,2,1,0:T(8,128)(2,1)S(1)} %bitcast.22, bf16[8,32,8,256]{3,2,1,0:T(8,128)(2,1)S(1)} %all-to-all-done.team_ref, ...), custom_call_target="tpu_custom_call" | custom-call | flops 536870912 | bytes 16777216 | tf_op jit(solution)/shard_map/pallas_call | solution.py:42
  92.9 0.1 collective-permute-start.5
  93.0 0.2 collective-permute-start.4
  93.1 6.0 %collective-permute-done.5 = bf16[8,32,256]{2,1,0:T(8,128)(2,1)S(1)} collective-permute-done((bf16[8,32,256]{2,1,0:T(8,128)(2,1)S(1)}, bf16[8,32,256]{2,1,0:T(8,128)(2,1)S(1)}, u32[]{:S(2)}, u32[]{:S(2)}) %collective-permute-start.5) | collective-permute-done | bytes 131104 | tf_op jit(solution)/shard_map/ppermute | solution.py:82
  99.1 0.0 collective-permute-done.4
  99.2 1.5 collective-permute-start.6
  100.7 1.5 collective-permute-start.7
  102.2 0.6 collective-permute-start.8
  102.7 1.1 shard_map.93
  103.8 7.5 %collective-permute-done.6.refs_1_ = bf16[3,8,32,256]{3,2,1,0:T(8,128)(2,1)S(1)} collective-permute-done((bf16[3,8,32,256]{3,2,1,0:T(8,128)(2,1)S(1)}, bf16[3,8,32,256]{3,2,1,0:T(8,128)(2,1)S(1)}, u32[]{:S(2)}, u32[]{:S(2)}) %collective-permute-start.6) | collective-permute-done | bytes 393248 | tf_op jit(solution)/shard_map/ppermute | solution.py:87
  111.3 6.9 %collective-permute-done.7.refs_2_ = bf16[3,8,32,256]{3,2,1,0:T(8,128)(2,1)S(1)} collective-permute-done((bf16[3,8,32,256]{3,2,1,0:T(8,128)(2,1)S(1)}, bf16[3,8,32,256]{3,2,1,0:T(8,128)(2,1)S(1)}, u32[]{:S(2)}, u32[]{:S(2)}) %collective-permute-start.7) | collective-permute-done | bytes 393248 | tf_op jit(solution)/shard_map/ppermute | solution.py:87
  118.2 7.2 %shard_map.89 = (f32[8,32,256]{2,1,0:T(8,128)S(1)}, f32[32,2048]{1,0:T(8,128)S(1)}) custom-call(s32[128]{0:T(128)S(1)} %fusion.slots_ref, bf16[8,16,256,256]{3,2,1,0:T(8,128)(2,1)S(1)} %bitcast.23, bf16[8,16,256,256]{3,2,1,0:T(8,128)(2,1)S(1)} %bitcast.24, bf16[3,8,32,256]{3,2,1,0:T(8,128)(2,1)S(1)} %pad_maximum_fusion.refs_0_, ...), custom_call_target="tpu_custom_call" | custom-call | flops 536870912 | bytes 16777216 | tf_op jit(solution)/shard_map/pallas_call | solution.py:42
  125.5 6.3 %shard_map.94 = s16[32,56,128]{2,1,0:T(8,128)(2,1)} custom-call(bf16[8,8,32,256]{3,2,1,0:T(8,128)(2,1)S(1)} %all-to-all-done.2.got_ref, f32[8,32,256]{2,1,0:T(8,128)S(1)} %get-tuple-element.29.adj_ref, f32[8,32,256]{2,1,0:T(8,128)S(1)} %get-tuple-element.30.zero_ref, f32[8,32,256]{2,1,0:T(8,128)S(1)} %get-tuple-element.31.one_ref, ...), custom_call_target="tpu_custom_call" | custom-call | tf_op jit(solution)/shard_map/pallas_call | solution.py:42
  131.8 2.6 %all-to-all-start.3 = ((s16[32,56,128]{2,1,0:T(8,128)(2,1)}), s16[32,56,128]{2,1,0:T(8,128)(2,1)S(1)}, u32[]{:S(2)}, u32[]{:S(2)}) async-start(s16[32,56,128]{2,1,0:T(8,128)(2,1)} %shard_map.94), calls=%async_computation.3 | async-start | bytes 917504 | tf_op jit(solution)/shard_map/all_to_all | solution.py:497
  134.4 1.0 copy.9
  135.3 14.0 %all-to-all-done.3.got_ref = s16[32,56,128]{2,1,0:T(8,128)(2,1)S(1)} async-done(((s16[32,56,128]{2,1,0:T(8,128)(2,1)}), s16[32,56,128]{2,1,0:T(8,128)(2,1)S(1)}, u32[]{:S(2)}, u32[]{:S(2)}) %all-to-all-start.3) | async-done | bytes 458784 | tf_op jit(solution)/shard_map/all_to_all | solution.py:497
  149.3 5.2 %shard_map.95 = f32[32,1024]{1,0:T(8,128)} custom-call(s16[32,56,128]{2,1,0:T(8,128)(2,1)S(1)} %all-to-all-done.3.got_ref), custom_call_target="tpu_custom_call" | custom-call | tf_op jit(solution)/shard_map/pallas_call | solution.py:42
  (19 shorter events, 0.1 us)
Async XLA Ops:
  0.7 1.0 copy-start.6
  1.6 0.9 copy-start.7
  2.6 0.9 copy-start.8
  3.8 1.0 copy-start.5
  4.9 8.7 %collective-permute-start.1 = (f32[3,8,8,256]{3,2,1,0:T(8,128)S(1)}, f32[3,8,8,256]{3,2,1,0:T(8,128)S(1)}, u32[]{:S(2)}, u32[]{:S(2)}) collective-permute-start(f32[3,8,8,256]{3,2,1,0:T(8,128)S(1)} %get-tuple-element.38), channel_id=1, source_target_pairs={{0,8},{8,0},{16,24},{24,16},{1,9},{9,1},{17,25},{25,17},{2,10},{10... | collective-permute-start | bytes 589832 | tf_op jit(solution)/shard_map/ppermute | solution.py:87
  7.9 10.6 %collective-permute-start.2 = (f32[3,8,8,256]{3,2,1,0:T(8,128)S(1)}, f32[3,8,8,256]{3,2,1,0:T(8,128)S(1)}, u32[]{:S(2)}, u32[]{:S(2)}) collective-permute-start(f32[3,8,8,256]{3,2,1,0:T(8,128)S(1)} %get-tuple-element.37), channel_id=1, source_target_pairs={{0,16},{8,24},{16,0},{24,8},{1,17},{9,25},{17,1},{25,9},{2,18},{10... | collective-permute-start | bytes 589832 | tf_op jit(solution)/shard_map/ppermute | solution.py:87
  9.4 9.1 %collective-permute-start.3 = (f32[3,8,8,256]{3,2,1,0:T(8,128)S(1)}, f32[3,8,8,256]{3,2,1,0:T(8,128)S(1)}, u32[]{:S(2)}, u32[]{:S(2)}) collective-permute-start(f32[3,8,8,256]{3,2,1,0:T(8,128)S(1)} %get-tuple-element.36), channel_id=1, source_target_pairs={{0,24},{8,16},{16,8},{24,0},{1,25},{9,17},{17,9},{25,1},{2,26},{10... | collective-permute-start | bytes 589832 | tf_op jit(solution)/shard_map/ppermute | solution.py:87
  18.5 5.8 %copy-start = (bf16[1,1,8,16,256,256]{5,4,3,2,1,0:T(8,128)(2,1)S(1)}, bf16[1,1,8,16,256,256]{5,4,3,2,1,0:T(8,128)(2,1)}, u32[]{:S(2)}) copy-start(bf16[1,1,8,16,256,256]{5,4,3,2,1,0:T(8,128)(2,1)} %param.10) | copy-start | bytes 50331652
  29.9 2.0 %collective-permute-start.9 = (bf16[4,8,32,256]{3,2,1,0:T(8,128)(2,1)S(1)}, bf16[4,8,32,256]{3,2,1,0:T(8,128)(2,1)S(1)}, u32[]{:S(2)}, u32[]{:S(2)}) collective-permute-start(bf16[4,8,32,256]{3,2,1,0:T(8,128)(2,1)S(1)} %get-tuple-element.24), channel_id=1, source_target_pairs={{0,1},{1,0},{2,3},{3,2},{4,5},{5,4},{6,7},{7,6},{8,9},{9,8},{10,11... | collective-permute-start | bytes 1572872 | tf_op jit(solution)/shard_map/ppermute | solution.py:79
  50.1 20.9 %all-to-all-start = ((bf16[8,32,8,256]{3,2,1,0:T(8,128)(2,1)}), bf16[8,32,8,256]{3,2,1,0:T(8,128)(2,1)S(1)}, u32[]{:S(2)}, u32[]{:S(2)}) async-start(bf16[8,32,8,256]{3,2,1,0:T(8,128)(2,1)} %copy-done.5), calls=%async_computation | async-start | bytes 2097152 | tf_op jit(solution)/shard_map/all_to_all | solution.py:90
  56.6 5.8 %copy-start.1 = (bf16[1,1,8,16,256,256]{5,4,3,2,1,0:T(8,128)(2,1)S(1)}, bf16[1,1,8,16,256,256]{5,4,3,2,1,0:T(8,128)(2,1)}, u32[]{:S(2)}) copy-start(bf16[1,1,8,16,256,256]{5,4,3,2,1,0:T(8,128)(2,1)} %param.10) | copy-start | bytes 50331652
  67.9 2.0 %collective-permute-start.10 = (bf16[4,8,32,256]{3,2,1,0:T(8,128)(2,1)S(1)}, bf16[4,8,32,256]{3,2,1,0:T(8,128)(2,1)S(1)}, u32[]{:S(2)}, u32[]{:S(2)}) collective-permute-start(bf16[4,8,32,256]{3,2,1,0:T(8,128)(2,1)S(1)} %get-tuple-element.27), channel_id=1, source_target_pairs={{0,1},{1,0},{2,3},{3,2},{4,5},{5,4},{6,7},{7,6},{8,9},{9,8},{10,11... | collective-permute-start | bytes 1572872 | tf_op jit(solution)/shard_map/ppermute | solution.py:79
  70.0 1.0 copy-start.4
  71.0 54.5 %all-to-all-start.2 = ((bf16[8,8,32,256]{3,2,1,0:T(8,128)(2,1)}), bf16[8,8,32,256]{3,2,1,0:T(8,128)(2,1)S(1)}, u32[]{:S(2)}, u32[]{:S(2)}) async-start(bf16[8,8,32,256]{3,2,1,0:T(8,128)(2,1)} %copy-done.4), calls=%async_computation.2 | async-start | bytes 2097152 | tf_op jit(solution)/shard_map/all_to_all | solution.py:90
  77.6 25.1 %copy-start.9 = (s32[1,1,2048,1]{2,3,1,0:T(1,128)S(1)}, s32[1,1,2048,1]{2,3,1,0:T(1,128)}, u32[]{:S(2)}) copy-start(s32[1,1,2048,1]{2,3,1,0:T(1,128)} %param.12) | copy-start | bytes 24580
  77.6 25.1 %copy-start.10 = (s32[1,1,2048]{2,1,0:T(1,128)S(1)}, s32[1,1,2048]{2,1,0:T(1,128)}, u32[]{:S(2)}) copy-start(s32[1,1,2048]{2,1,0:T(1,128)} %param.13) | copy-start | bytes 24580
  77.7 2.0 %collective-permute-start = (bf16[4,32,8,256]{3,2,1,0:T(8,128)(2,1)S(1)}, bf16[4,32,8,256]{3,2,1,0:T(8,128)(2,1)S(1)}, u32[]{:S(2)}, u32[]{:S(2)}) collective-permute-start(bf16[4,32,8,256]{3,2,1,0:T(8,128)(2,1)S(1)} %constant_dynamic-slice_fusion), channel_id=1, source_target_pairs={{0,1},{1,0},{2,3},{3,2},{4,5},{5,4},{6,7},{7,6},{8,9},{9,8},{10,11... | collective-permute-start | bytes 1572872 | tf_op jit(solution)/shard_map/ppermute | solution.py:79
  79.6 5.8 %copy-start.2 = (bf16[1,1,8,16,256,256]{5,4,3,2,1,0:T(8,128)(2,1)S(1)}, bf16[1,1,8,16,256,256]{5,4,3,2,1,0:T(8,128)(2,1)}, u32[]{:S(2)}) copy-start(bf16[1,1,8,16,256,256]{5,4,3,2,1,0:T(8,128)(2,1)} %param.10) | copy-start | bytes 50331652
  85.4 32.8 %copy-start.3 = (bf16[1,1,8,16,256,256]{5,4,3,2,1,0:T(8,128)(2,1)S(1)}, bf16[1,1,8,16,256,256]{5,4,3,2,1,0:T(8,128)(2,1)}, u32[]{:S(2)}) copy-start(bf16[1,1,8,16,256,256]{5,4,3,2,1,0:T(8,128)(2,1)} %param.10) | copy-start | bytes 50331652
  92.9 6.3 %collective-permute-start.5 = (bf16[8,32,256]{2,1,0:T(8,128)(2,1)S(1)}, bf16[8,32,256]{2,1,0:T(8,128)(2,1)S(1)}, u32[]{:S(2)}, u32[]{:S(2)}) collective-permute-start(bf16[8,32,256]{2,1,0:T(8,128)(2,1)S(1)} %get-tuple-element.21), channel_id=1, source_target_pairs={{0,7},{1,2},{2,1},{3,4},{4,3},{5,6},{6,5},{7,0},{8,15},{9,10},{10,... | collective-permute-start | bytes 393224 | tf_op jit(solution)/shard_map/ppermute | solution.py:82
  93.0 6.2 %collective-permute-start.4 = (bf16[8,32,256]{2,1,0:T(8,128)(2,1)S(1)}, bf16[8,32,256]{2,1,0:T(8,128)(2,1)S(1)}, u32[]{:S(2)}, u32[]{:S(2)}) collective-permute-start(bf16[8,32,256]{2,1,0:T(8,128)(2,1)S(1)} %get-tuple-element.21), channel_id=1, source_target_pairs={{0,1},{1,0},{2,3},{3,2},{4,5},{5,4},{6,7},{7,6},{8,9},{9,8},{10,11... | collective-permute-start | bytes 393224 | tf_op jit(solution)/shard_map/ppermute | solution.py:79
  99.2 12.1 %collective-permute-start.6 = (bf16[3,8,32,256]{3,2,1,0:T(8,128)(2,1)S(1)}, bf16[3,8,32,256]{3,2,1,0:T(8,128)(2,1)S(1)}, u32[]{:S(2)}, u32[]{:S(2)}) collective-permute-start(bf16[3,8,32,256]{3,2,1,0:T(8,128)(2,1)S(1)} %pad_maximum_fusion.refs_0_), channel_id=1, source_target_pairs={{0,8},{8,0},{16,24},{24,16},{1,9},{9,1},{17,25},{25,17},{2,10},{10... | collective-permute-start | bytes 1179656 | tf_op jit(solution)/shard_map/ppermute | solution.py:87
  100.7 17.5 %collective-permute-start.7 = (bf16[3,8,32,256]{3,2,1,0:T(8,128)(2,1)S(1)}, bf16[3,8,32,256]{3,2,1,0:T(8,128)(2,1)S(1)}, u32[]{:S(2)}, u32[]{:S(2)}) collective-permute-start(bf16[3,8,32,256]{3,2,1,0:T(8,128)(2,1)S(1)} %pad_maximum_fusion.refs_0_), channel_id=1, source_target_pairs={{0,16},{8,24},{16,0},{24,8},{1,17},{9,25},{17,1},{25,9},{2,18},{10... | collective-permute-start | bytes 1179656 | tf_op jit(solution)/shard_map/ppermute | solution.py:87
  102.2 16.0 %collective-permute-start.8 = (bf16[3,8,32,256]{3,2,1,0:T(8,128)(2,1)S(1)}, bf16[3,8,32,256]{3,2,1,0:T(8,128)(2,1)S(1)}, u32[]{:S(2)}, u32[]{:S(2)}) collective-permute-start(bf16[3,8,32,256]{3,2,1,0:T(8,128)(2,1)S(1)} %pad_maximum_fusion.refs_0_), channel_id=1, source_target_pairs={{0,24},{8,16},{16,8},{24,0},{1,25},{9,17},{17,9},{25,1},{2,26},{10... | collective-permute-start | bytes 1179656 | tf_op jit(solution)/shard_map/ppermute | solution.py:87
  131.8 17.6 %all-to-all-start.3 = ((s16[32,56,128]{2,1,0:T(8,128)(2,1)}), s16[32,56,128]{2,1,0:T(8,128)(2,1)S(1)}, u32[]{:S(2)}, u32[]{:S(2)}) async-start(s16[32,56,128]{2,1,0:T(8,128)(2,1)} %shard_map.94), calls=%async_computation.3 | async-start | bytes 917504 | tf_op jit(solution)/shard_map/all_to_all | solution.py:497

commit v3 on v2

--- a/solution.py
+++ b/solution.py
@@ -38,7 +38,7 @@
     return lax.broadcasted_iota(I32, dims, axis)
 
 
-def kernel_call(kernel, steps, scalars, ins, outs, args, scratch=(), limit=24 * MIB, flops=0):
+def kernel_call(kernel, steps, scalars, ins, outs, args, scratch=(), limit=50 * MIB, flops=0):
     return pl.pallas_call(
         kernel,
         out_shape=[o for _, o in outs],
@@ -128,6 +128,7 @@
             (along((1,) + piece, 0), shape((split,) + piece, F32)),
         ],
         (emissivity, blackbody, loss_weights),
+        limit=60 * MIB,
     )
 
     band = lax.axis_index("band")
@@ -196,7 +197,7 @@
             pay_ref[mine + s] = (own_ref[s] + near_ref[s].astype(F32)).astype(BF16)
             pay_ref[split - mine + s] = far_ref[s]
 
-    def collect(own, near, far):
+    def collect(own, near, far, before=None):
         (pay,) = kernel_call(
             merge,
             1,
@@ -205,6 +206,8 @@
             [(whole(team_shape), shape(team_shape, BF16))],
             (own, inner(near), far),
         )
+        if before is not None:
+            pay, _ = lax.optimization_barrier((pay, before))
         return team_exchange(pay)
 
     def products(slots_ref, m_refs, held, finish):
@@ -411,6 +414,7 @@
             count = jnp.maximum(total[at + 2 * bands : at + 2 * bands + 1], 1.0)
             out_ref[:, t * LANES : (t + 1) * LANES] = sums / count
 
+    slots, rank, labels = lax.optimization_barrier((slots, rank, labels))
     full, own, near, far = kernel_call(
         adjoint_first,
         4,
@@ -421,7 +425,7 @@
         total_scratch,
         flops=pass_flops,
     )
-    got_one = collect(own, near, far)
+    got_one = collect(own, near, far, start)
 
     mine = (1 - me % 2) * split
     start_near = inner(lax.dynamic_slice_in_dim(start, mine, split, axis=0))
@@ -436,7 +440,7 @@
         flops=pass_flops,
     )
     rad = jnp.stack([rad, inner(rad), outer(rad)])
-    rads = [rad] + [across(rad, d) for d in range(1, split)]
+    got_one, _ = lax.optimization_barrier((got_one, rad))
 
     adjoint_one, own, near, far = kernel_call(
         adjoint_second,
@@ -450,6 +454,7 @@
     )
     got_zero = collect(own, near, far)
 
+    rads = [rad] + [across(rad, d) for d in range(1, split)]
     one, radiosity = kernel_call(
         forward_second,
         4,

time: 155 us -> 157 us (1.013)
  local copies, waits for them, and re-layouts: 23.9 us -> 4.45 us
  blocking collectives: 18.1 us -> 0 us
  Pallas kernels: 38.9 us -> 54.4 us
  waiting for transfers between devices: 48.3 us -> 63.2 us
  starting transfers between devices: 24.3 us -> 33.5 us
    unnamed x23 -> x7, local copies, waits for them, and re-layouts: 23.1 us -> 2.37 us
    all_to_all x1 -> x0, blocking collectives: 18.1 us -> none  [team_exchange(): lax.all_to_all(block, ('band', 'patch'), 0, 0, axis_index_groups=teams, t...]
    ppermute x6, waiting for transfers between devices: 22.7 us -> 38.7 us  [across(): return lax.ppermute(block, 'band', [(i, i ^ d) for i in range(split)])]
    pallas_call x10, Pallas kernels: 38.9 us -> 54.4 us  [kernel_call(): pl.pallas_call(kernel, out_shape=[o for _, o in outs], grid_spec=pltpu.Pr...]
    all_to_all x2 -> x3, starting transfers between devices: 13.1 us -> 20.9 us  [team_exchange(): lax.all_to_all(block, ('band', 'patch'), 0, 0, axis_index_groups=teams, t...]
    ppermute x1, starting transfers between devices: 0.1 us -> 1.72 us  [outer(): lax.ppermute(block, 'patch', [(i, (i + (1 if i % 2 else -1)) % groups) fo...]
  transfers between devices with their start and end apart: 14 -> 15, of which waited for: 9 -> 10; matrix products, arithmetic and copies ran while one was open for 1% -> 2% of each run, Pallas kernels for 14% -> 19%
where the time goes in v3:
time: 157 us; the launch traced here: 156 us
  waiting for transfers between devices  63.2 us (40%)
  Pallas kernels  54.4 us (35%)
  starting transfers between devices  33.5 us (21%)
  local copies, waits for them, and re-layouts  4.45 us (3%)
    pallas_call x10, Pallas kernels, kernel_call(): pl.pallas_call(kernel, out_shape=[o for _, o in outs], grid_spec=pltpu.Pr...  54.4 us
    ppermute x6, waiting for transfers between devices, across(): return lax.ppermute(block, 'band', [(i, i ^ d) for i in range(split)])  38.7 us
    all_to_all x3, starting transfers between devices, team_exchange(): lax.all_to_all(block, ('band', 'patch'), 0, 0, axis_index_groups=teams, t...  20.9 us
    all_to_all x1, waiting for transfers between devices, body(): send = lax.all_to_all(send, ('band', 'patch'), 0, 0, tiled=True)  14 us
    ppermute x6, starting transfers between devices, across(): return lax.ppermute(block, 'band', [(i, i ^ d) for i in range(split)])  7.04 us
    ppermute x4, waiting for transfers between devices, inner(): return lax.ppermute(block, 'patch', [(i, i ^ 1) for i in range(groups)])  5.69 us
    ppermute x1, waiting for transfers between devices, outer(): lax.ppermute(block, 'patch', [(i, (i + (1 if i % 2 else -1)) % groups) fo...  4.87 us
    all_to_all x1, starting transfers between devices, body(): send = lax.all_to_all(send, ('band', 'patch'), 0, 0, tiled=True)  3.43 us
  transfers between devices with their start and end apart: 15, of which 10 were waited for; matrix products, arithmetic and copies ran while one was open for 2% of the time, Pallas kernels for 19%

profile of v3, /device:TPU:0, one launch (start us, length us, event | category | flops | bytes accessed | tf_op | source)
XLA Modules:
  0.0 156.4 jit_solution(12710304404011293192)
XLA Ops:
  0.6 3.5 %shard_map.87 = (bf16[8,32,8,256]{3,2,1,0:T(8,128)(2,1)}, f32[4,3,8,8,256]{4,3,2,1,0:T(8,128)}) custom-call(f32[8,8192]{1,0:T(8,128)} %e_ref.1, f32[8,8192]{1,0:T(8,128)} %b_ref.1, f32[8,8192]{1,0:T(8,128)} %w_ref.1), custom_call_target="tpu_custom_call" | custom-call | tf_op jit(solution)/shard_map/pallas_call | solution.py:42
  4.1 8.1 %all-to-all-start = ((bf16[8,32,8,256]{3,2,1,0:T(8,128)(2,1)}), bf16[8,32,8,256]{3,2,1,0:T(8,128)(2,1)S(1)}, u32[]{:S(2)}, u32[]{:S(2)}) async-start(bf16[8,32,8,256]{3,2,1,0:T(8,128)(2,1)} %get-tuple-element.26), calls=%async_computation | async-start | bytes 2097152 | tf_op jit(solution)/shard_map/all_to_all | solution.py:90
  12.3 1.3 dynamic-slice_bitcast_fusion
  13.6 1.5 collective-permute-start.1
  15.1 1.5 collective-permute-start.2
  16.6 0.6 collective-permute-start.3
  17.1 0.8 reshape.20
  17.9 0.0 copy-start
  17.9 0.7 copy-done
  18.6 0.0 copy-start.2
  18.6 0.7 copy-done.2
  19.3 1.0 shard_map.86
  20.4 10.0 %collective-permute-done.1.refs_1_ = f32[3,8,8,256]{3,2,1,0:T(8,128)S(1)} collective-permute-done((f32[3,8,8,256]{3,2,1,0:T(8,128)S(1)}, f32[3,8,8,256]{3,2,1,0:T(8,128)S(1)}, u32[]{:S(2)}, u32[]{:S(2)}) %collective-permute-start.1) | collective-permute-done | bytes 196640 | tf_op jit(solution)/shard_map/ppermute | solution.py:87
  30.3 0.8 collective-permute-done.2.refs_2_
  31.1 2.7 %collective-permute-done.3.refs_3_ = f32[3,8,8,256]{3,2,1,0:T(8,128)S(1)} collective-permute-done((f32[3,8,8,256]{3,2,1,0:T(8,128)S(1)}, f32[3,8,8,256]{3,2,1,0:T(8,128)S(1)}, u32[]{:S(2)}, u32[]{:S(2)}) %collective-permute-start.3) | collective-permute-done | bytes 196640 | tf_op jit(solution)/shard_map/ppermute | solution.py:87
  33.8 8.6 %shard_map.88 = (f32[3,8,32,256]{3,2,1,0:T(8,128)S(1)}, f32[4,8,32,256]{3,2,1,0:T(8,128)S(1)}, bf16[4,8,32,256]{3,2,1,0:T(8,128)(2,1)S(1)}, bf16[4,8,32,256]{3,2,1,0:T(8,128)(2,1)S(1)}) custom-call(s32[128]{0:T(128)S(1)} %fusion.slots_ref, bf16[8,16,256,256]{3,2,1,0:T(8,128)(2,1)} %bitcast.22, bf16[8,16,256,256]{3,2,1,0:T(8,128)(2,1)} %bitcast.23, ...), custom_call_target="tpu_custom_call" | custom-call | flops 536870912 | bytes 16777216 | tf_op jit(solution)/shard_map/pallas_call | solution.py:42
  42.4 0.1 collective-permute-start.9
  42.5 1.9 %collective-permute-done.9.near_ref = bf16[4,8,32,256]{3,2,1,0:T(8,128)(2,1)S(1)} collective-permute-done((bf16[4,8,32,256]{3,2,1,0:T(8,128)(2,1)S(1)}, bf16[4,8,32,256]{3,2,1,0:T(8,128)(2,1)S(1)}, u32[]{:S(2)}, u32[]{:S(2)}) %collective-permute-start.9) | collective-permute-done | bytes 524320 | tf_op jit(solution)/shard_map/ppermute | solution.py:79
  44.4 1.1 shard_map.91
  45.5 0.0 all-to-all-done.team_ref
  45.5 6.1 %all-to-all-start.1 = ((bf16[8,8,32,256]{3,2,1,0:T(8,128)(2,1)}), bf16[8,8,32,256]{3,2,1,0:T(8,128)(2,1)}, u32[]{:S(2)}, u32[]{:S(2)}) async-start(bf16[8,8,32,256]{3,2,1,0:T(8,128)(2,1)} %shard_map.91), calls=%async_computation.1 | async-start | bytes 2097152 | tf_op jit(solution)/shard_map/all_to_all | solution.py:90
  51.6 0.1 collective-permute-start
  51.7 1.9 %collective-permute-done.near_ref = bf16[4,32,8,256]{3,2,1,0:T(8,128)(2,1)S(1)} collective-permute-done((bf16[4,32,8,256]{3,2,1,0:T(8,128)(2,1)S(1)}, bf16[4,32,8,256]{3,2,1,0:T(8,128)(2,1)S(1)}, u32[]{:S(2)}, u32[]{:S(2)}) %collective-permute-start) | collective-permute-done | bytes 524320 | tf_op jit(solution)/shard_map/ppermute | solution.py:79
  53.6 9.6 %shard_map.89 = (f32[8,32,256]{2,1,0:T(8,128)S(1)}, bf16[8,32,256]{2,1,0:T(8,128)(2,1)S(1)}) custom-call(s32[128]{0:T(128)S(1)} %fusion.slots_ref, bf16[8,16,256,256]{3,2,1,0:T(8,128)(2,1)} %bitcast.24, bf16[8,16,256,256]{3,2,1,0:T(8,128)(2,1)} %bitcast.25, bf16[8,32,8,256]{3,2,1,0:T(8,128)(2,1)S(1)} %all-to-all-done.team_ref, ...), custom_call_target="tpu_custom_call" | custom-call | flops 536870912 | bytes 16777216 | tf_op jit(solution)/shard_map/pallas_call | solution.py:42
  63.2 0.2 collective-permute-start.4
  63.4 1.7 %collective-permute-start.5 = (bf16[8,32,256]{2,1,0:T(8,128)(2,1)S(1)}, bf16[8,32,256]{2,1,0:T(8,128)(2,1)S(1)}, u32[]{:S(2)}, u32[]{:S(2)}) collective-permute-start(bf16[8,32,256]{2,1,0:T(8,128)(2,1)S(1)} %get-tuple-element.29), channel_id=1, source_target_pairs={{0,7},{1,2},{2,1},{3,4},{4,3},{5,6},{6,5},{7,0},{8,15},{9,10},{10,... | collective-permute-start | bytes 393224 | tf_op jit(solution)/shard_map/ppermute | solution.py:82
  65.1 0.0 collective-permute-done.4
  65.1 4.9 %collective-permute-done.5 = bf16[8,32,256]{2,1,0:T(8,128)(2,1)S(1)} collective-permute-done((bf16[8,32,256]{2,1,0:T(8,128)(2,1)S(1)}, bf16[8,32,256]{2,1,0:T(8,128)(2,1)S(1)}, u32[]{:S(2)}, u32[]{:S(2)}) %collective-permute-start.5) | collective-permute-done | bytes 131104 | tf_op jit(solution)/shard_map/ppermute | solution.py:82
  70.0 0.0 all-to-all-done.1.got_ref
  70.0 8.6 %shard_map.92 = (f32[8,32,256]{2,1,0:T(8,128)S(1)}, f32[4,8,32,256]{3,2,1,0:T(8,128)S(1)}, bf16[4,8,32,256]{3,2,1,0:T(8,128)(2,1)S(1)}, bf16[4,8,32,256]{3,2,1,0:T(8,128)(2,1)S(1)}) custom-call(s32[128]{0:T(128)S(1)} %fusion.slots_ref, bf16[8,16,256,256]{3,2,1,0:T(8,128)(2,1)} %bitcast.26, bf16[8,16,256,256]{3,2,1,0:T(8,128)(2,1)} %bitcast.27, ...), custom_call_target="tpu_custom_call" | custom-call | flops 536870912 | bytes 16777216 | tf_op jit(solution)/shard_map/pallas_call | solution.py:42
  78.6 0.1 collective-permute-start.10
  78.7 1.9 %collective-permute-done.10.near_ref = bf16[4,8,32,256]{3,2,1,0:T(8,128)(2,1)S(1)} collective-permute-done((bf16[4,8,32,256]{3,2,1,0:T(8,128)(2,1)S(1)}, bf16[4,8,32,256]{3,2,1,0:T(8,128)(2,1)S(1)}, u32[]{:S(2)}, u32[]{:S(2)}) %collective-permute-start.10) | collective-permute-done | bytes 524320 | tf_op jit(solution)/shard_map/ppermute | solution.py:79
  80.6 1.1 shard_map.93
  81.7 6.6 %all-to-all-start.2 = ((bf16[8,8,32,256]{3,2,1,0:T(8,128)(2,1)}), bf16[8,8,32,256]{3,2,1,0:T(8,128)(2,1)S(1)}, u32[]{:S(2)}, u32[]{:S(2)}) async-start(bf16[8,8,32,256]{3,2,1,0:T(8,128)(2,1)} %shard_map.93), calls=%async_computation.2 | async-start | bytes 2097152 | tf_op jit(solution)/shard_map/all_to_all | solution.py:90
  88.4 1.5 collective-permute-start.6
  89.8 1.5 collective-permute-start.7
  91.3 0.6 collective-permute-start.8
  91.9 17.7 %collective-permute-done.6.refs_1_ = bf16[3,8,32,256]{3,2,1,0:T(8,128)(2,1)S(1)} collective-permute-done((bf16[3,8,32,256]{3,2,1,0:T(8,128)(2,1)S(1)}, bf16[3,8,32,256]{3,2,1,0:T(8,128)(2,1)S(1)}, u32[]{:S(2)}, u32[]{:S(2)}) %collective-permute-start.6) | collective-permute-done | bytes 393248 | tf_op jit(solution)/shard_map/ppermute | solution.py:87
  109.6 0.0 collective-permute-done.7.refs_2_
  109.6 7.6 %collective-permute-done.8.refs_3_ = bf16[3,8,32,256]{3,2,1,0:T(8,128)(2,1)S(1)} collective-permute-done((bf16[3,8,32,256]{3,2,1,0:T(8,128)(2,1)S(1)}, bf16[3,8,32,256]{3,2,1,0:T(8,128)(2,1)S(1)}, u32[]{:S(2)}, u32[]{:S(2)}) %collective-permute-start.8) | collective-permute-done | bytes 393248 | tf_op jit(solution)/shard_map/ppermute | solution.py:87
  117.1 9.4 %shard_map.90 = (f32[8,32,256]{2,1,0:T(8,128)S(1)}, f32[32,2048]{1,0:T(8,128)S(1)}) custom-call(s32[128]{0:T(128)S(1)} %fusion.slots_ref, bf16[8,16,256,256]{3,2,1,0:T(8,128)(2,1)} %bitcast.28, bf16[8,16,256,256]{3,2,1,0:T(8,128)(2,1)} %bitcast.29, bf16[3,8,32,256]{3,2,1,0:T(8,128)(2,1)S(1)} %pad_maximum_fusion.refs_0_, ...), custom_call_target="tpu_custom_call" | custom-call | flops 536870912 | bytes 16777216 | tf_op jit(solution)/shard_map/pallas_call | solution.py:42
  126.5 0.0 all-to-all-done.2.got_ref
  126.5 0.0 copy-done.1
  126.5 6.3 %shard_map.94 = s16[32,56,128]{2,1,0:T(8,128)(2,1)} custom-call(bf16[8,8,32,256]{3,2,1,0:T(8,128)(2,1)S(1)} %all-to-all-done.2.got_ref, f32[8,32,256]{2,1,0:T(8,128)S(1)} %get-tuple-element.39.adj_ref, f32[8,32,256]{2,1,0:T(8,128)S(1)} %get-tuple-element.40.zero_ref, f32[8,32,256]{2,1,0:T(8,128)S(1)} %get-tuple-element.41.one_ref, ...), custom_call_target="tpu_custom_call" | custom-call | tf_op jit(solution)/shard_map/pallas_call | solution.py:42
  132.8 3.4 %all-to-all-start.3 = ((s16[32,56,128]{2,1,0:T(8,128)(2,1)}), s16[32,56,128]{2,1,0:T(8,128)(2,1)S(1)}, u32[]{:S(2)}, u32[]{:S(2)}) async-start(s16[32,56,128]{2,1,0:T(8,128)(2,1)} %shard_map.94), calls=%async_computation.3 | async-start | bytes 917504 | tf_op jit(solution)/shard_map/all_to_all | solution.py:502
  136.3 1.0 copy.9
  137.2 14.0 %all-to-all-done.3.got_ref = s16[32,56,128]{2,1,0:T(8,128)(2,1)S(1)} async-done(((s16[32,56,128]{2,1,0:T(8,128)(2,1)}), s16[32,56,128]{2,1,0:T(8,128)(2,1)S(1)}, u32[]{:S(2)}, u32[]{:S(2)}) %all-to-all-start.3) | async-done | bytes 458784 | tf_op jit(solution)/shard_map/all_to_all | solution.py:502
  151.2 5.2 %shard_map.95 = f32[32,1024]{1,0:T(8,128)} custom-call(s16[32,56,128]{2,1,0:T(8,128)(2,1)S(1)} %all-to-all-done.3.got_ref), custom_call_target="tpu_custom_call" | custom-call | tf_op jit(solution)/shard_map/pallas_call | solution.py:42
  (4 shorter events, 0.1 us)
Async XLA Ops:
  4.1 41.3 %all-to-all-start = ((bf16[8,32,8,256]{3,2,1,0:T(8,128)(2,1)}), bf16[8,32,8,256]{3,2,1,0:T(8,128)(2,1)S(1)}, u32[]{:S(2)}, u32[]{:S(2)}) async-start(bf16[8,32,8,256]{3,2,1,0:T(8,128)(2,1)} %get-tuple-element.26), calls=%async_computation | async-start | bytes 2097152 | tf_op jit(solution)/shard_map/all_to_all | solution.py:90
  13.6 16.7 %collective-permute-start.1 = (f32[3,8,8,256]{3,2,1,0:T(8,128)S(1)}, f32[3,8,8,256]{3,2,1,0:T(8,128)S(1)}, u32[]{:S(2)}, u32[]{:S(2)}) collective-permute-start(f32[3,8,8,256]{3,2,1,0:T(8,128)S(1)} %get-tuple-element.48), channel_id=1, source_target_pairs={{0,8},{8,0},{16,24},{24,16},{1,9},{9,1},{17,25},{25,17},{2,10},{10... | collective-permute-start | bytes 589832 | tf_op jit(solution)/shard_map/ppermute | solution.py:87
  15.1 16.0 %collective-permute-start.2 = (f32[3,8,8,256]{3,2,1,0:T(8,128)S(1)}, f32[3,8,8,256]{3,2,1,0:T(8,128)S(1)}, u32[]{:S(2)}, u32[]{:S(2)}) collective-permute-start(f32[3,8,8,256]{3,2,1,0:T(8,128)S(1)} %get-tuple-element.47), channel_id=1, source_target_pairs={{0,16},{8,24},{16,0},{24,8},{1,17},{9,25},{17,1},{25,9},{2,18},{10... | collective-permute-start | bytes 589832 | tf_op jit(solution)/shard_map/ppermute | solution.py:87
  16.6 17.2 %collective-permute-start.3 = (f32[3,8,8,256]{3,2,1,0:T(8,128)S(1)}, f32[3,8,8,256]{3,2,1,0:T(8,128)S(1)}, u32[]{:S(2)}, u32[]{:S(2)}) collective-permute-start(f32[3,8,8,256]{3,2,1,0:T(8,128)S(1)} %get-tuple-element.46), channel_id=1, source_target_pairs={{0,24},{8,16},{16,8},{24,0},{1,25},{9,17},{17,9},{25,1},{2,26},{10... | collective-permute-start | bytes 589832 | tf_op jit(solution)/shard_map/ppermute | solution.py:87
  17.9 0.7 copy-start
  18.6 0.7 copy-start.2
  42.4 2.0 %collective-permute-start.9 = (bf16[4,8,32,256]{3,2,1,0:T(8,128)(2,1)S(1)}, bf16[4,8,32,256]{3,2,1,0:T(8,128)(2,1)S(1)}, u32[]{:S(2)}, u32[]{:S(2)}) collective-permute-start(bf16[4,8,32,256]{3,2,1,0:T(8,128)(2,1)S(1)} %get-tuple-element.32), channel_id=1, source_target_pairs={{0,1},{1,0},{2,3},{3,2},{4,5},{5,4},{6,7},{7,6},{8,9},{9,8},{10,11... | collective-permute-start | bytes 1572872 | tf_op jit(solution)/shard_map/ppermute | solution.py:79
  45.5 24.6 %all-to-all-start.1 = ((bf16[8,8,32,256]{3,2,1,0:T(8,128)(2,1)}), bf16[8,8,32,256]{3,2,1,0:T(8,128)(2,1)}, u32[]{:S(2)}, u32[]{:S(2)}) async-start(bf16[8,8,32,256]{3,2,1,0:T(8,128)(2,1)} %shard_map.91), calls=%async_computation.1 | async-start | bytes 2097152 | tf_op jit(solution)/shard_map/all_to_all | solution.py:90
  51.6 2.0 %collective-permute-start = (bf16[4,32,8,256]{3,2,1,0:T(8,128)(2,1)S(1)}, bf16[4,32,8,256]{3,2,1,0:T(8,128)(2,1)S(1)}, u32[]{:S(2)}, u32[]{:S(2)}) collective-permute-start(bf16[4,32,8,256]{3,2,1,0:T(8,128)(2,1)S(1)} %constant_dynamic-slice_fusion), channel_id=1, source_target_pairs={{0,1},{1,0},{2,3},{3,2},{4,5},{5,4},{6,7},{7,6},{8,9},{9,8},{10,11... | collective-permute-start | bytes 1572872 | tf_op jit(solution)/shard_map/ppermute | solution.py:79
  63.2 1.9 %collective-permute-start.4 = (bf16[8,32,256]{2,1,0:T(8,128)(2,1)S(1)}, bf16[8,32,256]{2,1,0:T(8,128)(2,1)S(1)}, u32[]{:S(2)}, u32[]{:S(2)}) collective-permute-start(bf16[8,32,256]{2,1,0:T(8,128)(2,1)S(1)} %get-tuple-element.29), channel_id=1, source_target_pairs={{0,1},{1,0},{2,3},{3,2},{4,5},{5,4},{6,7},{7,6},{8,9},{9,8},{10,11... | collective-permute-start | bytes 393224 | tf_op jit(solution)/shard_map/ppermute | solution.py:79
  63.4 6.6 %collective-permute-start.5 = (bf16[8,32,256]{2,1,0:T(8,128)(2,1)S(1)}, bf16[8,32,256]{2,1,0:T(8,128)(2,1)S(1)}, u32[]{:S(2)}, u32[]{:S(2)}) collective-permute-start(bf16[8,32,256]{2,1,0:T(8,128)(2,1)S(1)} %get-tuple-element.29), channel_id=1, source_target_pairs={{0,7},{1,2},{2,1},{3,4},{4,3},{5,6},{6,5},{7,0},{8,15},{9,10},{10,... | collective-permute-start | bytes 393224 | tf_op jit(solution)/shard_map/ppermute | solution.py:82
  78.6 2.0 %collective-permute-start.10 = (bf16[4,8,32,256]{3,2,1,0:T(8,128)(2,1)S(1)}, bf16[4,8,32,256]{3,2,1,0:T(8,128)(2,1)S(1)}, u32[]{:S(2)}, u32[]{:S(2)}) collective-permute-start(bf16[4,8,32,256]{3,2,1,0:T(8,128)(2,1)S(1)} %get-tuple-element.37), channel_id=1, source_target_pairs={{0,1},{1,0},{2,3},{3,2},{4,5},{5,4},{6,7},{7,6},{8,9},{9,8},{10,11... | collective-permute-start | bytes 1572872 | tf_op jit(solution)/shard_map/ppermute | solution.py:79
  81.7 44.8 %all-to-all-start.2 = ((bf16[8,8,32,256]{3,2,1,0:T(8,128)(2,1)}), bf16[8,8,32,256]{3,2,1,0:T(8,128)(2,1)S(1)}, u32[]{:S(2)}, u32[]{:S(2)}) async-start(bf16[8,8,32,256]{3,2,1,0:T(8,128)(2,1)} %shard_map.93), calls=%async_computation.2 | async-start | bytes 2097152 | tf_op jit(solution)/shard_map/all_to_all | solution.py:90
  88.4 38.2 %copy-start.1 = (s32[1,1,2048,1]{2,3,1,0:T(1,128)S(1)}, s32[1,1,2048,1]{2,3,1,0:T(1,128)}, u32[]{:S(2)}) copy-start(s32[1,1,2048,1]{2,3,1,0:T(1,128)} %param.12) | copy-start | bytes 24580
  88.4 21.2 %collective-permute-start.6 = (bf16[3,8,32,256]{3,2,1,0:T(8,128)(2,1)S(1)}, bf16[3,8,32,256]{3,2,1,0:T(8,128)(2,1)S(1)}, u32[]{:S(2)}, u32[]{:S(2)}) collective-permute-start(bf16[3,8,32,256]{3,2,1,0:T(8,128)(2,1)S(1)} %pad_maximum_fusion.refs_0_), channel_id=1, source_target_pairs={{0,8},{8,0},{16,24},{24,16},{1,9},{9,1},{17,25},{25,17},{2,10},{10... | collective-permute-start | bytes 1179656 | tf_op jit(solution)/shard_map/ppermute | solution.py:87
  89.8 19.7 %collective-permute-start.7 = (bf16[3,8,32,256]{3,2,1,0:T(8,128)(2,1)S(1)}, bf16[3,8,32,256]{3,2,1,0:T(8,128)(2,1)S(1)}, u32[]{:S(2)}, u32[]{:S(2)}) collective-permute-start(bf16[3,8,32,256]{3,2,1,0:T(8,128)(2,1)S(1)} %pad_maximum_fusion.refs_0_), channel_id=1, source_target_pairs={{0,16},{8,24},{16,0},{24,8},{1,17},{9,25},{17,1},{25,9},{2,18},{10... | collective-permute-start | bytes 1179656 | tf_op jit(solution)/shard_map/ppermute | solution.py:87
  91.3 25.8 %collective-permute-start.8 = (bf16[3,8,32,256]{3,2,1,0:T(8,128)(2,1)S(1)}, bf16[3,8,32,256]{3,2,1,0:T(8,128)(2,1)S(1)}, u32[]{:S(2)}, u32[]{:S(2)}) collective-permute-start(bf16[3,8,32,256]{3,2,1,0:T(8,128)(2,1)S(1)} %pad_maximum_fusion.refs_0_), channel_id=1, source_target_pairs={{0,24},{8,16},{16,8},{24,0},{1,25},{9,17},{17,9},{25,1},{2,26},{10... | collective-permute-start | bytes 1179656 | tf_op jit(solution)/shard_map/ppermute | solution.py:87
  132.8 18.4 %all-to-all-start.3 = ((s16[32,56,128]{2,1,0:T(8,128)(2,1)}), s16[32,56,128]{2,1,0:T(8,128)(2,1)S(1)}, u32[]{:S(2)}, u32[]{:S(2)}) async-start(s16[32,56,128]{2,1,0:T(8,128)(2,1)} %shard_map.94), calls=%async_computation.3 | async-start | bytes 917504 | tf_op jit(solution)/shard_map/all_to_all | solution.py:502

commit v4 on v2

--- a/solution.py
+++ b/solution.py
@@ -38,7 +38,7 @@
     return lax.broadcasted_iota(I32, dims, axis)
 
 
-def kernel_call(kernel, steps, scalars, ins, outs, args, scratch=(), limit=24 * MIB, flops=0):
+def kernel_call(kernel, steps, scalars, ins, outs, args, scratch=(), limit=50 * MIB, flops=0):
     return pl.pallas_call(
         kernel,
         out_shape=[o for _, o in outs],
@@ -69,12 +69,6 @@
     surfaces = rows // 2
     me = lax.axis_index("patch")
 
-    team_of = [(g, (g + 1) % groups) for g in range(1, groups, 2)]
-    teams = [[b * groups + g for g in pair for b in range(split)] for pair in team_of]
-
-    def place_in_team():
-        return 1 - lax.axis_index("patch") % 2
-
     def inner(block):
         return lax.ppermute(block, "patch", [(i, i ^ 1) for i in range(groups)])
 
@@ -86,10 +80,13 @@
     def across(block, d):
         return lax.ppermute(block, "band", [(i, i ^ d) for i in range(split)])
 
-    def team_exchange(block):
-        return lax.all_to_all(
-            block, ("band", "patch"), 0, 0, axis_index_groups=teams, tiled=True
-        )
+    def outer_across(block, d):
+        route = []
+        for i in range(split):
+            for g in range(groups):
+                beyond = (g + (1 if g % 2 else -1)) % groups
+                route.append((i * groups + g, (i ^ d) * groups + beyond))
+        return lax.ppermute(block, ("band", "patch"), route)
 
     columns = column_blocks.reshape(rb_count * depth)
     column_group = columns // per_group
@@ -97,46 +94,42 @@
     slots = third * per_group + columns % per_group
     matrix = view_blocks.reshape(rb_count, depth, width, width)
     block_shape = (rb_count, bands, width)
-    team_shape = (2 * split,) + block_shape
     part_shape = (split,) + block_shape
     pass_flops = 2 * bands * rb_count * depth * width * width
     once = rb_count // 4
     half = depth // 2
 
-    def prepare(e_ref, b_ref, w_ref, start_ref, full_ref):
-        for r in range(rb_count):
-            cut = slice(r * width, (r + 1) * width)
-            e, b, w = e_ref[:, cut], b_ref[:, cut], w_ref[:, cut]
-            start = (e * b).astype(BF16)
-            for d in range(2 * split):
-                start_ref[d, r] = start
-            full_ref[0, 0, r] = e
-            full_ref[0, 1, r] = b
-            full_ref[0, 2, r] = w
-
-    piece = (3, rb_count, part_bands, width)
-    start, full = kernel_call(
+    def prepare(e_ref, b_ref, w_ref, start_ref, *piece_refs):
+        band = lax.axis_index("band")
+        for c in range(per_group):
+            cut = slice(c * width, (c + 1) * width)
+            start_ref[c] = (e_ref[:, cut] * b_ref[:, cut]).astype(BF16)
+        for d in range(split):
+            cut = pl.ds(pl.multiple_of((band ^ d) * rows, rows), rows)
+            for a, ref in enumerate((e_ref, b_ref, w_ref)):
+                piece_refs[d][a] = ref[:, cut]
+
+    piece = (3, part_bands, rows)
+    start_shape = (per_group, part_bands, width)
+    start, *pieces = kernel_call(
         prepare,
-        split,
+        1,
         0,
-        [along((part_bands, rows), 1)] * 3,
-        [
-            (
-                along((2 * split, rb_count, part_bands, width), 1),
-                shape((2 * split, per_group, part_bands, width), BF16),
-            ),
-            (along((1,) + piece, 0), shape((split,) + piece, F32)),
-        ],
+        [whole((part_bands, per_group * width))] * 3,
+        [(whole(start_shape), shape(start_shape, BF16))]
+        + [(whole(piece), shape(piece, F32))] * split,
         (emissivity, blackbody, loss_weights),
-    )
-
-    band = lax.axis_index("band")
-    pieces = [
-        across(lax.dynamic_index_in_dim(full, band ^ d, keepdims=False), d) if d else
-        lax.dynamic_index_in_dim(full, band, keepdims=False)
-        for d in range(split)
-    ]
-    start = team_exchange(start)
+        limit=60 * MIB,
+    )
+    pieces = [across(pieces[d], d) if d else pieces[d] for d in range(split)]
+
+    def pair_of(block):
+        return jnp.stack([block, outer(block)])
+
+    def gather(pair, after):
+        pairs = [pair] + [across(pair, d) for d in range(1, split)]
+        pairs, _ = lax.optimization_barrier((pairs, after))
+        return pairs + [inner(jnp.stack([p[0] for p in pairs]))]
 
     def scatter_products(slots_ref, m_refs, value_of, outs, total):
         i = pl.program_id(0)
@@ -153,59 +146,76 @@
 
         @pl.when(i == pl.num_programs(0) - 1)
         def _():
-            for third_index, out_ref in enumerate(outs):
-                for s in range(split):
-                    at = third_index * per_group + s * rb_count
-                    out_ref[s] = total[at : at + rb_count].astype(out_ref.dtype)
+            own_ref, near_ref, *far_refs = outs
+            band = lax.axis_index("band")
+            for d in range(split):
+                at = (band ^ d) * rb_count
+                own_ref[d] = total[pl.ds(at, rb_count)]
+                near_ref[d] = total[pl.ds(per_group + at, rb_count)].astype(BF16)
+                far_refs[d][...] = total[pl.ds(2 * per_group + at, rb_count)].astype(BF16)
 
     matrix_specs = [
         pl.BlockSpec((once, half, width, width), lambda i, *_, h=h: (i, h, 0, 0)) for h in (0, 1)
     ]
-    part_outs = [(whole(part_shape), shape(part_shape, t)) for t in (F32, BF16, BF16)]
+    part_outs = [(whole(part_shape), shape(part_shape, t)) for t in (F32, BF16)]
+    part_outs += [(whole(block_shape), shape(block_shape, BF16))] * split
     total_scratch = [pltpu.VMEM((3 * per_group, bands, width), F32)]
     step_rows = along((once, bands, width), 0)
     full_rows = along((3, once, bands, width), 1)
 
     def adjoint_first(slots_ref, m0, m1, *refs):
-        piece_refs, (full_ref, own_ref, near_ref, far_ref, total) = refs[:split], refs[split:]
+        piece_refs, full_ref, outs, total = refs[:split], refs[split], refs[split + 1 : -1], refs[-1]
         b = lax.axis_index("band")
         for d in range(split):
             at = pl.ds(pl.multiple_of((b ^ d) * part_bands, part_bands), part_bands)
             for a in range(3):
                 for q in range(once):
-                    full_ref[a, q, at, :] = piece_refs[d][a, q]
+                    full_ref[a, q, at, :] = piece_refs[d][a, :, q * width : (q + 1) * width]
 
         def value_of(q):
             return ((1.0 - full_ref[0, q]) * full_ref[2, q]).astype(BF16)
 
-        scatter_products(slots_ref, (m0, m1), value_of, (own_ref, near_ref, far_ref), total)
-
-    def adjoint_second(slots_ref, m0, m1, got_ref, full_ref, one_ref, own_ref, near_ref, far_ref, total):
+        scatter_products(slots_ref, (m0, m1), value_of, outs, total)
+
+    def arrived(refs, q):
+        value = refs[0][q]
+        for ref in refs[1:]:
+            value = value + ref[q].astype(F32)
+        return value
+
+    def adjoint_second(slots_ref, m0, m1, *refs):
+        got_refs, (full_ref, one_ref), outs, total = (
+            refs[: 2 * split],
+            refs[2 * split : 2 * split + 2],
+            refs[2 * split + 2 : -1],
+            refs[-1],
+        )
+
         def value_of(q):
-            value = got_ref[0, q].astype(F32)
-            for s in range(1, 2 * split):
-                value = value + got_ref[s, q].astype(F32)
+            value = arrived(got_refs, q)
             one_ref[q] = value
             return ((1.0 - full_ref[0, q]) * value).astype(BF16)
 
-        scatter_products(slots_ref, (m0, m1), value_of, (own_ref, near_ref, far_ref), total)
-
-    def merge(own_ref, near_ref, far_ref, pay_ref):
-        mine = place_in_team() * split
-        for s in range(split):
-            pay_ref[mine + s] = (own_ref[s] + near_ref[s].astype(F32)).astype(BF16)
-            pay_ref[split - mine + s] = far_ref[s]
-
-    def collect(own, near, far):
-        (pay,) = kernel_call(
+        scatter_products(slots_ref, (m0, m1), value_of, outs, total)
+
+    def merge(own_ref, near_ref, kept_ref, *sent_refs):
+        kept_ref[...] = own_ref[0] + near_ref[0].astype(F32)
+        for d in range(1, split):
+            sent_refs[d - 1][...] = (own_ref[d] + near_ref[d].astype(F32)).astype(BF16)
+
+    def collect(own, near, *far):
+        near = inner(near)
+        far = [outer_across(far[d], d) for d in range(split)]
+        kept, *sent = kernel_call(
             merge,
             1,
             0,
-            [whole(part_shape)] * 3,
-            [(whole(team_shape), shape(team_shape, BF16))],
-            (own, inner(near), far),
+            [whole(part_shape)] * 2,
+            [(whole(block_shape), shape(block_shape, F32))]
+            + [(whole(block_shape), shape(block_shape, BF16))] * (split - 1),
+            (own, near),
         )
-        return team_exchange(pay)
+        return [kept] + [across(sent[d - 1], d) for d in range(1, split)] + far
 
     def products(slots_ref, m_refs, held, finish):
         i = pl.program_id(0)
@@ -216,38 +226,43 @@
                 value = value + nt(held[s], m_refs[k // half][q, k % half])
             finish(q, value)
 
-    def forward_first(slots_ref, m0, m1, team_ref, near_ref, full_ref, zero_ref, rad_ref, held):
+    def forward_first(slots_ref, m0, m1, *refs):
+        pair_refs, (near_ref, full_ref, zero_ref, rad_ref, held) = refs[:split], refs[split:]
+        band = lax.axis_index("band")
+
         @pl.when(pl.program_id(0) == 0)
         def _():
-            mine = place_in_team() * split
-
             def fill(c, carry):
-                for third_index, (ref, first) in enumerate(
-                    ((team_ref, mine), (near_ref, 0), (team_ref, split - mine))
-                ):
-                    parts = [ref[first + s, c].astype(F32) for s in range(split)]
+                for third_index in range(3):
+                    if third_index == 1:
+                        parts = [near_ref[d, c].astype(F32) for d in range(split)]
+                    else:
+                        parts = [ref[third_index // 2, c].astype(F32) for ref in pair_refs]
                     held[third_index * per_group + c] = jnp.concatenate(parts, axis=0).astype(BF16)
                 return carry
 
             lax.fori_loop(0, per_group, fill, 0)
 
         def finish(q, value):
-            zero_ref[q] = value
+            for d in range(split):
+                at = pl.ds(pl.multiple_of((band ^ d) * part_bands, part_bands), part_bands)
+                zero_ref[q, at, :] = value[d * part_bands : (d + 1) * part_bands]
             e, b = full_ref[0, q], full_ref[1, q]
-            rad_ref[q] = (e * b + (1.0 - e) * value).astype(BF16)
+            rad_ref[q] = (e * b + (1.0 - e) * zero_ref[q]).astype(BF16)
 
         products(slots_ref, (m0, m1), held, finish)
 
     def forward_second(slots_ref, m0, m1, *refs):
-        piece_refs, (full_ref, one_ref, rad_ref, held) = refs[:split], refs[split:]
+        pair_refs, (near_ref, full_ref, one_ref, rad_ref, held) = refs[:split], refs[split:]
 
         @pl.when(pl.program_id(0) == 0)
         def _():
             b = lax.axis_index("band")
             for d in range(split):
-                for third_index in range(3):
-                    at = third_index * per_group + (b ^ d) * rb_count
-                    held[pl.ds(at, rb_count)] = piece_refs[d][third_index]
+                at = (b ^ d) * rb_count
+                held[pl.ds(at, rb_count)] = pair_refs[d][0]
+                held[pl.ds(per_group + at, rb_count)] = near_ref[d]
+                held[pl.ds(2 * per_group + at, rb_count)] = pair_refs[d][1]
 
         def finish(q, value):
             one_ref[q] = value
@@ -299,10 +314,12 @@
 
     owners_once = 4
 
-    def pack_rows(
-        got_ref, adj_ref, zero_ref, one_ref, full_ref, owner_ref, rank_ref, label_ref,
-        send_ref, grad, digits, seated, most,
-    ):
+    def pack_rows(*refs):
+        got_refs = refs[: 2 * split]
+        adj_ref, zero_ref, one_ref, full_ref, owner_ref, rank_ref, label_ref = refs[
+            2 * split : 2 * split + 7
+        ]
+        send_ref, grad, digits, seated, most = refs[2 * split + 7 :]
         i = pl.program_id(0)
 
         @pl.when(i == 0)
@@ -312,10 +329,7 @@
         for q in range(once):
             b, w = full_ref[1, q], full_ref[2, q]
             a = adj_ref[q]
-            last = got_ref[0, q].astype(F32)
-            for s in range(1, 2 * split):
-                last = last + got_ref[s, q].astype(F32)
-            value = (w + a + last) * b - (w * one_ref[q] + a * zero_ref[q])
+            value = (w + a + arrived(got_refs, q)) * b - (w * one_ref[q] + a * zero_ref[q])
             cut = pl.ds(pl.multiple_of((i * once + q) * width, width), width)
             grad[:, cut] = value
             most[...] = jnp.maximum(most[...], jnp.max(jnp.abs(value), axis=1, keepdims=True))
@@ -411,50 +425,54 @@
             count = jnp.maximum(total[at + 2 * bands : at + 2 * bands + 1], 1.0)
             out_ref[:, t * LANES : (t + 1) * LANES] = sums / count
 
-    full, own, near, far = kernel_call(
+    start = pair_of(start)
+    slots, rank, labels, _ = lax.optimization_barrier((slots, rank, labels, start))
+    full, *parts = kernel_call(
         adjoint_first,
         4,
         1,
-        matrix_specs + [along((3, once, part_bands, width), 1)] * split,
+        matrix_specs + [along((3, part_bands, once * width), 2)] * split,
         [(full_rows, shape((3,) + block_shape, F32))] + part_outs,
         (slots, matrix, matrix) + tuple(pieces),
         total_scratch,
         flops=pass_flops,
     )
-    got_one = collect(own, near, far)
-
-    mine = (1 - me % 2) * split
-    start_near = inner(lax.dynamic_slice_in_dim(start, mine, split, axis=0))
+    starts = gather(start, parts[0])
+    got_one = collect(*parts)
+
     zero, rad = kernel_call(
         forward_first,
         4,
         1,
-        matrix_specs + [whole(start.shape), whole(start_near.shape), full_rows],
+        matrix_specs + [whole((2,) + start_shape)] * split
+        + [whole((split,) + start_shape), full_rows],
         [(step_rows, shape(block_shape, F32)), (step_rows, shape(block_shape, BF16))],
-        (slots, matrix, matrix, start, start_near, full),
+        (slots, matrix, matrix) + tuple(starts) + (full,),
         window_scratch,
         flops=pass_flops,
     )
-    rad = jnp.stack([rad, inner(rad), outer(rad)])
-    rads = [rad] + [across(rad, d) for d in range(1, split)]
-
-    adjoint_one, own, near, far = kernel_call(
+    rad = pair_of(rad)
+    got_one[0], _ = lax.optimization_barrier((got_one[0], rad))
+    rad, _ = lax.optimization_barrier((rad, got_one))
+
+    adjoint_one, *parts = kernel_call(
         adjoint_second,
         4,
         1,
-        matrix_specs + [along((2 * split, once, bands, width), 1), full_rows],
+        matrix_specs + [step_rows] * (2 * split) + [full_rows],
         [(step_rows, shape(block_shape, F32))] + part_outs,
-        (slots, matrix, matrix, got_one, full),
+        (slots, matrix, matrix) + tuple(got_one) + (full,),
         total_scratch,
         flops=pass_flops,
     )
-    got_zero = collect(own, near, far)
+    rads = gather(rad, parts[0])
+    got_zero = collect(*parts)
 
     one, radiosity = kernel_call(
         forward_second,
         4,
         1,
-        matrix_specs + [whole((3,) + block_shape)] * split + [full_rows],
+        matrix_specs + [whole((2,) + block_shape)] * split + [whole(part_shape), full_rows],
         [
             (step_rows, shape(block_shape, F32)),
             (along((bands, once * width), 1), shape((bands, rows), F32)),
@@ -468,8 +486,7 @@
         pack_rows,
         4,
         0,
-        [along((2 * split, once, bands, width), 1)]
-        + [step_rows] * 3
+        [step_rows] * (2 * split + 3)
         + [full_rows, whole((1, rows)), whole((1, rows)), whole((devices, seats))],
         [
             (
@@ -478,7 +495,7 @@
             )
         ],
         (
-            got_zero,
+            *got_zero,
             adjoint_one,
             zero,
             one,

time: 155 us -> 127 us (0.82)
  waiting for transfers between devices: 48.3 us -> 21.9 us
  starting transfers between devices: 24.3 us -> 45.5 us
  local copies, waits for them, and re-layouts: 23.9 us -> 5.37 us
  blocking collectives: 18.1 us -> 0 us
  Pallas kernels: 38.9 us -> 51.7 us
    unnamed x23 -> x11, local copies, waits for them, and re-layouts: 23.1 us -> 4.52 us
    ppermute x6 -> x15, waiting for transfers between devices: 22.7 us -> 4.54 us  [across(): return lax.ppermute(block, 'band', [(i, i ^ d) for i in range(split)])]
    all_to_all x1 -> x0, blocking collectives: 18.1 us -> none  [team_exchange(): lax.all_to_all(block, ('band', 'patch'), 0, 0, axis_index_groups=teams, t...]
    ppermute x0 -> x8, starting transfers between devices: none -> 17.6 us  [outer_across(): return lax.ppermute(block, ('band', 'patch'), route)]
    all_to_all x2 -> x0, starting transfers between devices: 13.1 us -> none  [team_exchange(): lax.all_to_all(block, ('band', 'patch'), 0, 0, axis_index_groups=teams, t...]
    pallas_call x10, Pallas kernels: 38.9 us -> 51.7 us  [kernel_call(): pl.pallas_call(kernel, out_shape=[o for _, o in outs], grid_spec=pltpu.Pr...]
    ppermute x6 -> x15, starting transfers between devices: 8.1 us -> 17 us  [across(): return lax.ppermute(block, 'band', [(i, i ^ d) for i in range(split)])]
    ppermute x1 -> x2, starting transfers between devices: 0.1 us -> 6.51 us  [outer(): lax.ppermute(block, 'patch', [(i, (i + (1 if i % 2 else -1)) % groups) fo...]
  transfers between devices with their start and end apart: 14 -> 30, of which waited for: 9 -> 9; matrix products, arithmetic and copies ran while one was open for 1% -> 2% of each run, Pallas kernels for 14% -> 30%
where the time goes in v4:
time: 127 us
  Pallas kernels  51.7 us (41%)
  starting transfers between devices  45.5 us (36%)
  waiting for transfers between devices  21.9 us (17%)
  local copies, waits for them, and re-layouts  5.37 us (4%)
    pallas_call x10, Pallas kernels, kernel_call(): pl.pallas_call(kernel, out_shape=[o for _, o in outs], grid_spec=pltpu.Pr...  51.7 us
    ppermute x8, starting transfers between devices, outer_across(): return lax.ppermute(block, ('band', 'patch'), route)  17.6 us
    ppermute x15, starting transfers between devices, across(): return lax.ppermute(block, 'band', [(i, i ^ d) for i in range(split)])  17 us
    all_to_all x1, waiting for transfers between devices, body(): send = lax.all_to_all(send, ('band', 'patch'), 0, 0, tiled=True)  14 us
    ppermute x2, starting transfers between devices, outer(): lax.ppermute(block, 'patch', [(i, (i + (1 if i % 2 else -1)) % groups) fo...  6.51 us
    ppermute x15, waiting for transfers between devices, across(): return lax.ppermute(block, 'band', [(i, i ^ d) for i in range(split)])  4.54 us
    unnamed x11, local copies, waits for them, and re-layouts  4.52 us
    ppermute x8, waiting for transfers between devices, outer_across(): return lax.ppermute(block, ('band', 'patch'), route)  3.41 us
  transfers between devices with their start and end apart: 30, of which 9 were waited for; matrix products, arithmetic and copies ran while one was open for 2% of the time, Pallas kernels for 30%

profile of v4, /device:TPU:0, one launch (start us, length us, event | category | flops | bytes accessed | tf_op | source)
XLA Modules:
  0.0 126.5 jit_solution(10025101961537345319)
XLA Ops:
  0.6 2.1 %shard_map.87 = (bf16[32,8,256]{2,1,0:T(8,128)(2,1)}, f32[3,8,2048]{2,1,0:T(8,128)}, f32[3,8,2048]{2,1,0:T(8,128)}, f32[3,8,2048]{2,1,0:T(8,128)}, f32[3,8,2048]{2,1,0:T(8,128)}) custom-call(f32[8,8192]{1,0:T(8,128)} %e_ref.1, f32[8,8192]{1,0:T(8,128)} %b_ref.1, f32[8,8192]{1,0:T(8,128)} %w_ref.1), custom_call_target="tpu_custom_call" | custom-call | tf_op jit(solution)/shard_map/pallas_call | solution.py:42
  2.7 4.5 %collective-permute-start = (bf16[32,8,256]{2,1,0:T(8,128)(2,1)}, bf16[32,8,256]{2,1,0:T(8,128)(2,1)S(1)}, u32[]{:S(2)}, u32[]{:S(2)}) collective-permute-start(bf16[32,8,256]{2,1,0:T(8,128)(2,1)} %get-tuple-element.50), channel_id=1, source_target_pairs={{0,7},{1,2},{2,1},{3,4},{4,3},{5,6},{6,5},{7,0},{8,15},{9,10},{10,... | collective-permute-start | bytes 393224 | tf_op jit(solution)/shard_map/ppermute | solution.py:76
  7.2 1.5 %collective-permute-start.4 = (f32[3,8,2048]{2,1,0:T(8,128)}, f32[3,8,2048]{2,1,0:T(8,128)S(1)}, u32[]{:S(2)}, u32[]{:S(2)}) collective-permute-start(f32[3,8,2048]{2,1,0:T(8,128)} %get-tuple-element.53), channel_id=1, source_target_pairs={{0,8},{8,0},{16,24},{24,16},{1,9},{9,1},{17,25},{25,17},{2,10},{10... | collective-permute-start | bytes 589832 | tf_op jit(solution)/shard_map/ppermute | solution.py:81
  8.7 1.5 %collective-permute-start.5 = (f32[3,8,2048]{2,1,0:T(8,128)}, f32[3,8,2048]{2,1,0:T(8,128)S(1)}, u32[]{:S(2)}, u32[]{:S(2)}) collective-permute-start(f32[3,8,2048]{2,1,0:T(8,128)} %get-tuple-element.54), channel_id=1, source_target_pairs={{0,16},{8,24},{16,0},{24,8},{1,17},{9,25},{17,1},{25,9},{2,18},{10... | collective-permute-start | bytes 589832 | tf_op jit(solution)/shard_map/ppermute | solution.py:81
  10.7 0.8 reshape.20
  11.4 0.7 copy-done.2
  12.1 0.7 copy-done.4
  12.8 1.0 shard_map.86
  13.9 0.9 pad_maximum_fusion.2.refs_0_
  14.8 1.6 %collective-permute-start.1 = (bf16[2,32,8,256]{3,2,1,0:T(8,128)(2,1)S(1)}, bf16[2,32,8,256]{3,2,1,0:T(8,128)(2,1)S(1)}, u32[]{:S(2)}, u32[]{:S(2)}) collective-permute-start(bf16[2,32,8,256]{3,2,1,0:T(8,128)(2,1)S(1)} %pad_maximum_fusion.2.refs_0_), channel_id=1, source_target_pairs={{0,8},{8,0},{16,24},{24,16},{1,9},{9,1},{17,25},{25,17},{2,10},{10... | collective-permute-start | bytes 786440 | tf_op jit(solution)/shard_map/ppermute | solution.py:81
  16.4 1.5 %collective-permute-start.2 = (bf16[2,32,8,256]{3,2,1,0:T(8,128)(2,1)S(1)}, bf16[2,32,8,256]{3,2,1,0:T(8,128)(2,1)S(1)}, u32[]{:S(2)}, u32[]{:S(2)}) collective-permute-start(bf16[2,32,8,256]{3,2,1,0:T(8,128)(2,1)S(1)} %pad_maximum_fusion.2.refs_0_), channel_id=1, source_target_pairs={{0,16},{8,24},{16,0},{24,8},{1,17},{9,25},{17,1},{25,9},{2,18},{10... | collective-permute-start | bytes 786440 | tf_op jit(solution)/shard_map/ppermute | solution.py:81
  17.9 0.5 collective-permute-start.3
  18.4 1.7 %collective-permute-done.6.refs_3_ = f32[3,8,2048]{2,1,0:T(8,128)S(1)} collective-permute-done((f32[3,8,2048]{2,1,0:T(8,128)}, f32[3,8,2048]{2,1,0:T(8,128)S(1)}, u32[]{:S(2)}, u32[]{:S(2)}) %collective-permute-start.6) | collective-permute-done | bytes 196640 | tf_op jit(solution)/shard_map/ppermute | solution.py:81
  20.1 0.9 copy-done.1
  21.1 8.6 %shard_map.88 = (f32[3,8,32,256]{3,2,1,0:T(8,128)S(1)}, f32[4,8,32,256]{3,2,1,0:T(8,128)S(1)}, bf16[4,8,32,256]{3,2,1,0:T(8,128)(2,1)S(1)}, bf16[8,32,256]{2,1,0...) custom-call(s32[128]{0:T(128)S(1)} %fusion.slots_ref, ...), custom_call_target="tpu_custom_call" | custom-call | flops 536870912 | bytes 16777216 | tf_op jit(solution)/shard_map/pallas_call | solution.py:42
  30.0 0.5 collective-permute-start.9
  30.5 1.7 %collective-permute-start.13 = (bf16[8,32,256]{2,1,0:T(8,128)(2,1)S(1)}, bf16[8,32,256]{2,1,0:T(8,128)(2,1)S(1)}, u32[]{:S(2)}, u32[]{:S(2)}) collective-permute-start(bf16[8,32,256]{2,1,0:T(8,128)(2,1)S(1)} %get-tuple-element.69), channel_id=1, source_target_pairs={{0,7},{1,2},{2,1},{3,4},{4,3},{5,6},{6,5},{7,0},{8,15},{9,10},{10,... | collective-permute-start | bytes 393224 | tf_op jit(solution)/shard_map/ppermute | solution.py:89
  32.2 2.3 %collective-permute-start.14 = (bf16[8,32,256]{2,1,0:T(8,128)(2,1)S(1)}, bf16[8,32,256]{2,1,0:T(8,128)(2,1)S(1)}, u32[]{:S(2)}, u32[]{:S(2)}) collective-permute-start(bf16[8,32,256]{2,1,0:T(8,128)(2,1)S(1)} %get-tuple-element.70), channel_id=1, source_target_pairs={{0,15},{1,10},{2,9},{3,12},{4,11},{5,14},{6,13},{7,8},{8,7},{9,2},... | collective-permute-start | bytes 393224 | tf_op jit(solution)/shard_map/ppermute | solution.py:89
  34.5 9.5 %shard_map.89 = (f32[8,32,256]{2,1,0:T(8,128)S(1)}, bf16[8,32,256]{2,1,0:T(8,128)(2,1)S(1)}) custom-call(s32[128]{0:T(128)S(1)} %fusion.slots_ref, bf16[8,16,256,256]{3,2,1,0:T(8,128)(2,1)} %bitcast.17, bf16[8,16,256,256]{3,2,1,0:T(8,128)(2,1)} %bitcast.18, bf16[2,32,8,256]{3,2,1,0:T(8,128)(2,1)S(1)} %pad_maximum_fusion.2.refs_0_, ...), custom_call_target="tpu_custom_call" | custom-call | flops 536870912 | bytes 16777216 | tf_op jit(solution)/shard_map/pallas_call | solution.py:42
  44.0 2.0 %collective-permute-start.8 = (bf16[8,32,256]{2,1,0:T(8,128)(2,1)S(1)}, bf16[8,32,256]{2,1,0:T(8,128)(2,1)S(1)}, u32[]{:S(2)}, u32[]{:S(2)}) collective-permute-start(bf16[8,32,256]{2,1,0:T(8,128)(2,1)S(1)} %get-tuple-element.62), channel_id=1, source_target_pairs={{0,7},{1,2},{2,1},{3,4},{4,3},{5,6},{6,5},{7,0},{8,15},{9,10},{10,... | collective-permute-start | bytes 393224 | tf_op jit(solution)/shard_map/ppermute | solution.py:76
  46.0 1.8 %collective-permute-start.15 = (bf16[8,32,256]{2,1,0:T(8,128)(2,1)S(1)}, bf16[8,32,256]{2,1,0:T(8,128)(2,1)S(1)}, u32[]{:S(2)}, u32[]{:S(2)}) collective-permute-start(bf16[8,32,256]{2,1,0:T(8,128)(2,1)S(1)} %get-tuple-element.71), channel_id=1, source_target_pairs={{0,23},{1,18},{2,17},{3,20},{4,19},{5,22},{6,21},{7,16},{8,31},{9,... | collective-permute-start | bytes 393224 | tf_op jit(solution)/shard_map/ppermute | solution.py:89
  47.9 2.8 %collective-permute-start.16 = (bf16[8,32,256]{2,1,0:T(8,128)(2,1)S(1)}, bf16[8,32,256]{2,1,0:T(8,128)(2,1)S(1)}, u32[]{:S(2)}, u32[]{:S(2)}) collective-permute-start(bf16[8,32,256]{2,1,0:T(8,128)(2,1)S(1)} %get-tuple-element.72), channel_id=1, source_target_pairs={{0,31},{1,26},{2,25},{3,28},{4,27},{5,30},{6,29},{7,24},{8,23},{9,... | collective-permute-start | bytes 393224 | tf_op jit(solution)/shard_map/ppermute | solution.py:89
  50.8 1.3 %collective-permute-start.10 = (bf16[8,32,256]{2,1,0:T(8,128)(2,1)S(1)}, bf16[8,32,256]{2,1,0:T(8,128)(2,1)S(1)}, u32[]{:S(2)}, u32[]{:S(2)}) collective-permute-start(bf16[8,32,256]{2,1,0:T(8,128)(2,1)S(1)} %get-tuple-element.66), channel_id=1, source_target_pairs={{0,8},{8,0},{16,24},{24,16},{1,9},{9,1},{17,25},{25,17},{2,10},{10... | collective-permute-start | bytes 393224 | tf_op jit(solution)/shard_map/ppermute | solution.py:81
  52.1 0.8 collective-permute-start.11
  52.9 1.4 %collective-permute-start.12 = (bf16[8,32,256]{2,1,0:T(8,128)(2,1)S(1)}, bf16[8,32,256]{2,1,0:T(8,128)(2,1)S(1)}, u32[]{:S(2)}, u32[]{:S(2)}) collective-permute-start(bf16[8,32,256]{2,1,0:T(8,128)(2,1)S(1)} %get-tuple-element.68), channel_id=1, source_target_pairs={{0,24},{8,16},{16,8},{24,0},{1,25},{9,17},{17,9},{25,1},{2,26},{10... | collective-permute-start | bytes 393224 | tf_op jit(solution)/shard_map/ppermute | solution.py:81
  54.4 0.5 collective-permute-done.15.refs_6_
  54.9 1.9 %collective-permute-done.16.refs_7_ = bf16[8,32,256]{2,1,0:T(8,128)(2,1)S(1)} collective-permute-done((bf16[8,32,256]{2,1,0:T(8,128)(2,1)S(1)}, bf16[8,32,256]{2,1,0:T(8,128)(2,1)S(1)}, u32[]{:S(2)}, u32[]{:S(2)}) %collective-permute-start.16) | collective-permute-done | bytes 131104 | tf_op jit(solution)/shard_map/ppermute | solution.py:89
  57.2 0.8 collective-permute-done.11.refs_2_
  58.0 1.4 %collective-permute-done.12.refs_3_ = bf16[8,32,256]{2,1,0:T(8,128)(2,1)S(1)} collective-permute-done((bf16[8,32,256]{2,1,0:T(8,128)(2,1)S(1)}, bf16[8,32,256]{2,1,0:T(8,128)(2,1)S(1)}, u32[]{:S(2)}, u32[]{:S(2)}) %collective-permute-start.12) | collective-permute-done | bytes 131104 | tf_op jit(solution)/shard_map/ppermute | solution.py:81
  59.4 0.9 collective-permute-start.17
  60.4 1.2 collective-permute-start.18
  61.6 1.4 %collective-permute-start.19 = (bf16[2,8,32,256]{3,2,1,0:T(8,128)(2,1)S(1)}, bf16[2,8,32,256]{3,2,1,0:T(8,128)(2,1)S(1)}, u32[]{:S(2)}, u32[]{:S(2)}) collective-permute-start(bf16[2,8,32,256]{3,2,1,0:T(8,128)(2,1)S(1)} %pad_maximum_fusion.3.refs_0_), channel_id=1, source_target_pairs={{0,24},{8,16},{16,8},{24,0},{1,25},{9,17},{17,9},{25,1},{2,26},{10... | collective-permute-start | bytes 786440 | tf_op jit(solution)/shard_map/ppermute | solution.py:81
  62.9 9.5 %shard_map.91 = (f32[8,32,256]{2,1,0:T(8,128)S(1)}, f32[4,8,32,256]{3,2,1,0:T(8,128)}, bf16[4,8,32,256]{3,2,1,0:T(8,128)(2,1)S(1)}, bf16[8,32,256]{2,1,0:T(8,128...) custom-call(s32[128]{0:T(128)S(1)} %fusion.slots_ref, ...), custom_call_target="tpu_custom_call" | custom-call | flops 536870912 | bytes 16777216 | tf_op jit(solution)/shard_map/pallas_call | solution.py:42
  72.6 0.6 collective-permute-start.20
  73.2 3.6 %collective-permute-start.25 = (bf16[8,32,256]{2,1,0:T(8,128)(2,1)S(1)}, bf16[8,32,256]{2,1,0:T(8,128)(2,1)S(1)}, u32[]{:S(2)}, u32[]{:S(2)}) collective-permute-start(bf16[8,32,256]{2,1,0:T(8,128)(2,1)S(1)} %get-tuple-element.85), channel_id=1, source_target_pairs={{0,7},{1,2},{2,1},{3,4},{4,3},{5,6},{6,5},{7,0},{8,15},{9,10},{10,... | collective-permute-start | bytes 393224 | tf_op jit(solution)/shard_map/ppermute | solution.py:89
  77.1 3.9 %collective-permute-start.27 = (bf16[8,32,256]{2,1,0:T(8,128)(2,1)S(1)}, bf16[8,32,256]{2,1,0:T(8,128)(2,1)S(1)}, u32[]{:S(2)}, u32[]{:S(2)}) collective-permute-start(bf16[8,32,256]{2,1,0:T(8,128)(2,1)S(1)} %get-tuple-element.87), channel_id=1, source_target_pairs={{0,23},{1,18},{2,17},{3,20},{4,19},{5,22},{6,21},{7,16},{8,31},{9,... | collective-permute-start | bytes 393224 | tf_op jit(solution)/shard_map/ppermute | solution.py:89
  81.0 1.2 collective-permute-start.28
  82.1 1.2 copy-done
  83.5 0.9 collective-permute-start.22
  84.4 1.0 collective-permute-done.26.refs_5_
  85.4 0.8 collective-permute-start.23
  86.2 1.2 collective-permute-start.24
  87.4 9.4 %shard_map.92 = (f32[8,32,256]{2,1,0:T(8,128)S(1)}, f32[32,2048]{1,0:T(8,128)S(1)}) custom-call(s32[128]{0:T(128)S(1)} %fusion.slots_ref, bf16[8,16,256,256]{3,2,1,0:T(8,128)(2,1)} %bitcast.21, bf16[8,16,256,256]{3,2,1,0:T(8,128)(2,1)} %bitcast.22, bf16[2,8,32,256]{3,2,1,0:T(8,128)(2,1)S(1)} %pad_maximum_fusion.3.refs_0_, ...), custom_call_target="tpu_custom_call" | custom-call | flops 536870912 | bytes 16777216 | tf_op jit(solution)/shard_map/pallas_call | solution.py:42
  96.8 6.3 %shard_map.94 = s16[32,56,128]{2,1,0:T(8,128)(2,1)} custom-call(f32[8,32,256]{2,1,0:T(8,128)S(1)} %get-tuple-element.81.refs_0_, bf16[8,32,256]{2,1,0:T(8,128)(2,1)S(1)} %collective-permute-done.22.refs_1_, bf16[8,32,256]{2,1,0:T(8,128)(2,1)S(1)} %collective-permute-done.23.refs_2_, bf16[8,32,256]{2,1,0:T(8,128)(2,1)S(1)} %collective-permute-done.24.refs_3_, ...), custom_call_target="tpu_custom_call" | custom-call | tf_op jit(solution)/shard_map/pallas_call | solution.py:42
  103.1 3.3 %all-to-all-start = ((s16[32,56,128]{2,1,0:T(8,128)(2,1)}), s16[32,56,128]{2,1,0:T(8,128)(2,1)S(1)}, u32[]{:S(2)}, u32[]{:S(2)}) async-start(s16[32,56,128]{2,1,0:T(8,128)(2,1)} %shard_map.94), calls=%async_computation | async-start | bytes 917504 | tf_op jit(solution)/shard_map/all_to_all | solution.py:514
  106.4 1.0 copy.9
  107.4 14.0 %all-to-all-done.got_ref = s16[32,56,128]{2,1,0:T(8,128)(2,1)S(1)} async-done(((s16[32,56,128]{2,1,0:T(8,128)(2,1)}), s16[32,56,128]{2,1,0:T(8,128)(2,1)S(1)}, u32[]{:S(2)}, u32[]{:S(2)}) %all-to-all-start) | async-done | bytes 458784 | tf_op jit(solution)/shard_map/all_to_all | solution.py:514
  121.4 5.2 %shard_map.95 = f32[32,1024]{1,0:T(8,128)} custom-call(s16[32,56,128]{2,1,0:T(8,128)(2,1)S(1)} %all-to-all-done.got_ref), custom_call_target="tpu_custom_call" | custom-call | tf_op jit(solution)/shard_map/pallas_call | solution.py:42
  (47 shorter events, 1.9 us)
Async XLA Ops:
  2.7 11.2 %collective-permute-start = (bf16[32,8,256]{2,1,0:T(8,128)(2,1)}, bf16[32,8,256]{2,1,0:T(8,128)(2,1)S(1)}, u32[]{:S(2)}, u32[]{:S(2)}) collective-permute-start(bf16[32,8,256]{2,1,0:T(8,128)(2,1)} %get-tuple-element.50), channel_id=1, source_target_pairs={{0,7},{1,2},{2,1},{3,4},{4,3},{5,6},{6,5},{7,0},{8,15},{9,10},{10,... | collective-permute-start | bytes 393224 | tf_op jit(solution)/shard_map/ppermute | solution.py:76
  7.2 10.7 %collective-permute-start.4 = (f32[3,8,2048]{2,1,0:T(8,128)}, f32[3,8,2048]{2,1,0:T(8,128)S(1)}, u32[]{:S(2)}, u32[]{:S(2)}) collective-permute-start(f32[3,8,2048]{2,1,0:T(8,128)} %get-tuple-element.53), channel_id=1, source_target_pairs={{0,8},{8,0},{16,24},{24,16},{1,9},{9,1},{17,25},{25,17},{2,10},{10... | collective-permute-start | bytes 589832 | tf_op jit(solution)/shard_map/ppermute | solution.py:81
  8.7 9.7 %collective-permute-start.5 = (f32[3,8,2048]{2,1,0:T(8,128)}, f32[3,8,2048]{2,1,0:T(8,128)S(1)}, u32[]{:S(2)}, u32[]{:S(2)}) collective-permute-start(f32[3,8,2048]{2,1,0:T(8,128)} %get-tuple-element.54), channel_id=1, source_target_pairs={{0,16},{8,24},{16,0},{24,8},{1,17},{9,25},{17,1},{25,9},{2,18},{10... | collective-permute-start | bytes 589832 | tf_op jit(solution)/shard_map/ppermute | solution.py:81
  10.2 9.9 %collective-permute-start.6 = (f32[3,8,2048]{2,1,0:T(8,128)}, f32[3,8,2048]{2,1,0:T(8,128)S(1)}, u32[]{:S(2)}, u32[]{:S(2)}) collective-permute-start(f32[3,8,2048]{2,1,0:T(8,128)} %get-tuple-element.55), channel_id=1, source_target_pairs={{0,24},{8,16},{16,8},{24,0},{1,25},{9,17},{17,9},{25,1},{2,26},{10... | collective-permute-start | bytes 589832 | tf_op jit(solution)/shard_map/ppermute | solution.py:81
  11.4 0.7 copy-start.2
  12.1 0.7 copy-start.4
  14.8 14.8 %collective-permute-start.1 = (bf16[2,32,8,256]{3,2,1,0:T(8,128)(2,1)S(1)}, bf16[2,32,8,256]{3,2,1,0:T(8,128)(2,1)S(1)}, u32[]{:S(2)}, u32[]{:S(2)}) collective-permute-start(bf16[2,32,8,256]{3,2,1,0:T(8,128)(2,1)S(1)} %pad_maximum_fusion.2.refs_0_), channel_id=1, source_target_pairs={{0,8},{8,0},{16,24},{24,16},{1,9},{9,1},{17,25},{25,17},{2,10},{10... | collective-permute-start | bytes 786440 | tf_op jit(solution)/shard_map/ppermute | solution.py:81
  16.4 13.4 %collective-permute-start.2 = (bf16[2,32,8,256]{3,2,1,0:T(8,128)(2,1)S(1)}, bf16[2,32,8,256]{3,2,1,0:T(8,128)(2,1)S(1)}, u32[]{:S(2)}, u32[]{:S(2)}) collective-permute-start(bf16[2,32,8,256]{3,2,1,0:T(8,128)(2,1)S(1)} %pad_maximum_fusion.2.refs_0_), channel_id=1, source_target_pairs={{0,16},{8,24},{16,0},{24,8},{1,17},{9,25},{17,1},{25,9},{2,18},{10... | collective-permute-start | bytes 786440 | tf_op jit(solution)/shard_map/ppermute | solution.py:81
  17.9 11.9 %collective-permute-start.3 = (bf16[2,32,8,256]{3,2,1,0:T(8,128)(2,1)S(1)}, bf16[2,32,8,256]{3,2,1,0:T(8,128)(2,1)S(1)}, u32[]{:S(2)}, u32[]{:S(2)}) collective-permute-start(bf16[2,32,8,256]{3,2,1,0:T(8,128)(2,1)S(1)} %pad_maximum_fusion.2.refs_0_), channel_id=1, source_target_pairs={{0,24},{8,16},{16,8},{24,0},{1,25},{9,17},{17,9},{25,1},{2,26},{10... | collective-permute-start | bytes 786440 | tf_op jit(solution)/shard_map/ppermute | solution.py:81
  20.1 0.9 copy-start.1
  29.9 4.5 %collective-permute-start.7 = (bf16[4,32,8,256]{3,2,1,0:T(8,128)(2,1)S(1)}, bf16[4,32,8,256]{3,2,1,0:T(8,128)(2,1)S(1)}, u32[]{:S(2)}, u32[]{:S(2)}) collective-permute-start(bf16[4,32,8,256]{3,2,1,0:T(8,128)(2,1)S(1)} %pad_maximum_fusion), channel_id=1, source_target_pairs={{0,1},{1,0},{2,3},{3,2},{4,5},{5,4},{6,7},{7,6},{8,9},{9,8},{10,11... | collective-permute-start | bytes 1572872 | tf_op jit(solution)/shard_map/ppermute | solution.py:73
  30.0 17.9 %collective-permute-start.9 = (bf16[4,8,32,256]{3,2,1,0:T(8,128)(2,1)S(1)}, bf16[4,8,32,256]{3,2,1,0:T(8,128)(2,1)S(1)}, u32[]{:S(2)}, u32[]{:S(2)}) collective-permute-start(bf16[4,8,32,256]{3,2,1,0:T(8,128)(2,1)S(1)} %get-tuple-element.63), channel_id=1, source_target_pairs={{0,1},{1,0},{2,3},{3,2},{4,5},{5,4},{6,7},{7,6},{8,9},{9,8},{10,11... | collective-permute-start | bytes 1572872 | tf_op jit(solution)/shard_map/ppermute | solution.py:73
  30.5 20.3 %collective-permute-start.13 = (bf16[8,32,256]{2,1,0:T(8,128)(2,1)S(1)}, bf16[8,32,256]{2,1,0:T(8,128)(2,1)S(1)}, u32[]{:S(2)}, u32[]{:S(2)}) collective-permute-start(bf16[8,32,256]{2,1,0:T(8,128)(2,1)S(1)} %get-tuple-element.69), channel_id=1, source_target_pairs={{0,7},{1,2},{2,1},{3,4},{4,3},{5,6},{6,5},{7,0},{8,15},{9,10},{10,... | collective-permute-start | bytes 393224 | tf_op jit(solution)/shard_map/ppermute | solution.py:89
  32.2 19.9 %collective-permute-start.14 = (bf16[8,32,256]{2,1,0:T(8,128)(2,1)S(1)}, bf16[8,32,256]{2,1,0:T(8,128)(2,1)S(1)}, u32[]{:S(2)}, u32[]{:S(2)}) collective-permute-start(bf16[8,32,256]{2,1,0:T(8,128)(2,1)S(1)} %get-tuple-element.70), channel_id=1, source_target_pairs={{0,15},{1,10},{2,9},{3,12},{4,11},{5,14},{6,13},{7,8},{8,7},{9,2},... | collective-permute-start | bytes 393224 | tf_op jit(solution)/shard_map/ppermute | solution.py:89
  44.0 8.9 %collective-permute-start.8 = (bf16[8,32,256]{2,1,0:T(8,128)(2,1)S(1)}, bf16[8,32,256]{2,1,0:T(8,128)(2,1)S(1)}, u32[]{:S(2)}, u32[]{:S(2)}) collective-permute-start(bf16[8,32,256]{2,1,0:T(8,128)(2,1)S(1)} %get-tuple-element.62), channel_id=1, source_target_pairs={{0,7},{1,2},{2,1},{3,4},{4,3},{5,6},{6,5},{7,0},{8,15},{9,10},{10,... | collective-permute-start | bytes 393224 | tf_op jit(solution)/shard_map/ppermute | solution.py:76
  46.0 8.9 %collective-permute-start.15 = (bf16[8,32,256]{2,1,0:T(8,128)(2,1)S(1)}, bf16[8,32,256]{2,1,0:T(8,128)(2,1)S(1)}, u32[]{:S(2)}, u32[]{:S(2)}) collective-permute-start(bf16[8,32,256]{2,1,0:T(8,128)(2,1)S(1)} %get-tuple-element.71), channel_id=1, source_target_pairs={{0,23},{1,18},{2,17},{3,20},{4,19},{5,22},{6,21},{7,16},{8,31},{9,... | collective-permute-start | bytes 393224 | tf_op jit(solution)/shard_map/ppermute | solution.py:89
  47.9 8.9 %collective-permute-start.16 = (bf16[8,32,256]{2,1,0:T(8,128)(2,1)S(1)}, bf16[8,32,256]{2,1,0:T(8,128)(2,1)S(1)}, u32[]{:S(2)}, u32[]{:S(2)}) collective-permute-start(bf16[8,32,256]{2,1,0:T(8,128)(2,1)S(1)} %get-tuple-element.72), channel_id=1, source_target_pairs={{0,31},{1,26},{2,25},{3,28},{4,27},{5,30},{6,29},{7,24},{8,23},{9,... | collective-permute-start | bytes 393224 | tf_op jit(solution)/shard_map/ppermute | solution.py:89
  50.8 6.4 %collective-permute-start.10 = (bf16[8,32,256]{2,1,0:T(8,128)(2,1)S(1)}, bf16[8,32,256]{2,1,0:T(8,128)(2,1)S(1)}, u32[]{:S(2)}, u32[]{:S(2)}) collective-permute-start(bf16[8,32,256]{2,1,0:T(8,128)(2,1)S(1)} %get-tuple-element.66), channel_id=1, source_target_pairs={{0,8},{8,0},{16,24},{24,16},{1,9},{9,1},{17,25},{25,17},{2,10},{10... | collective-permute-start | bytes 393224 | tf_op jit(solution)/shard_map/ppermute | solution.py:81
  52.1 5.9 %collective-permute-start.11 = (bf16[8,32,256]{2,1,0:T(8,128)(2,1)S(1)}, bf16[8,32,256]{2,1,0:T(8,128)(2,1)S(1)}, u32[]{:S(2)}, u32[]{:S(2)}) collective-permute-start(bf16[8,32,256]{2,1,0:T(8,128)(2,1)S(1)} %get-tuple-element.67), channel_id=1, source_target_pairs={{0,16},{8,24},{16,0},{24,8},{1,17},{9,25},{17,1},{25,9},{2,18},{10... | collective-permute-start | bytes 393224 | tf_op jit(solution)/shard_map/ppermute | solution.py:81
  52.9 6.5 %collective-permute-start.12 = (bf16[8,32,256]{2,1,0:T(8,128)(2,1)S(1)}, bf16[8,32,256]{2,1,0:T(8,128)(2,1)S(1)}, u32[]{:S(2)}, u32[]{:S(2)}) collective-permute-start(bf16[8,32,256]{2,1,0:T(8,128)(2,1)S(1)} %get-tuple-element.68), channel_id=1, source_target_pairs={{0,24},{8,16},{16,8},{24,0},{1,25},{9,17},{17,9},{25,1},{2,26},{10... | collective-permute-start | bytes 393224 | tf_op jit(solution)/shard_map/ppermute | solution.py:81
  59.4 13.0 %collective-permute-start.17 = (bf16[2,8,32,256]{3,2,1,0:T(8,128)(2,1)S(1)}, bf16[2,8,32,256]{3,2,1,0:T(8,128)(2,1)S(1)}, u32[]{:S(2)}, u32[]{:S(2)}) collective-permute-start(bf16[2,8,32,256]{3,2,1,0:T(8,128)(2,1)S(1)} %pad_maximum_fusion.3.refs_0_), channel_id=1, source_target_pairs={{0,8},{8,0},{16,24},{24,16},{1,9},{9,1},{17,25},{25,17},{2,10},{10... | collective-permute-start | bytes 786440 | tf_op jit(solution)/shard_map/ppermute | solution.py:81
  60.4 12.1 %collective-permute-start.18 = (bf16[2,8,32,256]{3,2,1,0:T(8,128)(2,1)S(1)}, bf16[2,8,32,256]{3,2,1,0:T(8,128)(2,1)S(1)}, u32[]{:S(2)}, u32[]{:S(2)}) collective-permute-start(bf16[2,8,32,256]{3,2,1,0:T(8,128)(2,1)S(1)} %pad_maximum_fusion.3.refs_0_), channel_id=1, source_target_pairs={{0,16},{8,24},{16,0},{24,8},{1,17},{9,25},{17,1},{25,9},{2,18},{10... | collective-permute-start | bytes 786440 | tf_op jit(solution)/shard_map/ppermute | solution.py:81
  61.6 10.9 %collective-permute-start.19 = (bf16[2,8,32,256]{3,2,1,0:T(8,128)(2,1)S(1)}, bf16[2,8,32,256]{3,2,1,0:T(8,128)(2,1)S(1)}, u32[]{:S(2)}, u32[]{:S(2)}) collective-permute-start(bf16[2,8,32,256]{3,2,1,0:T(8,128)(2,1)S(1)} %pad_maximum_fusion.3.refs_0_), channel_id=1, source_target_pairs={{0,24},{8,16},{16,8},{24,0},{1,25},{9,17},{17,9},{25,1},{2,26},{10... | collective-permute-start | bytes 786440 | tf_op jit(solution)/shard_map/ppermute | solution.py:81
  72.4 8.5 %collective-permute-start.21 = (bf16[4,8,32,256]{3,2,1,0:T(8,128)(2,1)S(1)}, bf16[4,8,32,256]{3,2,1,0:T(8,128)(2,1)S(1)}, u32[]{:S(2)}, u32[]{:S(2)}) collective-permute-start(bf16[4,8,32,256]{3,2,1,0:T(8,128)(2,1)S(1)} %get-tuple-element.80), channel_id=1, source_target_pairs={{0,1},{1,0},{2,3},{3,2},{4,5},{5,4},{6,7},{7,6},{8,9},{9,8},{10,11... | collective-permute-start | bytes 1572872 | tf_op jit(solution)/shard_map/ppermute | solution.py:73
  72.6 13.6 %collective-permute-start.20 = (bf16[4,8,32,256]{3,2,1,0:T(8,128)(2,1)S(1)}, bf16[4,8,32,256]{3,2,1,0:T(8,128)(2,1)S(1)}, u32[]{:S(2)}, u32[]{:S(2)}) collective-permute-start(bf16[4,8,32,256]{3,2,1,0:T(8,128)(2,1)S(1)} %pad_maximum_fusion.1), channel_id=1, source_target_pairs={{0,1},{1,0},{2,3},{3,2},{4,5},{5,4},{6,7},{7,6},{8,9},{9,8},{10,11... | collective-permute-start | bytes 1572872 | tf_op jit(solution)/shard_map/ppermute | solution.py:73
  73.2 10.3 %collective-permute-start.25 = (bf16[8,32,256]{2,1,0:T(8,128)(2,1)S(1)}, bf16[8,32,256]{2,1,0:T(8,128)(2,1)S(1)}, u32[]{:S(2)}, u32[]{:S(2)}) collective-permute-start(bf16[8,32,256]{2,1,0:T(8,128)(2,1)S(1)} %get-tuple-element.85), channel_id=1, source_target_pairs={{0,7},{1,2},{2,1},{3,4},{4,3},{5,6},{6,5},{7,0},{8,15},{9,10},{10,... | collective-permute-start | bytes 393224 | tf_op jit(solution)/shard_map/ppermute | solution.py:89
  76.8 8.6 %collective-permute-start.26 = (bf16[8,32,256]{2,1,0:T(8,128)(2,1)S(1)}, bf16[8,32,256]{2,1,0:T(8,128)(2,1)S(1)}, u32[]{:S(2)}, u32[]{:S(2)}) collective-permute-start(bf16[8,32,256]{2,1,0:T(8,128)(2,1)S(1)} %get-tuple-element.86), channel_id=1, source_target_pairs={{0,15},{1,10},{2,9},{3,12},{4,11},{5,14},{6,13},{7,8},{8,7},{9,2},... | collective-permute-start | bytes 393224 | tf_op jit(solution)/shard_map/ppermute | solution.py:89
  77.1 19.7 %collective-permute-start.27 = (bf16[8,32,256]{2,1,0:T(8,128)(2,1)S(1)}, bf16[8,32,256]{2,1,0:T(8,128)(2,1)S(1)}, u32[]{:S(2)}, u32[]{:S(2)}) collective-permute-start(bf16[8,32,256]{2,1,0:T(8,128)(2,1)S(1)} %get-tuple-element.87), channel_id=1, source_target_pairs={{0,23},{1,18},{2,17},{3,20},{4,19},{5,22},{6,21},{7,16},{8,31},{9,... | collective-permute-start | bytes 393224 | tf_op jit(solution)/shard_map/ppermute | solution.py:89
  81.0 15.8 %collective-permute-start.28 = (bf16[8,32,256]{2,1,0:T(8,128)(2,1)S(1)}, bf16[8,32,256]{2,1,0:T(8,128)(2,1)S(1)}, u32[]{:S(2)}, u32[]{:S(2)}) collective-permute-start(bf16[8,32,256]{2,1,0:T(8,128)(2,1)S(1)} %get-tuple-element.88), channel_id=1, source_target_pairs={{0,31},{1,26},{2,25},{3,28},{4,27},{5,30},{6,29},{7,24},{8,23},{9,... | collective-permute-start | bytes 393224 | tf_op jit(solution)/shard_map/ppermute | solution.py:89
  82.1 1.2 copy-start
  83.5 13.3 %collective-permute-start.22 = (bf16[8,32,256]{2,1,0:T(8,128)(2,1)S(1)}, bf16[8,32,256]{2,1,0:T(8,128)(2,1)S(1)}, u32[]{:S(2)}, u32[]{:S(2)}) collective-permute-start(bf16[8,32,256]{2,1,0:T(8,128)(2,1)S(1)} %get-tuple-element.82), channel_id=1, source_target_pairs={{0,8},{8,0},{16,24},{24,16},{1,9},{9,1},{17,25},{25,17},{2,10},{10... | collective-permute-start | bytes 393224 | tf_op jit(solution)/shard_map/ppermute | solution.py:81
  85.4 11.4 %collective-permute-start.23 = (bf16[8,32,256]{2,1,0:T(8,128)(2,1)S(1)}, bf16[8,32,256]{2,1,0:T(8,128)(2,1)S(1)}, u32[]{:S(2)}, u32[]{:S(2)}) collective-permute-start(bf16[8,32,256]{2,1,0:T(8,128)(2,1)S(1)} %get-tuple-element.83), channel_id=1, source_target_pairs={{0,16},{8,24},{16,0},{24,8},{1,17},{9,25},{17,1},{25,9},{2,18},{10... | collective-permute-start | bytes 393224 | tf_op jit(solution)/shard_map/ppermute | solution.py:81
  86.2 10.6 %copy-start.3 = (s32[1,1,2048,1]{2,3,1,0:T(1,128)S(1)}, s32[1,1,2048,1]{2,3,1,0:T(1,128)}, u32[]{:S(2)}) copy-start(s32[1,1,2048,1]{2,3,1,0:T(1,128)} %param.12) | copy-start | bytes 24580
  86.2 10.6 %collective-permute-start.24 = (bf16[8,32,256]{2,1,0:T(8,128)(2,1)S(1)}, bf16[8,32,256]{2,1,0:T(8,128)(2,1)S(1)}, u32[]{:S(2)}, u32[]{:S(2)}) collective-permute-start(bf16[8,32,256]{2,1,0:T(8,128)(2,1)S(1)} %get-tuple-element.84), channel_id=1, source_target_pairs={{0,24},{8,16},{16,8},{24,0},{1,25},{9,17},{17,9},{25,1},{2,26},{10... | collective-permute-start | bytes 393224 | tf_op jit(solution)/shard_map/ppermute | solution.py:81
  103.1 18.3 %all-to-all-start = ((s16[32,56,128]{2,1,0:T(8,128)(2,1)}), s16[32,56,128]{2,1,0:T(8,128)(2,1)S(1)}, u32[]{:S(2)}, u32[]{:S(2)}) async-start(s16[32,56,128]{2,1,0:T(8,128)(2,1)} %shard_map.94), calls=%async_computation | async-start | bytes 917504 | tf_op jit(solution)/shard_map/all_to_all | solution.py:514

commit v5 on v4

--- a/solution.py
+++ b/solution.py
@@ -38,7 +38,7 @@
     return lax.broadcasted_iota(I32, dims, axis)
 
 
-def kernel_call(kernel, steps, scalars, ins, outs, args, scratch=(), limit=50 * MIB, flops=0):
+def kernel_call(kernel, steps, scalars, ins, outs, args, scratch=(), limit=24 * MIB, flops=0):
     return pl.pallas_call(
         kernel,
         out_shape=[o for _, o in outs],
@@ -65,9 +65,10 @@
     rb_count, depth, width = view_blocks.shape[2:5]
     rows = rb_count * width
     per_group = split * rb_count
+    group_bits = per_group.bit_length() - 1
+    assert 1 << group_bits == per_group
     capacity = max(2, 3 * rows // devices)
     surfaces = rows // 2
-    me = lax.axis_index("patch")
 
     def inner(block):
         return lax.ppermute(block, "patch", [(i, i ^ 1) for i in range(groups)])
@@ -80,27 +81,23 @@
     def across(block, d):
         return lax.ppermute(block, "band", [(i, i ^ d) for i in range(split)])
 
-    def outer_across(block, d):
-        route = []
-        for i in range(split):
-            for g in range(groups):
-                beyond = (g + (1 if g % 2 else -1)) % groups
-                route.append((i * groups + g, (i ^ d) * groups + beyond))
-        return lax.ppermute(block, ("band", "patch"), route)
-
-    columns = column_blocks.reshape(rb_count * depth)
-    column_group = columns // per_group
-    third = jnp.where(column_group == me, 0, jnp.where(column_group == (me ^ 1), 1, 2))
-    slots = third * per_group + columns % per_group
     matrix = view_blocks.reshape(rb_count, depth, width, width)
     block_shape = (rb_count, bands, width)
     part_shape = (split,) + block_shape
     pass_flops = 2 * bands * rb_count * depth * width * width
     once = rb_count // 4
-    half = depth // 2
-
-    def prepare(e_ref, b_ref, w_ref, start_ref, *piece_refs):
+
+    def prepare(e_hbm, b_hbm, w_hbm, start_ref, *refs):
+        piece_refs, (e_ref, b_ref, w_ref, loaded) = refs[:split], refs[split:]
         band = lax.axis_index("band")
+        loads = [
+            pltpu.make_async_copy(source, target, loaded.at[a])
+            for a, (source, target) in enumerate(((e_hbm, e_ref), (b_hbm, b_ref), (w_hbm, w_ref)))
+        ]
+        for load in loads:
+            load.start()
+        for load in loads:
+            load.wait()
         for c in range(per_group):
             cut = slice(c * width, (c + 1) * width)
             start_ref[c] = (e_ref[:, cut] * b_ref[:, cut]).astype(BF16)
@@ -115,10 +112,11 @@
         prepare,
         1,
         0,
-        [whole((part_bands, per_group * width))] * 3,
+        [pl.BlockSpec(memory_space=pltpu.HBM)] * 3,
         [(whole(start_shape), shape(start_shape, BF16))]
         + [(whole(piece), shape(piece, F32))] * split,
         (emissivity, blackbody, loss_weights),
+        [pltpu.VMEM(emissivity.shape, F32)] * 3 + [pltpu.SemaphoreType.DMA((3,))],
         limit=60 * MIB,
     )
     pieces = [across(pieces[d], d) if d else pieces[d] for d in range(split)]
@@ -131,7 +129,7 @@
         pairs, _ = lax.optimization_barrier((pairs, after))
         return pairs + [inner(jnp.stack([p[0] for p in pairs]))]
 
-    def scatter_products(slots_ref, m_refs, value_of, outs, total):
+    def scatter_products(slots_ref, m_ref, value_of, outs, total):
         i = pl.program_id(0)
 
         @pl.when(i == 0)
@@ -141,29 +139,25 @@
         for q in range(once):
             u = value_of(q)
             for k in range(depth):
-                s = slots_ref[(i * once + q) * depth + k]
-                total[s] += nn(u, m_refs[k // half][q, k % half])
+                s = slots_ref[i * once + q, k]
+                total[s] += nn(u, m_ref[i * once + q, k])
 
         @pl.when(i == pl.num_programs(0) - 1)
         def _():
-            own_ref, near_ref, *far_refs = outs
+            own_ref, near_ref, far_ref = outs
             band = lax.axis_index("band")
             for d in range(split):
                 at = (band ^ d) * rb_count
                 own_ref[d] = total[pl.ds(at, rb_count)]
                 near_ref[d] = total[pl.ds(per_group + at, rb_count)].astype(BF16)
-                far_refs[d][...] = total[pl.ds(2 * per_group + at, rb_count)].astype(BF16)
-
-    matrix_specs = [
-        pl.BlockSpec((once, half, width, width), lambda i, *_, h=h: (i, h, 0, 0)) for h in (0, 1)
-    ]
-    part_outs = [(whole(part_shape), shape(part_shape, t)) for t in (F32, BF16)]
-    part_outs += [(whole(block_shape), shape(block_shape, BF16))] * split
+                far_ref[d] = total[pl.ds(2 * per_group + at, rb_count)].astype(BF16)
+
+    part_outs = [(whole(part_shape), shape(part_shape, t)) for t in (F32, BF16, BF16)]
     total_scratch = [pltpu.VMEM((3 * per_group, bands, width), F32)]
     step_rows = along((once, bands, width), 0)
     full_rows = along((3, once, bands, width), 1)
 
-    def adjoint_first(slots_ref, m0, m1, *refs):
+    def adjoint_first(slots_ref, m_ref, *refs):
         piece_refs, full_ref, outs, total = refs[:split], refs[split], refs[split + 1 : -1], refs[-1]
         b = lax.axis_index("band")
         for d in range(split):
@@ -175,7 +169,7 @@
         def value_of(q):
             return ((1.0 - full_ref[0, q]) * full_ref[2, q]).astype(BF16)
 
-        scatter_products(slots_ref, (m0, m1), value_of, outs, total)
+        scatter_products(slots_ref, m_ref, value_of, outs, total)
 
     def arrived(refs, q):
         value = refs[0][q]
@@ -183,11 +177,11 @@
             value = value + ref[q].astype(F32)
         return value
 
-    def adjoint_second(slots_ref, m0, m1, *refs):
+    def adjoint_second(slots_ref, m_ref, *refs):
         got_refs, (full_ref, one_ref), outs, total = (
-            refs[: 2 * split],
-            refs[2 * split : 2 * split + 2],
-            refs[2 * split + 2 : -1],
+            refs[:split],
+            refs[split : split + 2],
+            refs[split + 2 : -1],
             refs[-1],
         )
 
@@ -196,37 +190,38 @@
             one_ref[q] = value
             return ((1.0 - full_ref[0, q]) * value).astype(BF16)
 
-        scatter_products(slots_ref, (m0, m1), value_of, outs, total)
-
-    def merge(own_ref, near_ref, kept_ref, *sent_refs):
-        kept_ref[...] = own_ref[0] + near_ref[0].astype(F32)
-        for d in range(1, split):
-            sent_refs[d - 1][...] = (own_ref[d] + near_ref[d].astype(F32)).astype(BF16)
-
-    def collect(own, near, *far):
-        near = inner(near)
-        far = [outer_across(far[d], d) for d in range(split)]
+        scatter_products(slots_ref, m_ref, value_of, outs, total)
+
+    def merge(own_ref, near_ref, far_ref, kept_ref, *sent_refs):
+        for d in range(split):
+            value = own_ref[d] + near_ref[d].astype(F32) + far_ref[d].astype(F32)
+            if d:
+                sent_refs[d - 1][...] = value.astype(BF16)
+            else:
+                kept_ref[...] = value
+
+    def collect(own, near, far):
         kept, *sent = kernel_call(
             merge,
             1,
             0,
-            [whole(part_shape)] * 2,
+            [whole(part_shape)] * 3,
             [(whole(block_shape), shape(block_shape, F32))]
             + [(whole(block_shape), shape(block_shape, BF16))] * (split - 1),
-            (own, near),
+            (own, inner(near), outer(far)),
         )
-        return [kept] + [across(sent[d - 1], d) for d in range(1, split)] + far
-
-    def products(slots_ref, m_refs, held, finish):
+        return [kept] + [across(sent[d - 1], d) for d in range(1, split)]
+
+    def products(slots_ref, m_ref, held, finish):
         i = pl.program_id(0)
         for q in range(once):
             value = jnp.zeros((bands, width), F32)
             for k in range(depth):
-                s = slots_ref[(i * once + q) * depth + k]
-                value = value + nt(held[s], m_refs[k // half][q, k % half])
+                s = slots_ref[i * once + q, k]
+                value = value + nt(held[s], m_ref[i * once + q, k])
             finish(q, value)
 
-    def forward_first(slots_ref, m0, m1, *refs):
+    def forward_first(slots_ref, m_ref, *refs):
         pair_refs, (near_ref, full_ref, zero_ref, rad_ref, held) = refs[:split], refs[split:]
         band = lax.axis_index("band")
 
@@ -250,9 +245,9 @@
             e, b = full_ref[0, q], full_ref[1, q]
             rad_ref[q] = (e * b + (1.0 - e) * zero_ref[q]).astype(BF16)
 
-        products(slots_ref, (m0, m1), held, finish)
-
-    def forward_second(slots_ref, m0, m1, *refs):
+        products(slots_ref, m_ref, held, finish)
+
+    def forward_second(slots_ref, m_ref, *refs):
         pair_refs, (near_ref, full_ref, one_ref, rad_ref, held) = refs[:split], refs[split:]
 
         @pl.when(pl.program_id(0) == 0)
@@ -269,7 +264,7 @@
             e, b = full_ref[0, q], full_ref[1, q]
             rad_ref[:, q * width : (q + 1) * width] = e * b + (1.0 - e) * value
 
-        products(slots_ref, (m0, m1), held, finish)
+        products(slots_ref, m_ref, held, finish)
 
     window_scratch = [pltpu.VMEM((3 * per_group, bands, width), BF16)]
 
@@ -278,7 +273,20 @@
     value_rows = bands + (bands // 2 if tail else 0)
     send_rows = value_rows + 8
 
-    def route(owner_ref, surface_ref, rank_ref, label_ref):
+    def route(
+        matrix_ref, column_ref, owner_ref, surface_ref, m_ref, slot_ref, rank_ref, label_ref, loaded
+    ):
+        loads = [
+            pltpu.make_async_copy(matrix_ref.at[r], m_ref.at[r], loaded.at[r])
+            for r in range(rb_count)
+        ]
+        for load in loads:
+            load.start()
+        me = lax.axis_index("patch")
+        column = column_ref[...]
+        group = jnp.right_shift(column, group_bits)
+        third = jnp.where(group == me, 0, jnp.where(group == (me ^ 1), 1, 2))
+        slot_ref[...] = third * per_group + jnp.bitwise_and(column, per_group - 1)
         names = iota((devices, width), 0)
         upper = (iota((width, width), 0) <= iota((width, width), 1)).astype(BF16)
         seat = iota((seats, width), 0)
@@ -299,27 +307,38 @@
             found = found + nt(marks, seated)
         taken, high, low = (found[a * devices : (a + 1) * devices] for a in range(3))
         label_ref[...] = jnp.where(taken > 0.5, high * 128.0 + low, float(surfaces))
-
-    rank, labels = kernel_call(
+        for load in loads:
+            load.wait()
+
+    matrix, slots, rank, labels = kernel_call(
         route,
         1,
         0,
-        [whole((1, rows))] * 2,
+        [pl.BlockSpec(memory_space=pl.ANY), whole((rb_count, depth))] + [whole((1, rows))] * 2,
         [
+            (VMEM, pltpu.VMEM(matrix.shape, BF16)),
+            (whole((rb_count, depth)), shape((rb_count, depth), I32)),
             (whole((1, rows)), shape((1, rows), I32)),
             (whole((devices, seats)), shape((devices, seats), F32)),
         ],
-        (patch_owner.reshape(1, rows), patch_surface.reshape(1, rows)),
-    )
-
-    owners_once = 4
+        (
+            matrix,
+            column_blocks.reshape(rb_count, depth),
+            patch_owner.reshape(1, rows),
+            patch_surface.reshape(1, rows),
+        ),
+        [pltpu.SemaphoreType.DMA((rb_count,))],
+        limit=40 * MIB,
+    )
+
+    owners_once = 16
 
     def pack_rows(*refs):
-        got_refs = refs[: 2 * split]
+        got_refs = refs[:split]
         adj_ref, zero_ref, one_ref, full_ref, owner_ref, rank_ref, label_ref = refs[
-            2 * split : 2 * split + 7
+            split : split + 7
         ]
-        send_ref, grad, digits, seated, most = refs[2 * split + 7 :]
+        send_ref, grad, digits, seated, most = refs[split + 7 :]
         i = pl.program_id(0)
 
         @pl.when(i == 0)
@@ -376,7 +395,7 @@
 
             lax.fori_loop(0, devices // owners_once, step, 0)
 
-    sources_once = 4
+    sources_once = 16
     tops = surfaces // LANES
     lot = sources_once * LANES * (2 if tail else 1)
     top_rows = 2 * bands + 16
@@ -425,15 +444,15 @@
             count = jnp.maximum(total[at + 2 * bands : at + 2 * bands + 1], 1.0)
             out_ref[:, t * LANES : (t + 1) * LANES] = sums / count
 
-    start = pair_of(start)
+    start = jnp.stack(lax.optimization_barrier((start, outer(start), rank, pieces))[:2])
     slots, rank, labels, _ = lax.optimization_barrier((slots, rank, labels, start))
     full, *parts = kernel_call(
         adjoint_first,
         4,
         1,
-        matrix_specs + [along((3, part_bands, once * width), 2)] * split,
+        [VMEM] + [along((3, part_bands, once * width), 2)] * split,
         [(full_rows, shape((3,) + block_shape, F32))] + part_outs,
-        (slots, matrix, matrix) + tuple(pieces),
+        (slots, matrix) + tuple(pieces),
         total_scratch,
         flops=pass_flops,
     )
@@ -444,10 +463,10 @@
         forward_first,
         4,
         1,
-        matrix_specs + [whole((2,) + start_shape)] * split
+        [VMEM] + [whole((2,) + start_shape)] * split
         + [whole((split,) + start_shape), full_rows],
         [(step_rows, shape(block_shape, F32)), (step_rows, shape(block_shape, BF16))],
-        (slots, matrix, matrix) + tuple(starts) + (full,),
+        (slots, matrix) + tuple(starts) + (full,),
         window_scratch,
         flops=pass_flops,
     )
@@ -459,9 +478,9 @@
         adjoint_second,
         4,
         1,
-        matrix_specs + [step_rows] * (2 * split) + [full_rows],
+        [VMEM] + [step_rows] * split + [full_rows],
         [(step_rows, shape(block_shape, F32))] + part_outs,
-        (slots, matrix, matrix) + tuple(got_one) + (full,),
+        (slots, matrix) + tuple(got_one) + (full,),
         total_scratch,
         flops=pass_flops,
     )
@@ -472,12 +491,12 @@
         forward_second,
         4,
         1,
-        matrix_specs + [whole((2,) + block_shape)] * split + [whole(part_shape), full_rows],
+        [VMEM] + [whole((2,) + block_shape)] * split + [whole(part_shape), full_rows],
         [
             (step_rows, shape(block_shape, F32)),
             (along((bands, once * width), 1), shape((bands, rows), F32)),
         ],
-        (slots, matrix, matrix) + tuple(rads) + (full,),
+        (slots, matrix) + tuple(rads) + (full,),
         window_scratch,
         flops=pass_flops,
     )
@@ -486,7 +505,7 @@
         pack_rows,
         4,
         0,
-        [step_rows] * (2 * split + 3)
+        [step_rows] * (split + 3)
         + [full_rows, whole((1, rows)), whole((1, rows)), whole((devices, seats))],
         [
             (

time: 127 us -> 117 us (0.921)
  waiting for transfers between devices: 21.9 us -> 43.4 us
  starting transfers between devices: 45.5 us -> 30.1 us
  Pallas kernels: 51.7 us -> 40 us
  local copies, waits for them, and re-layouts: 5.37 us -> 1.77 us
    ppermute x8 -> x0, starting transfers between devices: 17.6 us -> none  [outer_across(): return lax.ppermute(block, ('band', 'patch'), route)]
    ppermute x2 -> x4, waiting for transfers between devices: 0.01 us -> 15.5 us  [outer(): lax.ppermute(block, 'patch', [(i, (i + (1 if i % 2 else -1)) % groups) fo...]
    pallas_call x10, Pallas kernels: 51.7 us -> 40 us  [kernel_call(): pl.pallas_call(kernel, out_shape=[o for _, o in outs], grid_spec=pltpu.Pr...]
    ppermute x15, waiting for transfers between devices: 4.54 us -> 13.9 us  [across(): return lax.ppermute(block, 'band', [(i, i ^ d) for i in range(split)])]
    ppermute x8 -> x0, waiting for transfers between devices: 3.41 us -> none  [outer_across(): return lax.ppermute(block, ('band', 'patch'), route)]
    unnamed x11 -> x15, local copies, waits for them, and re-layouts: 4.52 us -> 1.69 us
    ppermute x2 -> x4, starting transfers between devices: 6.51 us -> 8.57 us  [outer(): lax.ppermute(block, 'patch', [(i, (i + (1 if i % 2 else -1)) % groups) fo...]
    ppermute x15, starting transfers between devices: 17 us -> 18.7 us  [across(): return lax.ppermute(block, 'band', [(i, i ^ d) for i in range(split)])]
  transfers between devices with their start and end apart: 30 -> 24, of which waited for: 9 -> 8; matrix products, arithmetic and copies ran while one was open for 2% -> 1% of each run, Pallas kernels for 30% -> 25%
where the time goes in v5:
time: 117 us; the launch traced here: 116 us
  waiting for transfers between devices  43.4 us (37%)
  Pallas kernels  40 us (34%)
  starting transfers between devices  30.1 us (26%)
  local copies, waits for them, and re-layouts  1.77 us (2%)
    pallas_call x10, Pallas kernels, kernel_call(): pl.pallas_call(kernel, out_shape=[o for _, o in outs], grid_spec=pltpu.Pr...  40 us
    ppermute x15, starting transfers between devices, across(): return lax.ppermute(block, 'band', [(i, i ^ d) for i in range(split)])  18.7 us
    ppermute x4, waiting for transfers between devices, outer(): lax.ppermute(block, 'patch', [(i, (i + (1 if i % 2 else -1)) % groups) fo...  15.5 us
    all_to_all x1, waiting for transfers between devices, body(): send = lax.all_to_all(send, ('band', 'patch'), 0, 0, tiled=True)  14 us
    ppermute x15, waiting for transfers between devices, across(): return lax.ppermute(block, 'band', [(i, i ^ d) for i in range(split)])  13.9 us
    ppermute x4, starting transfers between devices, outer(): lax.ppermute(block, 'patch', [(i, (i + (1 if i % 2 else -1)) % groups) fo...  8.57 us
    all_to_all x1, starting transfers between devices, body(): send = lax.all_to_all(send, ('band', 'patch'), 0, 0, tiled=True)  2.6 us
  transfers between devices with their start and end apart: 24, of which 8 were waited for; matrix products, arithmetic and copies ran while one was open for 1% of the time, Pallas kernels for 25%

profile of v5, /device:TPU:0, one launch (start us, length us, event | category | flops | bytes accessed | tf_op | source)
XLA Modules:
  0.0 116.5 jit_solution(8540484041467316524)
XLA Ops:
  0.6 2.1 %shard_map.87 = (bf16[32,8,256]{2,1,0:T(8,128)(2,1)}, f32[3,8,2048]{2,1,0:T(8,128)}, f32[3,8,2048]{2,1,0:T(8,128)}, f32[3,8,2048]{2,1,0:T(8,128)}, f32[3,8,2048]{2,1,0:T(8,128)}) custom-call(f32[8,8192]{1,0:T(8,128)} %e_hbm.1, f32[8,8192]{1,0:T(8,128)} %b_hbm.1, f32[8,8192]{1,0:T(8,128)} %w_hbm.1), custom_call_target="tpu_custom_call" | custom-call | tf_op jit(solution)/shard_map/pallas_call | solution.py:42
  2.7 0.0 copy-start.6
  2.7 0.0 copy-start
  2.7 3.0 %collective-permute-start.1 = (f32[3,8,2048]{2,1,0:T(8,128)}, f32[3,8,2048]{2,1,0:T(8,128)S(1)}, u32[]{:S(2)}, u32[]{:S(2)}) collective-permute-start(f32[3,8,2048]{2,1,0:T(8,128)} %get-tuple-element.51), channel_id=1, source_target_pairs={{0,8},{8,0},{16,24},{24,16},{1,9},{9,1},{17,25},{25,17},{2,10},{10... | collective-permute-start | bytes 589832 | tf_op jit(solution)/shard_map/ppermute | solution.py:82
  5.7 1.5 %collective-permute-start.2 = (f32[3,8,2048]{2,1,0:T(8,128)}, f32[3,8,2048]{2,1,0:T(8,128)S(1)}, u32[]{:S(2)}, u32[]{:S(2)}) collective-permute-start(f32[3,8,2048]{2,1,0:T(8,128)} %get-tuple-element.52), channel_id=1, source_target_pairs={{0,16},{8,24},{16,0},{24,8},{1,17},{9,25},{17,1},{25,9},{2,18},{10... | collective-permute-start | bytes 589832 | tf_op jit(solution)/shard_map/ppermute | solution.py:82
  7.3 0.0 collective-permute-start.3
  7.3 2.7 %collective-permute-start = (bf16[32,8,256]{2,1,0:T(8,128)(2,1)}, bf16[32,8,256]{2,1,0:T(8,128)(2,1)S(1)}, u32[]{:S(2)}, u32[]{:S(2)}) collective-permute-start(bf16[32,8,256]{2,1,0:T(8,128)(2,1)} %get-tuple-element.54), channel_id=1, source_target_pairs={{0,7},{1,2},{2,1},{3,4},{4,3},{5,6},{6,5},{7,0},{8,15},{9,10},{10,... | collective-permute-start | bytes 393224 | tf_op jit(solution)/shard_map/ppermute | solution.py:77
  9.9 7.3 %shard_map.86 = (bf16[8,16,256,256]{3,2,1,0:T(8,128)(2,1)S(1)}, s32[8,16]{1,0:T(8,128)}, s32[1,2048]{1,0:T(1,128)}, f32[32,192]{1,0:T(8,128)}) custom-call(bf16[8,16,256,256]{3,2,1,0:T(8,128)(2,1)} %bitcast.13, s32[8,16]{1,0:T(8,128)} %bitcast.18, s32[1,2048]{1,0:T(1,128)} %bitcast.11, s32[1,2048]{1,0:T(1,128)} %bitcast.17), custom_call_target="tpu_custom_call" | custom-call | tf_op jit(solution)/shard_map/pallas_call | solution.py:42
  17.3 1.6 %collective-permute-start.4 = (bf16[2,32,8,256]{3,2,1,0:T(8,128)(2,1)S(1)}, bf16[2,32,8,256]{3,2,1,0:T(8,128)(2,1)S(1)}, u32[]{:S(2)}, u32[]{:S(2)}) collective-permute-start(bf16[2,32,8,256]{3,2,1,0:T(8,128)(2,1)S(1)} %pad_maximum_fusion.2.refs_0_), channel_id=1, source_target_pairs={{0,8},{8,0},{16,24},{24,16},{1,9},{9,1},{17,25},{25,17},{2,10},{10... | collective-permute-start | bytes 786440 | tf_op jit(solution)/shard_map/ppermute | solution.py:82
  18.9 1.5 %collective-permute-start.5 = (bf16[2,32,8,256]{3,2,1,0:T(8,128)(2,1)S(1)}, bf16[2,32,8,256]{3,2,1,0:T(8,128)(2,1)S(1)}, u32[]{:S(2)}, u32[]{:S(2)}) collective-permute-start(bf16[2,32,8,256]{3,2,1,0:T(8,128)(2,1)S(1)} %pad_maximum_fusion.2.refs_0_), channel_id=1, source_target_pairs={{0,16},{8,24},{16,0},{24,8},{1,17},{9,25},{17,1},{25,9},{2,18},{10... | collective-permute-start | bytes 786440 | tf_op jit(solution)/shard_map/ppermute | solution.py:82
  20.4 0.5 collective-permute-start.6
  20.9 0.7 copy-done.1
  21.6 4.6 %shard_map.88 = (f32[3,8,32,256]{3,2,1,0:T(8,128)S(1)}, f32[4,8,32,256]{3,2,1,0:T(8,128)S(1)}, bf16[4,8,32,256]{3,2,1,0:T(8,128)(2,1)S(1)}, bf16[4,8,32,256]{3,2,1,0:T(8,128)(2,1)S(1)}) custom-call(s32[8,16]{1,0:T(8,128)S(1)} %copy-done.1, bf16[8,16,256,256]{3,2,1,0:T(8,128)(2,1)S(1)} %get-tuple-element.57.m_ref, f32[3,8,2048]{2,1,0:T(8,128)S(1)} %copy-done, ...), custom_call_target="tpu_custom_call" | custom-call | flops 536870912 | bytes 16777216 | tf_op jit(solution)/shard_map/pallas_call | solution.py:42
  26.2 0.4 collective-permute-done.4.refs_1_
  26.6 5.3 %collective-permute-done.5.refs_2_ = bf16[2,32,8,256]{3,2,1,0:T(8,128)(2,1)S(1)} collective-permute-done((bf16[2,32,8,256]{3,2,1,0:T(8,128)(2,1)S(1)}, bf16[2,32,8,256]{3,2,1,0:T(8,128)(2,1)S(1)}, u32[]{:S(2)}, u32[]{:S(2)}) %collective-permute-start.5) | collective-permute-done | bytes 262176 | tf_op jit(solution)/shard_map/ppermute | solution.py:82
  32.0 0.1 pad_maximum_fusion
  32.1 0.1 collective-permute-start.7
  32.1 2.3 %collective-permute-start.10 = (bf16[4,8,32,256]{3,2,1,0:T(8,128)(2,1)S(1)}, bf16[4,8,32,256]{3,2,1,0:T(8,128)(2,1)S(1)}, u32[]{:S(2)}, u32[]{:S(2)}) collective-permute-start(bf16[4,8,32,256]{3,2,1,0:T(8,128)(2,1)S(1)} %get-tuple-element.66), channel_id=1, source_target_pairs={{0,7},{1,2},{2,1},{3,4},{4,3},{5,6},{6,5},{7,0},{8,15},{9,10},{10,... | collective-permute-start | bytes 1572872 | tf_op jit(solution)/shard_map/ppermute | solution.py:77
  34.5 6.4 %shard_map.89 = (f32[8,32,256]{2,1,0:T(8,128)S(1)}, bf16[8,32,256]{2,1,0:T(8,128)(2,1)S(1)}) custom-call(s32[8,16]{1,0:T(8,128)S(1)} %copy-done.1, bf16[8,16,256,256]{3,2,1,0:T(8,128)(2,1)S(1)} %get-tuple-element.57.m_ref, bf16[2,32,8,256]{3,2,1,0:T(8,128)(2,1)S(1)} %pad_maximum_fusion.2.refs_0_, bf16[2,32,8,256]{3,2,1,0:T(8,128)(2,1)S(1)} %collective-permute-done.4.refs_1_, ...), custom_call_target="tpu_custom_call" | custom-call | flops 536870912 | bytes 16777216 | tf_op jit(solution)/shard_map/pallas_call | solution.py:42
  40.9 2.0 %collective-permute-start.8 = (bf16[8,32,256]{2,1,0:T(8,128)(2,1)S(1)}, bf16[8,32,256]{2,1,0:T(8,128)(2,1)S(1)}, u32[]{:S(2)}, u32[]{:S(2)}) collective-permute-start(bf16[8,32,256]{2,1,0:T(8,128)(2,1)S(1)} %get-tuple-element.64), channel_id=1, source_target_pairs={{0,7},{1,2},{2,1},{3,4},{4,3},{5,6},{6,5},{7,0},{8,15},{9,10},{10,... | collective-permute-start | bytes 393224 | tf_op jit(solution)/shard_map/ppermute | solution.py:77
  42.9 4.6 %collective-permute-done.10.far_ref = bf16[4,8,32,256]{3,2,1,0:T(8,128)(2,1)S(1)} collective-permute-done((bf16[4,8,32,256]{3,2,1,0:T(8,128)(2,1)S(1)}, bf16[4,8,32,256]{3,2,1,0:T(8,128)(2,1)S(1)}, u32[]{:S(2)}, u32[]{:S(2)}) %collective-permute-start.10) | collective-permute-done | bytes 524320 | tf_op jit(solution)/shard_map/ppermute | solution.py:77
  47.4 0.2 shard_map.90
  47.6 1.8 %collective-permute-start.11 = (bf16[8,32,256]{2,1,0:T(8,128)(2,1)S(1)}, bf16[8,32,256]{2,1,0:T(8,128)(2,1)S(1)}, u32[]{:S(2)}, u32[]{:S(2)}) collective-permute-start(bf16[8,32,256]{2,1,0:T(8,128)(2,1)S(1)} %get-tuple-element.69), channel_id=1, source_target_pairs={{0,8},{8,0},{16,24},{24,16},{1,9},{9,1},{17,25},{25,17},{2,10},{10... | collective-permute-start | bytes 393224 | tf_op jit(solution)/shard_map/ppermute | solution.py:82
  49.4 0.3 collective-permute-start.12
  49.7 1.4 %collective-permute-start.13 = (bf16[8,32,256]{2,1,0:T(8,128)(2,1)S(1)}, bf16[8,32,256]{2,1,0:T(8,128)(2,1)S(1)}, u32[]{:S(2)}, u32[]{:S(2)}) collective-permute-start(bf16[8,32,256]{2,1,0:T(8,128)(2,1)S(1)} %get-tuple-element.71), channel_id=1, source_target_pairs={{0,24},{8,16},{16,8},{24,0},{1,25},{9,17},{17,9},{25,1},{2,26},{10... | collective-permute-start | bytes 393224 | tf_op jit(solution)/shard_map/ppermute | solution.py:82
  51.2 0.0 copy-start.4
  51.2 2.8 %collective-permute-done.11.refs_1_ = bf16[8,32,256]{2,1,0:T(8,128)(2,1)S(1)} collective-permute-done((bf16[8,32,256]{2,1,0:T(8,128)(2,1)S(1)}, bf16[8,32,256]{2,1,0:T(8,128)(2,1)S(1)}, u32[]{:S(2)}, u32[]{:S(2)}) %collective-permute-start.11) | collective-permute-done | bytes 131104 | tf_op jit(solution)/shard_map/ppermute | solution.py:82
  54.0 2.6 %collective-permute-done.12.refs_2_ = bf16[8,32,256]{2,1,0:T(8,128)(2,1)S(1)} collective-permute-done((bf16[8,32,256]{2,1,0:T(8,128)(2,1)S(1)}, bf16[8,32,256]{2,1,0:T(8,128)(2,1)S(1)}, u32[]{:S(2)}, u32[]{:S(2)}) %collective-permute-start.12) | collective-permute-done | bytes 131104 | tf_op jit(solution)/shard_map/ppermute | solution.py:82
  56.6 0.9 collective-permute-start.14
  57.4 1.0 collective-permute-start.15
  58.5 1.6 %collective-permute-start.16 = (bf16[2,8,32,256]{3,2,1,0:T(8,128)(2,1)S(1)}, bf16[2,8,32,256]{3,2,1,0:T(8,128)(2,1)S(1)}, u32[]{:S(2)}, u32[]{:S(2)}) collective-permute-start(bf16[2,8,32,256]{3,2,1,0:T(8,128)(2,1)S(1)} %pad_maximum_fusion.3.refs_0_), channel_id=1, source_target_pairs={{0,24},{8,16},{16,8},{24,0},{1,25},{9,17},{17,9},{25,1},{2,26},{10... | collective-permute-start | bytes 786440 | tf_op jit(solution)/shard_map/ppermute | solution.py:82
  60.1 4.5 %shard_map.91 = (f32[8,32,256]{2,1,0:T(8,128)S(1)}, f32[4,8,32,256]{3,2,1,0:T(8,128)S(1)}, bf16[4,8,32,256]{3,2,1,0:T(8,128)(2,1)S(1)}, bf16[4,8,32,256]{3,2,1,0:T(8,128)(2,1)S(1)}) custom-call(s32[8,16]{1,0:T(8,128)S(1)} %copy-done.2, bf16[8,16,256,256]{3,2,1,0:T(8,128)(2,1)S(1)} %get-tuple-element.57.m_ref, f32[8,32,256]{2,1,0:T(8,128)S(1)} %get-tuple-element.68.refs_0_, ...), custom_call_target="tpu_custom_call" | custom-call | flops 536870912 | bytes 16777216 | tf_op jit(solution)/shard_map/pallas_call | solution.py:42
  64.6 0.1 collective-permute-start.18
  64.6 1.6 %collective-permute-start.19 = (bf16[4,8,32,256]{3,2,1,0:T(8,128)(2,1)S(1)}, bf16[4,8,32,256]{3,2,1,0:T(8,128)(2,1)S(1)}, u32[]{:S(2)}, u32[]{:S(2)}) collective-permute-start(bf16[4,8,32,256]{3,2,1,0:T(8,128)(2,1)S(1)} %get-tuple-element.80), channel_id=1, source_target_pairs={{0,7},{1,2},{2,1},{3,4},{4,3},{5,6},{6,5},{7,0},{8,15},{9,10},{10,... | collective-permute-start | bytes 1572872 | tf_op jit(solution)/shard_map/ppermute | solution.py:77
  66.2 2.8 %collective-permute-done.15.refs_2_ = bf16[2,8,32,256]{3,2,1,0:T(8,128)(2,1)S(1)} collective-permute-done((bf16[2,8,32,256]{3,2,1,0:T(8,128)(2,1)S(1)}, bf16[2,8,32,256]{3,2,1,0:T(8,128)(2,1)S(1)}, u32[]{:S(2)}, u32[]{:S(2)}) %collective-permute-start.15) | collective-permute-done | bytes 262176 | tf_op jit(solution)/shard_map/ppermute | solution.py:82
  69.1 0.1 pad_maximum_fusion.1
  69.2 0.1 collective-permute-start.17
  69.2 11.0 %collective-permute-done.19.far_ref = bf16[4,8,32,256]{3,2,1,0:T(8,128)(2,1)S(1)} collective-permute-done((bf16[4,8,32,256]{3,2,1,0:T(8,128)(2,1)S(1)}, bf16[4,8,32,256]{3,2,1,0:T(8,128)(2,1)S(1)}, u32[]{:S(2)}, u32[]{:S(2)}) %collective-permute-start.19) | collective-permute-done | bytes 524320 | tf_op jit(solution)/shard_map/ppermute | solution.py:77
  80.2 0.2 shard_map.93
  80.4 1.4 %collective-permute-start.20 = (bf16[8,32,256]{2,1,0:T(8,128)(2,1)S(1)}, bf16[8,32,256]{2,1,0:T(8,128)(2,1)S(1)}, u32[]{:S(2)}, u32[]{:S(2)}) collective-permute-start(bf16[8,32,256]{2,1,0:T(8,128)(2,1)S(1)} %get-tuple-element.82), channel_id=1, source_target_pairs={{0,8},{8,0},{16,24},{24,16},{1,9},{9,1},{17,25},{25,17},{2,10},{10... | collective-permute-start | bytes 393224 | tf_op jit(solution)/shard_map/ppermute | solution.py:82
  81.8 0.6 collective-permute-start.21
  82.4 1.6 %collective-permute-start.22 = (bf16[8,32,256]{2,1,0:T(8,128)(2,1)S(1)}, bf16[8,32,256]{2,1,0:T(8,128)(2,1)S(1)}, u32[]{:S(2)}, u32[]{:S(2)}) collective-permute-start(bf16[8,32,256]{2,1,0:T(8,128)(2,1)S(1)} %get-tuple-element.84), channel_id=1, source_target_pairs={{0,24},{8,16},{16,8},{24,0},{1,25},{9,17},{17,9},{25,1},{2,26},{10... | collective-permute-start | bytes 393224 | tf_op jit(solution)/shard_map/ppermute | solution.py:82
  84.0 6.2 %shard_map.92 = (f32[8,32,256]{2,1,0:T(8,128)S(1)}, f32[32,2048]{1,0:T(8,128)S(1)}) custom-call(s32[8,16]{1,0:T(8,128)S(1)} %copy-done.2, bf16[8,16,256,256]{3,2,1,0:T(8,128)(2,1)S(1)} %get-tuple-element.57.m_ref, bf16[2,8,32,256]{3,2,1,0:T(8,128)(2,1)S(1)} %pad_maximum_fusion.3.refs_0_, bf16[2,8,32,256]{3,2,1,0:T(8,128)(2,1)S(1)} %collective-permute-done.14.refs_1_, ...), custom_call_target="tpu_custom_call" | custom-call | flops 536870912 | bytes 16777216 | tf_op jit(solution)/shard_map/pallas_call | solution.py:42
  90.2 4.6 %shard_map.94 = s16[32,56,128]{2,1,0:T(8,128)(2,1)} custom-call(f32[8,32,256]{2,1,0:T(8,128)S(1)} %get-tuple-element.81.refs_0_, bf16[8,32,256]{2,1,0:T(8,128)(2,1)S(1)} %collective-permute-done.20.refs_1_, bf16[8,32,256]{2,1,0:T(8,128)(2,1)S(1)} %collective-permute-done.21.refs_2_, bf16[8,32,256]{2,1,0:T(8,128)(2,1)S(1)} %collective-permute-done.22.refs_3_, ...), custom_call_target="tpu_custom_call" | custom-call | tf_op jit(solution)/shard_map/pallas_call | solution.py:42
  94.8 2.6 %all-to-all-start = ((s16[32,56,128]{2,1,0:T(8,128)(2,1)}), s16[32,56,128]{2,1,0:T(8,128)(2,1)S(1)}, u32[]{:S(2)}, u32[]{:S(2)}) async-start(s16[32,56,128]{2,1,0:T(8,128)(2,1)} %shard_map.94), calls=%async_computation | async-start | bytes 917504 | tf_op jit(solution)/shard_map/all_to_all | solution.py:533
  97.4 1.0 copy.9
  98.3 14.0 %all-to-all-done.got_ref = s16[32,56,128]{2,1,0:T(8,128)(2,1)S(1)} async-done(((s16[32,56,128]{2,1,0:T(8,128)(2,1)}), s16[32,56,128]{2,1,0:T(8,128)(2,1)S(1)}, u32[]{:S(2)}, u32[]{:S(2)}) %all-to-all-start) | async-done | bytes 458784 | tf_op jit(solution)/shard_map/all_to_all | solution.py:533
  112.3 4.1 %shard_map.95 = f32[32,1024]{1,0:T(8,128)} custom-call(s16[32,56,128]{2,1,0:T(8,128)(2,1)S(1)} %all-to-all-done.got_ref), custom_call_target="tpu_custom_call" | custom-call | tf_op jit(solution)/shard_map/pallas_call | solution.py:42
  (37 shorter events, 0.2 us)
Async XLA Ops:
  2.7 14.5 %copy-start.6 = (bf16[32,8,256]{2,1,0:T(8,128)(2,1)S(1)}, bf16[32,8,256]{2,1,0:T(8,128)(2,1)}, u32[]{:S(2)}) copy-start(bf16[32,8,256]{2,1,0:T(8,128)(2,1)} %get-tuple-element.54) | copy-start | bytes 393220
  2.7 18.1 %copy-start = (f32[3,8,2048]{2,1,0:T(8,128)S(1)}, f32[3,8,2048]{2,1,0:T(8,128)}, u32[]{:S(2)}) copy-start(f32[3,8,2048]{2,1,0:T(8,128)} %get-tuple-element.50.refs_0_) | copy-start | bytes 589828
  2.7 14.5 %collective-permute-start.1 = (f32[3,8,2048]{2,1,0:T(8,128)}, f32[3,8,2048]{2,1,0:T(8,128)S(1)}, u32[]{:S(2)}, u32[]{:S(2)}) collective-permute-start(f32[3,8,2048]{2,1,0:T(8,128)} %get-tuple-element.51), channel_id=1, source_target_pairs={{0,8},{8,0},{16,24},{24,16},{1,9},{9,1},{17,25},{25,17},{2,10},{10... | collective-permute-start | bytes 589832 | tf_op jit(solution)/shard_map/ppermute | solution.py:82
  5.7 11.5 %collective-permute-start.2 = (f32[3,8,2048]{2,1,0:T(8,128)}, f32[3,8,2048]{2,1,0:T(8,128)S(1)}, u32[]{:S(2)}, u32[]{:S(2)}) collective-permute-start(f32[3,8,2048]{2,1,0:T(8,128)} %get-tuple-element.52), channel_id=1, source_target_pairs={{0,16},{8,24},{16,0},{24,8},{1,17},{9,25},{17,1},{25,9},{2,18},{10... | collective-permute-start | bytes 589832 | tf_op jit(solution)/shard_map/ppermute | solution.py:82
  7.3 10.0 %collective-permute-start.3 = (f32[3,8,2048]{2,1,0:T(8,128)}, f32[3,8,2048]{2,1,0:T(8,128)S(1)}, u32[]{:S(2)}, u32[]{:S(2)}) collective-permute-start(f32[3,8,2048]{2,1,0:T(8,128)} %get-tuple-element.53), channel_id=1, source_target_pairs={{0,24},{8,16},{16,8},{24,0},{1,25},{9,17},{17,9},{25,1},{2,26},{10... | collective-permute-start | bytes 589832 | tf_op jit(solution)/shard_map/ppermute | solution.py:82
  7.3 9.9 %collective-permute-start = (bf16[32,8,256]{2,1,0:T(8,128)(2,1)}, bf16[32,8,256]{2,1,0:T(8,128)(2,1)S(1)}, u32[]{:S(2)}, u32[]{:S(2)}) collective-permute-start(bf16[32,8,256]{2,1,0:T(8,128)(2,1)} %get-tuple-element.54), channel_id=1, source_target_pairs={{0,7},{1,2},{2,1},{3,4},{4,3},{5,6},{6,5},{7,0},{8,15},{9,10},{10,... | collective-permute-start | bytes 393224 | tf_op jit(solution)/shard_map/ppermute | solution.py:77
  17.3 9.3 %collective-permute-start.4 = (bf16[2,32,8,256]{3,2,1,0:T(8,128)(2,1)S(1)}, bf16[2,32,8,256]{3,2,1,0:T(8,128)(2,1)S(1)}, u32[]{:S(2)}, u32[]{:S(2)}) collective-permute-start(bf16[2,32,8,256]{3,2,1,0:T(8,128)(2,1)S(1)} %pad_maximum_fusion.2.refs_0_), channel_id=1, source_target_pairs={{0,8},{8,0},{16,24},{24,16},{1,9},{9,1},{17,25},{25,17},{2,10},{10... | collective-permute-start | bytes 786440 | tf_op jit(solution)/shard_map/ppermute | solution.py:82
  18.9 13.0 %collective-permute-start.5 = (bf16[2,32,8,256]{3,2,1,0:T(8,128)(2,1)S(1)}, bf16[2,32,8,256]{3,2,1,0:T(8,128)(2,1)S(1)}, u32[]{:S(2)}, u32[]{:S(2)}) collective-permute-start(bf16[2,32,8,256]{3,2,1,0:T(8,128)(2,1)S(1)} %pad_maximum_fusion.2.refs_0_), channel_id=1, source_target_pairs={{0,16},{8,24},{16,0},{24,8},{1,17},{9,25},{17,1},{25,9},{2,18},{10... | collective-permute-start | bytes 786440 | tf_op jit(solution)/shard_map/ppermute | solution.py:82
  20.4 11.5 %collective-permute-start.6 = (bf16[2,32,8,256]{3,2,1,0:T(8,128)(2,1)S(1)}, bf16[2,32,8,256]{3,2,1,0:T(8,128)(2,1)S(1)}, u32[]{:S(2)}, u32[]{:S(2)}) collective-permute-start(bf16[2,32,8,256]{3,2,1,0:T(8,128)(2,1)S(1)} %pad_maximum_fusion.2.refs_0_), channel_id=1, source_target_pairs={{0,24},{8,16},{16,8},{24,0},{1,25},{9,17},{17,9},{25,1},{2,26},{10... | collective-permute-start | bytes 786440 | tf_op jit(solution)/shard_map/ppermute | solution.py:82
  20.9 0.7 copy-start.1
  21.6 38.5 %copy-start.2 = (s32[8,16]{1,0:T(8,128)S(1)}, s32[8,16]{1,0:T(8,128)}, u32[]{:S(2)}) copy-start(s32[8,16]{1,0:T(8,128)} %get-tuple-element.56.slots_ref) | copy-start | bytes 1540
  32.1 2.4 %collective-permute-start.7 = (bf16[4,32,8,256]{3,2,1,0:T(8,128)(2,1)S(1)}, bf16[4,32,8,256]{3,2,1,0:T(8,128)(2,1)S(1)}, u32[]{:S(2)}, u32[]{:S(2)}) collective-permute-start(bf16[4,32,8,256]{3,2,1,0:T(8,128)(2,1)S(1)} %pad_maximum_fusion), channel_id=1, source_target_pairs={{0,1},{1,0},{2,3},{3,2},{4,5},{5,4},{6,7},{7,6},{8,9},{9,8},{10,11... | collective-permute-start | bytes 1572872 | tf_op jit(solution)/shard_map/ppermute | solution.py:74
  32.1 15.3 %collective-permute-start.10 = (bf16[4,8,32,256]{3,2,1,0:T(8,128)(2,1)S(1)}, bf16[4,8,32,256]{3,2,1,0:T(8,128)(2,1)S(1)}, u32[]{:S(2)}, u32[]{:S(2)}) collective-permute-start(bf16[4,8,32,256]{3,2,1,0:T(8,128)(2,1)S(1)} %get-tuple-element.66), channel_id=1, source_target_pairs={{0,7},{1,2},{2,1},{3,4},{4,3},{5,6},{6,5},{7,0},{8,15},{9,10},{10,... | collective-permute-start | bytes 1572872 | tf_op jit(solution)/shard_map/ppermute | solution.py:77
  34.5 12.9 %collective-permute-start.9 = (bf16[4,8,32,256]{3,2,1,0:T(8,128)(2,1)S(1)}, bf16[4,8,32,256]{3,2,1,0:T(8,128)(2,1)S(1)}, u32[]{:S(2)}, u32[]{:S(2)}) collective-permute-start(bf16[4,8,32,256]{3,2,1,0:T(8,128)(2,1)S(1)} %get-tuple-element.65), channel_id=1, source_target_pairs={{0,1},{1,0},{2,3},{3,2},{4,5},{5,4},{6,7},{7,6},{8,9},{9,8},{10,11... | collective-permute-start | bytes 1572872 | tf_op jit(solution)/shard_map/ppermute | solution.py:74
  40.9 10.3 %collective-permute-start.8 = (bf16[8,32,256]{2,1,0:T(8,128)(2,1)S(1)}, bf16[8,32,256]{2,1,0:T(8,128)(2,1)S(1)}, u32[]{:S(2)}, u32[]{:S(2)}) collective-permute-start(bf16[8,32,256]{2,1,0:T(8,128)(2,1)S(1)} %get-tuple-element.64), channel_id=1, source_target_pairs={{0,7},{1,2},{2,1},{3,4},{4,3},{5,6},{6,5},{7,0},{8,15},{9,10},{10,... | collective-permute-start | bytes 393224 | tf_op jit(solution)/shard_map/ppermute | solution.py:77
  47.6 6.4 %collective-permute-start.11 = (bf16[8,32,256]{2,1,0:T(8,128)(2,1)S(1)}, bf16[8,32,256]{2,1,0:T(8,128)(2,1)S(1)}, u32[]{:S(2)}, u32[]{:S(2)}) collective-permute-start(bf16[8,32,256]{2,1,0:T(8,128)(2,1)S(1)} %get-tuple-element.69), channel_id=1, source_target_pairs={{0,8},{8,0},{16,24},{24,16},{1,9},{9,1},{17,25},{25,17},{2,10},{10... | collective-permute-start | bytes 393224 | tf_op jit(solution)/shard_map/ppermute | solution.py:82
  49.4 7.2 %collective-permute-start.12 = (bf16[8,32,256]{2,1,0:T(8,128)(2,1)S(1)}, bf16[8,32,256]{2,1,0:T(8,128)(2,1)S(1)}, u32[]{:S(2)}, u32[]{:S(2)}) collective-permute-start(bf16[8,32,256]{2,1,0:T(8,128)(2,1)S(1)} %get-tuple-element.70), channel_id=1, source_target_pairs={{0,16},{8,24},{16,0},{24,8},{1,17},{9,25},{17,1},{25,9},{2,18},{10... | collective-permute-start | bytes 393224 | tf_op jit(solution)/shard_map/ppermute | solution.py:82
  49.7 6.9 %collective-permute-start.13 = (bf16[8,32,256]{2,1,0:T(8,128)(2,1)S(1)}, bf16[8,32,256]{2,1,0:T(8,128)(2,1)S(1)}, u32[]{:S(2)}, u32[]{:S(2)}) collective-permute-start(bf16[8,32,256]{2,1,0:T(8,128)(2,1)S(1)} %get-tuple-element.71), channel_id=1, source_target_pairs={{0,24},{8,16},{16,8},{24,0},{1,25},{9,17},{17,9},{25,1},{2,26},{10... | collective-permute-start | bytes 393224 | tf_op jit(solution)/shard_map/ppermute | solution.py:82
  51.2 39.0 %copy-start.3 = (f32[32,192]{1,0:T(8,128)S(1)}, f32[32,192]{1,0:T(8,128)}, u32[]{:S(2)}) copy-start(f32[32,192]{1,0:T(8,128)} %get-tuple-element.89.refs_10_) | copy-start | bytes 73732
  51.2 39.0 %copy-start.4 = (s32[1,1,2048,1]{2,3,1,0:T(1,128)S(1)}, s32[1,1,2048,1]{2,3,1,0:T(1,128)}, u32[]{:S(2)}) copy-start(s32[1,1,2048,1]{2,3,1,0:T(1,128)} %param.12) | copy-start | bytes 24580
  51.2 39.0 %copy-start.5 = (s32[1,2048]{1,0:T(1,128)S(1)}, s32[1,2048]{1,0:T(1,128)}, u32[]{:S(2)}) copy-start(s32[1,2048]{1,0:T(1,128)} %get-tuple-element.88.refs_9_) | copy-start | bytes 24580
  56.6 9.6 %collective-permute-start.14 = (bf16[2,8,32,256]{3,2,1,0:T(8,128)(2,1)S(1)}, bf16[2,8,32,256]{3,2,1,0:T(8,128)(2,1)S(1)}, u32[]{:S(2)}, u32[]{:S(2)}) collective-permute-start(bf16[2,8,32,256]{3,2,1,0:T(8,128)(2,1)S(1)} %pad_maximum_fusion.3.refs_0_), channel_id=1, source_target_pairs={{0,8},{8,0},{16,24},{24,16},{1,9},{9,1},{17,25},{25,17},{2,10},{10... | collective-permute-start | bytes 786440 | tf_op jit(solution)/shard_map/ppermute | solution.py:82
  57.4 11.6 %collective-permute-start.15 = (bf16[2,8,32,256]{3,2,1,0:T(8,128)(2,1)S(1)}, bf16[2,8,32,256]{3,2,1,0:T(8,128)(2,1)S(1)}, u32[]{:S(2)}, u32[]{:S(2)}) collective-permute-start(bf16[2,8,32,256]{3,2,1,0:T(8,128)(2,1)S(1)} %pad_maximum_fusion.3.refs_0_), channel_id=1, source_target_pairs={{0,16},{8,24},{16,0},{24,8},{1,17},{9,25},{17,1},{25,9},{2,18},{10... | collective-permute-start | bytes 786440 | tf_op jit(solution)/shard_map/ppermute | solution.py:82
  58.5 10.5 %collective-permute-start.16 = (bf16[2,8,32,256]{3,2,1,0:T(8,128)(2,1)S(1)}, bf16[2,8,32,256]{3,2,1,0:T(8,128)(2,1)S(1)}, u32[]{:S(2)}, u32[]{:S(2)}) collective-permute-start(bf16[2,8,32,256]{3,2,1,0:T(8,128)(2,1)S(1)} %pad_maximum_fusion.3.refs_0_), channel_id=1, source_target_pairs={{0,24},{8,16},{16,8},{24,0},{1,25},{9,17},{17,9},{25,1},{2,26},{10... | collective-permute-start | bytes 786440 | tf_op jit(solution)/shard_map/ppermute | solution.py:82
  64.6 4.7 %collective-permute-start.18 = (bf16[4,8,32,256]{3,2,1,0:T(8,128)(2,1)S(1)}, bf16[4,8,32,256]{3,2,1,0:T(8,128)(2,1)S(1)}, u32[]{:S(2)}, u32[]{:S(2)}) collective-permute-start(bf16[4,8,32,256]{3,2,1,0:T(8,128)(2,1)S(1)} %get-tuple-element.79), channel_id=1, source_target_pairs={{0,1},{1,0},{2,3},{3,2},{4,5},{5,4},{6,7},{7,6},{8,9},{9,8},{10,11... | collective-permute-start | bytes 1572872 | tf_op jit(solution)/shard_map/ppermute | solution.py:74
  64.6 15.6 %collective-permute-start.19 = (bf16[4,8,32,256]{3,2,1,0:T(8,128)(2,1)S(1)}, bf16[4,8,32,256]{3,2,1,0:T(8,128)(2,1)S(1)}, u32[]{:S(2)}, u32[]{:S(2)}) collective-permute-start(bf16[4,8,32,256]{3,2,1,0:T(8,128)(2,1)S(1)} %get-tuple-element.80), channel_id=1, source_target_pairs={{0,7},{1,2},{2,1},{3,4},{4,3},{5,6},{6,5},{7,0},{8,15},{9,10},{10,... | collective-permute-start | bytes 1572872 | tf_op jit(solution)/shard_map/ppermute | solution.py:77
  69.2 14.8 %collective-permute-start.17 = (bf16[4,8,32,256]{3,2,1,0:T(8,128)(2,1)S(1)}, bf16[4,8,32,256]{3,2,1,0:T(8,128)(2,1)S(1)}, u32[]{:S(2)}, u32[]{:S(2)}) collective-permute-start(bf16[4,8,32,256]{3,2,1,0:T(8,128)(2,1)S(1)} %pad_maximum_fusion.1), channel_id=1, source_target_pairs={{0,1},{1,0},{2,3},{3,2},{4,5},{5,4},{6,7},{7,6},{8,9},{9,8},{10,11... | collective-permute-start | bytes 1572872 | tf_op jit(solution)/shard_map/ppermute | solution.py:74
  80.4 9.8 %collective-permute-start.20 = (bf16[8,32,256]{2,1,0:T(8,128)(2,1)S(1)}, bf16[8,32,256]{2,1,0:T(8,128)(2,1)S(1)}, u32[]{:S(2)}, u32[]{:S(2)}) collective-permute-start(bf16[8,32,256]{2,1,0:T(8,128)(2,1)S(1)} %get-tuple-element.82), channel_id=1, source_target_pairs={{0,8},{8,0},{16,24},{24,16},{1,9},{9,1},{17,25},{25,17},{2,10},{10... | collective-permute-start | bytes 393224 | tf_op jit(solution)/shard_map/ppermute | solution.py:82
  81.8 8.4 %collective-permute-start.21 = (bf16[8,32,256]{2,1,0:T(8,128)(2,1)S(1)}, bf16[8,32,256]{2,1,0:T(8,128)(2,1)S(1)}, u32[]{:S(2)}, u32[]{:S(2)}) collective-permute-start(bf16[8,32,256]{2,1,0:T(8,128)(2,1)S(1)} %get-tuple-element.83), channel_id=1, source_target_pairs={{0,16},{8,24},{16,0},{24,8},{1,17},{9,25},{17,1},{25,9},{2,18},{10... | collective-permute-start | bytes 393224 | tf_op jit(solution)/shard_map/ppermute | solution.py:82
  82.4 7.8 %collective-permute-start.22 = (bf16[8,32,256]{2,1,0:T(8,128)(2,1)S(1)}, bf16[8,32,256]{2,1,0:T(8,128)(2,1)S(1)}, u32[]{:S(2)}, u32[]{:S(2)}) collective-permute-start(bf16[8,32,256]{2,1,0:T(8,128)(2,1)S(1)} %get-tuple-element.84), channel_id=1, source_target_pairs={{0,24},{8,16},{16,8},{24,0},{1,25},{9,17},{17,9},{25,1},{2,26},{10... | collective-permute-start | bytes 393224 | tf_op jit(solution)/shard_map/ppermute | solution.py:82
  94.8 17.6 %all-to-all-start = ((s16[32,56,128]{2,1,0:T(8,128)(2,1)}), s16[32,56,128]{2,1,0:T(8,128)(2,1)S(1)}, u32[]{:S(2)}, u32[]{:S(2)}) async-start(s16[32,56,128]{2,1,0:T(8,128)(2,1)} %shard_map.94), calls=%async_computation | async-start | bytes 917504 | tf_op jit(solution)/shard_map/all_to_all | solution.py:533

commit v6 on v5

--- a/solution.py
+++ b/solution.py
@@ -12,6 +12,18 @@
 MIB = 1 << 20
 VMEM = pl.BlockSpec(memory_space=pltpu.VMEM)
 TOP = 32767.0
+RANGES = ((0.099, 0.901), (0.199, 2.001), (0.499, 1.501))
+
+
+def coded(value, a):
+    low, high = RANGES[a]
+    scaled = (value - low) * (65535.0 / (high - low)) - 32768.0
+    return jnp.round(jnp.clip(scaled, -32768.0, 32767.0)).astype(jnp.int32).astype(jnp.int16)
+
+
+def decoded(code, a):
+    low, high = RANGES[a]
+    return (code.astype(F32) + 32768.0) * ((high - low) / 65535.0) + low
 
 
 def shape(dims, dtype):
@@ -104,7 +116,7 @@
         for d in range(split):
             cut = pl.ds(pl.multiple_of((band ^ d) * rows, rows), rows)
             for a, ref in enumerate((e_ref, b_ref, w_ref)):
-                piece_refs[d][a] = ref[:, cut]
+                piece_refs[d][a] = coded(ref[:, cut], a)
 
     piece = (3, part_bands, rows)
     start_shape = (per_group, part_bands, width)
@@ -114,7 +126,7 @@
         0,
         [pl.BlockSpec(memory_space=pltpu.HBM)] * 3,
         [(whole(start_shape), shape(start_shape, BF16))]
-        + [(whole(piece), shape(piece, F32))] * split,
+        + [(whole(piece), shape(piece, jnp.int16))] * split,
         (emissivity, blackbody, loss_weights),
         [pltpu.VMEM(emissivity.shape, F32)] * 3 + [pltpu.SemaphoreType.DMA((3,))],
         limit=60 * MIB,
@@ -164,7 +176,8 @@
             at = pl.ds(pl.multiple_of((b ^ d) * part_bands, part_bands), part_bands)
             for a in range(3):
                 for q in range(once):
-                    full_ref[a, q, at, :] = piece_refs[d][a, :, q * width : (q + 1) * width]
+                    code = piece_refs[d][a, :, q * width : (q + 1) * width]
+                    full_ref[a, q, at, :] = decoded(code, a)
 
         def value_of(q):
             return ((1.0 - full_ref[0, q]) * full_ref[2, q]).astype(BF16)
@@ -331,7 +344,7 @@
         limit=40 * MIB,
     )
 
-    owners_once = 16
+    owners_once = 32
 
     def pack_rows(*refs):
         got_refs = refs[:split]
@@ -395,7 +408,7 @@
 
             lax.fori_loop(0, devices // owners_once, step, 0)
 
-    sources_once = 16
+    sources_once = 32
     tops = surfaces // LANES
     lot = sources_once * LANES * (2 if tail else 1)
     top_rows = 2 * bands + 16

time: 117 us -> 115 us (0.983)
  waiting for transfers between devices: 43.4 us -> 41.3 us
  starting transfers between devices: 30.1 us -> 31.4 us
    ppermute x4, starting transfers between devices: 8.57 us -> 10.8 us  [outer(): lax.ppermute(block, 'patch', [(i, (i + (1 if i % 2 else -1)) % groups) fo...]
    ppermute x15, waiting for transfers between devices: 13.9 us -> 12 us  [across(): return lax.ppermute(block, 'band', [(i, i ^ d) for i in range(split)])]
  transfers between devices with their start and end apart: 24 -> 24, of which waited for: 8 -> 7; matrix products, arithmetic and copies ran while one was open for 1% -> 1% of each run, Pallas kernels for 25% -> 26%
where the time goes in v6:
time: 115 us
  waiting for transfers between devices  41.3 us (36%)
  Pallas kernels  39.1 us (34%)
  starting transfers between devices  31.4 us (27%)
  local copies, waits for them, and re-layouts  1.76 us (2%)
    pallas_call x10, Pallas kernels, kernel_call(): pl.pallas_call(kernel, out_shape=[o for _, o in outs], grid_spec=pltpu.Pr...  39.1 us
    ppermute x15, starting transfers between devices, across(): return lax.ppermute(block, 'band', [(i, i ^ d) for i in range(split)])  17.6 us
    ppermute x4, waiting for transfers between devices, outer(): lax.ppermute(block, 'patch', [(i, (i + (1 if i % 2 else -1)) % groups) fo...  15.5 us
    all_to_all x1, waiting for transfers between devices, body(): send = lax.all_to_all(send, ('band', 'patch'), 0, 0, tiled=True)  13.8 us
    ppermute x15, waiting for transfers between devices, across(): return lax.ppermute(block, 'band', [(i, i ^ d) for i in range(split)])  12 us
    ppermute x4, starting transfers between devices, outer(): lax.ppermute(block, 'patch', [(i, (i + (1 if i % 2 else -1)) % groups) fo...  10.8 us
    all_to_all x1, starting transfers between devices, body(): send = lax.all_to_all(send, ('band', 'patch'), 0, 0, tiled=True)  2.78 us
  transfers between devices with their start and end apart: 24, of which 7 were waited for; matrix products, arithmetic and copies ran while one was open for 1% of the time, Pallas kernels for 26%

profile of v6, /device:TPU:0, one launch (start us, length us, event | category | flops | bytes accessed | tf_op | source)
XLA Modules:
  0.0 114.7 jit_solution(5867386691095592872)
XLA Ops:
  0.6 2.0 %shard_map.87 = (bf16[32,8,256]{2,1,0:T(8,128)(2,1)}, s16[3,8,2048]{2,1,0:T(8,128)(2,1)}, s16[3,8,2048]{2,1,0:T(8,128)(2,1)}, s16[3,8,2048]{2,1,0:T(8,128)(2,1)}, s16[3,8,2048]{2,1,0:T(8,128)(2,1)}) custom-call(f32[8,8192]{1,0:T(8,128)} %e_hbm.1, f32[8,8192]{1,0:T(8,128)} %b_hbm.1, f32[8,8192]{1,0:T(8,128)} %w_hbm.1), custom_call_target="tpu_custom_call" | custom-call | tf_op jit(solution)/shard_map/pallas_call | solution.py:54
  2.6 0.0 copy-start.6
  2.6 0.0 copy-start
  2.7 4.6 %collective-permute-start = (bf16[32,8,256]{2,1,0:T(8,128)(2,1)}, bf16[32,8,256]{2,1,0:T(8,128)(2,1)S(1)}, u32[]{:S(2)}, u32[]{:S(2)}) collective-permute-start(bf16[32,8,256]{2,1,0:T(8,128)(2,1)} %get-tuple-element.54), channel_id=1, source_target_pairs={{0,7},{1,2},{2,1},{3,4},{4,3},{5,6},{6,5},{7,0},{8,15},{9,10},{10,... | collective-permute-start | bytes 393224 | tf_op jit(solution)/shard_map/ppermute | solution.py:89
  7.2 1.5 %collective-permute-start.1 = (s16[3,8,2048]{2,1,0:T(8,128)(2,1)}, s16[3,8,2048]{2,1,0:T(8,128)(2,1)S(1)}, u32[]{:S(2)}, u32[]{:S(2)}) collective-permute-start(s16[3,8,2048]{2,1,0:T(8,128)(2,1)} %get-tuple-element.51), channel_id=1, source_target_pairs={{0,8},{8,0},{16,24},{24,16},{1,9},{9,1},{17,25},{25,17},{2,10},{10... | collective-permute-start | bytes 294920 | tf_op jit(solution)/shard_map/ppermute | solution.py:94
  8.7 1.5 %collective-permute-start.2 = (s16[3,8,2048]{2,1,0:T(8,128)(2,1)}, s16[3,8,2048]{2,1,0:T(8,128)(2,1)S(1)}, u32[]{:S(2)}, u32[]{:S(2)}) collective-permute-start(s16[3,8,2048]{2,1,0:T(8,128)(2,1)} %get-tuple-element.52), channel_id=1, source_target_pairs={{0,16},{8,24},{16,0},{24,8},{1,17},{9,25},{17,1},{25,9},{2,18},{10... | collective-permute-start | bytes 294920 | tf_op jit(solution)/shard_map/ppermute | solution.py:94
  10.2 0.5 collective-permute-start.3
  10.7 7.3 %shard_map.86 = (bf16[8,16,256,256]{3,2,1,0:T(8,128)(2,1)S(1)}, s32[8,16]{1,0:T(8,128)}, s32[1,2048]{1,0:T(1,128)}, f32[32,192]{1,0:T(8,128)}) custom-call(bf16[8,16,256,256]{3,2,1,0:T(8,128)(2,1)} %bitcast.13, s32[8,16]{1,0:T(8,128)} %bitcast.18, s32[1,2048]{1,0:T(1,128)} %bitcast.11, s32[1,2048]{1,0:T(1,128)} %bitcast.17), custom_call_target="tpu_custom_call" | custom-call | tf_op jit(solution)/shard_map/pallas_call | solution.py:54
  18.0 0.0 collective-permute-done.1.refs_1_
  18.1 1.6 %collective-permute-start.4 = (bf16[2,32,8,256]{3,2,1,0:T(8,128)(2,1)S(1)}, bf16[2,32,8,256]{3,2,1,0:T(8,128)(2,1)S(1)}, u32[]{:S(2)}, u32[]{:S(2)}) collective-permute-start(bf16[2,32,8,256]{3,2,1,0:T(8,128)(2,1)S(1)} %pad_maximum_fusion.2.refs_0_), channel_id=1, source_target_pairs={{0,8},{8,0},{16,24},{24,16},{1,9},{9,1},{17,25},{25,17},{2,10},{10... | collective-permute-start | bytes 786440 | tf_op jit(solution)/shard_map/ppermute | solution.py:94
  19.6 1.5 %collective-permute-start.5 = (bf16[2,32,8,256]{3,2,1,0:T(8,128)(2,1)S(1)}, bf16[2,32,8,256]{3,2,1,0:T(8,128)(2,1)S(1)}, u32[]{:S(2)}, u32[]{:S(2)}) collective-permute-start(bf16[2,32,8,256]{3,2,1,0:T(8,128)(2,1)S(1)} %pad_maximum_fusion.2.refs_0_), channel_id=1, source_target_pairs={{0,16},{8,24},{16,0},{24,8},{1,17},{9,25},{17,1},{25,9},{2,18},{10... | collective-permute-start | bytes 786440 | tf_op jit(solution)/shard_map/ppermute | solution.py:94
  21.1 0.5 collective-permute-start.6
  21.6 0.7 copy-done.1
  22.3 4.7 %shard_map.88 = (f32[3,8,32,256]{3,2,1,0:T(8,128)S(1)}, f32[4,8,32,256]{3,2,1,0:T(8,128)S(1)}, bf16[4,8,32,256]{3,2,1,0:T(8,128)(2,1)S(1)}, bf16[4,8,32,256]{3,2,1,0:T(8,128)(2,1)S(1)}) custom-call(s32[8,16]{1,0:T(8,128)S(1)} %copy-done.1, bf16[8,16,256,256]{3,2,1,0:T(8,128)(2,1)S(1)} %get-tuple-element.57.m_ref, s16[3,8,2048]{2,1,0:T(8,128)(2,1)S(1)} %copy-done, ...), custom_call_target="tpu_custom_call" | custom-call | flops 536870912 | bytes 16777216 | tf_op jit(solution)/shard_map/pallas_call | solution.py:54
  27.0 4.0 %collective-permute-done.5.refs_2_ = bf16[2,32,8,256]{3,2,1,0:T(8,128)(2,1)S(1)} collective-permute-done((bf16[2,32,8,256]{3,2,1,0:T(8,128)(2,1)S(1)}, bf16[2,32,8,256]{3,2,1,0:T(8,128)(2,1)S(1)}, u32[]{:S(2)}, u32[]{:S(2)}) %collective-permute-start.5) | collective-permute-done | bytes 262176 | tf_op jit(solution)/shard_map/ppermute | solution.py:94
  31.1 0.1 pad_maximum_fusion
  31.1 0.1 collective-permute-start.7
  31.2 2.3 %collective-permute-start.10 = (bf16[4,8,32,256]{3,2,1,0:T(8,128)(2,1)S(1)}, bf16[4,8,32,256]{3,2,1,0:T(8,128)(2,1)S(1)}, u32[]{:S(2)}, u32[]{:S(2)}) collective-permute-start(bf16[4,8,32,256]{3,2,1,0:T(8,128)(2,1)S(1)} %get-tuple-element.66), channel_id=1, source_target_pairs={{0,7},{1,2},{2,1},{3,4},{4,3},{5,6},{6,5},{7,0},{8,15},{9,10},{10,... | collective-permute-start | bytes 1572872 | tf_op jit(solution)/shard_map/ppermute | solution.py:89
  33.6 6.4 %shard_map.89 = (f32[8,32,256]{2,1,0:T(8,128)S(1)}, bf16[8,32,256]{2,1,0:T(8,128)(2,1)S(1)}) custom-call(s32[8,16]{1,0:T(8,128)S(1)} %copy-done.2, bf16[8,16,256,256]{3,2,1,0:T(8,128)(2,1)S(1)} %get-tuple-element.57.m_ref, bf16[2,32,8,256]{3,2,1,0:T(8,128)(2,1)S(1)} %pad_maximum_fusion.2.refs_0_, bf16[2,32,8,256]{3,2,1,0:T(8,128)(2,1)S(1)} %collective-permute-done.4.refs_1_, ...), custom_call_target="tpu_custom_call" | custom-call | flops 536870912 | bytes 16777216 | tf_op jit(solution)/shard_map/pallas_call | solution.py:54
  40.0 2.0 %collective-permute-start.8 = (bf16[8,32,256]{2,1,0:T(8,128)(2,1)S(1)}, bf16[8,32,256]{2,1,0:T(8,128)(2,1)S(1)}, u32[]{:S(2)}, u32[]{:S(2)}) collective-permute-start(bf16[8,32,256]{2,1,0:T(8,128)(2,1)S(1)} %get-tuple-element.64), channel_id=1, source_target_pairs={{0,7},{1,2},{2,1},{3,4},{4,3},{5,6},{6,5},{7,0},{8,15},{9,10},{10,... | collective-permute-start | bytes 393224 | tf_op jit(solution)/shard_map/ppermute | solution.py:89
  41.9 4.6 %collective-permute-done.10.far_ref = bf16[4,8,32,256]{3,2,1,0:T(8,128)(2,1)S(1)} collective-permute-done((bf16[4,8,32,256]{3,2,1,0:T(8,128)(2,1)S(1)}, bf16[4,8,32,256]{3,2,1,0:T(8,128)(2,1)S(1)}, u32[]{:S(2)}, u32[]{:S(2)}) %collective-permute-start.10) | collective-permute-done | bytes 524320 | tf_op jit(solution)/shard_map/ppermute | solution.py:89
  46.5 0.2 shard_map.90
  46.7 1.3 %collective-permute-start.11 = (bf16[8,32,256]{2,1,0:T(8,128)(2,1)S(1)}, bf16[8,32,256]{2,1,0:T(8,128)(2,1)S(1)}, u32[]{:S(2)}, u32[]{:S(2)}) collective-permute-start(bf16[8,32,256]{2,1,0:T(8,128)(2,1)S(1)} %get-tuple-element.69), channel_id=1, source_target_pairs={{0,8},{8,0},{16,24},{24,16},{1,9},{9,1},{17,25},{25,17},{2,10},{10... | collective-permute-start | bytes 393224 | tf_op jit(solution)/shard_map/ppermute | solution.py:94
  48.0 0.8 collective-permute-start.12
  48.8 1.4 %collective-permute-start.13 = (bf16[8,32,256]{2,1,0:T(8,128)(2,1)S(1)}, bf16[8,32,256]{2,1,0:T(8,128)(2,1)S(1)}, u32[]{:S(2)}, u32[]{:S(2)}) collective-permute-start(bf16[8,32,256]{2,1,0:T(8,128)(2,1)S(1)} %get-tuple-element.71), channel_id=1, source_target_pairs={{0,24},{8,16},{16,8},{24,0},{1,25},{9,17},{17,9},{25,1},{2,26},{10... | collective-permute-start | bytes 393224 | tf_op jit(solution)/shard_map/ppermute | solution.py:94
  50.3 0.0 copy-start.4
  50.3 2.4 %collective-permute-done.11.refs_1_ = bf16[8,32,256]{2,1,0:T(8,128)(2,1)S(1)} collective-permute-done((bf16[8,32,256]{2,1,0:T(8,128)(2,1)S(1)}, bf16[8,32,256]{2,1,0:T(8,128)(2,1)S(1)}, u32[]{:S(2)}, u32[]{:S(2)}) %collective-permute-start.11) | collective-permute-done | bytes 131104 | tf_op jit(solution)/shard_map/ppermute | solution.py:94
  52.7 2.8 %collective-permute-done.12.refs_2_ = bf16[8,32,256]{2,1,0:T(8,128)(2,1)S(1)} collective-permute-done((bf16[8,32,256]{2,1,0:T(8,128)(2,1)S(1)}, bf16[8,32,256]{2,1,0:T(8,128)(2,1)S(1)}, u32[]{:S(2)}, u32[]{:S(2)}) %collective-permute-start.12) | collective-permute-done | bytes 131104 | tf_op jit(solution)/shard_map/ppermute | solution.py:94
  55.4 1.1 collective-permute-start.14
  56.6 1.1 collective-permute-start.15
  57.7 1.2 %collective-permute-start.16 = (bf16[2,8,32,256]{3,2,1,0:T(8,128)(2,1)S(1)}, bf16[2,8,32,256]{3,2,1,0:T(8,128)(2,1)S(1)}, u32[]{:S(2)}, u32[]{:S(2)}) collective-permute-start(bf16[2,8,32,256]{3,2,1,0:T(8,128)(2,1)S(1)} %pad_maximum_fusion.3.refs_0_), channel_id=1, source_target_pairs={{0,24},{8,16},{16,8},{24,0},{1,25},{9,17},{17,9},{25,1},{2,26},{10... | collective-permute-start | bytes 786440 | tf_op jit(solution)/shard_map/ppermute | solution.py:94
  58.9 4.5 %shard_map.91 = (f32[8,32,256]{2,1,0:T(8,128)S(1)}, f32[4,8,32,256]{3,2,1,0:T(8,128)S(1)}, bf16[4,8,32,256]{3,2,1,0:T(8,128)(2,1)S(1)}, bf16[4,8,32,256]{3,2,1,0:T(8,128)(2,1)S(1)}) custom-call(s32[8,16]{1,0:T(8,128)S(1)} %copy-done.2, bf16[8,16,256,256]{3,2,1,0:T(8,128)(2,1)S(1)} %get-tuple-element.57.m_ref, f32[8,32,256]{2,1,0:T(8,128)S(1)} %get-tuple-element.68.refs_0_, ...), custom_call_target="tpu_custom_call" | custom-call | flops 536870912 | bytes 16777216 | tf_op jit(solution)/shard_map/pallas_call | solution.py:54
  63.4 0.1 collective-permute-start.18
  63.5 1.9 %collective-permute-start.19 = (bf16[4,8,32,256]{3,2,1,0:T(8,128)(2,1)S(1)}, bf16[4,8,32,256]{3,2,1,0:T(8,128)(2,1)S(1)}, u32[]{:S(2)}, u32[]{:S(2)}) collective-permute-start(bf16[4,8,32,256]{3,2,1,0:T(8,128)(2,1)S(1)} %get-tuple-element.80), channel_id=1, source_target_pairs={{0,7},{1,2},{2,1},{3,4},{4,3},{5,6},{6,5},{7,0},{8,15},{9,10},{10,... | collective-permute-start | bytes 1572872 | tf_op jit(solution)/shard_map/ppermute | solution.py:89
  65.4 2.9 %collective-permute-done.15.refs_2_ = bf16[2,8,32,256]{3,2,1,0:T(8,128)(2,1)S(1)} collective-permute-done((bf16[2,8,32,256]{3,2,1,0:T(8,128)(2,1)S(1)}, bf16[2,8,32,256]{3,2,1,0:T(8,128)(2,1)S(1)}, u32[]{:S(2)}, u32[]{:S(2)}) %collective-permute-start.15) | collective-permute-done | bytes 262176 | tf_op jit(solution)/shard_map/ppermute | solution.py:94
  68.3 0.1 pad_maximum_fusion.1
  68.4 0.1 collective-permute-start.17
  68.5 10.9 %collective-permute-done.19.far_ref = bf16[4,8,32,256]{3,2,1,0:T(8,128)(2,1)S(1)} collective-permute-done((bf16[4,8,32,256]{3,2,1,0:T(8,128)(2,1)S(1)}, bf16[4,8,32,256]{3,2,1,0:T(8,128)(2,1)S(1)}, u32[]{:S(2)}, u32[]{:S(2)}) %collective-permute-start.19) | collective-permute-done | bytes 524320 | tf_op jit(solution)/shard_map/ppermute | solution.py:89
  79.4 0.2 shard_map.93
  79.6 1.3 %collective-permute-start.20 = (bf16[8,32,256]{2,1,0:T(8,128)(2,1)S(1)}, bf16[8,32,256]{2,1,0:T(8,128)(2,1)S(1)}, u32[]{:S(2)}, u32[]{:S(2)}) collective-permute-start(bf16[8,32,256]{2,1,0:T(8,128)(2,1)S(1)} %get-tuple-element.82), channel_id=1, source_target_pairs={{0,8},{8,0},{16,24},{24,16},{1,9},{9,1},{17,25},{25,17},{2,10},{10... | collective-permute-start | bytes 393224 | tf_op jit(solution)/shard_map/ppermute | solution.py:94
  80.9 0.9 collective-permute-start.21
  81.7 1.4 %collective-permute-start.22 = (bf16[8,32,256]{2,1,0:T(8,128)(2,1)S(1)}, bf16[8,32,256]{2,1,0:T(8,128)(2,1)S(1)}, u32[]{:S(2)}, u32[]{:S(2)}) collective-permute-start(bf16[8,32,256]{2,1,0:T(8,128)(2,1)S(1)} %get-tuple-element.84), channel_id=1, source_target_pairs={{0,24},{8,16},{16,8},{24,0},{1,25},{9,17},{17,9},{25,1},{2,26},{10... | collective-permute-start | bytes 393224 | tf_op jit(solution)/shard_map/ppermute | solution.py:94
  83.2 6.2 %shard_map.92 = (f32[8,32,256]{2,1,0:T(8,128)S(1)}, f32[32,2048]{1,0:T(8,128)S(1)}) custom-call(s32[8,16]{1,0:T(8,128)S(1)} %copy-done.2, bf16[8,16,256,256]{3,2,1,0:T(8,128)(2,1)S(1)} %get-tuple-element.57.m_ref, bf16[2,8,32,256]{3,2,1,0:T(8,128)(2,1)S(1)} %pad_maximum_fusion.3.refs_0_, bf16[2,8,32,256]{3,2,1,0:T(8,128)(2,1)S(1)} %collective-permute-done.14.refs_1_, ...), custom_call_target="tpu_custom_call" | custom-call | flops 536870912 | bytes 16777216 | tf_op jit(solution)/shard_map/pallas_call | solution.py:54
  89.4 4.0 %shard_map.94 = s16[32,56,128]{2,1,0:T(8,128)(2,1)} custom-call(f32[8,32,256]{2,1,0:T(8,128)S(1)} %get-tuple-element.81.refs_0_, bf16[8,32,256]{2,1,0:T(8,128)(2,1)S(1)} %collective-permute-done.20.refs_1_, bf16[8,32,256]{2,1,0:T(8,128)(2,1)S(1)} %collective-permute-done.21.refs_2_, bf16[8,32,256]{2,1,0:T(8,128)(2,1)S(1)} %collective-permute-done.22.refs_3_, ...), custom_call_target="tpu_custom_call" | custom-call | tf_op jit(solution)/shard_map/pallas_call | solution.py:54
  93.4 2.8 %all-to-all-start = ((s16[32,56,128]{2,1,0:T(8,128)(2,1)}), s16[32,56,128]{2,1,0:T(8,128)(2,1)S(1)}, u32[]{:S(2)}, u32[]{:S(2)}) async-start(s16[32,56,128]{2,1,0:T(8,128)(2,1)} %shard_map.94), calls=%async_computation | async-start | bytes 917504 | tf_op jit(solution)/shard_map/all_to_all | solution.py:546
  96.2 1.0 copy.9
  97.2 13.8 %all-to-all-done.got_ref = s16[32,56,128]{2,1,0:T(8,128)(2,1)S(1)} async-done(((s16[32,56,128]{2,1,0:T(8,128)(2,1)}), s16[32,56,128]{2,1,0:T(8,128)(2,1)S(1)}, u32[]{:S(2)}, u32[]{:S(2)}) %all-to-all-start) | async-done | bytes 458784 | tf_op jit(solution)/shard_map/all_to_all | solution.py:546
  110.9 3.8 %shard_map.95 = f32[32,1024]{1,0:T(8,128)} custom-call(s16[32,56,128]{2,1,0:T(8,128)(2,1)S(1)} %all-to-all-done.got_ref), custom_call_target="tpu_custom_call" | custom-call | tf_op jit(solution)/shard_map/pallas_call | solution.py:54
  (37 shorter events, 0.2 us)
Async XLA Ops:
  2.6 15.4 %copy-start.6 = (bf16[32,8,256]{2,1,0:T(8,128)(2,1)S(1)}, bf16[32,8,256]{2,1,0:T(8,128)(2,1)}, u32[]{:S(2)}) copy-start(bf16[32,8,256]{2,1,0:T(8,128)(2,1)} %get-tuple-element.54) | copy-start | bytes 393220
  2.6 19.0 %copy-start = (s16[3,8,2048]{2,1,0:T(8,128)(2,1)S(1)}, s16[3,8,2048]{2,1,0:T(8,128)(2,1)}, u32[]{:S(2)}) copy-start(s16[3,8,2048]{2,1,0:T(8,128)(2,1)} %get-tuple-element.50.refs_0_) | copy-start | bytes 294916
  2.7 15.4 %collective-permute-start = (bf16[32,8,256]{2,1,0:T(8,128)(2,1)}, bf16[32,8,256]{2,1,0:T(8,128)(2,1)S(1)}, u32[]{:S(2)}, u32[]{:S(2)}) collective-permute-start(bf16[32,8,256]{2,1,0:T(8,128)(2,1)} %get-tuple-element.54), channel_id=1, source_target_pairs={{0,7},{1,2},{2,1},{3,4},{4,3},{5,6},{6,5},{7,0},{8,15},{9,10},{10,... | collective-permute-start | bytes 393224 | tf_op jit(solution)/shard_map/ppermute | solution.py:89
  7.2 10.8 %collective-permute-start.1 = (s16[3,8,2048]{2,1,0:T(8,128)(2,1)}, s16[3,8,2048]{2,1,0:T(8,128)(2,1)S(1)}, u32[]{:S(2)}, u32[]{:S(2)}) collective-permute-start(s16[3,8,2048]{2,1,0:T(8,128)(2,1)} %get-tuple-element.51), channel_id=1, source_target_pairs={{0,8},{8,0},{16,24},{24,16},{1,9},{9,1},{17,25},{25,17},{2,10},{10... | collective-permute-start | bytes 294920 | tf_op jit(solution)/shard_map/ppermute | solution.py:94
  8.7 9.3 %collective-permute-start.2 = (s16[3,8,2048]{2,1,0:T(8,128)(2,1)}, s16[3,8,2048]{2,1,0:T(8,128)(2,1)S(1)}, u32[]{:S(2)}, u32[]{:S(2)}) collective-permute-start(s16[3,8,2048]{2,1,0:T(8,128)(2,1)} %get-tuple-element.52), channel_id=1, source_target_pairs={{0,16},{8,24},{16,0},{24,8},{1,17},{9,25},{17,1},{25,9},{2,18},{10... | collective-permute-start | bytes 294920 | tf_op jit(solution)/shard_map/ppermute | solution.py:94
  10.2 7.8 %collective-permute-start.3 = (s16[3,8,2048]{2,1,0:T(8,128)(2,1)}, s16[3,8,2048]{2,1,0:T(8,128)(2,1)S(1)}, u32[]{:S(2)}, u32[]{:S(2)}) collective-permute-start(s16[3,8,2048]{2,1,0:T(8,128)(2,1)} %get-tuple-element.53), channel_id=1, source_target_pairs={{0,24},{8,16},{16,8},{24,0},{1,25},{9,17},{17,9},{25,1},{2,26},{10... | collective-permute-start | bytes 294920 | tf_op jit(solution)/shard_map/ppermute | solution.py:94
  18.0 15.6 %copy-start.2 = (s32[8,16]{1,0:T(8,128)S(1)}, s32[8,16]{1,0:T(8,128)}, u32[]{:S(2)}) copy-start(s32[8,16]{1,0:T(8,128)} %get-tuple-element.56.slots_ref) | copy-start | bytes 1540
  18.1 8.9 %collective-permute-start.4 = (bf16[2,32,8,256]{3,2,1,0:T(8,128)(2,1)S(1)}, bf16[2,32,8,256]{3,2,1,0:T(8,128)(2,1)S(1)}, u32[]{:S(2)}, u32[]{:S(2)}) collective-permute-start(bf16[2,32,8,256]{3,2,1,0:T(8,128)(2,1)S(1)} %pad_maximum_fusion.2.refs_0_), channel_id=1, source_target_pairs={{0,8},{8,0},{16,24},{24,16},{1,9},{9,1},{17,25},{25,17},{2,10},{10... | collective-permute-start | bytes 786440 | tf_op jit(solution)/shard_map/ppermute | solution.py:94
  19.6 11.4 %collective-permute-start.5 = (bf16[2,32,8,256]{3,2,1,0:T(8,128)(2,1)S(1)}, bf16[2,32,8,256]{3,2,1,0:T(8,128)(2,1)S(1)}, u32[]{:S(2)}, u32[]{:S(2)}) collective-permute-start(bf16[2,32,8,256]{3,2,1,0:T(8,128)(2,1)S(1)} %pad_maximum_fusion.2.refs_0_), channel_id=1, source_target_pairs={{0,16},{8,24},{16,0},{24,8},{1,17},{9,25},{17,1},{25,9},{2,18},{10... | collective-permute-start | bytes 786440 | tf_op jit(solution)/shard_map/ppermute | solution.py:94
  21.1 9.8 %collective-permute-start.6 = (bf16[2,32,8,256]{3,2,1,0:T(8,128)(2,1)S(1)}, bf16[2,32,8,256]{3,2,1,0:T(8,128)(2,1)S(1)}, u32[]{:S(2)}, u32[]{:S(2)}) collective-permute-start(bf16[2,32,8,256]{3,2,1,0:T(8,128)(2,1)S(1)} %pad_maximum_fusion.2.refs_0_), channel_id=1, source_target_pairs={{0,24},{8,16},{16,8},{24,0},{1,25},{9,17},{17,9},{25,1},{2,26},{10... | collective-permute-start | bytes 786440 | tf_op jit(solution)/shard_map/ppermute | solution.py:94
  21.6 0.7 copy-start.1
  31.1 2.4 %collective-permute-start.7 = (bf16[4,32,8,256]{3,2,1,0:T(8,128)(2,1)S(1)}, bf16[4,32,8,256]{3,2,1,0:T(8,128)(2,1)S(1)}, u32[]{:S(2)}, u32[]{:S(2)}) collective-permute-start(bf16[4,32,8,256]{3,2,1,0:T(8,128)(2,1)S(1)} %pad_maximum_fusion), channel_id=1, source_target_pairs={{0,1},{1,0},{2,3},{3,2},{4,5},{5,4},{6,7},{7,6},{8,9},{9,8},{10,11... | collective-permute-start | bytes 1572872 | tf_op jit(solution)/shard_map/ppermute | solution.py:86
  31.2 15.3 %collective-permute-start.10 = (bf16[4,8,32,256]{3,2,1,0:T(8,128)(2,1)S(1)}, bf16[4,8,32,256]{3,2,1,0:T(8,128)(2,1)S(1)}, u32[]{:S(2)}, u32[]{:S(2)}) collective-permute-start(bf16[4,8,32,256]{3,2,1,0:T(8,128)(2,1)S(1)} %get-tuple-element.66), channel_id=1, source_target_pairs={{0,7},{1,2},{2,1},{3,4},{4,3},{5,6},{6,5},{7,0},{8,15},{9,10},{10,... | collective-permute-start | bytes 1572872 | tf_op jit(solution)/shard_map/ppermute | solution.py:89
  33.6 12.9 %collective-permute-start.9 = (bf16[4,8,32,256]{3,2,1,0:T(8,128)(2,1)S(1)}, bf16[4,8,32,256]{3,2,1,0:T(8,128)(2,1)S(1)}, u32[]{:S(2)}, u32[]{:S(2)}) collective-permute-start(bf16[4,8,32,256]{3,2,1,0:T(8,128)(2,1)S(1)} %get-tuple-element.65), channel_id=1, source_target_pairs={{0,1},{1,0},{2,3},{3,2},{4,5},{5,4},{6,7},{7,6},{8,9},{9,8},{10,11... | collective-permute-start | bytes 1572872 | tf_op jit(solution)/shard_map/ppermute | solution.py:86
  40.0 10.3 %collective-permute-start.8 = (bf16[8,32,256]{2,1,0:T(8,128)(2,1)S(1)}, bf16[8,32,256]{2,1,0:T(8,128)(2,1)S(1)}, u32[]{:S(2)}, u32[]{:S(2)}) collective-permute-start(bf16[8,32,256]{2,1,0:T(8,128)(2,1)S(1)} %get-tuple-element.64), channel_id=1, source_target_pairs={{0,7},{1,2},{2,1},{3,4},{4,3},{5,6},{6,5},{7,0},{8,15},{9,10},{10,... | collective-permute-start | bytes 393224 | tf_op jit(solution)/shard_map/ppermute | solution.py:89
  46.7 6.0 %collective-permute-start.11 = (bf16[8,32,256]{2,1,0:T(8,128)(2,1)S(1)}, bf16[8,32,256]{2,1,0:T(8,128)(2,1)S(1)}, u32[]{:S(2)}, u32[]{:S(2)}) collective-permute-start(bf16[8,32,256]{2,1,0:T(8,128)(2,1)S(1)} %get-tuple-element.69), channel_id=1, source_target_pairs={{0,8},{8,0},{16,24},{24,16},{1,9},{9,1},{17,25},{25,17},{2,10},{10... | collective-permute-start | bytes 393224 | tf_op jit(solution)/shard_map/ppermute | solution.py:94
  48.0 7.5 %collective-permute-start.12 = (bf16[8,32,256]{2,1,0:T(8,128)(2,1)S(1)}, bf16[8,32,256]{2,1,0:T(8,128)(2,1)S(1)}, u32[]{:S(2)}, u32[]{:S(2)}) collective-permute-start(bf16[8,32,256]{2,1,0:T(8,128)(2,1)S(1)} %get-tuple-element.70), channel_id=1, source_target_pairs={{0,16},{8,24},{16,0},{24,8},{1,17},{9,25},{17,1},{25,9},{2,18},{10... | collective-permute-start | bytes 393224 | tf_op jit(solution)/shard_map/ppermute | solution.py:94
  48.8 6.6 %collective-permute-start.13 = (bf16[8,32,256]{2,1,0:T(8,128)(2,1)S(1)}, bf16[8,32,256]{2,1,0:T(8,128)(2,1)S(1)}, u32[]{:S(2)}, u32[]{:S(2)}) collective-permute-start(bf16[8,32,256]{2,1,0:T(8,128)(2,1)S(1)} %get-tuple-element.71), channel_id=1, source_target_pairs={{0,24},{8,16},{16,8},{24,0},{1,25},{9,17},{17,9},{25,1},{2,26},{10... | collective-permute-start | bytes 393224 | tf_op jit(solution)/shard_map/ppermute | solution.py:94
  50.3 39.1 %copy-start.3 = (f32[32,192]{1,0:T(8,128)S(1)}, f32[32,192]{1,0:T(8,128)}, u32[]{:S(2)}) copy-start(f32[32,192]{1,0:T(8,128)} %get-tuple-element.89.refs_10_) | copy-start | bytes 73732
  50.3 39.1 %copy-start.4 = (s32[1,1,2048,1]{2,3,1,0:T(1,128)S(1)}, s32[1,1,2048,1]{2,3,1,0:T(1,128)}, u32[]{:S(2)}) copy-start(s32[1,1,2048,1]{2,3,1,0:T(1,128)} %param.12) | copy-start | bytes 24580
  50.3 39.1 %copy-start.5 = (s32[1,2048]{1,0:T(1,128)S(1)}, s32[1,2048]{1,0:T(1,128)}, u32[]{:S(2)}) copy-start(s32[1,2048]{1,0:T(1,128)} %get-tuple-element.88.refs_9_) | copy-start | bytes 24580
  55.4 10.0 %collective-permute-start.14 = (bf16[2,8,32,256]{3,2,1,0:T(8,128)(2,1)S(1)}, bf16[2,8,32,256]{3,2,1,0:T(8,128)(2,1)S(1)}, u32[]{:S(2)}, u32[]{:S(2)}) collective-permute-start(bf16[2,8,32,256]{3,2,1,0:T(8,128)(2,1)S(1)} %pad_maximum_fusion.3.refs_0_), channel_id=1, source_target_pairs={{0,8},{8,0},{16,24},{24,16},{1,9},{9,1},{17,25},{25,17},{2,10},{10... | collective-permute-start | bytes 786440 | tf_op jit(solution)/shard_map/ppermute | solution.py:94
  56.6 11.7 %collective-permute-start.15 = (bf16[2,8,32,256]{3,2,1,0:T(8,128)(2,1)S(1)}, bf16[2,8,32,256]{3,2,1,0:T(8,128)(2,1)S(1)}, u32[]{:S(2)}, u32[]{:S(2)}) collective-permute-start(bf16[2,8,32,256]{3,2,1,0:T(8,128)(2,1)S(1)} %pad_maximum_fusion.3.refs_0_), channel_id=1, source_target_pairs={{0,16},{8,24},{16,0},{24,8},{1,17},{9,25},{17,1},{25,9},{2,18},{10... | collective-permute-start | bytes 786440 | tf_op jit(solution)/shard_map/ppermute | solution.py:94
  57.7 10.6 %collective-permute-start.16 = (bf16[2,8,32,256]{3,2,1,0:T(8,128)(2,1)S(1)}, bf16[2,8,32,256]{3,2,1,0:T(8,128)(2,1)S(1)}, u32[]{:S(2)}, u32[]{:S(2)}) collective-permute-start(bf16[2,8,32,256]{3,2,1,0:T(8,128)(2,1)S(1)} %pad_maximum_fusion.3.refs_0_), channel_id=1, source_target_pairs={{0,24},{8,16},{16,8},{24,0},{1,25},{9,17},{17,9},{25,1},{2,26},{10... | collective-permute-start | bytes 786440 | tf_op jit(solution)/shard_map/ppermute | solution.py:94
  63.4 5.1 %collective-permute-start.18 = (bf16[4,8,32,256]{3,2,1,0:T(8,128)(2,1)S(1)}, bf16[4,8,32,256]{3,2,1,0:T(8,128)(2,1)S(1)}, u32[]{:S(2)}, u32[]{:S(2)}) collective-permute-start(bf16[4,8,32,256]{3,2,1,0:T(8,128)(2,1)S(1)} %get-tuple-element.79), channel_id=1, source_target_pairs={{0,1},{1,0},{2,3},{3,2},{4,5},{5,4},{6,7},{7,6},{8,9},{9,8},{10,11... | collective-permute-start | bytes 1572872 | tf_op jit(solution)/shard_map/ppermute | solution.py:86
  63.5 15.9 %collective-permute-start.19 = (bf16[4,8,32,256]{3,2,1,0:T(8,128)(2,1)S(1)}, bf16[4,8,32,256]{3,2,1,0:T(8,128)(2,1)S(1)}, u32[]{:S(2)}, u32[]{:S(2)}) collective-permute-start(bf16[4,8,32,256]{3,2,1,0:T(8,128)(2,1)S(1)} %get-tuple-element.80), channel_id=1, source_target_pairs={{0,7},{1,2},{2,1},{3,4},{4,3},{5,6},{6,5},{7,0},{8,15},{9,10},{10,... | collective-permute-start | bytes 1572872 | tf_op jit(solution)/shard_map/ppermute | solution.py:89
  68.4 14.7 %collective-permute-start.17 = (bf16[4,8,32,256]{3,2,1,0:T(8,128)(2,1)S(1)}, bf16[4,8,32,256]{3,2,1,0:T(8,128)(2,1)S(1)}, u32[]{:S(2)}, u32[]{:S(2)}) collective-permute-start(bf16[4,8,32,256]{3,2,1,0:T(8,128)(2,1)S(1)} %pad_maximum_fusion.1), channel_id=1, source_target_pairs={{0,1},{1,0},{2,3},{3,2},{4,5},{5,4},{6,7},{7,6},{8,9},{9,8},{10,11... | collective-permute-start | bytes 1572872 | tf_op jit(solution)/shard_map/ppermute | solution.py:86
  79.6 9.7 %collective-permute-start.20 = (bf16[8,32,256]{2,1,0:T(8,128)(2,1)S(1)}, bf16[8,32,256]{2,1,0:T(8,128)(2,1)S(1)}, u32[]{:S(2)}, u32[]{:S(2)}) collective-permute-start(bf16[8,32,256]{2,1,0:T(8,128)(2,1)S(1)} %get-tuple-element.82), channel_id=1, source_target_pairs={{0,8},{8,0},{16,24},{24,16},{1,9},{9,1},{17,25},{25,17},{2,10},{10... | collective-permute-start | bytes 393224 | tf_op jit(solution)/shard_map/ppermute | solution.py:94
  80.9 8.5 %collective-permute-start.21 = (bf16[8,32,256]{2,1,0:T(8,128)(2,1)S(1)}, bf16[8,32,256]{2,1,0:T(8,128)(2,1)S(1)}, u32[]{:S(2)}, u32[]{:S(2)}) collective-permute-start(bf16[8,32,256]{2,1,0:T(8,128)(2,1)S(1)} %get-tuple-element.83), channel_id=1, source_target_pairs={{0,16},{8,24},{16,0},{24,8},{1,17},{9,25},{17,1},{25,9},{2,18},{10... | collective-permute-start | bytes 393224 | tf_op jit(solution)/shard_map/ppermute | solution.py:94
  81.7 7.6 %collective-permute-start.22 = (bf16[8,32,256]{2,1,0:T(8,128)(2,1)S(1)}, bf16[8,32,256]{2,1,0:T(8,128)(2,1)S(1)}, u32[]{:S(2)}, u32[]{:S(2)}) collective-permute-start(bf16[8,32,256]{2,1,0:T(8,128)(2,1)S(1)} %get-tuple-element.84), channel_id=1, source_target_pairs={{0,24},{8,16},{16,8},{24,0},{1,25},{9,17},{17,9},{25,1},{2,26},{10... | collective-permute-start | bytes 393224 | tf_op jit(solution)/shard_map/ppermute | solution.py:94
  93.4 17.6 %all-to-all-start = ((s16[32,56,128]{2,1,0:T(8,128)(2,1)}), s16[32,56,128]{2,1,0:T(8,128)(2,1)S(1)}, u32[]{:S(2)}, u32[]{:S(2)}) async-start(s16[32,56,128]{2,1,0:T(8,128)(2,1)} %shard_map.94), calls=%async_computation | async-start | bytes 917504 | tf_op jit(solution)/shard_map/all_to_all | solution.py:546

commit v7 on v6

--- a/solution.py
+++ b/solution.py
@@ -169,8 +169,19 @@
     step_rows = along((once, bands, width), 0)
     full_rows = along((3, once, bands, width), 1)
 
-    def adjoint_first(slots_ref, m_ref, *refs):
-        piece_refs, full_ref, outs, total = refs[:split], refs[split], refs[split + 1 : -1], refs[-1]
+    def adjoint_first(slots_ref, matrix_ref, *refs):
+        piece_refs, (full_ref, m_ref), outs = refs[:split], refs[split : split + 2], refs[split + 2 : -2]
+        total, arrivals = refs[-2:]
+        i = pl.program_id(0)
+
+        def copy_of(r):
+            return pltpu.make_async_copy(matrix_ref.at[r], m_ref.at[r], arrivals.at[r])
+
+        @pl.when(i == 0)
+        def _():
+            for r in range(rb_count):
+                copy_of(r).start()
+
         b = lax.axis_index("band")
         for d in range(split):
             at = pl.ds(pl.multiple_of((b ^ d) * part_bands, part_bands), part_bands)
@@ -180,6 +191,7 @@
                     full_ref[a, q, at, :] = decoded(code, a)
 
         def value_of(q):
+            copy_of(i * once + q).wait()
             return ((1.0 - full_ref[0, q]) * full_ref[2, q]).astype(BF16)
 
         scatter_products(slots_ref, m_ref, value_of, outs, total)
@@ -286,15 +298,7 @@
     value_rows = bands + (bands // 2 if tail else 0)
     send_rows = value_rows + 8
 
-    def route(
-        matrix_ref, column_ref, owner_ref, surface_ref, m_ref, slot_ref, rank_ref, label_ref, loaded
-    ):
-        loads = [
-            pltpu.make_async_copy(matrix_ref.at[r], m_ref.at[r], loaded.at[r])
-            for r in range(rb_count)
-        ]
-        for load in loads:
-            load.start()
+    def route(column_ref, owner_ref, surface_ref, slot_ref, rank_ref, label_ref):
         me = lax.axis_index("patch")
         column = column_ref[...]
         group = jnp.right_shift(column, group_bits)
@@ -320,28 +324,23 @@
             found = found + nt(marks, seated)
         taken, high, low = (found[a * devices : (a + 1) * devices] for a in range(3))
         label_ref[...] = jnp.where(taken > 0.5, high * 128.0 + low, float(surfaces))
-        for load in loads:
-            load.wait()
-
-    matrix, slots, rank, labels = kernel_call(
+
+    slots, rank, labels = kernel_call(
         route,
         1,
         0,
-        [pl.BlockSpec(memory_space=pl.ANY), whole((rb_count, depth))] + [whole((1, rows))] * 2,
+        [whole((rb_count, depth))] + [whole((1, rows))] * 2,
         [
-            (VMEM, pltpu.VMEM(matrix.shape, BF16)),
             (whole((rb_count, depth)), shape((rb_count, depth), I32)),
             (whole((1, rows)), shape((1, rows), I32)),
             (whole((devices, seats)), shape((devices, seats), F32)),
         ],
         (
-            matrix,
             column_blocks.reshape(rb_count, depth),
             patch_owner.reshape(1, rows),
             patch_surface.reshape(1, rows),
         ),
-        [pltpu.SemaphoreType.DMA((rb_count,))],
-        limit=40 * MIB,
+        limit=60 * MIB,
     )
 
     owners_once = 32
@@ -459,14 +458,19 @@
 
     start = jnp.stack(lax.optimization_barrier((start, outer(start), rank, pieces))[:2])
     slots, rank, labels, _ = lax.optimization_barrier((slots, rank, labels, start))
-    full, *parts = kernel_call(
+    full, matrix, *parts = kernel_call(
         adjoint_first,
         4,
         1,
-        [VMEM] + [along((3, part_bands, once * width), 2)] * split,
-        [(full_rows, shape((3,) + block_shape, F32))] + part_outs,
+        [pl.BlockSpec(memory_space=pl.ANY)] + [along((3, part_bands, once * width), 2)] * split,
+        [
+            (full_rows, shape((3,) + block_shape, F32)),
+            (VMEM, pltpu.VMEM(matrix.shape, BF16)),
+        ]
+        + part_outs,
         (slots, matrix) + tuple(pieces),
-        total_scratch,
+        total_scratch + [pltpu.SemaphoreType.DMA((rb_count,))],
+        limit=24 * MIB,
         flops=pass_flops,
     )
     starts = gather(start, parts[0])

time: 115 us -> 113 us (0.983)
  waiting for transfers between devices: 41.3 us -> 38.7 us
  Pallas kernels: 39.1 us -> 36.8 us
    pallas_call x10, Pallas kernels: 39.1 us -> 36.8 us  [kernel_call(): pl.pallas_call(kernel, out_shape=[o for _, o in outs], grid_spec=pltpu.Pr...]
    ppermute x4, waiting for transfers between devices: 15.5 us -> 13.3 us  [outer(): lax.ppermute(block, 'patch', [(i, (i + (1 if i % 2 else -1)) % groups) fo...]
    unnamed x15 -> x11, local copies, waits for them, and re-layouts: 1.68 us -> 2.55 us
  transfers between devices with their start and end apart: 24 -> 24, of which waited for: 7 -> 9; matrix products, arithmetic and copies ran while one was open for 1% -> 1% of each run, Pallas kernels for 26% -> 24%
where the time goes in v7:
time: 113 us
  waiting for transfers between devices  38.7 us (34%)
  Pallas kernels  36.8 us (33%)
  starting transfers between devices  32.5 us (29%)
  local copies, waits for them, and re-layouts  2.63 us (2%)
    pallas_call x10, Pallas kernels, kernel_call(): pl.pallas_call(kernel, out_shape=[o for _, o in outs], grid_spec=pltpu.Pr...  36.8 us
    ppermute x15, starting transfers between devices, across(): return lax.ppermute(block, 'band', [(i, i ^ d) for i in range(split)])  17.6 us
    all_to_all x1, waiting for transfers between devices, body(): send = lax.all_to_all(send, ('band', 'patch'), 0, 0, tiled=True)  13.8 us
    ppermute x4, waiting for transfers between devices, outer(): lax.ppermute(block, 'patch', [(i, (i + (1 if i % 2 else -1)) % groups) fo...  13.3 us
    ppermute x4, starting transfers between devices, outer(): lax.ppermute(block, 'patch', [(i, (i + (1 if i % 2 else -1)) % groups) fo...  11.7 us
    ppermute x15, waiting for transfers between devices, across(): return lax.ppermute(block, 'band', [(i, i ^ d) for i in range(split)])  11.6 us
    all_to_all x1, starting transfers between devices, body(): send = lax.all_to_all(send, ('band', 'patch'), 0, 0, tiled=True)  2.91 us
    unnamed x11, local copies, waits for them, and re-layouts  2.55 us
  transfers between devices with their start and end apart: 24, of which 9 were waited for; matrix products, arithmetic and copies ran while one was open for 1% of the time, Pallas kernels for 24%

profile of v7, /device:TPU:0, one launch (start us, length us, event | category | flops | bytes accessed | tf_op | source)
XLA Modules:
  0.0 112.6 jit_solution(589555070508527316)
XLA Ops:
  0.6 2.0 %shard_map.87 = (bf16[32,8,256]{2,1,0:T(8,128)(2,1)}, s16[3,8,2048]{2,1,0:T(8,128)(2,1)}, s16[3,8,2048]{2,1,0:T(8,128)(2,1)}, s16[3,8,2048]{2,1,0:T(8,128)(2,1)}, s16[3,8,2048]{2,1,0:T(8,128)(2,1)}) custom-call(f32[8,8192]{1,0:T(8,128)} %e_hbm.1, f32[8,8192]{1,0:T(8,128)} %b_hbm.1, f32[8,8192]{1,0:T(8,128)} %w_hbm.1), custom_call_target="tpu_custom_call" | custom-call | tf_op jit(solution)/shard_map/pallas_call | solution.py:54
  2.6 4.6 %collective-permute-start = (bf16[32,8,256]{2,1,0:T(8,128)(2,1)}, bf16[32,8,256]{2,1,0:T(8,128)(2,1)S(1)}, u32[]{:S(2)}, u32[]{:S(2)}) collective-permute-start(bf16[32,8,256]{2,1,0:T(8,128)(2,1)} %get-tuple-element.54), channel_id=1, source_target_pairs={{0,7},{1,2},{2,1},{3,4},{4,3},{5,6},{6,5},{7,0},{8,15},{9,10},{10,... | collective-permute-start | bytes 393224 | tf_op jit(solution)/shard_map/ppermute | solution.py:89
  7.2 1.5 %collective-permute-start.1 = (s16[3,8,2048]{2,1,0:T(8,128)(2,1)}, s16[3,8,2048]{2,1,0:T(8,128)(2,1)S(1)}, u32[]{:S(2)}, u32[]{:S(2)}) collective-permute-start(s16[3,8,2048]{2,1,0:T(8,128)(2,1)} %get-tuple-element.51), channel_id=1, source_target_pairs={{0,8},{8,0},{16,24},{24,16},{1,9},{9,1},{17,25},{25,17},{2,10},{10... | collective-permute-start | bytes 294920 | tf_op jit(solution)/shard_map/ppermute | solution.py:94
  8.7 1.5 %collective-permute-start.2 = (s16[3,8,2048]{2,1,0:T(8,128)(2,1)}, s16[3,8,2048]{2,1,0:T(8,128)(2,1)S(1)}, u32[]{:S(2)}, u32[]{:S(2)}) collective-permute-start(s16[3,8,2048]{2,1,0:T(8,128)(2,1)} %get-tuple-element.52), channel_id=1, source_target_pairs={{0,16},{8,24},{16,0},{24,8},{1,17},{9,25},{17,1},{25,9},{2,18},{10... | collective-permute-start | bytes 294920 | tf_op jit(solution)/shard_map/ppermute | solution.py:94
  10.2 0.5 collective-permute-start.3
  10.7 2.4 %shard_map.86 = (s32[8,16]{1,0:T(8,128)}, s32[1,2048]{1,0:T(1,128)}, f32[32,192]{1,0:T(8,128)}) custom-call(s32[8,16]{1,0:T(8,128)} %bitcast.18, s32[1,2048]{1,0:T(1,128)} %bitcast.11, s32[1,2048]{1,0:T(1,128)} %bitcast.17), custom_call_target="tpu_custom_call" | custom-call | tf_op jit(solution)/shard_map/pallas_call | solution.py:54
  13.1 1.3 %collective-permute-done.2.refs_2_ = s16[3,8,2048]{2,1,0:T(8,128)(2,1)S(1)} collective-permute-done((s16[3,8,2048]{2,1,0:T(8,128)(2,1)}, s16[3,8,2048]{2,1,0:T(8,128)(2,1)S(1)}, u32[]{:S(2)}, u32[]{:S(2)}) %collective-permute-start.2) | collective-permute-done | bytes 98336 | tf_op jit(solution)/shard_map/ppermute | solution.py:94
  14.3 1.6 %collective-permute-done.3.refs_3_ = s16[3,8,2048]{2,1,0:T(8,128)(2,1)S(1)} collective-permute-done((s16[3,8,2048]{2,1,0:T(8,128)(2,1)}, s16[3,8,2048]{2,1,0:T(8,128)(2,1)S(1)}, u32[]{:S(2)}, u32[]{:S(2)}) %collective-permute-start.3) | collective-permute-done | bytes 98336 | tf_op jit(solution)/shard_map/ppermute | solution.py:94
  15.9 0.9 pad_maximum_fusion.2.refs_0_
  16.9 0.6 collective-permute-start.4
  17.5 0.5 collective-permute-start.5
  18.0 2.4 %collective-permute-start.6 = (bf16[2,32,8,256]{3,2,1,0:T(8,128)(2,1)S(1)}, bf16[2,32,8,256]{3,2,1,0:T(8,128)(2,1)S(1)}, u32[]{:S(2)}, u32[]{:S(2)}) collective-permute-start(bf16[2,32,8,256]{3,2,1,0:T(8,128)(2,1)S(1)} %pad_maximum_fusion.2.refs_0_), channel_id=1, source_target_pairs={{0,24},{8,16},{16,8},{24,0},{1,25},{9,17},{17,9},{25,1},{2,26},{10... | collective-permute-start | bytes 786440 | tf_op jit(solution)/shard_map/ppermute | solution.py:94
  20.4 0.9 copy-done
  21.3 0.7 copy-done.1
  22.0 7.3 %shard_map.88 = (f32[3,8,32,256]{3,2,1,0:T(8,128)S(1)}, bf16[8,16,256,256]{3,2,1,0:T(8,128)(2,1)S(1)}, f32[4,8,32,256]{3,2,1,0:T(8,128)S(1)}, bf16[4,8,32,256]{3...) custom-call(s32[8,16]{1,0:T(8,128)S(1)} %copy-done.1, bf16[8,16,256,256]{3,2,1,0:T(8,128)(2,1)} %bitcast.13, ...), custom_call_target="tpu_custom_call" | custom-call | flops 536870912 | bytes 16777216 | tf_op jit(solution)/shard_map/pallas_call | solution.py:54
  29.4 0.1 pad_maximum_fusion
  29.4 0.1 collective-permute-start.7
  29.5 2.3 %collective-permute-start.10 = (bf16[4,8,32,256]{3,2,1,0:T(8,128)(2,1)S(1)}, bf16[4,8,32,256]{3,2,1,0:T(8,128)(2,1)S(1)}, u32[]{:S(2)}, u32[]{:S(2)}) collective-permute-start(bf16[4,8,32,256]{3,2,1,0:T(8,128)(2,1)S(1)} %get-tuple-element.66), channel_id=1, source_target_pairs={{0,7},{1,2},{2,1},{3,4},{4,3},{5,6},{6,5},{7,0},{8,15},{9,10},{10,... | collective-permute-start | bytes 1572872 | tf_op jit(solution)/shard_map/ppermute | solution.py:89
  31.9 6.4 %shard_map.89 = (f32[8,32,256]{2,1,0:T(8,128)S(1)}, bf16[8,32,256]{2,1,0:T(8,128)(2,1)S(1)}) custom-call(s32[8,16]{1,0:T(8,128)S(1)} %copy-done.1, bf16[8,16,256,256]{3,2,1,0:T(8,128)(2,1)S(1)} %get-tuple-element.57.m_ref, bf16[2,32,8,256]{3,2,1,0:T(8,128)(2,1)S(1)} %pad_maximum_fusion.2.refs_0_, bf16[2,32,8,256]{3,2,1,0:T(8,128)(2,1)S(1)} %collective-permute-done.4.refs_1_, ...), custom_call_target="tpu_custom_call" | custom-call | flops 536870912 | bytes 16777216 | tf_op jit(solution)/shard_map/pallas_call | solution.py:54
  38.2 2.0 %collective-permute-start.8 = (bf16[8,32,256]{2,1,0:T(8,128)(2,1)S(1)}, bf16[8,32,256]{2,1,0:T(8,128)(2,1)S(1)}, u32[]{:S(2)}, u32[]{:S(2)}) collective-permute-start(bf16[8,32,256]{2,1,0:T(8,128)(2,1)S(1)} %get-tuple-element.64), channel_id=1, source_target_pairs={{0,7},{1,2},{2,1},{3,4},{4,3},{5,6},{6,5},{7,0},{8,15},{9,10},{10,... | collective-permute-start | bytes 393224 | tf_op jit(solution)/shard_map/ppermute | solution.py:89
  40.3 4.4 %collective-permute-done.10.far_ref = bf16[4,8,32,256]{3,2,1,0:T(8,128)(2,1)S(1)} collective-permute-done((bf16[4,8,32,256]{3,2,1,0:T(8,128)(2,1)S(1)}, bf16[4,8,32,256]{3,2,1,0:T(8,128)(2,1)S(1)}, u32[]{:S(2)}, u32[]{:S(2)}) %collective-permute-start.10) | collective-permute-done | bytes 524320 | tf_op jit(solution)/shard_map/ppermute | solution.py:89
  44.7 0.2 shard_map.90
  44.9 1.3 %collective-permute-start.11 = (bf16[8,32,256]{2,1,0:T(8,128)(2,1)S(1)}, bf16[8,32,256]{2,1,0:T(8,128)(2,1)S(1)}, u32[]{:S(2)}, u32[]{:S(2)}) collective-permute-start(bf16[8,32,256]{2,1,0:T(8,128)(2,1)S(1)} %get-tuple-element.69), channel_id=1, source_target_pairs={{0,8},{8,0},{16,24},{24,16},{1,9},{9,1},{17,25},{25,17},{2,10},{10... | collective-permute-start | bytes 393224 | tf_op jit(solution)/shard_map/ppermute | solution.py:94
  46.2 2.3 %collective-permute-start.13 = (bf16[8,32,256]{2,1,0:T(8,128)(2,1)S(1)}, bf16[8,32,256]{2,1,0:T(8,128)(2,1)S(1)}, u32[]{:S(2)}, u32[]{:S(2)}) collective-permute-start(bf16[8,32,256]{2,1,0:T(8,128)(2,1)S(1)} %get-tuple-element.71), channel_id=1, source_target_pairs={{0,24},{8,16},{16,8},{24,0},{1,25},{9,17},{17,9},{25,1},{2,26},{10... | collective-permute-start | bytes 393224 | tf_op jit(solution)/shard_map/ppermute | solution.py:94
  48.5 0.0 copy-start.3
  48.5 2.2 %collective-permute-done.11.refs_1_ = bf16[8,32,256]{2,1,0:T(8,128)(2,1)S(1)} collective-permute-done((bf16[8,32,256]{2,1,0:T(8,128)(2,1)S(1)}, bf16[8,32,256]{2,1,0:T(8,128)(2,1)S(1)}, u32[]{:S(2)}, u32[]{:S(2)}) %collective-permute-start.11) | collective-permute-done | bytes 131104 | tf_op jit(solution)/shard_map/ppermute | solution.py:94
  50.7 3.3 %collective-permute-done.12.refs_2_ = bf16[8,32,256]{2,1,0:T(8,128)(2,1)S(1)} collective-permute-done((bf16[8,32,256]{2,1,0:T(8,128)(2,1)S(1)}, bf16[8,32,256]{2,1,0:T(8,128)(2,1)S(1)}, u32[]{:S(2)}, u32[]{:S(2)}) %collective-permute-start.12) | collective-permute-done | bytes 131104 | tf_op jit(solution)/shard_map/ppermute | solution.py:94
  54.0 0.8 collective-permute-start.14
  54.8 0.9 collective-permute-start.15
  55.7 1.8 %collective-permute-start.16 = (bf16[2,8,32,256]{3,2,1,0:T(8,128)(2,1)S(1)}, bf16[2,8,32,256]{3,2,1,0:T(8,128)(2,1)S(1)}, u32[]{:S(2)}, u32[]{:S(2)}) collective-permute-start(bf16[2,8,32,256]{3,2,1,0:T(8,128)(2,1)S(1)} %pad_maximum_fusion.3.refs_0_), channel_id=1, source_target_pairs={{0,24},{8,16},{16,8},{24,0},{1,25},{9,17},{17,9},{25,1},{2,26},{10... | collective-permute-start | bytes 786440 | tf_op jit(solution)/shard_map/ppermute | solution.py:94
  57.5 4.5 %shard_map.91 = (f32[8,32,256]{2,1,0:T(8,128)S(1)}, f32[4,8,32,256]{3,2,1,0:T(8,128)S(1)}, bf16[4,8,32,256]{3,2,1,0:T(8,128)(2,1)S(1)}, bf16[4,8,32,256]{3,2,1,0:T(8,128)(2,1)S(1)}) custom-call(s32[8,16]{1,0:T(8,128)S(1)} %copy-done.1, bf16[8,16,256,256]{3,2,1,0:T(8,128)(2,1)S(1)} %get-tuple-element.57.m_ref, f32[8,32,256]{2,1,0:T(8,128)S(1)} %get-tuple-element.68.refs_0_, ...), custom_call_target="tpu_custom_call" | custom-call | flops 536870912 | bytes 16777216 | tf_op jit(solution)/shard_map/pallas_call | solution.py:54
  61.9 0.1 collective-permute-start.18
  62.0 2.8 %collective-permute-start.19 = (bf16[4,8,32,256]{3,2,1,0:T(8,128)(2,1)S(1)}, bf16[4,8,32,256]{3,2,1,0:T(8,128)(2,1)S(1)}, u32[]{:S(2)}, u32[]{:S(2)}) collective-permute-start(bf16[4,8,32,256]{3,2,1,0:T(8,128)(2,1)S(1)} %get-tuple-element.80), channel_id=1, source_target_pairs={{0,7},{1,2},{2,1},{3,4},{4,3},{5,6},{6,5},{7,0},{8,15},{9,10},{10,... | collective-permute-start | bytes 1572872 | tf_op jit(solution)/shard_map/ppermute | solution.py:89
  64.8 1.4 %collective-permute-done.15.refs_2_ = bf16[2,8,32,256]{3,2,1,0:T(8,128)(2,1)S(1)} collective-permute-done((bf16[2,8,32,256]{3,2,1,0:T(8,128)(2,1)S(1)}, bf16[2,8,32,256]{3,2,1,0:T(8,128)(2,1)S(1)}, u32[]{:S(2)}, u32[]{:S(2)}) %collective-permute-start.15) | collective-permute-done | bytes 262176 | tf_op jit(solution)/shard_map/ppermute | solution.py:94
  66.2 1.9 %collective-permute-done.16.refs_3_ = bf16[2,8,32,256]{3,2,1,0:T(8,128)(2,1)S(1)} collective-permute-done((bf16[2,8,32,256]{3,2,1,0:T(8,128)(2,1)S(1)}, bf16[2,8,32,256]{3,2,1,0:T(8,128)(2,1)S(1)}, u32[]{:S(2)}, u32[]{:S(2)}) %collective-permute-start.16) | collective-permute-done | bytes 262176 | tf_op jit(solution)/shard_map/ppermute | solution.py:94
  68.2 0.1 pad_maximum_fusion.1
  68.2 0.1 collective-permute-start.17
  68.3 8.9 %collective-permute-done.19.far_ref = bf16[4,8,32,256]{3,2,1,0:T(8,128)(2,1)S(1)} collective-permute-done((bf16[4,8,32,256]{3,2,1,0:T(8,128)(2,1)S(1)}, bf16[4,8,32,256]{3,2,1,0:T(8,128)(2,1)S(1)}, u32[]{:S(2)}, u32[]{:S(2)}) %collective-permute-start.19) | collective-permute-done | bytes 524320 | tf_op jit(solution)/shard_map/ppermute | solution.py:89
  77.2 0.2 shard_map.93
  77.4 1.4 %collective-permute-start.20 = (bf16[8,32,256]{2,1,0:T(8,128)(2,1)S(1)}, bf16[8,32,256]{2,1,0:T(8,128)(2,1)S(1)}, u32[]{:S(2)}, u32[]{:S(2)}) collective-permute-start(bf16[8,32,256]{2,1,0:T(8,128)(2,1)S(1)} %get-tuple-element.82), channel_id=1, source_target_pairs={{0,8},{8,0},{16,24},{24,16},{1,9},{9,1},{17,25},{25,17},{2,10},{10... | collective-permute-start | bytes 393224 | tf_op jit(solution)/shard_map/ppermute | solution.py:94
  78.8 0.3 collective-permute-start.21
  79.1 1.8 %collective-permute-start.22 = (bf16[8,32,256]{2,1,0:T(8,128)(2,1)S(1)}, bf16[8,32,256]{2,1,0:T(8,128)(2,1)S(1)}, u32[]{:S(2)}, u32[]{:S(2)}) collective-permute-start(bf16[8,32,256]{2,1,0:T(8,128)(2,1)S(1)} %get-tuple-element.84), channel_id=1, source_target_pairs={{0,24},{8,16},{16,8},{24,0},{1,25},{9,17},{17,9},{25,1},{2,26},{10... | collective-permute-start | bytes 393224 | tf_op jit(solution)/shard_map/ppermute | solution.py:94
  80.9 6.2 %shard_map.92 = (f32[8,32,256]{2,1,0:T(8,128)S(1)}, f32[32,2048]{1,0:T(8,128)S(1)}) custom-call(s32[8,16]{1,0:T(8,128)S(1)} %copy-done.1, bf16[8,16,256,256]{3,2,1,0:T(8,128)(2,1)S(1)} %get-tuple-element.57.m_ref, bf16[2,8,32,256]{3,2,1,0:T(8,128)(2,1)S(1)} %pad_maximum_fusion.3.refs_0_, bf16[2,8,32,256]{3,2,1,0:T(8,128)(2,1)S(1)} %collective-permute-done.14.refs_1_, ...), custom_call_target="tpu_custom_call" | custom-call | flops 536870912 | bytes 16777216 | tf_op jit(solution)/shard_map/pallas_call | solution.py:54
  87.2 4.0 %shard_map.94 = s16[32,56,128]{2,1,0:T(8,128)(2,1)} custom-call(f32[8,32,256]{2,1,0:T(8,128)S(1)} %get-tuple-element.81.refs_0_, bf16[8,32,256]{2,1,0:T(8,128)(2,1)S(1)} %collective-permute-done.20.refs_1_, bf16[8,32,256]{2,1,0:T(8,128)(2,1)S(1)} %collective-permute-done.21.refs_2_, bf16[8,32,256]{2,1,0:T(8,128)(2,1)S(1)} %collective-permute-done.22.refs_3_, ...), custom_call_target="tpu_custom_call" | custom-call | tf_op jit(solution)/shard_map/pallas_call | solution.py:54
  91.2 2.9 %all-to-all-start = ((s16[32,56,128]{2,1,0:T(8,128)(2,1)}), s16[32,56,128]{2,1,0:T(8,128)(2,1)S(1)}, u32[]{:S(2)}, u32[]{:S(2)}) async-start(s16[32,56,128]{2,1,0:T(8,128)(2,1)} %shard_map.94), calls=%async_computation | async-start | bytes 917504 | tf_op jit(solution)/shard_map/all_to_all | solution.py:550
  94.1 1.0 copy.9
  95.1 13.8 %all-to-all-done.got_ref = s16[32,56,128]{2,1,0:T(8,128)(2,1)S(1)} async-done(((s16[32,56,128]{2,1,0:T(8,128)(2,1)}), s16[32,56,128]{2,1,0:T(8,128)(2,1)S(1)}, u32[]{:S(2)}, u32[]{:S(2)}) %all-to-all-start) | async-done | bytes 458784 | tf_op jit(solution)/shard_map/all_to_all | solution.py:550
  108.9 3.8 %shard_map.95 = f32[32,1024]{1,0:T(8,128)} custom-call(s16[32,56,128]{2,1,0:T(8,128)(2,1)S(1)} %all-to-all-done.got_ref), custom_call_target="tpu_custom_call" | custom-call | tf_op jit(solution)/shard_map/pallas_call | solution.py:54
  (33 shorter events, 0.2 us)
Async XLA Ops:
  2.6 13.3 %collective-permute-start = (bf16[32,8,256]{2,1,0:T(8,128)(2,1)}, bf16[32,8,256]{2,1,0:T(8,128)(2,1)S(1)}, u32[]{:S(2)}, u32[]{:S(2)}) collective-permute-start(bf16[32,8,256]{2,1,0:T(8,128)(2,1)} %get-tuple-element.54), channel_id=1, source_target_pairs={{0,7},{1,2},{2,1},{3,4},{4,3},{5,6},{6,5},{7,0},{8,15},{9,10},{10,... | collective-permute-start | bytes 393224 | tf_op jit(solution)/shard_map/ppermute | solution.py:89
  7.2 5.9 %collective-permute-start.1 = (s16[3,8,2048]{2,1,0:T(8,128)(2,1)}, s16[3,8,2048]{2,1,0:T(8,128)(2,1)S(1)}, u32[]{:S(2)}, u32[]{:S(2)}) collective-permute-start(s16[3,8,2048]{2,1,0:T(8,128)(2,1)} %get-tuple-element.51), channel_id=1, source_target_pairs={{0,8},{8,0},{16,24},{24,16},{1,9},{9,1},{17,25},{25,17},{2,10},{10... | collective-permute-start | bytes 294920 | tf_op jit(solution)/shard_map/ppermute | solution.py:94
  8.7 5.7 %collective-permute-start.2 = (s16[3,8,2048]{2,1,0:T(8,128)(2,1)}, s16[3,8,2048]{2,1,0:T(8,128)(2,1)S(1)}, u32[]{:S(2)}, u32[]{:S(2)}) collective-permute-start(s16[3,8,2048]{2,1,0:T(8,128)(2,1)} %get-tuple-element.52), channel_id=1, source_target_pairs={{0,16},{8,24},{16,0},{24,8},{1,17},{9,25},{17,1},{25,9},{2,18},{10... | collective-permute-start | bytes 294920 | tf_op jit(solution)/shard_map/ppermute | solution.py:94
  10.2 5.7 %collective-permute-start.3 = (s16[3,8,2048]{2,1,0:T(8,128)(2,1)}, s16[3,8,2048]{2,1,0:T(8,128)(2,1)S(1)}, u32[]{:S(2)}, u32[]{:S(2)}) collective-permute-start(s16[3,8,2048]{2,1,0:T(8,128)(2,1)} %get-tuple-element.53), channel_id=1, source_target_pairs={{0,24},{8,16},{16,8},{24,0},{1,25},{9,17},{17,9},{25,1},{2,26},{10... | collective-permute-start | bytes 294920 | tf_op jit(solution)/shard_map/ppermute | solution.py:94
  16.9 12.4 %collective-permute-start.4 = (bf16[2,32,8,256]{3,2,1,0:T(8,128)(2,1)S(1)}, bf16[2,32,8,256]{3,2,1,0:T(8,128)(2,1)S(1)}, u32[]{:S(2)}, u32[]{:S(2)}) collective-permute-start(bf16[2,32,8,256]{3,2,1,0:T(8,128)(2,1)S(1)} %pad_maximum_fusion.2.refs_0_), channel_id=1, source_target_pairs={{0,8},{8,0},{16,24},{24,16},{1,9},{9,1},{17,25},{25,17},{2,10},{10... | collective-permute-start | bytes 786440 | tf_op jit(solution)/shard_map/ppermute | solution.py:94
  17.5 11.8 %collective-permute-start.5 = (bf16[2,32,8,256]{3,2,1,0:T(8,128)(2,1)S(1)}, bf16[2,32,8,256]{3,2,1,0:T(8,128)(2,1)S(1)}, u32[]{:S(2)}, u32[]{:S(2)}) collective-permute-start(bf16[2,32,8,256]{3,2,1,0:T(8,128)(2,1)S(1)} %pad_maximum_fusion.2.refs_0_), channel_id=1, source_target_pairs={{0,16},{8,24},{16,0},{24,8},{1,17},{9,25},{17,1},{25,9},{2,18},{10... | collective-permute-start | bytes 786440 | tf_op jit(solution)/shard_map/ppermute | solution.py:94
  18.0 11.3 %collective-permute-start.6 = (bf16[2,32,8,256]{3,2,1,0:T(8,128)(2,1)S(1)}, bf16[2,32,8,256]{3,2,1,0:T(8,128)(2,1)S(1)}, u32[]{:S(2)}, u32[]{:S(2)}) collective-permute-start(bf16[2,32,8,256]{3,2,1,0:T(8,128)(2,1)S(1)} %pad_maximum_fusion.2.refs_0_), channel_id=1, source_target_pairs={{0,24},{8,16},{16,8},{24,0},{1,25},{9,17},{17,9},{25,1},{2,26},{10... | collective-permute-start | bytes 786440 | tf_op jit(solution)/shard_map/ppermute | solution.py:94
  20.4 0.9 copy-start
  21.3 0.7 copy-start.1
  29.4 2.4 %collective-permute-start.7 = (bf16[4,32,8,256]{3,2,1,0:T(8,128)(2,1)S(1)}, bf16[4,32,8,256]{3,2,1,0:T(8,128)(2,1)S(1)}, u32[]{:S(2)}, u32[]{:S(2)}) collective-permute-start(bf16[4,32,8,256]{3,2,1,0:T(8,128)(2,1)S(1)} %pad_maximum_fusion), channel_id=1, source_target_pairs={{0,1},{1,0},{2,3},{3,2},{4,5},{5,4},{6,7},{7,6},{8,9},{9,8},{10,11... | collective-permute-start | bytes 1572872 | tf_op jit(solution)/shard_map/ppermute | solution.py:86
  29.5 15.2 %collective-permute-start.10 = (bf16[4,8,32,256]{3,2,1,0:T(8,128)(2,1)S(1)}, bf16[4,8,32,256]{3,2,1,0:T(8,128)(2,1)S(1)}, u32[]{:S(2)}, u32[]{:S(2)}) collective-permute-start(bf16[4,8,32,256]{3,2,1,0:T(8,128)(2,1)S(1)} %get-tuple-element.66), channel_id=1, source_target_pairs={{0,7},{1,2},{2,1},{3,4},{4,3},{5,6},{6,5},{7,0},{8,15},{9,10},{10,... | collective-permute-start | bytes 1572872 | tf_op jit(solution)/shard_map/ppermute | solution.py:89
  31.8 12.9 %collective-permute-start.9 = (bf16[4,8,32,256]{3,2,1,0:T(8,128)(2,1)S(1)}, bf16[4,8,32,256]{3,2,1,0:T(8,128)(2,1)S(1)}, u32[]{:S(2)}, u32[]{:S(2)}) collective-permute-start(bf16[4,8,32,256]{3,2,1,0:T(8,128)(2,1)S(1)} %get-tuple-element.65), channel_id=1, source_target_pairs={{0,1},{1,0},{2,3},{3,2},{4,5},{5,4},{6,7},{7,6},{8,9},{9,8},{10,11... | collective-permute-start | bytes 1572872 | tf_op jit(solution)/shard_map/ppermute | solution.py:86
  38.2 10.2 %collective-permute-start.8 = (bf16[8,32,256]{2,1,0:T(8,128)(2,1)S(1)}, bf16[8,32,256]{2,1,0:T(8,128)(2,1)S(1)}, u32[]{:S(2)}, u32[]{:S(2)}) collective-permute-start(bf16[8,32,256]{2,1,0:T(8,128)(2,1)S(1)} %get-tuple-element.64), channel_id=1, source_target_pairs={{0,7},{1,2},{2,1},{3,4},{4,3},{5,6},{6,5},{7,0},{8,15},{9,10},{10,... | collective-permute-start | bytes 393224 | tf_op jit(solution)/shard_map/ppermute | solution.py:89
  44.9 5.8 %collective-permute-start.11 = (bf16[8,32,256]{2,1,0:T(8,128)(2,1)S(1)}, bf16[8,32,256]{2,1,0:T(8,128)(2,1)S(1)}, u32[]{:S(2)}, u32[]{:S(2)}) collective-permute-start(bf16[8,32,256]{2,1,0:T(8,128)(2,1)S(1)} %get-tuple-element.69), channel_id=1, source_target_pairs={{0,8},{8,0},{16,24},{24,16},{1,9},{9,1},{17,25},{25,17},{2,10},{10... | collective-permute-start | bytes 393224 | tf_op jit(solution)/shard_map/ppermute | solution.py:94
  46.2 7.8 %collective-permute-start.12 = (bf16[8,32,256]{2,1,0:T(8,128)(2,1)S(1)}, bf16[8,32,256]{2,1,0:T(8,128)(2,1)S(1)}, u32[]{:S(2)}, u32[]{:S(2)}) collective-permute-start(bf16[8,32,256]{2,1,0:T(8,128)(2,1)S(1)} %get-tuple-element.70), channel_id=1, source_target_pairs={{0,16},{8,24},{16,0},{24,8},{1,17},{9,25},{17,1},{25,9},{2,18},{10... | collective-permute-start | bytes 393224 | tf_op jit(solution)/shard_map/ppermute | solution.py:94
  46.2 7.8 %collective-permute-start.13 = (bf16[8,32,256]{2,1,0:T(8,128)(2,1)S(1)}, bf16[8,32,256]{2,1,0:T(8,128)(2,1)S(1)}, u32[]{:S(2)}, u32[]{:S(2)}) collective-permute-start(bf16[8,32,256]{2,1,0:T(8,128)(2,1)S(1)} %get-tuple-element.71), channel_id=1, source_target_pairs={{0,24},{8,16},{16,8},{24,0},{1,25},{9,17},{17,9},{25,1},{2,26},{10... | collective-permute-start | bytes 393224 | tf_op jit(solution)/shard_map/ppermute | solution.py:94
  48.5 38.7 %copy-start.2 = (f32[32,192]{1,0:T(8,128)S(1)}, f32[32,192]{1,0:T(8,128)}, u32[]{:S(2)}) copy-start(f32[32,192]{1,0:T(8,128)} %get-tuple-element.89.refs_10_) | copy-start | bytes 73732
  48.5 38.7 %copy-start.3 = (s32[1,1,2048,1]{2,3,1,0:T(1,128)S(1)}, s32[1,1,2048,1]{2,3,1,0:T(1,128)}, u32[]{:S(2)}) copy-start(s32[1,1,2048,1]{2,3,1,0:T(1,128)} %param.12) | copy-start | bytes 24580
  48.5 38.6 %copy-start.4 = (s32[1,2048]{1,0:T(1,128)S(1)}, s32[1,2048]{1,0:T(1,128)}, u32[]{:S(2)}) copy-start(s32[1,2048]{1,0:T(1,128)} %get-tuple-element.88.refs_9_) | copy-start | bytes 24580
  54.0 10.8 %collective-permute-start.14 = (bf16[2,8,32,256]{3,2,1,0:T(8,128)(2,1)S(1)}, bf16[2,8,32,256]{3,2,1,0:T(8,128)(2,1)S(1)}, u32[]{:S(2)}, u32[]{:S(2)}) collective-permute-start(bf16[2,8,32,256]{3,2,1,0:T(8,128)(2,1)S(1)} %pad_maximum_fusion.3.refs_0_), channel_id=1, source_target_pairs={{0,8},{8,0},{16,24},{24,16},{1,9},{9,1},{17,25},{25,17},{2,10},{10... | collective-permute-start | bytes 786440 | tf_op jit(solution)/shard_map/ppermute | solution.py:94
  54.8 11.4 %collective-permute-start.15 = (bf16[2,8,32,256]{3,2,1,0:T(8,128)(2,1)S(1)}, bf16[2,8,32,256]{3,2,1,0:T(8,128)(2,1)S(1)}, u32[]{:S(2)}, u32[]{:S(2)}) collective-permute-start(bf16[2,8,32,256]{3,2,1,0:T(8,128)(2,1)S(1)} %pad_maximum_fusion.3.refs_0_), channel_id=1, source_target_pairs={{0,16},{8,24},{16,0},{24,8},{1,17},{9,25},{17,1},{25,9},{2,18},{10... | collective-permute-start | bytes 786440 | tf_op jit(solution)/shard_map/ppermute | solution.py:94
  55.7 12.4 %collective-permute-start.16 = (bf16[2,8,32,256]{3,2,1,0:T(8,128)(2,1)S(1)}, bf16[2,8,32,256]{3,2,1,0:T(8,128)(2,1)S(1)}, u32[]{:S(2)}, u32[]{:S(2)}) collective-permute-start(bf16[2,8,32,256]{3,2,1,0:T(8,128)(2,1)S(1)} %pad_maximum_fusion.3.refs_0_), channel_id=1, source_target_pairs={{0,24},{8,16},{16,8},{24,0},{1,25},{9,17},{17,9},{25,1},{2,26},{10... | collective-permute-start | bytes 786440 | tf_op jit(solution)/shard_map/ppermute | solution.py:94
  61.9 6.4 %collective-permute-start.18 = (bf16[4,8,32,256]{3,2,1,0:T(8,128)(2,1)S(1)}, bf16[4,8,32,256]{3,2,1,0:T(8,128)(2,1)S(1)}, u32[]{:S(2)}, u32[]{:S(2)}) collective-permute-start(bf16[4,8,32,256]{3,2,1,0:T(8,128)(2,1)S(1)} %get-tuple-element.79), channel_id=1, source_target_pairs={{0,1},{1,0},{2,3},{3,2},{4,5},{5,4},{6,7},{7,6},{8,9},{9,8},{10,11... | collective-permute-start | bytes 1572872 | tf_op jit(solution)/shard_map/ppermute | solution.py:86
  62.0 15.2 %collective-permute-start.19 = (bf16[4,8,32,256]{3,2,1,0:T(8,128)(2,1)S(1)}, bf16[4,8,32,256]{3,2,1,0:T(8,128)(2,1)S(1)}, u32[]{:S(2)}, u32[]{:S(2)}) collective-permute-start(bf16[4,8,32,256]{3,2,1,0:T(8,128)(2,1)S(1)} %get-tuple-element.80), channel_id=1, source_target_pairs={{0,7},{1,2},{2,1},{3,4},{4,3},{5,6},{6,5},{7,0},{8,15},{9,10},{10,... | collective-permute-start | bytes 1572872 | tf_op jit(solution)/shard_map/ppermute | solution.py:89
  68.2 12.7 %collective-permute-start.17 = (bf16[4,8,32,256]{3,2,1,0:T(8,128)(2,1)S(1)}, bf16[4,8,32,256]{3,2,1,0:T(8,128)(2,1)S(1)}, u32[]{:S(2)}, u32[]{:S(2)}) collective-permute-start(bf16[4,8,32,256]{3,2,1,0:T(8,128)(2,1)S(1)} %pad_maximum_fusion.1), channel_id=1, source_target_pairs={{0,1},{1,0},{2,3},{3,2},{4,5},{5,4},{6,7},{7,6},{8,9},{9,8},{10,11... | collective-permute-start | bytes 1572872 | tf_op jit(solution)/shard_map/ppermute | solution.py:86
  77.4 9.8 %collective-permute-start.20 = (bf16[8,32,256]{2,1,0:T(8,128)(2,1)S(1)}, bf16[8,32,256]{2,1,0:T(8,128)(2,1)S(1)}, u32[]{:S(2)}, u32[]{:S(2)}) collective-permute-start(bf16[8,32,256]{2,1,0:T(8,128)(2,1)S(1)} %get-tuple-element.82), channel_id=1, source_target_pairs={{0,8},{8,0},{16,24},{24,16},{1,9},{9,1},{17,25},{25,17},{2,10},{10... | collective-permute-start | bytes 393224 | tf_op jit(solution)/shard_map/ppermute | solution.py:94
  78.8 8.3 %collective-permute-start.21 = (bf16[8,32,256]{2,1,0:T(8,128)(2,1)S(1)}, bf16[8,32,256]{2,1,0:T(8,128)(2,1)S(1)}, u32[]{:S(2)}, u32[]{:S(2)}) collective-permute-start(bf16[8,32,256]{2,1,0:T(8,128)(2,1)S(1)} %get-tuple-element.83), channel_id=1, source_target_pairs={{0,16},{8,24},{16,0},{24,8},{1,17},{9,25},{17,1},{25,9},{2,18},{10... | collective-permute-start | bytes 393224 | tf_op jit(solution)/shard_map/ppermute | solution.py:94
  79.1 8.0 %collective-permute-start.22 = (bf16[8,32,256]{2,1,0:T(8,128)(2,1)S(1)}, bf16[8,32,256]{2,1,0:T(8,128)(2,1)S(1)}, u32[]{:S(2)}, u32[]{:S(2)}) collective-permute-start(bf16[8,32,256]{2,1,0:T(8,128)(2,1)S(1)} %get-tuple-element.84), channel_id=1, source_target_pairs={{0,24},{8,16},{16,8},{24,0},{1,25},{9,17},{17,9},{25,1},{2,26},{10... | collective-permute-start | bytes 393224 | tf_op jit(solution)/shard_map/ppermute | solution.py:94
  91.2 17.7 %all-to-all-start = ((s16[32,56,128]{2,1,0:T(8,128)(2,1)}), s16[32,56,128]{2,1,0:T(8,128)(2,1)S(1)}, u32[]{:S(2)}, u32[]{:S(2)}) async-start(s16[32,56,128]{2,1,0:T(8,128)(2,1)} %shard_map.94), calls=%async_computation | async-start | bytes 917504 | tf_op jit(solution)/shard_map/all_to_all | solution.py:550

commit v8 on v7

--- a/solution.py
+++ b/solution.py
@@ -97,7 +97,7 @@
     block_shape = (rb_count, bands, width)
     part_shape = (split,) + block_shape
     pass_flops = 2 * bands * rb_count * depth * width * width
-    once = rb_count // 4
+    once = rb_count // 2
 
     def prepare(e_hbm, b_hbm, w_hbm, start_ref, *refs):
         piece_refs, (e_ref, b_ref, w_ref, loaded) = refs[:split], refs[split:]
@@ -460,7 +460,7 @@
     slots, rank, labels, _ = lax.optimization_barrier((slots, rank, labels, start))
     full, matrix, *parts = kernel_call(
         adjoint_first,
-        4,
+        2,
         1,
         [pl.BlockSpec(memory_space=pl.ANY)] + [along((3, part_bands, once * width), 2)] * split,
         [
@@ -478,7 +478,7 @@
 
     zero, rad = kernel_call(
         forward_first,
-        4,
+        2,
         1,
         [VMEM] + [whole((2,) + start_shape)] * split
         + [whole((split,) + start_shape), full_rows],
@@ -493,7 +493,7 @@
 
     adjoint_one, *parts = kernel_call(
         adjoint_second,
-        4,
+        2,
         1,
         [VMEM] + [step_rows] * split + [full_rows],
         [(step_rows, shape(block_shape, F32))] + part_outs,
@@ -506,7 +506,7 @@
 
     one, radiosity = kernel_call(
         forward_second,
-        4,
+        2,
         1,
         [VMEM] + [whole((2,) + block_shape)] * split + [whole(part_shape), full_rows],
         [
@@ -520,7 +520,7 @@
 
     (send,) = kernel_call(
         pack_rows,
-        4,
+        2,
         0,
         [step_rows] * (split + 3)
         + [full_rows, whole((1, rows)), whole((1, rows)), whole((devices, seats))],

time: 113 us -> 112 us (level)
  transfers between devices with their start and end apart: 24 -> 24, of which waited for: 9 -> 9; matrix products, arithmetic and copies ran while one was open for 1% -> 1% of each run, Pallas kernels for 24% -> 23%
where the time goes in v8:
time: 112 us
  waiting for transfers between devices  39 us (35%)
  Pallas kernels  35.8 us (32%)
  starting transfers between devices  32.5 us (29%)
  local copies, waits for them, and re-layouts  2.63 us (2%)
    pallas_call x10, Pallas kernels, kernel_call(): pl.pallas_call(kernel, out_shape=[o for _, o in outs], grid_spec=pltpu.Pr...  35.8 us
    ppermute x15, starting transfers between devices, across(): return lax.ppermute(block, 'band', [(i, i ^ d) for i in range(split)])  17.6 us
    all_to_all x1, waiting for transfers between devices, body(): send = lax.all_to_all(send, ('band', 'patch'), 0, 0, tiled=True)  13.8 us
    ppermute x4, waiting for transfers between devices, outer(): lax.ppermute(block, 'patch', [(i, (i + (1 if i % 2 else -1)) % groups) fo...  13.4 us
    ppermute x15, waiting for transfers between devices, across(): return lax.ppermute(block, 'band', [(i, i ^ d) for i in range(split)])  11.8 us
    ppermute x4, starting transfers between devices, outer(): lax.ppermute(block, 'patch', [(i, (i + (1 if i % 2 else -1)) % groups) fo...  11.7 us
    all_to_all x1, starting transfers between devices, body(): send = lax.all_to_all(send, ('band', 'patch'), 0, 0, tiled=True)  2.92 us
    unnamed x11, local copies, waits for them, and re-layouts  2.55 us
  transfers between devices with their start and end apart: 24, of which 9 were waited for; matrix products, arithmetic and copies ran while one was open for 1% of the time, Pallas kernels for 23%

profile of v8, /device:TPU:0, one launch (start us, length us, event | category | flops | bytes accessed | tf_op | source)
XLA Modules:
  0.0 112.0 jit_solution(15125809131308902286)
XLA Ops:
  0.6 2.0 %shard_map.87 = (bf16[32,8,256]{2,1,0:T(8,128)(2,1)}, s16[3,8,2048]{2,1,0:T(8,128)(2,1)}, s16[3,8,2048]{2,1,0:T(8,128)(2,1)}, s16[3,8,2048]{2,1,0:T(8,128)(2,1)}, s16[3,8,2048]{2,1,0:T(8,128)(2,1)}) custom-call(f32[8,8192]{1,0:T(8,128)} %e_hbm.1, f32[8,8192]{1,0:T(8,128)} %b_hbm.1, f32[8,8192]{1,0:T(8,128)} %w_hbm.1), custom_call_target="tpu_custom_call" | custom-call | tf_op jit(solution)/shard_map/pallas_call | solution.py:54
  2.6 4.6 %collective-permute-start = (bf16[32,8,256]{2,1,0:T(8,128)(2,1)}, bf16[32,8,256]{2,1,0:T(8,128)(2,1)S(1)}, u32[]{:S(2)}, u32[]{:S(2)}) collective-permute-start(bf16[32,8,256]{2,1,0:T(8,128)(2,1)} %get-tuple-element.54), channel_id=1, source_target_pairs={{0,7},{1,2},{2,1},{3,4},{4,3},{5,6},{6,5},{7,0},{8,15},{9,10},{10,... | collective-permute-start | bytes 393224 | tf_op jit(solution)/shard_map/ppermute | solution.py:89
  7.2 1.5 %collective-permute-start.1 = (s16[3,8,2048]{2,1,0:T(8,128)(2,1)}, s16[3,8,2048]{2,1,0:T(8,128)(2,1)S(1)}, u32[]{:S(2)}, u32[]{:S(2)}) collective-permute-start(s16[3,8,2048]{2,1,0:T(8,128)(2,1)} %get-tuple-element.51), channel_id=1, source_target_pairs={{0,8},{8,0},{16,24},{24,16},{1,9},{9,1},{17,25},{25,17},{2,10},{10... | collective-permute-start | bytes 294920 | tf_op jit(solution)/shard_map/ppermute | solution.py:94
  8.7 1.5 %collective-permute-start.2 = (s16[3,8,2048]{2,1,0:T(8,128)(2,1)}, s16[3,8,2048]{2,1,0:T(8,128)(2,1)S(1)}, u32[]{:S(2)}, u32[]{:S(2)}) collective-permute-start(s16[3,8,2048]{2,1,0:T(8,128)(2,1)} %get-tuple-element.52), channel_id=1, source_target_pairs={{0,16},{8,24},{16,0},{24,8},{1,17},{9,25},{17,1},{25,9},{2,18},{10... | collective-permute-start | bytes 294920 | tf_op jit(solution)/shard_map/ppermute | solution.py:94
  10.2 0.5 collective-permute-start.3
  10.7 2.4 %shard_map.86 = (s32[8,16]{1,0:T(8,128)}, s32[1,2048]{1,0:T(1,128)}, f32[32,192]{1,0:T(8,128)}) custom-call(s32[8,16]{1,0:T(8,128)} %bitcast.18, s32[1,2048]{1,0:T(1,128)} %bitcast.11, s32[1,2048]{1,0:T(1,128)} %bitcast.17), custom_call_target="tpu_custom_call" | custom-call | tf_op jit(solution)/shard_map/pallas_call | solution.py:54
  13.1 1.3 %collective-permute-done.2.refs_2_ = s16[3,8,2048]{2,1,0:T(8,128)(2,1)S(1)} collective-permute-done((s16[3,8,2048]{2,1,0:T(8,128)(2,1)}, s16[3,8,2048]{2,1,0:T(8,128)(2,1)S(1)}, u32[]{:S(2)}, u32[]{:S(2)}) %collective-permute-start.2) | collective-permute-done | bytes 98336 | tf_op jit(solution)/shard_map/ppermute | solution.py:94
  14.3 1.6 %collective-permute-done.3.refs_3_ = s16[3,8,2048]{2,1,0:T(8,128)(2,1)S(1)} collective-permute-done((s16[3,8,2048]{2,1,0:T(8,128)(2,1)}, s16[3,8,2048]{2,1,0:T(8,128)(2,1)S(1)}, u32[]{:S(2)}, u32[]{:S(2)}) %collective-permute-start.3) | collective-permute-done | bytes 98336 | tf_op jit(solution)/shard_map/ppermute | solution.py:94
  15.9 0.9 pad_maximum_fusion.2.refs_0_
  16.9 0.6 collective-permute-start.4
  17.5 0.5 collective-permute-start.5
  18.0 2.4 %collective-permute-start.6 = (bf16[2,32,8,256]{3,2,1,0:T(8,128)(2,1)S(1)}, bf16[2,32,8,256]{3,2,1,0:T(8,128)(2,1)S(1)}, u32[]{:S(2)}, u32[]{:S(2)}) collective-permute-start(bf16[2,32,8,256]{3,2,1,0:T(8,128)(2,1)S(1)} %pad_maximum_fusion.2.refs_0_), channel_id=1, source_target_pairs={{0,24},{8,16},{16,8},{24,0},{1,25},{9,17},{17,9},{25,1},{2,26},{10... | collective-permute-start | bytes 786440 | tf_op jit(solution)/shard_map/ppermute | solution.py:94
  20.4 0.9 copy-done
  21.3 0.7 copy-done.1
  22.0 7.3 %shard_map.88 = (f32[3,8,32,256]{3,2,1,0:T(8,128)S(1)}, bf16[8,16,256,256]{3,2,1,0:T(8,128)(2,1)S(1)}, f32[4,8,32,256]{3,2,1,0:T(8,128)S(1)}, bf16[4,8,32,256]{3...) custom-call(s32[8,16]{1,0:T(8,128)S(1)} %copy-done.1, bf16[8,16,256,256]{3,2,1,0:T(8,128)(2,1)} %bitcast.13, ...), custom_call_target="tpu_custom_call" | custom-call | flops 536870912 | bytes 16777216 | tf_op jit(solution)/shard_map/pallas_call | solution.py:54
  29.4 0.1 pad_maximum_fusion
  29.5 0.1 collective-permute-start.7
  29.6 2.3 %collective-permute-start.10 = (bf16[4,8,32,256]{3,2,1,0:T(8,128)(2,1)S(1)}, bf16[4,8,32,256]{3,2,1,0:T(8,128)(2,1)S(1)}, u32[]{:S(2)}, u32[]{:S(2)}) collective-permute-start(bf16[4,8,32,256]{3,2,1,0:T(8,128)(2,1)S(1)} %get-tuple-element.66), channel_id=1, source_target_pairs={{0,7},{1,2},{2,1},{3,4},{4,3},{5,6},{6,5},{7,0},{8,15},{9,10},{10,... | collective-permute-start | bytes 1572872 | tf_op jit(solution)/shard_map/ppermute | solution.py:89
  31.9 6.1 %shard_map.89 = (f32[8,32,256]{2,1,0:T(8,128)S(1)}, bf16[8,32,256]{2,1,0:T(8,128)(2,1)S(1)}) custom-call(s32[8,16]{1,0:T(8,128)S(1)} %copy-done.1, bf16[8,16,256,256]{3,2,1,0:T(8,128)(2,1)S(1)} %get-tuple-element.57.m_ref, bf16[2,32,8,256]{3,2,1,0:T(8,128)(2,1)S(1)} %pad_maximum_fusion.2.refs_0_, bf16[2,32,8,256]{3,2,1,0:T(8,128)(2,1)S(1)} %collective-permute-done.4.refs_1_, ...), custom_call_target="tpu_custom_call" | custom-call | flops 536870912 | bytes 16777216 | tf_op jit(solution)/shard_map/pallas_call | solution.py:54
  37.9 2.0 %collective-permute-start.8 = (bf16[8,32,256]{2,1,0:T(8,128)(2,1)S(1)}, bf16[8,32,256]{2,1,0:T(8,128)(2,1)S(1)}, u32[]{:S(2)}, u32[]{:S(2)}) collective-permute-start(bf16[8,32,256]{2,1,0:T(8,128)(2,1)S(1)} %get-tuple-element.64), channel_id=1, source_target_pairs={{0,7},{1,2},{2,1},{3,4},{4,3},{5,6},{6,5},{7,0},{8,15},{9,10},{10,... | collective-permute-start | bytes 393224 | tf_op jit(solution)/shard_map/ppermute | solution.py:89
  40.0 4.8 %collective-permute-done.10.far_ref = bf16[4,8,32,256]{3,2,1,0:T(8,128)(2,1)S(1)} collective-permute-done((bf16[4,8,32,256]{3,2,1,0:T(8,128)(2,1)S(1)}, bf16[4,8,32,256]{3,2,1,0:T(8,128)(2,1)S(1)}, u32[]{:S(2)}, u32[]{:S(2)}) %collective-permute-start.10) | collective-permute-done | bytes 524320 | tf_op jit(solution)/shard_map/ppermute | solution.py:89
  44.8 0.2 shard_map.90
  45.0 1.2 %collective-permute-start.11 = (bf16[8,32,256]{2,1,0:T(8,128)(2,1)S(1)}, bf16[8,32,256]{2,1,0:T(8,128)(2,1)S(1)}, u32[]{:S(2)}, u32[]{:S(2)}) collective-permute-start(bf16[8,32,256]{2,1,0:T(8,128)(2,1)S(1)} %get-tuple-element.69), channel_id=1, source_target_pairs={{0,8},{8,0},{16,24},{24,16},{1,9},{9,1},{17,25},{25,17},{2,10},{10... | collective-permute-start | bytes 393224 | tf_op jit(solution)/shard_map/ppermute | solution.py:94
  46.2 2.4 %collective-permute-start.13 = (bf16[8,32,256]{2,1,0:T(8,128)(2,1)S(1)}, bf16[8,32,256]{2,1,0:T(8,128)(2,1)S(1)}, u32[]{:S(2)}, u32[]{:S(2)}) collective-permute-start(bf16[8,32,256]{2,1,0:T(8,128)(2,1)S(1)} %get-tuple-element.71), channel_id=1, source_target_pairs={{0,24},{8,16},{16,8},{24,0},{1,25},{9,17},{17,9},{25,1},{2,26},{10... | collective-permute-start | bytes 393224 | tf_op jit(solution)/shard_map/ppermute | solution.py:94
  48.6 0.0 copy-start.3
  48.6 2.2 %collective-permute-done.11.refs_1_ = bf16[8,32,256]{2,1,0:T(8,128)(2,1)S(1)} collective-permute-done((bf16[8,32,256]{2,1,0:T(8,128)(2,1)S(1)}, bf16[8,32,256]{2,1,0:T(8,128)(2,1)S(1)}, u32[]{:S(2)}, u32[]{:S(2)}) %collective-permute-start.11) | collective-permute-done | bytes 131104 | tf_op jit(solution)/shard_map/ppermute | solution.py:94
  50.9 3.1 %collective-permute-done.12.refs_2_ = bf16[8,32,256]{2,1,0:T(8,128)(2,1)S(1)} collective-permute-done((bf16[8,32,256]{2,1,0:T(8,128)(2,1)S(1)}, bf16[8,32,256]{2,1,0:T(8,128)(2,1)S(1)}, u32[]{:S(2)}, u32[]{:S(2)}) %collective-permute-start.12) | collective-permute-done | bytes 131104 | tf_op jit(solution)/shard_map/ppermute | solution.py:94
  54.0 0.9 collective-permute-start.14
  54.9 0.8 collective-permute-start.15
  55.7 1.8 %collective-permute-start.16 = (bf16[2,8,32,256]{3,2,1,0:T(8,128)(2,1)S(1)}, bf16[2,8,32,256]{3,2,1,0:T(8,128)(2,1)S(1)}, u32[]{:S(2)}, u32[]{:S(2)}) collective-permute-start(bf16[2,8,32,256]{3,2,1,0:T(8,128)(2,1)S(1)} %pad_maximum_fusion.3.refs_0_), channel_id=1, source_target_pairs={{0,24},{8,16},{16,8},{24,0},{1,25},{9,17},{17,9},{25,1},{2,26},{10... | collective-permute-start | bytes 786440 | tf_op jit(solution)/shard_map/ppermute | solution.py:94
  57.5 4.2 %shard_map.91 = (f32[8,32,256]{2,1,0:T(8,128)S(1)}, f32[4,8,32,256]{3,2,1,0:T(8,128)S(1)}, bf16[4,8,32,256]{3,2,1,0:T(8,128)(2,1)S(1)}, bf16[4,8,32,256]{3,2,1,0:T(8,128)(2,1)S(1)}) custom-call(s32[8,16]{1,0:T(8,128)S(1)} %copy-done.1, bf16[8,16,256,256]{3,2,1,0:T(8,128)(2,1)S(1)} %get-tuple-element.57.m_ref, f32[8,32,256]{2,1,0:T(8,128)S(1)} %get-tuple-element.68.refs_0_, ...), custom_call_target="tpu_custom_call" | custom-call | flops 536870912 | bytes 16777216 | tf_op jit(solution)/shard_map/pallas_call | solution.py:54
  61.7 0.1 collective-permute-start.18
  61.8 2.8 %collective-permute-start.19 = (bf16[4,8,32,256]{3,2,1,0:T(8,128)(2,1)S(1)}, bf16[4,8,32,256]{3,2,1,0:T(8,128)(2,1)S(1)}, u32[]{:S(2)}, u32[]{:S(2)}) collective-permute-start(bf16[4,8,32,256]{3,2,1,0:T(8,128)(2,1)S(1)} %get-tuple-element.80), channel_id=1, source_target_pairs={{0,7},{1,2},{2,1},{3,4},{4,3},{5,6},{6,5},{7,0},{8,15},{9,10},{10,... | collective-permute-start | bytes 1572872 | tf_op jit(solution)/shard_map/ppermute | solution.py:89
  64.6 1.7 %collective-permute-done.15.refs_2_ = bf16[2,8,32,256]{3,2,1,0:T(8,128)(2,1)S(1)} collective-permute-done((bf16[2,8,32,256]{3,2,1,0:T(8,128)(2,1)S(1)}, bf16[2,8,32,256]{3,2,1,0:T(8,128)(2,1)S(1)}, u32[]{:S(2)}, u32[]{:S(2)}) %collective-permute-start.15) | collective-permute-done | bytes 262176 | tf_op jit(solution)/shard_map/ppermute | solution.py:94
  66.2 1.9 %collective-permute-done.16.refs_3_ = bf16[2,8,32,256]{3,2,1,0:T(8,128)(2,1)S(1)} collective-permute-done((bf16[2,8,32,256]{3,2,1,0:T(8,128)(2,1)S(1)}, bf16[2,8,32,256]{3,2,1,0:T(8,128)(2,1)S(1)}, u32[]{:S(2)}, u32[]{:S(2)}) %collective-permute-start.16) | collective-permute-done | bytes 262176 | tf_op jit(solution)/shard_map/ppermute | solution.py:94
  68.2 0.1 pad_maximum_fusion.1
  68.2 0.1 collective-permute-start.17
  68.3 8.6 %collective-permute-done.19.far_ref = bf16[4,8,32,256]{3,2,1,0:T(8,128)(2,1)S(1)} collective-permute-done((bf16[4,8,32,256]{3,2,1,0:T(8,128)(2,1)S(1)}, bf16[4,8,32,256]{3,2,1,0:T(8,128)(2,1)S(1)}, u32[]{:S(2)}, u32[]{:S(2)}) %collective-permute-start.19) | collective-permute-done | bytes 524320 | tf_op jit(solution)/shard_map/ppermute | solution.py:89
  77.0 0.2 shard_map.93
  77.1 1.6 %collective-permute-start.20 = (bf16[8,32,256]{2,1,0:T(8,128)(2,1)S(1)}, bf16[8,32,256]{2,1,0:T(8,128)(2,1)S(1)}, u32[]{:S(2)}, u32[]{:S(2)}) collective-permute-start(bf16[8,32,256]{2,1,0:T(8,128)(2,1)S(1)} %get-tuple-element.82), channel_id=1, source_target_pairs={{0,8},{8,0},{16,24},{24,16},{1,9},{9,1},{17,25},{25,17},{2,10},{10... | collective-permute-start | bytes 393224 | tf_op jit(solution)/shard_map/ppermute | solution.py:94
  78.7 0.2 collective-permute-start.21
  78.9 1.8 %collective-permute-start.22 = (bf16[8,32,256]{2,1,0:T(8,128)(2,1)S(1)}, bf16[8,32,256]{2,1,0:T(8,128)(2,1)S(1)}, u32[]{:S(2)}, u32[]{:S(2)}) collective-permute-start(bf16[8,32,256]{2,1,0:T(8,128)(2,1)S(1)} %get-tuple-element.84), channel_id=1, source_target_pairs={{0,24},{8,16},{16,8},{24,0},{1,25},{9,17},{17,9},{25,1},{2,26},{10... | collective-permute-start | bytes 393224 | tf_op jit(solution)/shard_map/ppermute | solution.py:94
  80.7 5.9 %shard_map.92 = (f32[8,32,256]{2,1,0:T(8,128)S(1)}, f32[32,2048]{1,0:T(8,128)S(1)}) custom-call(s32[8,16]{1,0:T(8,128)S(1)} %copy-done.1, bf16[8,16,256,256]{3,2,1,0:T(8,128)(2,1)S(1)} %get-tuple-element.57.m_ref, bf16[2,8,32,256]{3,2,1,0:T(8,128)(2,1)S(1)} %pad_maximum_fusion.3.refs_0_, bf16[2,8,32,256]{3,2,1,0:T(8,128)(2,1)S(1)} %collective-permute-done.14.refs_1_, ...), custom_call_target="tpu_custom_call" | custom-call | flops 536870912 | bytes 16777216 | tf_op jit(solution)/shard_map/pallas_call | solution.py:54
  86.7 3.8 %shard_map.94 = s16[32,56,128]{2,1,0:T(8,128)(2,1)} custom-call(f32[8,32,256]{2,1,0:T(8,128)S(1)} %get-tuple-element.81.refs_0_, bf16[8,32,256]{2,1,0:T(8,128)(2,1)S(1)} %collective-permute-done.20.refs_1_, bf16[8,32,256]{2,1,0:T(8,128)(2,1)S(1)} %collective-permute-done.21.refs_2_, bf16[8,32,256]{2,1,0:T(8,128)(2,1)S(1)} %collective-permute-done.22.refs_3_, ...), custom_call_target="tpu_custom_call" | custom-call | tf_op jit(solution)/shard_map/pallas_call | solution.py:54
  90.5 2.9 %all-to-all-start = ((s16[32,56,128]{2,1,0:T(8,128)(2,1)}), s16[32,56,128]{2,1,0:T(8,128)(2,1)S(1)}, u32[]{:S(2)}, u32[]{:S(2)}) async-start(s16[32,56,128]{2,1,0:T(8,128)(2,1)} %shard_map.94), calls=%async_computation | async-start | bytes 917504 | tf_op jit(solution)/shard_map/all_to_all | solution.py:550
  93.4 1.0 copy.9
  94.4 13.8 %all-to-all-done.got_ref = s16[32,56,128]{2,1,0:T(8,128)(2,1)S(1)} async-done(((s16[32,56,128]{2,1,0:T(8,128)(2,1)}), s16[32,56,128]{2,1,0:T(8,128)(2,1)S(1)}, u32[]{:S(2)}, u32[]{:S(2)}) %all-to-all-start) | async-done | bytes 458784 | tf_op jit(solution)/shard_map/all_to_all | solution.py:550
  108.2 3.8 %shard_map.95 = f32[32,1024]{1,0:T(8,128)} custom-call(s16[32,56,128]{2,1,0:T(8,128)(2,1)S(1)} %all-to-all-done.got_ref), custom_call_target="tpu_custom_call" | custom-call | tf_op jit(solution)/shard_map/pallas_call | solution.py:54
  (33 shorter events, 0.2 us)
Async XLA Ops:
  2.6 13.3 %collective-permute-start = (bf16[32,8,256]{2,1,0:T(8,128)(2,1)}, bf16[32,8,256]{2,1,0:T(8,128)(2,1)S(1)}, u32[]{:S(2)}, u32[]{:S(2)}) collective-permute-start(bf16[32,8,256]{2,1,0:T(8,128)(2,1)} %get-tuple-element.54), channel_id=1, source_target_pairs={{0,7},{1,2},{2,1},{3,4},{4,3},{5,6},{6,5},{7,0},{8,15},{9,10},{10,... | collective-permute-start | bytes 393224 | tf_op jit(solution)/shard_map/ppermute | solution.py:89
  7.2 5.9 %collective-permute-start.1 = (s16[3,8,2048]{2,1,0:T(8,128)(2,1)}, s16[3,8,2048]{2,1,0:T(8,128)(2,1)S(1)}, u32[]{:S(2)}, u32[]{:S(2)}) collective-permute-start(s16[3,8,2048]{2,1,0:T(8,128)(2,1)} %get-tuple-element.51), channel_id=1, source_target_pairs={{0,8},{8,0},{16,24},{24,16},{1,9},{9,1},{17,25},{25,17},{2,10},{10... | collective-permute-start | bytes 294920 | tf_op jit(solution)/shard_map/ppermute | solution.py:94
  8.7 5.7 %collective-permute-start.2 = (s16[3,8,2048]{2,1,0:T(8,128)(2,1)}, s16[3,8,2048]{2,1,0:T(8,128)(2,1)S(1)}, u32[]{:S(2)}, u32[]{:S(2)}) collective-permute-start(s16[3,8,2048]{2,1,0:T(8,128)(2,1)} %get-tuple-element.52), channel_id=1, source_target_pairs={{0,16},{8,24},{16,0},{24,8},{1,17},{9,25},{17,1},{25,9},{2,18},{10... | collective-permute-start | bytes 294920 | tf_op jit(solution)/shard_map/ppermute | solution.py:94
  10.2 5.7 %collective-permute-start.3 = (s16[3,8,2048]{2,1,0:T(8,128)(2,1)}, s16[3,8,2048]{2,1,0:T(8,128)(2,1)S(1)}, u32[]{:S(2)}, u32[]{:S(2)}) collective-permute-start(s16[3,8,2048]{2,1,0:T(8,128)(2,1)} %get-tuple-element.53), channel_id=1, source_target_pairs={{0,24},{8,16},{16,8},{24,0},{1,25},{9,17},{17,9},{25,1},{2,26},{10... | collective-permute-start | bytes 294920 | tf_op jit(solution)/shard_map/ppermute | solution.py:94
  16.9 12.4 %collective-permute-start.4 = (bf16[2,32,8,256]{3,2,1,0:T(8,128)(2,1)S(1)}, bf16[2,32,8,256]{3,2,1,0:T(8,128)(2,1)S(1)}, u32[]{:S(2)}, u32[]{:S(2)}) collective-permute-start(bf16[2,32,8,256]{3,2,1,0:T(8,128)(2,1)S(1)} %pad_maximum_fusion.2.refs_0_), channel_id=1, source_target_pairs={{0,8},{8,0},{16,24},{24,16},{1,9},{9,1},{17,25},{25,17},{2,10},{10... | collective-permute-start | bytes 786440 | tf_op jit(solution)/shard_map/ppermute | solution.py:94
  17.5 11.8 %collective-permute-start.5 = (bf16[2,32,8,256]{3,2,1,0:T(8,128)(2,1)S(1)}, bf16[2,32,8,256]{3,2,1,0:T(8,128)(2,1)S(1)}, u32[]{:S(2)}, u32[]{:S(2)}) collective-permute-start(bf16[2,32,8,256]{3,2,1,0:T(8,128)(2,1)S(1)} %pad_maximum_fusion.2.refs_0_), channel_id=1, source_target_pairs={{0,16},{8,24},{16,0},{24,8},{1,17},{9,25},{17,1},{25,9},{2,18},{10... | collective-permute-start | bytes 786440 | tf_op jit(solution)/shard_map/ppermute | solution.py:94
  18.0 11.3 %collective-permute-start.6 = (bf16[2,32,8,256]{3,2,1,0:T(8,128)(2,1)S(1)}, bf16[2,32,8,256]{3,2,1,0:T(8,128)(2,1)S(1)}, u32[]{:S(2)}, u32[]{:S(2)}) collective-permute-start(bf16[2,32,8,256]{3,2,1,0:T(8,128)(2,1)S(1)} %pad_maximum_fusion.2.refs_0_), channel_id=1, source_target_pairs={{0,24},{8,16},{16,8},{24,0},{1,25},{9,17},{17,9},{25,1},{2,26},{10... | collective-permute-start | bytes 786440 | tf_op jit(solution)/shard_map/ppermute | solution.py:94
  20.4 0.9 copy-start
  21.3 0.7 copy-start.1
  29.5 2.4 %collective-permute-start.7 = (bf16[4,32,8,256]{3,2,1,0:T(8,128)(2,1)S(1)}, bf16[4,32,8,256]{3,2,1,0:T(8,128)(2,1)S(1)}, u32[]{:S(2)}, u32[]{:S(2)}) collective-permute-start(bf16[4,32,8,256]{3,2,1,0:T(8,128)(2,1)S(1)} %pad_maximum_fusion), channel_id=1, source_target_pairs={{0,1},{1,0},{2,3},{3,2},{4,5},{5,4},{6,7},{7,6},{8,9},{9,8},{10,11... | collective-permute-start | bytes 1572872 | tf_op jit(solution)/shard_map/ppermute | solution.py:86
  29.6 15.3 %collective-permute-start.10 = (bf16[4,8,32,256]{3,2,1,0:T(8,128)(2,1)S(1)}, bf16[4,8,32,256]{3,2,1,0:T(8,128)(2,1)S(1)}, u32[]{:S(2)}, u32[]{:S(2)}) collective-permute-start(bf16[4,8,32,256]{3,2,1,0:T(8,128)(2,1)S(1)} %get-tuple-element.66), channel_id=1, source_target_pairs={{0,7},{1,2},{2,1},{3,4},{4,3},{5,6},{6,5},{7,0},{8,15},{9,10},{10,... | collective-permute-start | bytes 1572872 | tf_op jit(solution)/shard_map/ppermute | solution.py:89
  31.8 13.0 %collective-permute-start.9 = (bf16[4,8,32,256]{3,2,1,0:T(8,128)(2,1)S(1)}, bf16[4,8,32,256]{3,2,1,0:T(8,128)(2,1)S(1)}, u32[]{:S(2)}, u32[]{:S(2)}) collective-permute-start(bf16[4,8,32,256]{3,2,1,0:T(8,128)(2,1)S(1)} %get-tuple-element.65), channel_id=1, source_target_pairs={{0,1},{1,0},{2,3},{3,2},{4,5},{5,4},{6,7},{7,6},{8,9},{9,8},{10,11... | collective-permute-start | bytes 1572872 | tf_op jit(solution)/shard_map/ppermute | solution.py:86
  37.9 10.6 %collective-permute-start.8 = (bf16[8,32,256]{2,1,0:T(8,128)(2,1)S(1)}, bf16[8,32,256]{2,1,0:T(8,128)(2,1)S(1)}, u32[]{:S(2)}, u32[]{:S(2)}) collective-permute-start(bf16[8,32,256]{2,1,0:T(8,128)(2,1)S(1)} %get-tuple-element.64), channel_id=1, source_target_pairs={{0,7},{1,2},{2,1},{3,4},{4,3},{5,6},{6,5},{7,0},{8,15},{9,10},{10,... | collective-permute-start | bytes 393224 | tf_op jit(solution)/shard_map/ppermute | solution.py:89
  45.0 5.9 %collective-permute-start.11 = (bf16[8,32,256]{2,1,0:T(8,128)(2,1)S(1)}, bf16[8,32,256]{2,1,0:T(8,128)(2,1)S(1)}, u32[]{:S(2)}, u32[]{:S(2)}) collective-permute-start(bf16[8,32,256]{2,1,0:T(8,128)(2,1)S(1)} %get-tuple-element.69), channel_id=1, source_target_pairs={{0,8},{8,0},{16,24},{24,16},{1,9},{9,1},{17,25},{25,17},{2,10},{10... | collective-permute-start | bytes 393224 | tf_op jit(solution)/shard_map/ppermute | solution.py:94
  46.2 7.8 %collective-permute-start.12 = (bf16[8,32,256]{2,1,0:T(8,128)(2,1)S(1)}, bf16[8,32,256]{2,1,0:T(8,128)(2,1)S(1)}, u32[]{:S(2)}, u32[]{:S(2)}) collective-permute-start(bf16[8,32,256]{2,1,0:T(8,128)(2,1)S(1)} %get-tuple-element.70), channel_id=1, source_target_pairs={{0,16},{8,24},{16,0},{24,8},{1,17},{9,25},{17,1},{25,9},{2,18},{10... | collective-permute-start | bytes 393224 | tf_op jit(solution)/shard_map/ppermute | solution.py:94
  46.2 7.8 %collective-permute-start.13 = (bf16[8,32,256]{2,1,0:T(8,128)(2,1)S(1)}, bf16[8,32,256]{2,1,0:T(8,128)(2,1)S(1)}, u32[]{:S(2)}, u32[]{:S(2)}) collective-permute-start(bf16[8,32,256]{2,1,0:T(8,128)(2,1)S(1)} %get-tuple-element.71), channel_id=1, source_target_pairs={{0,24},{8,16},{16,8},{24,0},{1,25},{9,17},{17,9},{25,1},{2,26},{10... | collective-permute-start | bytes 393224 | tf_op jit(solution)/shard_map/ppermute | solution.py:94
  48.6 38.1 %copy-start.2 = (f32[32,192]{1,0:T(8,128)S(1)}, f32[32,192]{1,0:T(8,128)}, u32[]{:S(2)}) copy-start(f32[32,192]{1,0:T(8,128)} %get-tuple-element.89.refs_10_) | copy-start | bytes 73732
  48.6 38.1 %copy-start.3 = (s32[1,1,2048,1]{2,3,1,0:T(1,128)S(1)}, s32[1,1,2048,1]{2,3,1,0:T(1,128)}, u32[]{:S(2)}) copy-start(s32[1,1,2048,1]{2,3,1,0:T(1,128)} %param.12) | copy-start | bytes 24580
  48.6 38.1 %copy-start.4 = (s32[1,2048]{1,0:T(1,128)S(1)}, s32[1,2048]{1,0:T(1,128)}, u32[]{:S(2)}) copy-start(s32[1,2048]{1,0:T(1,128)} %get-tuple-element.88.refs_9_) | copy-start | bytes 24580
  54.0 10.6 %collective-permute-start.14 = (bf16[2,8,32,256]{3,2,1,0:T(8,128)(2,1)S(1)}, bf16[2,8,32,256]{3,2,1,0:T(8,128)(2,1)S(1)}, u32[]{:S(2)}, u32[]{:S(2)}) collective-permute-start(bf16[2,8,32,256]{3,2,1,0:T(8,128)(2,1)S(1)} %pad_maximum_fusion.3.refs_0_), channel_id=1, source_target_pairs={{0,8},{8,0},{16,24},{24,16},{1,9},{9,1},{17,25},{25,17},{2,10},{10... | collective-permute-start | bytes 786440 | tf_op jit(solution)/shard_map/ppermute | solution.py:94
  54.9 11.4 %collective-permute-start.15 = (bf16[2,8,32,256]{3,2,1,0:T(8,128)(2,1)S(1)}, bf16[2,8,32,256]{3,2,1,0:T(8,128)(2,1)S(1)}, u32[]{:S(2)}, u32[]{:S(2)}) collective-permute-start(bf16[2,8,32,256]{3,2,1,0:T(8,128)(2,1)S(1)} %pad_maximum_fusion.3.refs_0_), channel_id=1, source_target_pairs={{0,16},{8,24},{16,0},{24,8},{1,17},{9,25},{17,1},{25,9},{2,18},{10... | collective-permute-start | bytes 786440 | tf_op jit(solution)/shard_map/ppermute | solution.py:94
  55.7 12.4 %collective-permute-start.16 = (bf16[2,8,32,256]{3,2,1,0:T(8,128)(2,1)S(1)}, bf16[2,8,32,256]{3,2,1,0:T(8,128)(2,1)S(1)}, u32[]{:S(2)}, u32[]{:S(2)}) collective-permute-start(bf16[2,8,32,256]{3,2,1,0:T(8,128)(2,1)S(1)} %pad_maximum_fusion.3.refs_0_), channel_id=1, source_target_pairs={{0,24},{8,16},{16,8},{24,0},{1,25},{9,17},{17,9},{25,1},{2,26},{10... | collective-permute-start | bytes 786440 | tf_op jit(solution)/shard_map/ppermute | solution.py:94
  61.7 6.6 %collective-permute-start.18 = (bf16[4,8,32,256]{3,2,1,0:T(8,128)(2,1)S(1)}, bf16[4,8,32,256]{3,2,1,0:T(8,128)(2,1)S(1)}, u32[]{:S(2)}, u32[]{:S(2)}) collective-permute-start(bf16[4,8,32,256]{3,2,1,0:T(8,128)(2,1)S(1)} %get-tuple-element.79), channel_id=1, source_target_pairs={{0,1},{1,0},{2,3},{3,2},{4,5},{5,4},{6,7},{7,6},{8,9},{9,8},{10,11... | collective-permute-start | bytes 1572872 | tf_op jit(solution)/shard_map/ppermute | solution.py:86
  61.8 15.2 %collective-permute-start.19 = (bf16[4,8,32,256]{3,2,1,0:T(8,128)(2,1)S(1)}, bf16[4,8,32,256]{3,2,1,0:T(8,128)(2,1)S(1)}, u32[]{:S(2)}, u32[]{:S(2)}) collective-permute-start(bf16[4,8,32,256]{3,2,1,0:T(8,128)(2,1)S(1)} %get-tuple-element.80), channel_id=1, source_target_pairs={{0,7},{1,2},{2,1},{3,4},{4,3},{5,6},{6,5},{7,0},{8,15},{9,10},{10,... | collective-permute-start | bytes 1572872 | tf_op jit(solution)/shard_map/ppermute | solution.py:89
  68.2 12.4 %collective-permute-start.17 = (bf16[4,8,32,256]{3,2,1,0:T(8,128)(2,1)S(1)}, bf16[4,8,32,256]{3,2,1,0:T(8,128)(2,1)S(1)}, u32[]{:S(2)}, u32[]{:S(2)}) collective-permute-start(bf16[4,8,32,256]{3,2,1,0:T(8,128)(2,1)S(1)} %pad_maximum_fusion.1), channel_id=1, source_target_pairs={{0,1},{1,0},{2,3},{3,2},{4,5},{5,4},{6,7},{7,6},{8,9},{9,8},{10,11... | collective-permute-start | bytes 1572872 | tf_op jit(solution)/shard_map/ppermute | solution.py:86
  77.1 9.5 %collective-permute-start.20 = (bf16[8,32,256]{2,1,0:T(8,128)(2,1)S(1)}, bf16[8,32,256]{2,1,0:T(8,128)(2,1)S(1)}, u32[]{:S(2)}, u32[]{:S(2)}) collective-permute-start(bf16[8,32,256]{2,1,0:T(8,128)(2,1)S(1)} %get-tuple-element.82), channel_id=1, source_target_pairs={{0,8},{8,0},{16,24},{24,16},{1,9},{9,1},{17,25},{25,17},{2,10},{10... | collective-permute-start | bytes 393224 | tf_op jit(solution)/shard_map/ppermute | solution.py:94
  78.7 7.9 %collective-permute-start.21 = (bf16[8,32,256]{2,1,0:T(8,128)(2,1)S(1)}, bf16[8,32,256]{2,1,0:T(8,128)(2,1)S(1)}, u32[]{:S(2)}, u32[]{:S(2)}) collective-permute-start(bf16[8,32,256]{2,1,0:T(8,128)(2,1)S(1)} %get-tuple-element.83), channel_id=1, source_target_pairs={{0,16},{8,24},{16,0},{24,8},{1,17},{9,25},{17,1},{25,9},{2,18},{10... | collective-permute-start | bytes 393224 | tf_op jit(solution)/shard_map/ppermute | solution.py:94
  78.9 7.8 %collective-permute-start.22 = (bf16[8,32,256]{2,1,0:T(8,128)(2,1)S(1)}, bf16[8,32,256]{2,1,0:T(8,128)(2,1)S(1)}, u32[]{:S(2)}, u32[]{:S(2)}) collective-permute-start(bf16[8,32,256]{2,1,0:T(8,128)(2,1)S(1)} %get-tuple-element.84), channel_id=1, source_target_pairs={{0,24},{8,16},{16,8},{24,0},{1,25},{9,17},{17,9},{25,1},{2,26},{10... | collective-permute-start | bytes 393224 | tf_op jit(solution)/shard_map/ppermute | solution.py:94
  90.5 17.7 %all-to-all-start = ((s16[32,56,128]{2,1,0:T(8,128)(2,1)}), s16[32,56,128]{2,1,0:T(8,128)(2,1)S(1)}, u32[]{:S(2)}, u32[]{:S(2)}) async-start(s16[32,56,128]{2,1,0:T(8,128)(2,1)} %shard_map.94), calls=%async_computation | async-start | bytes 917504 | tf_op jit(solution)/shard_map/all_to_all | solution.py:550
